TPU v7x, 32 devices: a whole 2x2x4 slice. The times are simulated.
32 devices in a mesh: prow: 8 (over y, x, core), pcol: 4 (over z).
Axes of the slice: x: 2, y: 2, z: 4, core: 2. Of those that a mesh axis runs over, the one named last changes fastest.
Arguments:
- panel: float32 [32768, 512], P('prow', 'pcol'), may hold values from -0.08 to 0.08
- slab: float32 [32768, 2048], P('prow', 'pcol'), may hold values from -6 to 6
- pivots: int32 [512], replicated, may hold values from 512 to 32767, as said below
- diag_inverse: float32 [512, 512], replicated, as said below
Outputs:
- updated: float32 [32768, 2048], P('prow', 'pcol')
Inputs may be any that keep to these rules, and one draw needn't show every extreme that they name: `pivots`: 512 distinct row indices, each below the diagonal block; their owners along prow are uneven. `diag_inverse`: unit lower triangular.
All inputs are finite; a program needn't handle non-finite values.
Results may differ from a plain program's by a relative error of at most 0.000053.
Values sent between devices are 32-bit elements; how exact they have to be, the bound alone decides.
No kernel may reach another device: no remote copies, remote signals or barrier semaphores. Data moves between devices by JAX's collectives and lax.ppermute only.
A program may use at most 128 MiB of HBM per device.

v0:
```python
import jax
import jax.numpy as jnp
from jax import lax
from jax.sharding import PartitionSpec as P


def from_root(value, axis, source):
    kept = jnp.where(lax.axis_index(axis) == source, value, 0).astype(value.dtype)
    return lax.psum(kept, axis)


def shards(panel, slab, pivots, diag_inverse):
    rows_here = slab.shape[0]
    width_here = slab.shape[1]
    block_size = diag_inverse.shape[0]
    first_row = lax.axis_index("prow") * rows_here
    local_row = pivots - first_row
    owned = (local_row >= 0) & (local_row < rows_here)
    safe_row = jnp.clip(local_row, 0, rows_here - 1)
    picked = jnp.where(owned[:, None], slab[safe_row], 0.0)
    top_block = lax.psum(picked, "prow")
    upper = jnp.dot(
        diag_inverse, top_block, precision=lax.Precision.HIGHEST, preferred_element_type=jnp.float32
    )
    old_top = from_root(slab[:block_size], "prow", 0)
    target_row = jnp.where(owned, local_row, rows_here)
    swapped = slab.at[target_row].set(old_top, mode="drop")
    product = jnp.dot(
        lax.all_gather(panel, "pcol", axis=1, tiled=True),
        upper,
        precision=lax.Precision.HIGHEST,
        preferred_element_type=jnp.float32,
    )
    updated = swapped - product
    global_row = first_row + jnp.arange(rows_here, dtype=jnp.int32)
    upper_padded = jnp.concatenate(
        [upper, jnp.zeros((rows_here - block_size, width_here), jnp.float32)], axis=0
    )
    return jnp.where((global_row < block_size)[:, None], upper_padded, updated)


def solution(mesh):
    in_specs = (P("prow", "pcol"), P("prow", "pcol"), P(), P())
    out_specs = P("prow", "pcol")
    return jax.shard_map(shards, mesh=mesh, in_specs=in_specs, out_specs=out_specs, check_vma=False)
```

profile of v0, /device:TPU:0, one launch (start us, length us, event | category | flops | bytes accessed | tf_op | source)
XLA Modules:
  0.0 213.0 jit_solution(16660323267572027275)
XLA Ops:
  7.4 0.0 copy-start
  7.4 0.0 copy-start.2
  7.4 0.0 all-reduce.4.cloned.1.call-start
  7.4 7.9 %copy.11 = f32[4096,512]{1,0:T(8,128)} copy(f32[4096,512]{1,0:T(8,128)} %param.5) | data formatting | bytes 16777216
  15.2 0.0 copy-done.2
  15.3 5.4 %gather_fusion = f32[512,512]{1,0:T(8,128)S(1)} fusion(f32[4096,512]{1,0:T(8,128)} %copy.11, s32[1024]{0:T(1024)S(1)} %pad_clamp_fusion), kind=kCustom, calls=%fused_computation | custom fusion | bytes 2099200 | tf_op jit(solution)/shard_map/gather | solution.py:20
  20.7 2.8 %slice_select_fusion = (f32[512,512]{1,0:T(8,128)}, f32[512,512]{1,0:T(8,128)}) fusion(f32[4096,512]{1,0:T(8,128)} %copy.11, pred[]{:T(512)S(6)} %eq.3, f32[512,512]{1,0:T(8,128)S(1)} %gather_fusion, pred[512]{0:T(512)(128)(4,1)S(1)} %compare_and_fusion), kind=kLoop, calls=%fused_computation.4 | loop fusion | flops 524288 | bytes 4194817 | tf_op jit(solution)/shard_map/jit(_where)/select_n | solution.py:8
  23.5 0.0 all-reduce.4.cloned.1.call-update
  23.5 0.0 all-gather.2.cloned.1.call-start
  23.5 0.5 all-gather.2.cloned.1.call-update
  24.1 63.8 %all-reduce.4.cloned.1.call-done = (f32[512,512]{1,0:T(8,128)}, f32[512,512]{1,0:T(8,128)}) async-done(((f32[512,512]{1,0:T(8,128)}, f32[512,512]{1,0:T(8,128)}), (f32[512,512]{1,0:T(8,128)}, f32[512,512]{1,0:T(8,128)})) %all-reduce.4.cloned.1.call-update) | async-done | bytes 2097168 | tf_op jit(solution)/shard_map/psum | solution.py:9
  87.9 9.7 %scatter_fusion = f32[4096,512]{1,0:T(8,128)} fusion(f32[4096,512]{1,0:T(8,128)} %copy.11, s32[512]{0:T(512)S(1)} %get-tuple-element.8, f32[512,512]{1,0:T(8,128)} %get-tuple-element.5), kind=kCustom, calls=%fused_computation.1 | custom fusion | bytes 3147776 | tf_op jit(solution)/shard_map/scatter | solution.py:27
  97.6 0.0 copy-start.1
  97.6 9.0 %copy.5 = f32[4096,512]{0,1:T(8,128)} copy(f32[4096,512]{1,0:T(8,128)} %scatter_fusion) | data formatting | bytes 16777216 | tf_op jit(solution)/shard_map/scatter | solution.py:27
  106.7 0.0 copy-done
  106.7 0.0 copy-done.1
  106.7 3.5 %fusion.1 = f32[512,512]{1,0:T(8,128)S(1)} fusion(f32[512,512]{1,0:T(8,128)S(1)} %copy-done.1, f32[512,512]{1,0:T(8,128)S(1)} %copy-done), kind=kOutput, calls=%fused_computation.11 | convolution fusion | flops 1610612736 | bytes 3145728 | tf_op jit(solution)/shard_map/dot_general | solution.py:22
  110.1 67.1 %all-gather.2.cloned.1.call-done = f32[4096,512]{1,0:T(8,128)} async-done(((f32[4096,128]{1,0:T(8,128)}), f32[4096,512]{1,0:T(8,128)}) %all-gather.2.cloned.1.call-update) | async-done | bytes 8388624 | tf_op jit(solution)/shard_map/all_gather | solution.py:29
  177.2 19.4 %fusion = f32[4096,512]{0,1:T(8,128)} fusion(f32[4096,512]{0,1:T(8,128)} %copy.5, f32[512,512]{0,1:T(8,128)S(1)} %bitcast.9, f32[512,512]{1,0:T(8,128)S(1)} %fusion.1, f32[4096,512]{1,0:T(8,128)} %all-gather.2.cloned.1.call-done, pred[4096]{0:T(1024)(128)(4,1)S(1)} %add_compare_fusion), kind=kOutput, calls=%fused_computation.3 | convolution fusion | flops 12889096192 | bytes 27267072 | tf_op jit(solution)/shard_map/dot_general | solution.py:28
  196.6 8.9 %copy.6 = f32[4096,512]{1,0:T(8,128)} copy(f32[4096,512]{0,1:T(8,128)} %fusion) | data formatting | bytes 16777216 | tf_op jit(solution)/shard_map/jit(_where)/select_n | solution.py:39
  (4 shorter events, 0.0 us)
Async XLA Ops:
  7.4 99.3 %copy-start = (f32[512,512]{1,0:T(8,128)S(1)}, f32[512,512]{1,0:T(8,128)}, u32[]{:S(2)}) copy-start(f32[512,512]{1,0:T(8,128)} %param.7) | copy-start | bytes 3145732
  7.4 7.9 %copy-start.2 = (s32[512]{0:T(512)S(1)}, s32[512]{0:T(512)}, u32[]{:S(2)}) copy-start(s32[512]{0:T(512)} %param.6) | copy-start | bytes 6148
  7.4 80.5 %all-reduce.4.cloned.1.call-start = ((), (), s32[]{:S(2)}) async-start(), calls=%async_computation.1 | async-start | bytes 4194304 | tf_op jit(solution)/shard_map/psum | solution.py:9
  23.5 153.7 %all-gather.2.cloned.1.call-start = ((), (), s32[]{:S(2)}) async-start(), calls=%async_computation | async-start | bytes 10485760 | tf_op jit(solution)/shard_map/all_gather | solution.py:29
  97.6 9.1 %copy-start.1 = (f32[512,512]{1,0:T(8,128)S(1)}, f32[512,512]{1,0:T(8,128)}, u32[]{:S(2)}) copy-start(f32[512,512]{1,0:T(8,128)} %get-tuple-element.6) | copy-start | bytes 3145732
Sparse Core Ops, SparseCore 0:
  23.6 64.2 all-reduce.3
Sparse Core Ops, SparseCore 1:
  25.5 151.6 all-gather.1
where the time goes:
time: 214 us; the launch traced here: 213 us
  waiting for transfers between devices  131 us (61%)
  local copies, waits for them, and re-layouts  41 us (19%)
  matrix products  22.8 us (11%)
  between operations  14.9 us (7%)
  other arithmetic  2.79 us (1%)
    all_gather x1, waiting for transfers between devices, shards(): lax.all_gather(panel, 'pcol', axis=1, tiled=True)  67.1 us
    psum x1, waiting for transfers between devices, from_root(): return lax.psum(kept, axis)  63.8 us
    dot_general x1, matrix products, shards(): jnp.dot(lax.all_gather(panel, 'pcol', axis=1, tiled=True), upper, precisi...  19.4 us
    scatter x2, local copies, waits for them, and re-layouts, shards(): swapped = slab.at[target_row].set(old_top, mode='drop')  18.8 us
    select_n x1, local copies, waits for them, and re-layouts, shards(): return jnp.where((global_row < block_size)[:, None], upper_padded, updated)  8.94 us
    unnamed x7, local copies, waits for them, and re-layouts  7.87 us
    gather x1, local copies, waits for them, and re-layouts, shards(): picked = jnp.where(owned[:, None], slab[safe_row], 0.0)  5.41 us
  transfers between devices with their start and end apart: 2, of which 2 were waited for; matrix products, arithmetic and copies ran while one was open for 10% of the time, Pallas kernels for 0%

commit v1 on v0

v1 whole, which is shorter than its diff:
```python
import jax
import jax.numpy as jnp
from jax import lax
from jax.experimental import pallas as pl
from jax.experimental.pallas import tpu as pltpu
from jax.sharding import PartitionSpec as P

SWAP = [(0, 1), (1, 0), (2, 3), (3, 2)]
ACROSS = [(0, 2), (1, 3), (2, 0), (3, 1)]
MIDDLE = [(1, 2), (2, 1)]
ENDS = [(2, 3), (1, 0)]
PIECES = (12, 4)
TILE = 512
VMEM_LIMIT = 60 << 20
SMALL = pl.CostEstimate(flops=0, bytes_accessed=0, transcendentals=0)


def split(x):
    high = x.astype(jnp.bfloat16)
    low = (x - high.astype(jnp.float32)).astype(jnp.bfloat16)
    return high, low


def product(left, right):
    left_high, left_low = split(left)
    right_high, right_low = split(right)

    def dot(a, b):
        return jnp.dot(a, b, preferred_element_type=jnp.float32)

    return dot(left_high, right_high) + (dot(left_high, right_low) + dot(left_low, right_high))


def pick_kernel(info, pivots, slab, send, keep, rows, sem):
    copy = pltpu.make_async_copy(slab, rows, sem)
    copy.start()
    place = info[1]
    count = rows.shape[0]
    block = send.shape[0]
    first = place * count
    send[...] = jnp.zeros_like(send)
    keep[...] = jnp.zeros_like(keep)
    copy.wait()

    def fill(picked, top):
        @pl.when(place == 0)
        def _():
            top[...] = rows[:block, :]

        @pl.loop(0, block)
        def _(k):
            row = pivots[k] - first

            @pl.when((row >= 0) & (row < count))
            def _():
                picked[pl.ds(k, 1), :] = rows[pl.ds(row, 1), :]

    @pl.when(place % 2 == 0)
    def _():
        fill(keep, send)

    @pl.when(place % 2 == 1)
    def _():
        fill(send, keep)


def pick(info, pivots, slab, block):
    columns = slab.shape[1]
    shape = jax.ShapeDtypeStruct((block, columns), slab.dtype)
    return pl.pallas_call(
        pick_kernel,
        out_shape=(shape, shape),
        grid_spec=pltpu.PrefetchScalarGridSpec(
            num_scalar_prefetch=2,
            grid=(),
            in_specs=[pl.BlockSpec(memory_space=pl.ANY)],
            out_specs=[pl.BlockSpec(memory_space=pltpu.VMEM)] * 2,
            scratch_shapes=[pltpu.VMEM(slab.shape, slab.dtype), pltpu.SemaphoreType.DMA],
        ),
        compiler_params=pltpu.CompilerParams(vmem_limit_bytes=VMEM_LIMIT),
        cost_estimate=SMALL,
        name="pick",
    )(info, pivots, slab)


def swap_kernel(tile, info, pivots, slab, total, other, own, inverse, out, upper, rows, in_sem, out_sem):
    copy = pltpu.make_async_copy(slab, rows, in_sem)
    copy.start()
    column, place = info[0], info[1]
    count, width = own.shape
    block = upper.shape[0]
    first = place * count

    def fill(picked, old_top):
        upper[...] = product(inverse[...], picked[...])
        copy.wait()

        @pl.loop(0, block)
        def _(k):
            row = pivots[k] - first

            @pl.when((row >= 0) & (row < count))
            def _():
                rows[pl.ds(row, 1), :] = old_top[pl.ds(k, 1), :]

    @pl.when(place % 2 == 0)
    def _():
        fill(total, other)

    @pl.when(place % 2 == 1)
    def _():
        fill(other, total)

    mine = upper[pl.ds(pl.multiple_of(column * width, width), width), :]

    @pl.loop(0, count // tile)
    def _(t):
        part = pl.ds(pl.multiple_of(t * tile, tile), tile)
        rows[part, :] = rows[part, :] - product(own[part, :], mine)

        @pl.when((place == 0) & (t < block // tile))
        def _():
            rows[part, :] = upper[pl.ds(pl.multiple_of(jnp.minimum(t * tile, block - tile), tile), tile), :]

        pltpu.make_async_copy(rows.at[part, :], out.at[part, :], out_sem).start()

    pltpu.make_async_copy(rows, out, out_sem).wait()


def swap(info, pivots, slab, total, other, own, inverse):
    block = inverse.shape[0]
    return pl.pallas_call(
        lambda *refs: swap_kernel(min(TILE, block), *refs),
        out_shape=(
            jax.ShapeDtypeStruct(slab.shape, slab.dtype),
            jax.ShapeDtypeStruct((block, slab.shape[1]), slab.dtype),
        ),
        grid_spec=pltpu.PrefetchScalarGridSpec(
            num_scalar_prefetch=2,
            grid=(),
            in_specs=[pl.BlockSpec(memory_space=pl.ANY)] + [pl.BlockSpec(memory_space=pltpu.VMEM)] * 4,
            out_specs=(pl.BlockSpec(memory_space=pl.ANY), pl.BlockSpec(memory_space=pltpu.VMEM)),
            scratch_shapes=[
                pltpu.VMEM(slab.shape, slab.dtype),
                pltpu.SemaphoreType.DMA,
                pltpu.SemaphoreType.DMA,
            ],
        ),
        compiler_params=pltpu.CompilerParams(vmem_limit_bytes=VMEM_LIMIT),
        cost_estimate=SMALL,
        name="swap",
    )(info, pivots, slab, total, other, own, inverse)


def update_kernel(first_row, block, shards, info, base, *refs):
    *blocks, out = refs
    panels, uppers = blocks[: len(blocks) - len(shards)], blocks[len(blocks) - len(shards) :]
    tile = base.shape[0]
    panels = [panel[...] for panel in panels]
    if len(panels) > len(uppers):
        panels = [panels[0] + panels[1]]
    delta = product(panels[0], uppers[0][...])
    for panel, upper in zip(panels[1:], uppers[1:]):
        delta += product(panel, upper[...])
    if first_row < block:
        start = first_row + pl.program_id(0) * tile
        delta = jnp.where((info[1] == 0) & (start < block), 0.0, delta)
    out[...] = base[...] - delta


def update(info, base, panels, shards, upper, first_row, count):
    columns = base.shape[1]
    width = panels[0].shape[1]
    block = upper.shape[0]
    tile = min(TILE, count)
    shift = first_row // tile
    here = lambda i, info: (i + shift, 0)
    plain = lambda i, info: (i, 0)
    return pl.pallas_call(
        lambda *refs: update_kernel(first_row, block, shards, *refs),
        out_shape=jax.ShapeDtypeStruct(base.shape, base.dtype),
        grid_spec=pltpu.PrefetchScalarGridSpec(
            num_scalar_prefetch=1,
            grid=(count // tile,),
            in_specs=[pl.BlockSpec((tile, columns), here)]
            + [pl.BlockSpec((tile, width), here if p.shape[0] != count else plain) for p in panels]
            + [pl.BlockSpec((width, columns), lambda i, info, s=s: (info[0] ^ s, 0)) for s in shards],
            out_specs=pl.BlockSpec((tile, columns), here),
        ),
        input_output_aliases={1: 0},
        compiler_params=pltpu.CompilerParams(vmem_limit_bytes=VMEM_LIMIT),
        cost_estimate=SMALL,
        name="update",
    )(info, base, *panels, *([upper] * len(shards)))


def exchange(value, bit, count):
    return lax.ppermute(value, "prow", [(i, i ^ (1 << bit)) for i in range(count)])


def solution(mesh):
    row_parts, column_parts = mesh.shape["prow"], mesh.shape["pcol"]
    bits = row_parts.bit_length() - 1
    if column_parts != 4 or row_parts != 1 << bits or bits < 1:
        raise ValueError("unsupported mesh")

    def shards(panel, slab, pivots, diag_inverse):
        rows_here = slab.shape[0]
        block = diag_inverse.shape[0]
        place = lax.axis_index("prow")
        column = lax.axis_index("pcol")
        info = jnp.stack([column, place]).astype(jnp.int32)

        starts, pieces, at = [], [], 0
        for part in PIECES:
            size = rows_here * part // sum(PIECES)
            starts.append(at)
            pieces.append(panel[at : at + size])
            at += size
        near = lax.ppermute(panel, "pcol", SWAP)
        across = [lax.ppermute(piece, "pcol", ACROSS) for piece in pieces]

        def gather_rows(slab, pivots):
            send, keep = pick(info, pivots, slab, block)
            total = keep + exchange(send, 0, row_parts)
            for bit in range(1, bits):
                total = total + exchange(total, bit, row_parts)
            other = exchange(total, 0, row_parts)
            return total, other

        def no_rows(slab, pivots):
            return slab[:block], slab[:block]

        total, other = lax.cond(pivots[0] >= 0, gather_rows, no_rows, slab, pivots)
        across, _ = lax.optimization_barrier((across, total))
        result, upper = swap(info, pivots, slab, total, other, panel, diag_inverse)

        ends = [lax.ppermute(piece, "pcol", ENDS) for piece in across]
        later, near = lax.optimization_barrier((pieces, near))
        middle = [lax.ppermute(piece, "pcol", MIDDLE) for piece in later]
        for start, piece in zip(starts, across):
            result = update(info, result, [near, piece], (1, 2), upper, start, piece.shape[0])
        for start, end, mid in zip(starts, ends, middle):
            result = update(info, result, [end, mid], (3,), upper, start, end.shape[0])
        return result

    in_specs = (P("prow", "pcol"), P("prow", "pcol"), P(), P())
    return jax.shard_map(
        shards, mesh=mesh, in_specs=in_specs, out_specs=P("prow", "pcol"), check_vma=False
    )
```

time: 214 us -> 161 us (0.75)
  the two profiles are of different devices: /device:TPU:0 before, /device:TPU:14 now
where the time goes in v1:
time: 161 us; the launch traced here: 160 us
  waiting for transfers between devices  70 us (43%)
  Pallas kernels  63 us (39%)
  starting transfers between devices  16.9 us (10%)
  local copies, waits for them, and re-layouts  6.52 us (4%)
  other arithmetic  2.94 us (2%)
    ppermute x4, waiting for transfers between devices, exchange(): lax.ppermute(value, 'prow', [(i, i ^ 1 << bit) for i in range(count)])  54.9 us
    pallas_call x4, Pallas kernels, update(): pl.pallas_call(lambda *refs: update_kernel(first_row, block, shards, *ref...  29.6 us
    pallas_call x1, Pallas kernels, swap(): pl.pallas_call(lambda *refs: swap_kernel(min(TILE, block), *refs), out_sh...  20.6 us
    ppermute x2, waiting for transfers between devices, shards(): across = [lax.ppermute(piece, 'pcol', ACROSS) for piece in pieces]  15.1 us
    pallas_call x1, Pallas kernels, pick(): pl.pallas_call(pick_kernel, out_shape=(shape, shape), grid_spec=pltpu.Pre...  12.8 us
    ppermute x2, starting transfers between devices, shards(): ends = [lax.ppermute(piece, 'pcol', ENDS) for piece in across]  6.77 us
    ppermute x2, starting transfers between devices, shards(): middle = [lax.ppermute(piece, 'pcol', MIDDLE) for piece in later]  5.83 us
    slice x2, local copies, waits for them, and re-layouts, shards(): pieces.append(panel[at:at + size])  3.76 us
  transfers between devices with their start and end apart: 11, of which 5 were waited for; matrix products, arithmetic and copies ran while one was open for 5% of the time, Pallas kernels for 37%

profile of v1, /device:TPU:14, one launch (start us, length us, event | category | flops | bytes accessed | tf_op | source)
XLA Modules:
  0.0 160.0 jit_solution(7201097268890085986)
XLA Ops:
  0.0 0.4 collective-permute-start.4
  0.5 2.7 %slice.14 = f32[3072,128]{1,0:T(8,128)} slice(f32[4096,128]{1,0:T(8,128)} %refs_5_.1), slice={[0:3072], [0:128]} | slice | bytes 3145728 | tf_op jit(solution)/shard_map/slice | solution.py:218
  3.1 2.6 %collective-permute-start.5 = (f32[3072,128]{1,0:T(8,128)}, f32[3072,128]{1,0:T(8,128)}, u32[]{:S(2)}, u32[]{:S(2)}) collective-permute-start(f32[3072,128]{1,0:T(8,128)} %slice.14), channel_id=1, source_target_pairs={{0,2},{1,3},{2,0},{3,1},{4,6},{5,7},{6,4},{7,5},{8,10},{9,11},{10,... | collective-permute-start | bytes 4718600 | tf_op jit(solution)/shard_map/ppermute | solution.py:221
  5.7 1.1 slice.15
  6.8 0.0 copy-start.4
  6.8 0.4 collective-permute-start.6
  7.2 1.2 slice.13
  8.9 0.1 pad_add_fusion.refs_0_
  9.0 0.0 copy-done.4
  9.0 71.4 %conditional.1 = (f32[512,512]{1,0:T(8,128)}, f32[512,512]{1,0:T(8,128)}) conditional(s32[]{:T(128)} %bitcast.2, f32[4096,512]{1,0:T(8,128)} %refs_2_.1, (s32[2]{0:T(128)S(1)}, s32[512]{0:T(512)}, f32[4096,512]{1,0:T(8,128)}) %tuple.15), branch_computations={%region_0.0_spmd, %region_1.0_spmd} | conditional | flops 786432 | bytes 26214576 | solution.py:234
  9.0 12.8 %pick.1 = (f32[512,512]{1,0:T(8,128)}, f32[512,512]{1,0:T(8,128)}) custom-call(s32[2]{0:T(128)S(1)} %get-tuple-element.12.info, s32[512]{0:T(512)} %get-tuple-element.13.pivots, f32[4096,512]{1,0:T(8,128)} %get-tuple-element.14.slab), custom_call_target="tpu_custom_call" | custom-call | tf_op jit(solution)/shard_map/cond/branch_1_fun/pick/pallas_call | solution.py:70
  21.8 0.1 collective-permute-start
  21.9 2.9 %collective-permute-done = f32[512,512]{1,0:T(8,128)S(1)} collective-permute-done((f32[512,512]{1,0:T(8,128)}, f32[512,512]{1,0:T(8,128)S(1)}, u32[]{:S(2)}, u32[]{:S(2)}) %collective-permute-start) | collective-permute-done | bytes 1048608 | tf_op jit(solution)/shard_map/cond/branch_1_fun/ppermute | solution.py:198
  24.8 1.5 add.6
  26.2 0.7 collective-permute-start.1
  26.9 24.6 %collective-permute-done.1 = f32[512,512]{1,0:T(8,128)S(1)} collective-permute-done((f32[512,512]{1,0:T(8,128)S(1)}, f32[512,512]{1,0:T(8,128)S(1)}, u32[]{:S(2)}, u32[]{:S(2)}) %collective-permute-start.1) | collective-permute-done | bytes 1048608 | tf_op jit(solution)/shard_map/cond/branch_1_fun/ppermute | solution.py:198
  51.5 0.2 add.7
  51.7 0.1 collective-permute-start.2
  51.8 24.5 %collective-permute-done.2 = f32[512,512]{1,0:T(8,128)S(1)} collective-permute-done((f32[512,512]{1,0:T(8,128)S(1)}, f32[512,512]{1,0:T(8,128)S(1)}, u32[]{:S(2)}, u32[]{:S(2)}) %collective-permute-start.2) | collective-permute-done | bytes 1048608 | tf_op jit(solution)/shard_map/cond/branch_1_fun/ppermute | solution.py:198
  76.2 1.2 add.8
  77.4 0.0 collective-permute-start.3
  77.4 3.0 %collective-permute-done.3 = f32[512,512]{1,0:T(8,128)} collective-permute-done((f32[512,512]{1,0:T(8,128)}, f32[512,512]{1,0:T(8,128)}, u32[]{:S(2)}, u32[]{:S(2)}) %collective-permute-start.3) | collective-permute-done | bytes 1048608 | tf_op jit(solution)/shard_map/cond/branch_1_fun/ppermute | solution.py:198
  80.4 15.1 %collective-permute-done.6.refs_3_ = f32[1024,128]{1,0:T(8,128)S(1)} collective-permute-done((f32[1024,128]{1,0:T(8,128)S(1)}, f32[1024,128]{1,0:T(8,128)S(1)}, u32[]{:S(2)}, u32[]{:S(2)}) %collective-permute-start.6) | collective-permute-done | bytes 524320 | tf_op jit(solution)/shard_map/ppermute | solution.py:221
  95.5 0.0 copy-start.1
  95.5 0.0 collective-permute-done.5.refs_3_
  95.5 5.4 %collective-permute-start.7 = (f32[3072,128]{1,0:T(8,128)}, f32[3072,128]{1,0:T(8,128)}, u32[]{:S(2)}, u32[]{:S(2)}) collective-permute-start(f32[3072,128]{1,0:T(8,128)} %collective-permute-done.5.refs_3_), channel_id=1, source_target_pairs={{2,3},{1,0},{6,7},{5,4},{10,11},{9,8},{14,15},{13,12},{18,19},{17,... | collective-permute-start | bytes 4718600 | tf_op jit(solution)/shard_map/ppermute | solution.py:238
  101.0 0.0 collective-permute-done.4.refs_2_
  101.0 0.0 copy-start
  101.0 3.5 %collective-permute-start.8 = (f32[3072,128]{1,0:T(8,128)}, f32[3072,128]{1,0:T(8,128)}, u32[]{:S(2)}, u32[]{:S(2)}) collective-permute-start(f32[3072,128]{1,0:T(8,128)} %slice.14), channel_id=1, source_target_pairs={{1,2},{2,1},{5,6},{6,5},{9,10},{10,9},{13,14},{14,13},{17,18},{18,... | collective-permute-start | bytes 4718600 | tf_op jit(solution)/shard_map/ppermute | solution.py:240
  104.5 1.3 collective-permute-start.9
  105.8 2.4 %collective-permute-start.10 = (f32[1024,128]{1,0:T(8,128)}, f32[1024,128]{1,0:T(8,128)S(1)}, u32[]{:S(2)}, u32[]{:S(2)}) collective-permute-start(f32[1024,128]{1,0:T(8,128)} %copy-done.4), channel_id=1, source_target_pairs={{1,2},{2,1},{5,6},{6,5},{9,10},{10,9},{13,14},{14,13},{17,18},{18,... | collective-permute-start | bytes 1572872 | tf_op jit(solution)/shard_map/ppermute | solution.py:240
  108.2 20.6 %swap.1 = (f32[4096,512]{1,0:T(8,128)}, f32[512,512]{1,0:T(8,128)}) custom-call(s32[2]{0:T(128)S(1)} %pad_add_fusion.refs_0_, s32[512]{0:T(512)} %refs_1_.1, f32[4096,512]{1,0:T(8,128)} %refs_2_.1, f32[512,512]{1,0:T(8,128)} %get-tuple-element.26.refs_3_, f32[512,512]{1,0:T(8,128)} %get-tuple-element.27.refs_4_, f32[4096,128]{1,0:T(8,128)} %refs_5_.1, ...), custom_call_target="tpu_custom_call" | custom-call | tf_op jit(solution)/shard_map/swap/pallas_call | solution.py:132
  128.8 0.0 copy-done
  128.8 10.7 %update.4.refs_1_ = f32[4096,512]{1,0:T(8,128)} custom-call(s32[2]{0:T(128)S(1)} %pad_add_fusion.refs_0_, f32[4096,512]{1,0:T(8,128)} %get-tuple-element.28.refs_1_, f32[4096,128]{1,0:T(8,128)} %copy-done, f32[3072,128]{1,0:T(8,128)} %collective-permute-done.5.refs_3_, f32[512,512]{1,0:T(8,128)} %get-tuple-element.31.refs_4_.refs_5_, ...), custom_call_target="tpu_custom_call", output_to_operand_aliasing={{}: (1, {})} | custom-call | tf_op jit(solution)/shard_map/update/pallas_call | solution.py:179
  139.6 0.0 copy-done.1
  139.6 5.1 %update.5.refs_1_ = f32[4096,512]{1,0:T(8,128)} custom-call(s32[2]{0:T(128)S(1)} %pad_add_fusion.refs_0_, f32[4096,512]{1,0:T(8,128)} %update.4.refs_1_, f32[4096,128]{1,0:T(8,128)} %copy-done, f32[1024,128]{1,0:T(8,128)} %copy-done.1, f32[512,512]{1,0:T(8,128)} %get-tuple-element.31.refs_4_.refs_5_, ...), custom_call_target="tpu_custom_call", output_to_operand_aliasing={{}: (1, {})} | custom-call | tf_op jit(solution)/shard_map/update/pallas_call | solution.py:179
  144.7 0.0 collective-permute-done.7.refs_2_
  144.7 0.0 collective-permute-done.8.refs_3_
  144.7 9.6 %update.6.refs_1_ = f32[4096,512]{1,0:T(8,128)} custom-call(s32[2]{0:T(128)S(1)} %pad_add_fusion.refs_0_, f32[4096,512]{1,0:T(8,128)} %update.5.refs_1_, f32[3072,128]{1,0:T(8,128)} %collective-permute-done.7.refs_2_, f32[3072,128]{1,0:T(8,128)} %collective-permute-done.8.refs_3_, ...), custom_call_target="tpu_custom_call", output_to_operand_aliasing={{}: (1, {})} | custom-call | tf_op jit(solution)/shard_map/update/pallas_call | solution.py:179
  154.2 0.0 collective-permute-done.9.refs_2_
  154.2 0.0 copy-start.2
  154.2 0.0 collective-permute-done.10.refs_3_
  154.2 0.8 copy-done.2
  155.0 0.0 copy-start.3
  155.0 0.8 copy-done.3
  155.8 4.2 %update.7 = f32[4096,512]{1,0:T(8,128)} custom-call(s32[2]{0:T(128)S(1)} %pad_add_fusion.refs_0_, f32[4096,512]{1,0:T(8,128)} %update.6.refs_1_, f32[1024,128]{1,0:T(8,128)} %copy-done.2, f32[1024,128]{1,0:T(8,128)} %copy-done.3, f32[512,512]{1,0:T(8,128)} %get-tuple-element.31.refs_4_.refs_5_), custom_call_target="tpu_custom_call", output_to_operand_aliasing={{}: (1, {})} | custom-call | tf_op jit(solution)/shard_map/update/pallas_call | solution.py:179
Async XLA Ops:
  0.0 101.0 %collective-permute-start.4 = (f32[4096,128]{1,0:T(8,128)}, f32[4096,128]{1,0:T(8,128)S(1)}, u32[]{:S(2)}, u32[]{:S(2)}) collective-permute-start(f32[4096,128]{1,0:T(8,128)} %refs_5_.1), channel_id=1, source_target_pairs={{0,1},{1,0},{2,3},{3,2},{4,5},{5,4},{6,7},{7,6},{8,9},{9,8},{10,11... | collective-permute-start | bytes 6291464 | tf_op jit(solution)/shard_map/ppermute | solution.py:220
  3.1 92.4 %collective-permute-start.5 = (f32[3072,128]{1,0:T(8,128)}, f32[3072,128]{1,0:T(8,128)}, u32[]{:S(2)}, u32[]{:S(2)}) collective-permute-start(f32[3072,128]{1,0:T(8,128)} %slice.14), channel_id=1, source_target_pairs={{0,2},{1,3},{2,0},{3,1},{4,6},{5,7},{6,4},{7,5},{8,10},{9,11},{10,... | collective-permute-start | bytes 4718600 | tf_op jit(solution)/shard_map/ppermute | solution.py:221
  6.8 2.2 %copy-start.4 = (f32[1024,128]{1,0:T(8,128)}, f32[1024,128]{1,0:T(8,128)S(1)}, u32[]{:S(2)}) copy-start(f32[1024,128]{1,0:T(8,128)S(1)} %slice.15) | copy-start | bytes 1572868
  6.8 88.7 %collective-permute-start.6 = (f32[1024,128]{1,0:T(8,128)S(1)}, f32[1024,128]{1,0:T(8,128)S(1)}, u32[]{:S(2)}, u32[]{:S(2)}) collective-permute-start(f32[1024,128]{1,0:T(8,128)S(1)} %slice.15), channel_id=1, source_target_pairs={{0,2},{1,3},{2,0},{3,1},{4,6},{5,7},{6,4},{7,5},{8,10},{9,11},{10,... | collective-permute-start | bytes 1572872 | tf_op jit(solution)/shard_map/ppermute | solution.py:221
  21.8 2.9 %collective-permute-start = (f32[512,512]{1,0:T(8,128)}, f32[512,512]{1,0:T(8,128)S(1)}, u32[]{:S(2)}, u32[]{:S(2)}) collective-permute-start(f32[512,512]{1,0:T(8,128)} %get-tuple-element.16), channel_id=1, source_target_pairs={{0,4},{4,0},{8,12},{12,8},{16,20},{20,16},{24,28},{28,24},{1,5},{5... | collective-permute-start | bytes 3145736 | tf_op jit(solution)/shard_map/cond/branch_1_fun/ppermute | solution.py:198
  26.2 25.3 %collective-permute-start.1 = (f32[512,512]{1,0:T(8,128)S(1)}, f32[512,512]{1,0:T(8,128)S(1)}, u32[]{:S(2)}, u32[]{:S(2)}) collective-permute-start(f32[512,512]{1,0:T(8,128)S(1)} %add.6), channel_id=1, source_target_pairs={{0,8},{4,12},{8,0},{12,4},{16,24},{20,28},{24,16},{28,20},{1,9},{5... | collective-permute-start | bytes 3145736 | tf_op jit(solution)/shard_map/cond/branch_1_fun/ppermute | solution.py:198
  51.7 24.5 %collective-permute-start.2 = (f32[512,512]{1,0:T(8,128)S(1)}, f32[512,512]{1,0:T(8,128)S(1)}, u32[]{:S(2)}, u32[]{:S(2)}) collective-permute-start(f32[512,512]{1,0:T(8,128)S(1)} %add.7), channel_id=1, source_target_pairs={{0,16},{4,20},{8,24},{12,28},{16,0},{20,4},{24,8},{28,12},{1,17},{... | collective-permute-start | bytes 3145736 | tf_op jit(solution)/shard_map/cond/branch_1_fun/ppermute | solution.py:198
  77.4 3.0 %collective-permute-start.3 = (f32[512,512]{1,0:T(8,128)}, f32[512,512]{1,0:T(8,128)}, u32[]{:S(2)}, u32[]{:S(2)}) collective-permute-start(f32[512,512]{1,0:T(8,128)} %add.8), channel_id=1, source_target_pairs={{0,4},{4,0},{8,12},{12,8},{16,20},{20,16},{24,28},{28,24},{1,5},{5... | collective-permute-start | bytes 3145736 | tf_op jit(solution)/shard_map/cond/branch_1_fun/ppermute | solution.py:198
  95.5 44.0 %copy-start.1 = (f32[1024,128]{1,0:T(8,128)}, f32[1024,128]{1,0:T(8,128)S(1)}, u32[]{:S(2)}) copy-start(f32[1024,128]{1,0:T(8,128)S(1)} %collective-permute-done.6.refs_3_) | copy-start | bytes 1572868
  95.5 49.1 %collective-permute-start.7 = (f32[3072,128]{1,0:T(8,128)}, f32[3072,128]{1,0:T(8,128)}, u32[]{:S(2)}, u32[]{:S(2)}) collective-permute-start(f32[3072,128]{1,0:T(8,128)} %collective-permute-done.5.refs_3_), channel_id=1, source_target_pairs={{2,3},{1,0},{6,7},{5,4},{10,11},{9,8},{14,15},{13,12},{18,19},{17,... | collective-permute-start | bytes 4718600 | tf_op jit(solution)/shard_map/ppermute | solution.py:238
  101.0 27.8 %copy-start = (f32[4096,128]{1,0:T(8,128)}, f32[4096,128]{1,0:T(8,128)S(1)}, u32[]{:S(2)}) copy-start(f32[4096,128]{1,0:T(8,128)S(1)} %collective-permute-done.4.refs_2_) | copy-start | bytes 6291460
  101.0 43.7 %collective-permute-start.8 = (f32[3072,128]{1,0:T(8,128)}, f32[3072,128]{1,0:T(8,128)}, u32[]{:S(2)}, u32[]{:S(2)}) collective-permute-start(f32[3072,128]{1,0:T(8,128)} %slice.14), channel_id=1, source_target_pairs={{1,2},{2,1},{5,6},{6,5},{9,10},{10,9},{13,14},{14,13},{17,18},{18,... | collective-permute-start | bytes 4718600 | tf_op jit(solution)/shard_map/ppermute | solution.py:240
  104.5 49.8 %collective-permute-start.9 = (f32[1024,128]{1,0:T(8,128)S(1)}, f32[1024,128]{1,0:T(8,128)S(1)}, u32[]{:S(2)}, u32[]{:S(2)}) collective-permute-start(f32[1024,128]{1,0:T(8,128)S(1)} %collective-permute-done.6.refs_3_), channel_id=1, source_target_pairs={{2,3},{1,0},{6,7},{5,4},{10,11},{9,8},{14,15},{13,12},{18,19},{17,... | collective-permute-start | bytes 1572872 | tf_op jit(solution)/shard_map/ppermute | solution.py:238
  105.8 48.4 %collective-permute-start.10 = (f32[1024,128]{1,0:T(8,128)}, f32[1024,128]{1,0:T(8,128)S(1)}, u32[]{:S(2)}, u32[]{:S(2)}) collective-permute-start(f32[1024,128]{1,0:T(8,128)} %copy-done.4), channel_id=1, source_target_pairs={{1,2},{2,1},{5,6},{6,5},{9,10},{10,9},{13,14},{14,13},{17,18},{18,... | collective-permute-start | bytes 1572872 | tf_op jit(solution)/shard_map/ppermute | solution.py:240
  154.2 0.8 copy-start.2
  155.0 0.8 copy-start.3

commit v2 on v1

v2 whole, which is shorter than its diff:
```python
import jax
import jax.numpy as jnp
from jax import lax
from jax.experimental import pallas as pl
from jax.experimental.pallas import tpu as pltpu
from jax.sharding import PartitionSpec as P

SWAP = [(0, 1), (1, 0), (2, 3), (3, 2)]
ACROSS = [(0, 2), (1, 3), (2, 0), (3, 1)]
MIDDLE = [(1, 2), (2, 1)]
ENDS = [(2, 3), (1, 0)]
PIECES = (14, 2)
TILE = 512
LAST_TILE = 128
SMALL = pl.CostEstimate(flops=0, bytes_accessed=0, transcendentals=0)
HBM = pl.BlockSpec(memory_space=pl.ANY)
VMEM = pl.BlockSpec(memory_space=pltpu.VMEM)


def split(x):
    high = x.astype(jnp.bfloat16)
    low = (x - high.astype(jnp.float32)).astype(jnp.bfloat16)
    return high, low


def left_terms(x):
    high, low = split(x)
    return jnp.concatenate([high, high, low], axis=1)


def right_terms(x):
    high, low = split(x)
    return jnp.concatenate([high, low, high], axis=0)


def dot(a, b):
    return jnp.dot(a, b, preferred_element_type=jnp.float32)


def aligned(start, size):
    return pl.ds(pl.multiple_of(start, size), size)


def pick_kernel(info, pivots, slab, send, keep, rows, sem, top_sem):
    copy = pltpu.make_async_copy(slab, rows, sem)
    copy.start()
    place = info[1]
    count = rows.shape[0]
    block = send.shape[0]
    first = place * count

    def fill(picked, top):
        load = pltpu.make_async_copy(slab.at[pl.ds(0, block), :], top, top_sem)

        @pl.when(place == 0)
        def _():
            load.start()

        @pl.when(place != 0)
        def _():
            top[...] = jnp.zeros_like(top)

        copy.wait()

        @pl.loop(0, block // 8)
        def _(group):
            base = pl.multiple_of(group * 8, 8)
            for j in range(8):
                row = pivots[base + j] - first
                owned = (row >= 0) & (row < count)
                value = rows[pl.ds(jnp.where(owned, row, 0), 1), :]
                picked[pl.ds(base + j, 1), :] = jnp.where(owned, value, 0.0)

        @pl.when(place == 0)
        def _():
            load.wait()

    @pl.when(place % 2 == 0)
    def _():
        fill(keep, send)

    @pl.when(place % 2 == 1)
    def _():
        fill(send, keep)


def pick(info, pivots, slab, block):
    columns = slab.shape[1]
    shape = jax.ShapeDtypeStruct((block, columns), slab.dtype)
    return pl.pallas_call(
        pick_kernel,
        out_shape=(shape, shape),
        grid_spec=pltpu.PrefetchScalarGridSpec(
            num_scalar_prefetch=2,
            grid=(),
            in_specs=[HBM],
            out_specs=(VMEM, VMEM),
            scratch_shapes=[
                pltpu.VMEM(slab.shape, slab.dtype),
                pltpu.SemaphoreType.DMA,
                pltpu.SemaphoreType.DMA,
            ],
        ),
        compiler_params=pltpu.CompilerParams(vmem_limit_bytes=16 << 20),
        cost_estimate=SMALL,
        name="pick",
    )(info, pivots, slab)


def upper_kernel(width, info, total, other, inverse, upper, terms):
    block = upper.shape[0]

    def fill(picked):
        upper[...] = dot(left_terms(inverse[...]), right_terms(picked[...]))

    @pl.when(info[1] % 2 == 0)
    def _():
        fill(total)

    @pl.when(info[1] % 2 == 1)
    def _():
        fill(other)

    for shard in range(block // width):
        terms[pl.ds(shard * 3 * width, 3 * width), :] = right_terms(upper[pl.ds(shard * width, width), :])


def make_upper(info, total, other, inverse, width):
    block, columns = total.shape
    return pl.pallas_call(
        lambda *refs: upper_kernel(width, *refs),
        out_shape=(
            jax.ShapeDtypeStruct((block, columns), total.dtype),
            jax.ShapeDtypeStruct((3 * block, columns), jnp.bfloat16),
        ),
        grid_spec=pltpu.PrefetchScalarGridSpec(
            num_scalar_prefetch=1,
            grid=(),
            in_specs=[VMEM] * 3,
            out_specs=(VMEM, VMEM),
        ),
        compiler_params=pltpu.CompilerParams(vmem_limit_bytes=24 << 20),
        cost_estimate=SMALL,
        name="upper",
    )(info, total, other, inverse)


def main_kernel(tile, info, pivots, slab, total, other, own, near, *refs):
    *across, upper, terms, out, own_rows, near_rows, across_rows, sem, panel_sem = refs
    copy = pltpu.make_async_copy(slab, out, sem)
    copy.start()
    loads = [(own, own_rows), (near, near_rows)]
    at = 0
    for piece in across:
        loads.append((piece, across_rows.at[pl.ds(at, piece.shape[0]), :]))
        at += piece.shape[0]
    loads = [pltpu.make_async_copy(a, b, panel_sem.at[i]) for i, (a, b) in enumerate(loads)]
    for load in loads:
        load.start()
    column, place = info[0], info[1]
    count, width = own_rows.shape
    block = upper.shape[0]
    first = place * count
    copy.wait()

    def fill(old_top):
        @pl.loop(0, block // 8)
        def _(group):
            base = pl.multiple_of(group * 8, 8)
            for j in range(8):
                row = pivots[base + j] - first
                owned = (row >= 0) & (row < count)
                place_at = pl.ds(jnp.where(owned, row, 0), 1)
                out[place_at, :] = jnp.where(owned, old_top[pl.ds(base + j, 1), :], out[place_at, :])

    @pl.when(place % 2 == 0)
    def _():
        fill(other)

    @pl.when(place % 2 == 1)
    def _():
        fill(total)

    for load in loads:
        load.wait()

    @pl.loop(0, count // tile)
    def _(t):
        part = aligned(t * tile, tile)
        left = [left_terms(panel[part, :]) for panel in (own_rows, near_rows, across_rows)]
        right = [terms[aligned((column ^ shard) * 3 * width, 3 * width), :] for shard in range(3)]
        out[part, :] = out[part, :] - dot(jnp.concatenate(left, axis=1), jnp.concatenate(right, axis=0))

        @pl.when((place == 0) & (t < block // tile))
        def _():
            out[part, :] = upper[aligned(jnp.minimum(t * tile, block - tile), tile), :]


def main_update(info, pivots, slab, total, other, own, near, across, upper, terms):
    block = upper.shape[0]
    return pl.pallas_call(
        lambda *refs: main_kernel(min(TILE, block), *refs),
        out_shape=jax.ShapeDtypeStruct(slab.shape, slab.dtype),
        grid_spec=pltpu.PrefetchScalarGridSpec(
            num_scalar_prefetch=2,
            grid=(),
            in_specs=[HBM, VMEM, VMEM, HBM, HBM] + [HBM] * len(across) + [VMEM, VMEM],
            out_specs=VMEM,
            scratch_shapes=[pltpu.VMEM(own.shape, own.dtype)] * 3
            + [pltpu.SemaphoreType.DMA, pltpu.SemaphoreType.DMA((2 + len(across),))],
        ),
        compiler_params=pltpu.CompilerParams(vmem_limit_bytes=32 << 20),
        cost_estimate=SMALL,
        name="main_update",
    )(info, pivots, slab, total, other, own, near, *across, upper, terms)


def last_kernel(first_row, block, tile, info, base, ends, middle, terms, *refs):
    out = refs[-1]
    step = pl.program_id(0)
    part = aligned(step * tile, tile)
    delta = dot(left_terms(ends[part, :] + middle[part, :]), terms[...])
    if first_row < block:
        keep = (info[1] == 0) & (first_row + step * tile < block)
        delta = jnp.where(keep, 0.0, delta)
    out[...] = base[aligned(first_row + step * tile, tile), :] - delta


def last_update(info, base, ends, middle, terms, block, first_row, tile, done):
    columns = base.shape[1]
    count, width = ends.shape
    shift = first_row // tile
    return pl.pallas_call(
        lambda *refs: last_kernel(first_row, block, tile, *refs),
        out_shape=jax.ShapeDtypeStruct(base.shape, base.dtype),
        grid_spec=pltpu.PrefetchScalarGridSpec(
            num_scalar_prefetch=1,
            grid=(count // tile,),
            in_specs=[VMEM] * 3
            + [pl.BlockSpec((3 * width, columns), lambda i, info: (info[0] ^ 3, 0))]
            + [HBM] * len(done),
            out_specs=pl.BlockSpec((tile, columns), lambda i, info: (i + shift, 0)),
        ),
        input_output_aliases={5: 0} if done else {},
        compiler_params=pltpu.CompilerParams(vmem_limit_bytes=24 << 20),
        cost_estimate=SMALL,
        name="last_update",
    )(info, base, ends, middle, terms, *done)


def exchange(value, bit, count):
    return lax.ppermute(value, "prow", [(i, i ^ (1 << bit)) for i in range(count)])


def solution(mesh):
    row_parts, column_parts = mesh.shape["prow"], mesh.shape["pcol"]
    bits = row_parts.bit_length() - 1
    if column_parts != 4 or row_parts != 1 << bits or bits < 1:
        raise ValueError("unsupported mesh")

    def shards(panel, slab, pivots, diag_inverse):
        rows_here = slab.shape[0]
        width = panel.shape[1]
        block = diag_inverse.shape[0]
        place = lax.axis_index("prow")
        column = lax.axis_index("pcol")
        info = jnp.stack([column, place]).astype(jnp.int32)

        starts, pieces, at = [], [], 0
        for part in PIECES:
            size = rows_here * part // sum(PIECES)
            starts.append(at)
            pieces.append(panel[at : at + size])
            at += size
        near = lax.ppermute(panel, "pcol", SWAP)
        across = [lax.ppermute(piece, "pcol", ACROSS) for piece in pieces]

        def gather_rows(slab, pivots):
            send, keep = pick(info, pivots, slab, block)
            total = keep + exchange(send, 0, row_parts)
            for bit in range(1, bits):
                total = total + exchange(total, bit, row_parts)
            return total, exchange(total, 0, row_parts)

        def no_rows(slab, pivots):
            return slab[:block], slab[:block]

        total, other = lax.cond(pivots[0] >= 0, gather_rows, no_rows, slab, pivots)
        upper, terms = make_upper(info, total, other, diag_inverse, width)
        across, _ = lax.optimization_barrier((across, upper))
        ends = [lax.ppermute(piece, "pcol", ENDS) for piece in across]
        later, near = lax.optimization_barrier((pieces, near))
        middle = [lax.ppermute(piece, "pcol", MIDDLE) for piece in later]
        base = main_update(info, pivots, slab, total, other, panel, near, across, upper, terms)
        done = []
        for start, end, mid in zip(starts, ends, middle):
            tile = LAST_TILE if done else TILE
            done = [last_update(info, base, end, mid, terms, block, start, min(tile, block), done)]
        return done[0]

    in_specs = (P("prow", "pcol"), P("prow", "pcol"), P(), P())
    return jax.shard_map(
        shards, mesh=mesh, in_specs=in_specs, out_specs=P("prow", "pcol"), check_vma=False
    )
```

time: 161 us -> 154 us (0.957)
  Pallas kernels: 63 us -> 34.4 us
  waiting for transfers between devices: 70 us -> 97.1 us
  local copies, waits for them, and re-layouts: 6.52 us -> 4.28 us
    pallas_call x5 -> x4, Pallas kernels: 50.2 us -> 27.7 us  [the longest x1 15.6 us: main_update(): pl.pallas_call(lambda *refs: main_kernel(min(TILE, block), *refs), out_sh...]
    ppermute x2, waiting for transfers between devices: 0.01 us -> 17.9 us  [shards(): ends = [lax.ppermute(piece, 'pcol', ENDS) for piece in across]]
    pallas_call x1, Pallas kernels: 12.8 us -> 6.75 us  [pick(): pl.pallas_call(pick_kernel, out_shape=(shape, shape), grid_spec=pltpu.Pre...]
    ppermute x2, waiting for transfers between devices: 15.1 us -> 20.5 us  [shards(): across = [lax.ppermute(piece, 'pcol', ACROSS) for piece in pieces]]
    ppermute x2, waiting for transfers between devices: 0.01 us -> 4.42 us  [shards(): middle = [lax.ppermute(piece, 'pcol', MIDDLE) for piece in later]]
  transfers between devices with their start and end apart: 11 -> 11, of which waited for: 5 -> 7; matrix products, arithmetic and copies ran while one was open for 5% -> 4% of each run, Pallas kernels for 37% -> 21%
where the time goes in v2:
time: 154 us
  waiting for transfers between devices  97.1 us (63%)
  Pallas kernels  34.4 us (22%)
  starting transfers between devices  16 us (10%)
  local copies, waits for them, and re-layouts  4.28 us (3%)
  other arithmetic  1.66 us (1%)
    ppermute x4, waiting for transfers between devices, exchange(): lax.ppermute(value, 'prow', [(i, i ^ 1 << bit) for i in range(count)])  54.3 us
    ppermute x2, waiting for transfers between devices, shards(): across = [lax.ppermute(piece, 'pcol', ACROSS) for piece in pieces]  20.5 us
    ppermute x2, waiting for transfers between devices, shards(): ends = [lax.ppermute(piece, 'pcol', ENDS) for piece in across]  17.9 us
    pallas_call x1, Pallas kernels, main_update(): pl.pallas_call(lambda *refs: main_kernel(min(TILE, block), *refs), out_sh...  15.6 us
    pallas_call x2, Pallas kernels, last_update(): pl.pallas_call(lambda *refs: last_kernel(first_row, block, tile, *refs),...  8.87 us
    pallas_call x1, Pallas kernels, pick(): pl.pallas_call(pick_kernel, out_shape=(shape, shape), grid_spec=pltpu.Pre...  6.75 us
    ppermute x2, starting transfers between devices, shards(): middle = [lax.ppermute(piece, 'pcol', MIDDLE) for piece in later]  5.84 us
    ppermute x2, starting transfers between devices, shards(): ends = [lax.ppermute(piece, 'pcol', ENDS) for piece in across]  5.49 us
  transfers between devices with their start and end apart: 11, of which 7 were waited for; matrix products, arithmetic and copies ran while one was open for 4% of the time, Pallas kernels for 21%

profile of v2, /device:TPU:14, one launch (start us, length us, event | category | flops | bytes accessed | tf_op | source)
XLA Modules:
  0.0 154.1 jit_solution(10783333270136549142)
XLA Ops:
  0.0 0.0 copy-start
  0.0 0.0 copy-start.2
  0.0 0.4 collective-permute-start.4
  0.5 3.0 %slice.14 = f32[3584,128]{1,0:T(8,128)} slice(f32[4096,128]{1,0:T(8,128)} %refs_5_.1), slice={[0:3584], [0:128]} | slice | bytes 3670016 | tf_op jit(solution)/shard_map/slice | solution.py:273
  3.5 2.6 %collective-permute-start.5 = (f32[3584,128]{1,0:T(8,128)}, f32[3584,128]{1,0:T(8,128)}, u32[]{:S(2)}, u32[]{:S(2)}) collective-permute-start(f32[3584,128]{1,0:T(8,128)} %slice.14), channel_id=1, source_target_pairs={{0,2},{1,3},{2,0},{3,1},{4,6},{5,7},{6,4},{7,5},{8,10},{9,11},{10,... | collective-permute-start | bytes 5505032 | tf_op jit(solution)/shard_map/ppermute | solution.py:276
  6.1 0.0 copy-done
  6.1 0.7 slice.15
  6.8 0.3 collective-permute-start.6
  7.2 0.0 copy-done.2
  7.2 0.5 slice.13
  8.2 0.1 pad_add_fusion.refs_0_
  8.3 0.0 copy-start.1
  8.3 63.9 %conditional.1 = (f32[512,512]{1,0:T(8,128)}, f32[512,512]{1,0:T(8,128)}) conditional(s32[]{:T(128)} %bitcast.2, f32[4096,512]{1,0:T(8,128)} %refs_2_.1, (s32[2]{0:T(128)S(1)}, s32[512]{0:T(512)S(1)}, f32[4096,512]{1,0:T(8,128)}) %tuple.20), branch_computations={%region_0.0_spmd, %region_1.0_spmd} | conditional | flops 786432 | bytes 26214576 | solution.py:288
  8.3 6.7 %pick.1 = (f32[512,512]{1,0:T(8,128)S(1)}, f32[512,512]{1,0:T(8,128)S(1)}) custom-call(s32[2]{0:T(128)S(1)} %get-tuple-element.12.info, s32[512]{0:T(512)S(1)} %get-tuple-element.13.pivots, f32[4096,512]{1,0:T(8,128)} %get-tuple-element.14.slab), custom_call_target="tpu_custom_call" | custom-call | tf_op jit(solution)/shard_map/cond/branch_1_fun/pick/pallas_call | solution.py:90
  15.1 0.1 collective-permute-start
  15.1 2.6 %collective-permute-done = f32[512,512]{1,0:T(8,128)S(1)} collective-permute-done((f32[512,512]{1,0:T(8,128)S(1)}, f32[512,512]{1,0:T(8,128)S(1)}, u32[]{:S(2)}, u32[]{:S(2)}) %collective-permute-start) | collective-permute-done | bytes 1048608 | tf_op jit(solution)/shard_map/cond/branch_1_fun/ppermute | solution.py:252
  17.8 0.2 add.6
  18.0 0.6 collective-permute-start.1
  18.6 24.7 %collective-permute-done.1 = f32[512,512]{1,0:T(8,128)S(1)} collective-permute-done((f32[512,512]{1,0:T(8,128)S(1)}, f32[512,512]{1,0:T(8,128)S(1)}, u32[]{:S(2)}, u32[]{:S(2)}) %collective-permute-start.1) | collective-permute-done | bytes 1048608 | tf_op jit(solution)/shard_map/cond/branch_1_fun/ppermute | solution.py:252
  43.3 0.2 add.7
  43.5 0.6 collective-permute-start.2
  44.1 24.0 %collective-permute-done.2 = f32[512,512]{1,0:T(8,128)S(1)} collective-permute-done((f32[512,512]{1,0:T(8,128)S(1)}, f32[512,512]{1,0:T(8,128)S(1)}, u32[]{:S(2)}, u32[]{:S(2)}) %collective-permute-start.2) | collective-permute-done | bytes 1048608 | tf_op jit(solution)/shard_map/cond/branch_1_fun/ppermute | solution.py:252
  68.0 1.2 add.8
  69.2 0.0 collective-permute-start.3
  69.2 3.0 %collective-permute-done.3 = f32[512,512]{1,0:T(8,128)} collective-permute-done((f32[512,512]{1,0:T(8,128)}, f32[512,512]{1,0:T(8,128)}, u32[]{:S(2)}, u32[]{:S(2)}) %collective-permute-start.3) | collective-permute-done | bytes 1048608 | tf_op jit(solution)/shard_map/cond/branch_1_fun/ppermute | solution.py:252
  72.2 0.0 copy-done.1
  72.2 3.2 %upper.1 = (f32[512,512]{1,0:T(8,128)S(1)}, bf16[1536,512]{1,0:T(8,128)(2,1)S(1)}) custom-call(s32[2]{0:T(128)S(1)} %pad_add_fusion.refs_0_, f32[512,512]{1,0:T(8,128)} %get-tuple-element.26.refs_1_.refs_3_, f32[512,512]{1,0:T(8,128)} %get-tuple-element.27.refs_2_.refs_4_, f32[512,512]{1,0:T(8,128)S(1)} %copy-done.1), custom_call_target="tpu_custom_call" | custom-call | tf_op jit(solution)/shard_map/upper/pallas_call | solution.py:130
  75.5 20.5 %collective-permute-done.6.refs_8_ = f32[512,128]{1,0:T(8,128)S(1)} collective-permute-done((f32[512,128]{1,0:T(8,128)}, f32[512,128]{1,0:T(8,128)S(1)}, u32[]{:S(2)}, u32[]{:S(2)}) %collective-permute-start.6) | collective-permute-done | bytes 262176 | tf_op jit(solution)/shard_map/ppermute | solution.py:276
  95.9 0.0 collective-permute-done.5.refs_7_
  95.9 4.2 %collective-permute-start.9 = (f32[3584,128]{1,0:T(8,128)}, f32[3584,128]{1,0:T(8,128)S(1)}, u32[]{:S(2)}, u32[]{:S(2)}) collective-permute-start(f32[3584,128]{1,0:T(8,128)} %collective-permute-done.5.refs_7_), channel_id=1, source_target_pairs={{2,3},{1,0},{6,7},{5,4},{10,11},{9,8},{14,15},{13,12},{18,19},{17,... | collective-permute-start | bytes 5505032 | tf_op jit(solution)/shard_map/ppermute | solution.py:291
  100.1 0.0 collective-permute-done.4.refs_6_
  100.1 3.6 %collective-permute-start.10 = (f32[3584,128]{1,0:T(8,128)}, f32[3584,128]{1,0:T(8,128)S(1)}, u32[]{:S(2)}, u32[]{:S(2)}) collective-permute-start(f32[3584,128]{1,0:T(8,128)} %slice.14), channel_id=1, source_target_pairs={{1,2},{2,1},{5,6},{6,5},{9,10},{10,9},{13,14},{14,13},{17,18},{18,... | collective-permute-start | bytes 5505032 | tf_op jit(solution)/shard_map/ppermute | solution.py:293
  103.7 1.3 collective-permute-start.7
  105.0 2.3 %collective-permute-start.8 = (f32[512,128]{1,0:T(8,128)}, f32[512,128]{1,0:T(8,128)S(1)}, u32[]{:S(2)}, u32[]{:S(2)}) collective-permute-start(f32[512,128]{1,0:T(8,128)} %slice.15), channel_id=1, source_target_pairs={{1,2},{2,1},{5,6},{6,5},{9,10},{10,9},{13,14},{14,13},{17,18},{18,... | collective-permute-start | bytes 786440 | tf_op jit(solution)/shard_map/ppermute | solution.py:293
  107.3 15.6 %main_update.1.refs_1_ = f32[4096,512]{1,0:T(8,128)S(1)} custom-call(s32[2]{0:T(128)S(1)} %pad_add_fusion.refs_0_, s32[512]{0:T(512)S(1)} %copy-done.2, f32[4096,512]{1,0:T(8,128)} %refs_2_.1, f32[512,512]{1,0:T(8,128)} %get-tuple-element.26.refs_1_.refs_3_, f32[512,512]{1,0:T(8,128)} %get-tuple-element.27.refs_2_.refs_4_, f32[4096,128]{1,0:T(8,128)S(1)} %copy-done, ...), custom_call_target="tpu_custom_call" | custom-call | tf_op jit(solution)/shard_map/main_update/pallas_call | solution.py:201
  122.9 17.9 %collective-permute-done.9.refs_2_ = f32[3584,128]{1,0:T(8,128)S(1)} collective-permute-done((f32[3584,128]{1,0:T(8,128)}, f32[3584,128]{1,0:T(8,128)S(1)}, u32[]{:S(2)}, u32[]{:S(2)}) %collective-permute-start.9) | collective-permute-done | bytes 1835040 | tf_op jit(solution)/shard_map/ppermute | solution.py:291
  140.8 4.4 %collective-permute-done.10.refs_3_ = f32[3584,128]{1,0:T(8,128)S(1)} collective-permute-done((f32[3584,128]{1,0:T(8,128)}, f32[3584,128]{1,0:T(8,128)S(1)}, u32[]{:S(2)}, u32[]{:S(2)}) %collective-permute-start.10) | collective-permute-done | bytes 1835040 | tf_op jit(solution)/shard_map/ppermute | solution.py:293
  145.2 6.2 %last_update.2.refs_5_ = f32[4096,512]{1,0:T(8,128)} custom-call(s32[2]{0:T(128)S(1)} %pad_add_fusion.refs_0_, f32[4096,512]{1,0:T(8,128)S(1)} %main_update.1.refs_1_, f32[3584,128]{1,0:T(8,128)S(1)} %collective-permute-done.9.refs_2_, f32[3584,128]{1,0:T(8,128)S(1)} %collective-permute-done.10.refs_3_, bf16[1536,512]{1,0:T(8,128)(2,1)S(1)} %get-tuple-element.32.refs_10_.refs_4_), custom_call_target="tpu_custom_call" | custom-call | tf_op jit(solution)/shard_map/last_update/pallas_call | solution.py:233
  151.4 0.0 collective-permute-done.7.refs_2_
  151.4 0.0 collective-permute-done.8.refs_3_
  151.4 2.7 %last_update.3 = f32[4096,512]{1,0:T(8,128)} custom-call(s32[2]{0:T(128)S(1)} %pad_add_fusion.refs_0_, f32[4096,512]{1,0:T(8,128)S(1)} %main_update.1.refs_1_, f32[512,128]{1,0:T(8,128)S(1)} %collective-permute-done.7.refs_2_, f32[512,128]{1,0:T(8,128)S(1)} %collective-permute-done.8.refs_3_, ...), custom_call_target="tpu_custom_call", output_to_operand_aliasing={{}: (5, {})} | custom-call | tf_op jit(solution)/shard_map/last_update/pallas_call | solution.py:233
Async XLA Ops:
  0.0 6.1 %copy-start = (f32[4096,128]{1,0:T(8,128)S(1)}, f32[4096,128]{1,0:T(8,128)}, u32[]{:S(2)}) copy-start(f32[4096,128]{1,0:T(8,128)} %refs_5_.1) | copy-start | bytes 6291460
  0.0 7.2 %copy-start.2 = (s32[512]{0:T(512)S(1)}, s32[512]{0:T(512)}, u32[]{:S(2)}) copy-start(s32[512]{0:T(512)} %refs_1_.1) | copy-start | bytes 6148
  0.0 100.1 %collective-permute-start.4 = (f32[4096,128]{1,0:T(8,128)}, f32[4096,128]{1,0:T(8,128)}, u32[]{:S(2)}, u32[]{:S(2)}) collective-permute-start(f32[4096,128]{1,0:T(8,128)} %refs_5_.1), channel_id=1, source_target_pairs={{0,1},{1,0},{2,3},{3,2},{4,5},{5,4},{6,7},{7,6},{8,9},{9,8},{10,11... | collective-permute-start | bytes 6291464 | tf_op jit(solution)/shard_map/ppermute | solution.py:275
  3.5 92.4 %collective-permute-start.5 = (f32[3584,128]{1,0:T(8,128)}, f32[3584,128]{1,0:T(8,128)}, u32[]{:S(2)}, u32[]{:S(2)}) collective-permute-start(f32[3584,128]{1,0:T(8,128)} %slice.14), channel_id=1, source_target_pairs={{0,2},{1,3},{2,0},{3,1},{4,6},{5,7},{6,4},{7,5},{8,10},{9,11},{10,... | collective-permute-start | bytes 5505032 | tf_op jit(solution)/shard_map/ppermute | solution.py:276
  6.8 89.1 %collective-permute-start.6 = (f32[512,128]{1,0:T(8,128)}, f32[512,128]{1,0:T(8,128)S(1)}, u32[]{:S(2)}, u32[]{:S(2)}) collective-permute-start(f32[512,128]{1,0:T(8,128)} %slice.15), channel_id=1, source_target_pairs={{0,2},{1,3},{2,0},{3,1},{4,6},{5,7},{6,4},{7,5},{8,10},{9,11},{10,... | collective-permute-start | bytes 786440 | tf_op jit(solution)/shard_map/ppermute | solution.py:276
  8.3 63.9 %copy-start.1 = (f32[512,512]{1,0:T(8,128)S(1)}, f32[512,512]{1,0:T(8,128)}, u32[]{:S(2)}) copy-start(f32[512,512]{1,0:T(8,128)} %refs_3_.1) | copy-start | bytes 3145732
  15.1 2.7 %collective-permute-start = (f32[512,512]{1,0:T(8,128)S(1)}, f32[512,512]{1,0:T(8,128)S(1)}, u32[]{:S(2)}, u32[]{:S(2)}) collective-permute-start(f32[512,512]{1,0:T(8,128)S(1)} %get-tuple-element.16), channel_id=1, source_target_pairs={{0,4},{4,0},{8,12},{12,8},{16,20},{20,16},{24,28},{28,24},{1,5},{5... | collective-permute-start | bytes 3145736 | tf_op jit(solution)/shard_map/cond/branch_1_fun/ppermute | solution.py:252
  18.0 25.3 %collective-permute-start.1 = (f32[512,512]{1,0:T(8,128)S(1)}, f32[512,512]{1,0:T(8,128)S(1)}, u32[]{:S(2)}, u32[]{:S(2)}) collective-permute-start(f32[512,512]{1,0:T(8,128)S(1)} %add.6), channel_id=1, source_target_pairs={{0,8},{4,12},{8,0},{12,4},{16,24},{20,28},{24,16},{28,20},{1,9},{5... | collective-permute-start | bytes 3145736 | tf_op jit(solution)/shard_map/cond/branch_1_fun/ppermute | solution.py:252
  43.5 24.5 %collective-permute-start.2 = (f32[512,512]{1,0:T(8,128)S(1)}, f32[512,512]{1,0:T(8,128)S(1)}, u32[]{:S(2)}, u32[]{:S(2)}) collective-permute-start(f32[512,512]{1,0:T(8,128)S(1)} %add.7), channel_id=1, source_target_pairs={{0,16},{4,20},{8,24},{12,28},{16,0},{20,4},{24,8},{28,12},{1,17},{... | collective-permute-start | bytes 3145736 | tf_op jit(solution)/shard_map/cond/branch_1_fun/ppermute | solution.py:252
  69.2 3.0 %collective-permute-start.3 = (f32[512,512]{1,0:T(8,128)}, f32[512,512]{1,0:T(8,128)}, u32[]{:S(2)}, u32[]{:S(2)}) collective-permute-start(f32[512,512]{1,0:T(8,128)} %add.8), channel_id=1, source_target_pairs={{0,4},{4,0},{8,12},{12,8},{16,20},{20,16},{24,28},{28,24},{1,5},{5... | collective-permute-start | bytes 3145736 | tf_op jit(solution)/shard_map/cond/branch_1_fun/ppermute | solution.py:252
  95.9 44.8 %collective-permute-start.9 = (f32[3584,128]{1,0:T(8,128)}, f32[3584,128]{1,0:T(8,128)S(1)}, u32[]{:S(2)}, u32[]{:S(2)}) collective-permute-start(f32[3584,128]{1,0:T(8,128)} %collective-permute-done.5.refs_7_), channel_id=1, source_target_pairs={{2,3},{1,0},{6,7},{5,4},{10,11},{9,8},{14,15},{13,12},{18,19},{17,... | collective-permute-start | bytes 5505032 | tf_op jit(solution)/shard_map/ppermute | solution.py:291
  100.1 45.1 %collective-permute-start.10 = (f32[3584,128]{1,0:T(8,128)}, f32[3584,128]{1,0:T(8,128)S(1)}, u32[]{:S(2)}, u32[]{:S(2)}) collective-permute-start(f32[3584,128]{1,0:T(8,128)} %slice.14), channel_id=1, source_target_pairs={{1,2},{2,1},{5,6},{6,5},{9,10},{10,9},{13,14},{14,13},{17,18},{18,... | collective-permute-start | bytes 5505032 | tf_op jit(solution)/shard_map/ppermute | solution.py:293
  103.7 47.7 %collective-permute-start.7 = (f32[512,128]{1,0:T(8,128)S(1)}, f32[512,128]{1,0:T(8,128)S(1)}, u32[]{:S(2)}, u32[]{:S(2)}) collective-permute-start(f32[512,128]{1,0:T(8,128)S(1)} %collective-permute-done.6.refs_8_), channel_id=1, source_target_pairs={{2,3},{1,0},{6,7},{5,4},{10,11},{9,8},{14,15},{13,12},{18,19},{17,... | collective-permute-start | bytes 786440 | tf_op jit(solution)/shard_map/ppermute | solution.py:291
  105.0 46.4 %collective-permute-start.8 = (f32[512,128]{1,0:T(8,128)}, f32[512,128]{1,0:T(8,128)S(1)}, u32[]{:S(2)}, u32[]{:S(2)}) collective-permute-start(f32[512,128]{1,0:T(8,128)} %slice.15), channel_id=1, source_target_pairs={{1,2},{2,1},{5,6},{6,5},{9,10},{10,9},{13,14},{14,13},{17,18},{18,... | collective-permute-start | bytes 786440 | tf_op jit(solution)/shard_map/ppermute | solution.py:293

commit v3 on v2

--- a/solution.py
+++ b/solution.py
@@ -9,9 +9,9 @@
 ACROSS = [(0, 2), (1, 3), (2, 0), (3, 1)]
 MIDDLE = [(1, 2), (2, 1)]
 ENDS = [(2, 3), (1, 0)]
-PIECES = (14, 2)
+PIECES = (7, 6, 3)
 TILE = 512
-LAST_TILE = 128
+LAST_TILE = 256
 SMALL = pl.CostEstimate(flops=0, bytes_accessed=0, transcendentals=0)
 HBM = pl.BlockSpec(memory_space=pl.ANY)
 VMEM = pl.BlockSpec(memory_space=pltpu.VMEM)
@@ -39,6 +39,31 @@
 
 def aligned(start, size):
     return pl.ds(pl.multiple_of(start, size), size)
+
+
+def cut_kernel(spans, panel, *refs):
+    outs, sem = refs[:-1], refs[-1]
+    copies = [
+        pltpu.make_async_copy(panel.at[pl.ds(start, size), :], out, sem.at[i])
+        for i, ((start, size), out) in enumerate(zip(spans, outs))
+    ]
+    for copy in copies:
+        copy.start()
+    for copy in copies:
+        copy.wait()
+
+
+def cut(panel, spans):
+    return pl.pallas_call(
+        lambda *refs: cut_kernel(spans, *refs),
+        out_shape=tuple(jax.ShapeDtypeStruct((size, panel.shape[1]), panel.dtype) for _, size in spans),
+        in_specs=[HBM],
+        out_specs=tuple([VMEM] * len(spans)),
+        scratch_shapes=[pltpu.SemaphoreType.DMA((len(spans),))],
+        compiler_params=pltpu.CompilerParams(vmem_limit_bytes=8 << 20),
+        cost_estimate=SMALL,
+        name="cut",
+    )(panel)
 
 
 def pick_kernel(info, pivots, slab, send, keep, rows, sem, top_sem):
@@ -215,37 +240,45 @@
     )(info, pivots, slab, total, other, own, near, *across, upper, terms)
 
 
-def last_kernel(first_row, block, tile, info, base, ends, middle, terms, *refs):
-    out = refs[-1]
-    step = pl.program_id(0)
-    part = aligned(step * tile, tile)
-    delta = dot(left_terms(ends[part, :] + middle[part, :]), terms[...])
-    if first_row < block:
-        keep = (info[1] == 0) & (first_row + step * tile < block)
-        delta = jnp.where(keep, 0.0, delta)
-    out[...] = base[aligned(first_row + step * tile, tile), :] - delta
-
-
-def last_update(info, base, ends, middle, terms, block, first_row, tile, done):
+def last_kernel(first_row, block, tile, parts, info, base, terms, *refs):
+    ends, middle = refs[:parts], refs[parts]
+    out, result, sem = refs[-3:]
+    count, width = middle.shape
+    right = terms[aligned((info[0] ^ 3) * 3 * width, 3 * width), :]
+    copies = []
+    at = 0
+    for end in ends:
+        for inner in range(0, end.shape[0], tile):
+            part = pl.ds(at, tile)
+            delta = dot(left_terms(end[pl.ds(inner, tile), :] + middle[part, :]), right)
+            row = first_row + at
+            if row < block:
+                delta = jnp.where(info[1] == 0, 0.0, delta)
+            result[part, :] = base[pl.ds(row, tile), :] - delta
+            copies.append(pltpu.make_async_copy(result.at[part, :], out.at[pl.ds(row, tile), :], sem))
+            copies[-1].start()
+            at += tile
+    pltpu.make_async_copy(result, out.at[pl.ds(first_row, count), :], sem).wait()
+
+
+def last_update(info, base, terms, ends, middle, block, first_row, tile, done):
     columns = base.shape[1]
-    count, width = ends.shape
-    shift = first_row // tile
-    return pl.pallas_call(
-        lambda *refs: last_kernel(first_row, block, tile, *refs),
+    count = middle.shape[0]
+    return pl.pallas_call(
+        lambda *refs: last_kernel(first_row, block, tile, len(ends), *refs),
         out_shape=jax.ShapeDtypeStruct(base.shape, base.dtype),
         grid_spec=pltpu.PrefetchScalarGridSpec(
             num_scalar_prefetch=1,
-            grid=(count // tile,),
-            in_specs=[VMEM] * 3
-            + [pl.BlockSpec((3 * width, columns), lambda i, info: (info[0] ^ 3, 0))]
-            + [HBM] * len(done),
-            out_specs=pl.BlockSpec((tile, columns), lambda i, info: (i + shift, 0)),
-        ),
-        input_output_aliases={5: 0} if done else {},
+            grid=(),
+            in_specs=[VMEM] * (3 + len(ends)) + [HBM] * len(done),
+            out_specs=HBM,
+            scratch_shapes=[pltpu.VMEM((count, columns), base.dtype), pltpu.SemaphoreType.DMA],
+        ),
+        input_output_aliases={4 + len(ends): 0} if done else {},
         compiler_params=pltpu.CompilerParams(vmem_limit_bytes=24 << 20),
         cost_estimate=SMALL,
         name="last_update",
-    )(info, base, ends, middle, terms, *done)
+    )(info, base, terms, *ends, middle, *done)
 
 
 def exchange(value, bit, count):
@@ -266,14 +299,12 @@
         column = lax.axis_index("pcol")
         info = jnp.stack([column, place]).astype(jnp.int32)
 
-        starts, pieces, at = [], [], 0
-        for part in PIECES:
-            size = rows_here * part // sum(PIECES)
-            starts.append(at)
-            pieces.append(panel[at : at + size])
-            at += size
+        first, second, last = (rows_here * part // sum(PIECES) for part in PIECES)
+        early = first + second
+        pieces = cut(panel, [(0, first), (first, second + last)])
+        across = [lax.ppermute(piece, "pcol", ACROSS) for piece in pieces]
+        panel, _ = lax.optimization_barrier((panel, pieces))
         near = lax.ppermute(panel, "pcol", SWAP)
-        across = [lax.ppermute(piece, "pcol", ACROSS) for piece in pieces]
 
         def gather_rows(slab, pivots):
             send, keep = pick(info, pivots, slab, block)
@@ -287,16 +318,15 @@
 
         total, other = lax.cond(pivots[0] >= 0, gather_rows, no_rows, slab, pivots)
         upper, terms = make_upper(info, total, other, diag_inverse, width)
-        across, _ = lax.optimization_barrier((across, upper))
-        ends = [lax.ppermute(piece, "pcol", ENDS) for piece in across]
-        later, near = lax.optimization_barrier((pieces, near))
-        middle = [lax.ppermute(piece, "pcol", MIDDLE) for piece in later]
+        head, later, upper = lax.optimization_barrier((across[0], panel, upper))
+        most, tail = cut(later, [(0, early), (early, last)])
+        ends = [lax.ppermute(piece, "pcol", ENDS) for piece in (head, across[1][:second], across[1][second:])]
+        middle = lax.ppermute(most, "pcol", MIDDLE)
+        tail, near = lax.optimization_barrier((tail, near))
+        middle_tail = lax.ppermute(tail, "pcol", MIDDLE)
         base = main_update(info, pivots, slab, total, other, panel, near, across, upper, terms)
-        done = []
-        for start, end, mid in zip(starts, ends, middle):
-            tile = LAST_TILE if done else TILE
-            done = [last_update(info, base, end, mid, terms, block, start, min(tile, block), done)]
-        return done[0]
+        result = last_update(info, base, terms, ends[:2], middle, block, 0, LAST_TILE, [])
+        return last_update(info, base, terms, ends[2:], middle_tail, block, early, LAST_TILE, [result])
 
     in_specs = (P("prow", "pcol"), P("prow", "pcol"), P(), P())
     return jax.shard_map(

time: 154 us -> 145 us (0.942); the launches traced: 154 us -> 143 us
  waiting for transfers between devices: 97.1 us -> 86.7 us
  local copies, waits for them, and re-layouts: 4.28 us -> 1.83 us
    ppermute x2, waiting for transfers between devices: 20.5 us -> 13.2 us  [shards(): across = [lax.ppermute(piece, 'pcol', ACROSS) for piece in pieces]]
    slice x2, local copies, waits for them, and re-layouts: 3.77 us -> 0.08 us  [the longest x1 0.05 us: shards(): across[1][:second]]
    ppermute x4 -> x5, waiting for transfers between devices: 22.3 us -> 19.3 us  [the longest x3 17.2 us: shards(): lax.ppermute(piece, 'pcol', ENDS)]
    pallas_call x2 -> x4, Pallas kernels: 8.87 us -> 10.1 us  [the longest x2 5.65 us: last_update(): pl.pallas_call(lambda *refs: last_kernel(first_row, block, tile, len(ends...]
    ppermute x4 -> x5, starting transfers between devices: 11.3 us -> 12.1 us  [the longest x1 4.61 us: shards(): middle = lax.ppermute(most, 'pcol', MIDDLE)]
  transfers between devices with their start and end apart: 11 -> 12, of which waited for: 7 -> 9; matrix products, arithmetic and copies ran while one was open for 4% -> 2% of each run, Pallas kernels for 21% -> 21%
where the time goes in v3:
time: 145 us; the launch traced here: 143 us
  waiting for transfers between devices  86.7 us (60%)
  Pallas kernels  35.6 us (25%)
  starting transfers between devices  16.8 us (12%)
  local copies, waits for them, and re-layouts  1.83 us (1%)
  other arithmetic  1.68 us (1%)
    ppermute x4, waiting for transfers between devices, exchange(): lax.ppermute(value, 'prow', [(i, i ^ 1 << bit) for i in range(count)])  54.2 us
    ppermute x3, waiting for transfers between devices, shards(): lax.ppermute(piece, 'pcol', ENDS)  17.2 us
    pallas_call x1, Pallas kernels, main_update(): pl.pallas_call(lambda *refs: main_kernel(min(TILE, block), *refs), out_sh...  15.6 us
    ppermute x2, waiting for transfers between devices, shards(): across = [lax.ppermute(piece, 'pcol', ACROSS) for piece in pieces]  13.2 us
    pallas_call x1, Pallas kernels, pick(): pl.pallas_call(pick_kernel, out_shape=(shape, shape), grid_spec=pltpu.Pre...  6.75 us
    pallas_call x2, Pallas kernels, last_update(): pl.pallas_call(lambda *refs: last_kernel(first_row, block, tile, len(ends...  5.65 us
    ppermute x1, starting transfers between devices, shards(): middle = lax.ppermute(most, 'pcol', MIDDLE)  4.61 us
    pallas_call x2, Pallas kernels, cut(): pl.pallas_call(lambda *refs: cut_kernel(spans, *refs), out_shape=tuple((j...  4.42 us
  transfers between devices with their start and end apart: 12, of which 9 were waited for; matrix products, arithmetic and copies ran while one was open for 2% of the time, Pallas kernels for 21%

profile of v3, /device:TPU:14, one launch (start us, length us, event | category | flops | bytes accessed | tf_op | source)
XLA Modules:
  0.0 143.4 jit_solution(16730746228671107403)
XLA Ops:
  0.0 0.0 copy-start.1
  0.0 2.9 %cut.2 = (f32[1792,128]{1,0:T(8,128)}, f32[2304,128]{1,0:T(8,128)}) custom-call(f32[4096,128]{1,0:T(8,128)} %refs_5_), custom_call_target="tpu_custom_call" | custom-call | tf_op jit(solution)/shard_map/cut/pallas_call | solution.py:57
  2.9 2.7 %collective-permute-start.4 = (f32[1792,128]{1,0:T(8,128)}, f32[1792,128]{1,0:T(8,128)}, u32[]{:S(2)}, u32[]{:S(2)}) collective-permute-start(f32[1792,128]{1,0:T(8,128)} %get-tuple-element.33), channel_id=1, source_target_pairs={{0,2},{1,3},{2,0},{3,1},{4,6},{5,7},{6,4},{7,5},{8,10},{9,11},{10,... | collective-permute-start | bytes 2752520 | tf_op jit(solution)/shard_map/ppermute | solution.py:305
  5.6 0.4 collective-permute-start.5
  6.0 0.3 collective-permute-start.6
  6.3 0.0 copy-done.1
  6.3 0.5 slice.13
  7.5 0.1 pad_add_fusion.refs_0_
  7.6 63.8 %conditional.1 = (f32[512,512]{1,0:T(8,128)}, f32[512,512]{1,0:T(8,128)}) conditional(s32[]{:T(128)} %bitcast.2, f32[4096,512]{1,0:T(8,128)} %refs_2_.1, (s32[2]{0:T(128)S(1)}, s32[512]{0:T(512)S(1)}, f32[4096,512]{1,0:T(8,128)}) %tuple.22), branch_computations={%region_0.0_spmd, %region_1.0_spmd} | conditional | flops 786432 | bytes 26214576 | solution.py:319
  7.6 6.7 %pick.1 = (f32[512,512]{1,0:T(8,128)S(1)}, f32[512,512]{1,0:T(8,128)S(1)}) custom-call(s32[2]{0:T(128)S(1)} %get-tuple-element.12.info, s32[512]{0:T(512)S(1)} %get-tuple-element.13.pivots, f32[4096,512]{1,0:T(8,128)} %get-tuple-element.14.slab), custom_call_target="tpu_custom_call" | custom-call | tf_op jit(solution)/shard_map/cond/branch_1_fun/pick/pallas_call | solution.py:115
  14.3 0.1 collective-permute-start
  14.4 2.6 %collective-permute-done = f32[512,512]{1,0:T(8,128)S(1)} collective-permute-done((f32[512,512]{1,0:T(8,128)S(1)}, f32[512,512]{1,0:T(8,128)S(1)}, u32[]{:S(2)}, u32[]{:S(2)}) %collective-permute-start) | collective-permute-done | bytes 1048608 | tf_op jit(solution)/shard_map/cond/branch_1_fun/ppermute | solution.py:285
  17.1 0.2 add.6
  17.3 0.6 collective-permute-start.1
  17.9 24.7 %collective-permute-done.1 = f32[512,512]{1,0:T(8,128)S(1)} collective-permute-done((f32[512,512]{1,0:T(8,128)S(1)}, f32[512,512]{1,0:T(8,128)S(1)}, u32[]{:S(2)}, u32[]{:S(2)}) %collective-permute-start.1) | collective-permute-done | bytes 1048608 | tf_op jit(solution)/shard_map/cond/branch_1_fun/ppermute | solution.py:285
  42.5 0.2 add.7
  42.8 0.6 collective-permute-start.2
  43.3 23.9 %collective-permute-done.2 = f32[512,512]{1,0:T(8,128)S(1)} collective-permute-done((f32[512,512]{1,0:T(8,128)S(1)}, f32[512,512]{1,0:T(8,128)S(1)}, u32[]{:S(2)}, u32[]{:S(2)}) %collective-permute-start.2) | collective-permute-done | bytes 1048608 | tf_op jit(solution)/shard_map/cond/branch_1_fun/ppermute | solution.py:285
  67.2 1.2 add.8
  68.4 0.0 collective-permute-start.3
  68.4 3.0 %collective-permute-done.3 = f32[512,512]{1,0:T(8,128)} collective-permute-done((f32[512,512]{1,0:T(8,128)}, f32[512,512]{1,0:T(8,128)}, u32[]{:S(2)}, u32[]{:S(2)}) %collective-permute-start.3) | collective-permute-done | bytes 1048608 | tf_op jit(solution)/shard_map/cond/branch_1_fun/ppermute | solution.py:285
  71.4 0.0 copy-start
  71.4 1.2 copy-done
  72.6 3.2 %upper.1 = (f32[512,512]{1,0:T(8,128)S(1)}, bf16[1536,512]{1,0:T(8,128)(2,1)S(1)}) custom-call(s32[2]{0:T(128)S(1)} %pad_add_fusion.refs_0_, f32[512,512]{1,0:T(8,128)} %get-tuple-element.31.refs_1_.refs_3_, f32[512,512]{1,0:T(8,128)} %get-tuple-element.32.refs_2_.refs_4_, f32[512,512]{1,0:T(8,128)S(1)} %copy-done), custom_call_target="tpu_custom_call" | custom-call | tf_op jit(solution)/shard_map/upper/pallas_call | solution.py:155
  75.9 0.0 collective-permute-done.4.refs_7_
  75.9 1.5 %cut.3 = (f32[3328,128]{1,0:T(8,128)S(1)}, f32[768,128]{1,0:T(8,128)S(1)}) custom-call(f32[4096,128]{1,0:T(8,128)} %refs_5_), custom_call_target="tpu_custom_call" | custom-call | tf_op jit(solution)/shard_map/cut/pallas_call | solution.py:57
  77.4 4.6 %collective-permute-start.11 = (f32[3328,128]{1,0:T(8,128)S(1)}, f32[3328,128]{1,0:T(8,128)S(1)}, u32[]{:S(2)}, u32[]{:S(2)}) collective-permute-start(f32[3328,128]{1,0:T(8,128)S(1)} %get-tuple-element.44), channel_id=1, source_target_pairs={{1,2},{2,1},{5,6},{6,5},{9,10},{10,9},{13,14},{14,13},{17,18},{18,... | collective-permute-start | bytes 5111816 | tf_op jit(solution)/shard_map/ppermute | solution.py:324
  82.0 1.3 collective-permute-start.9
  83.4 13.2 %collective-permute-done.6.refs_8_ = f32[2304,128]{1,0:T(8,128)S(1)} collective-permute-done((f32[2304,128]{1,0:T(8,128)}, f32[2304,128]{1,0:T(8,128)S(1)}, u32[]{:S(2)}, u32[]{:S(2)}) %collective-permute-start.6) | collective-permute-done | bytes 1179680 | tf_op jit(solution)/shard_map/ppermute | solution.py:305
  96.5 0.1 slice.17
  96.6 1.7 %collective-permute-start.10 = (f32[1536,128]{1,0:T(8,128)S(1)}, f32[1536,128]{1,0:T(8,128)S(1)}, u32[]{:S(2)}, u32[]{:S(2)}) collective-permute-start(f32[1536,128]{1,0:T(8,128)S(1)} %slice.17), channel_id=1, source_target_pairs={{2,3},{1,0},{6,7},{5,4},{10,11},{9,8},{14,15},{13,12},{18,19},{17,... | collective-permute-start | bytes 2359304 | tf_op jit(solution)/shard_map/ppermute | solution.py:323
  98.3 1.3 collective-permute-start.7
  99.6 0.0 collective-permute-done.5.refs_6_
  99.6 3.2 %collective-permute-start.8 = (f32[768,128]{1,0:T(8,128)S(1)}, f32[768,128]{1,0:T(8,128)S(1)}, u32[]{:S(2)}, u32[]{:S(2)}) collective-permute-start(f32[768,128]{1,0:T(8,128)S(1)} %get-tuple-element.42), channel_id=1, source_target_pairs={{1,2},{2,1},{5,6},{6,5},{9,10},{10,9},{13,14},{14,13},{17,18},{18,... | collective-permute-start | bytes 1179656 | tf_op jit(solution)/shard_map/ppermute | solution.py:326
  102.8 15.6 %main_update.1.refs_1_ = f32[4096,512]{1,0:T(8,128)S(1)} custom-call(s32[2]{0:T(128)S(1)} %pad_add_fusion.refs_0_, s32[512]{0:T(512)S(1)} %copy-done.1, f32[4096,512]{1,0:T(8,128)} %refs_2_.1, f32[512,512]{1,0:T(8,128)} %get-tuple-element.31.refs_1_.refs_3_, f32[512,512]{1,0:T(8,128)} %get-tuple-element.32.refs_2_.refs_4_, f32[4096,128]{1,0:T(8,128)} %refs_5_, ...), custom_call_target="tpu_custom_call" | custom-call | tf_op jit(solution)/shard_map/main_update/pallas_call | solution.py:226
  118.4 0.0 collective-permute-done.9.refs_3_
  118.4 14.3 %collective-permute-done.10.refs_4_ = f32[1536,128]{1,0:T(8,128)S(1)} collective-permute-done((f32[1536,128]{1,0:T(8,128)S(1)}, f32[1536,128]{1,0:T(8,128)S(1)}, u32[]{:S(2)}, u32[]{:S(2)}) %collective-permute-start.10) | collective-permute-done | bytes 786464 | tf_op jit(solution)/shard_map/ppermute | solution.py:323
  132.6 0.4 collective-permute-done.11.refs_5_
  133.0 3.7 %last_update.2.refs_5_ = f32[4096,512]{1,0:T(8,128)} custom-call(s32[2]{0:T(128)S(1)} %pad_add_fusion.refs_0_, f32[4096,512]{1,0:T(8,128)S(1)} %main_update.1.refs_1_, bf16[1536,512]{1,0:T(8,128)(2,1)S(1)} %get-tuple-element.41.refs_10_.refs_2_, f32[1792,128]{1,0:T(8,128)S(1)} %collective-permute-done.9.refs_3_, ...), custom_call_target="tpu_custom_call" | custom-call | tf_op jit(solution)/shard_map/last_update/pallas_call | solution.py:267
  136.7 2.9 %collective-permute-done.7.refs_3_ = f32[768,128]{1,0:T(8,128)S(1)} collective-permute-done((f32[768,128]{1,0:T(8,128)S(1)}, f32[768,128]{1,0:T(8,128)S(1)}, u32[]{:S(2)}, u32[]{:S(2)}) %collective-permute-start.7) | collective-permute-done | bytes 393248 | tf_op jit(solution)/shard_map/ppermute | solution.py:323
  139.6 1.8 %collective-permute-done.8.refs_4_ = f32[768,128]{1,0:T(8,128)S(1)} collective-permute-done((f32[768,128]{1,0:T(8,128)S(1)}, f32[768,128]{1,0:T(8,128)S(1)}, u32[]{:S(2)}, u32[]{:S(2)}) %collective-permute-start.8) | collective-permute-done | bytes 393248 | tf_op jit(solution)/shard_map/ppermute | solution.py:326
  141.4 2.0 %last_update.3 = f32[4096,512]{1,0:T(8,128)} custom-call(s32[2]{0:T(128)S(1)} %pad_add_fusion.refs_0_, f32[4096,512]{1,0:T(8,128)S(1)} %main_update.1.refs_1_, bf16[1536,512]{1,0:T(8,128)(2,1)S(1)} %get-tuple-element.41.refs_10_.refs_2_, f32[768,128]{1,0:T(8,128)S(1)} %collective-permute-done.7.refs_3_, ...), custom_call_target="tpu_custom_call", output_to_operand_aliasing={{}: (5, {})} | custom-call | tf_op jit(solution)/shard_map/last_update/pallas_call | solution.py:267
  (1 shorter events, 0.0 us)
Async XLA Ops:
  0.0 6.3 %copy-start.1 = (s32[512]{0:T(512)S(1)}, s32[512]{0:T(512)}, u32[]{:S(2)}) copy-start(s32[512]{0:T(512)} %refs_1_.1) | copy-start | bytes 6148
  2.9 73.0 %collective-permute-start.4 = (f32[1792,128]{1,0:T(8,128)}, f32[1792,128]{1,0:T(8,128)}, u32[]{:S(2)}, u32[]{:S(2)}) collective-permute-start(f32[1792,128]{1,0:T(8,128)} %get-tuple-element.33), channel_id=1, source_target_pairs={{0,2},{1,3},{2,0},{3,1},{4,6},{5,7},{6,4},{7,5},{8,10},{9,11},{10,... | collective-permute-start | bytes 2752520 | tf_op jit(solution)/shard_map/ppermute | solution.py:305
  5.6 94.1 %collective-permute-start.5 = (f32[4096,128]{1,0:T(8,128)}, f32[4096,128]{1,0:T(8,128)S(1)}, u32[]{:S(2)}, u32[]{:S(2)}) collective-permute-start(f32[4096,128]{1,0:T(8,128)} %refs_5_), channel_id=1, source_target_pairs={{0,1},{1,0},{2,3},{3,2},{4,5},{5,4},{6,7},{7,6},{8,9},{9,8},{10,11... | collective-permute-start | bytes 6291464 | tf_op jit(solution)/shard_map/ppermute | solution.py:307
  6.0 90.5 %collective-permute-start.6 = (f32[2304,128]{1,0:T(8,128)}, f32[2304,128]{1,0:T(8,128)S(1)}, u32[]{:S(2)}, u32[]{:S(2)}) collective-permute-start(f32[2304,128]{1,0:T(8,128)} %get-tuple-element.34), channel_id=1, source_target_pairs={{0,2},{1,3},{2,0},{3,1},{4,6},{5,7},{6,4},{7,5},{8,10},{9,11},{10,... | collective-permute-start | bytes 3538952 | tf_op jit(solution)/shard_map/ppermute | solution.py:305
  14.3 2.7 %collective-permute-start = (f32[512,512]{1,0:T(8,128)S(1)}, f32[512,512]{1,0:T(8,128)S(1)}, u32[]{:S(2)}, u32[]{:S(2)}) collective-permute-start(f32[512,512]{1,0:T(8,128)S(1)} %get-tuple-element.16), channel_id=1, source_target_pairs={{0,4},{4,0},{8,12},{12,8},{16,20},{20,16},{24,28},{28,24},{1,5},{5... | collective-permute-start | bytes 3145736 | tf_op jit(solution)/shard_map/cond/branch_1_fun/ppermute | solution.py:285
  17.3 25.3 %collective-permute-start.1 = (f32[512,512]{1,0:T(8,128)S(1)}, f32[512,512]{1,0:T(8,128)S(1)}, u32[]{:S(2)}, u32[]{:S(2)}) collective-permute-start(f32[512,512]{1,0:T(8,128)S(1)} %add.6), channel_id=1, source_target_pairs={{0,8},{4,12},{8,0},{12,4},{16,24},{20,28},{24,16},{28,20},{1,9},{5... | collective-permute-start | bytes 3145736 | tf_op jit(solution)/shard_map/cond/branch_1_fun/ppermute | solution.py:285
  42.8 24.4 %collective-permute-start.2 = (f32[512,512]{1,0:T(8,128)S(1)}, f32[512,512]{1,0:T(8,128)S(1)}, u32[]{:S(2)}, u32[]{:S(2)}) collective-permute-start(f32[512,512]{1,0:T(8,128)S(1)} %add.7), channel_id=1, source_target_pairs={{0,16},{4,20},{8,24},{12,28},{16,0},{20,4},{24,8},{28,12},{1,17},{... | collective-permute-start | bytes 3145736 | tf_op jit(solution)/shard_map/cond/branch_1_fun/ppermute | solution.py:285
  68.4 3.0 %collective-permute-start.3 = (f32[512,512]{1,0:T(8,128)}, f32[512,512]{1,0:T(8,128)}, u32[]{:S(2)}, u32[]{:S(2)}) collective-permute-start(f32[512,512]{1,0:T(8,128)} %add.8), channel_id=1, source_target_pairs={{0,4},{4,0},{8,12},{12,8},{16,20},{20,16},{24,28},{28,24},{1,5},{5... | collective-permute-start | bytes 3145736 | tf_op jit(solution)/shard_map/cond/branch_1_fun/ppermute | solution.py:285
  71.4 1.2 copy-start
  77.4 55.6 %collective-permute-start.11 = (f32[3328,128]{1,0:T(8,128)S(1)}, f32[3328,128]{1,0:T(8,128)S(1)}, u32[]{:S(2)}, u32[]{:S(2)}) collective-permute-start(f32[3328,128]{1,0:T(8,128)S(1)} %get-tuple-element.44), channel_id=1, source_target_pairs={{1,2},{2,1},{5,6},{6,5},{9,10},{10,9},{13,14},{14,13},{17,18},{18,... | collective-permute-start | bytes 5111816 | tf_op jit(solution)/shard_map/ppermute | solution.py:324
  82.0 36.3 %collective-permute-start.9 = (f32[1792,128]{1,0:T(8,128)}, f32[1792,128]{1,0:T(8,128)S(1)}, u32[]{:S(2)}, u32[]{:S(2)}) collective-permute-start(f32[1792,128]{1,0:T(8,128)} %collective-permute-done.4.refs_7_), channel_id=1, source_target_pairs={{2,3},{1,0},{6,7},{5,4},{10,11},{9,8},{14,15},{13,12},{18,19},{17,... | collective-permute-start | bytes 2752520 | tf_op jit(solution)/shard_map/ppermute | solution.py:323
  96.6 36.0 %collective-permute-start.10 = (f32[1536,128]{1,0:T(8,128)S(1)}, f32[1536,128]{1,0:T(8,128)S(1)}, u32[]{:S(2)}, u32[]{:S(2)}) collective-permute-start(f32[1536,128]{1,0:T(8,128)S(1)} %slice.17), channel_id=1, source_target_pairs={{2,3},{1,0},{6,7},{5,4},{10,11},{9,8},{14,15},{13,12},{18,19},{17,... | collective-permute-start | bytes 2359304 | tf_op jit(solution)/shard_map/ppermute | solution.py:323
  98.3 41.3 %collective-permute-start.7 = (f32[768,128]{1,0:T(8,128)S(1)}, f32[768,128]{1,0:T(8,128)S(1)}, u32[]{:S(2)}, u32[]{:S(2)}) collective-permute-start(f32[768,128]{1,0:T(8,128)S(1)} %slice.16), channel_id=1, source_target_pairs={{2,3},{1,0},{6,7},{5,4},{10,11},{9,8},{14,15},{13,12},{18,19},{17,... | collective-permute-start | bytes 1179656 | tf_op jit(solution)/shard_map/ppermute | solution.py:323
  99.6 41.8 %collective-permute-start.8 = (f32[768,128]{1,0:T(8,128)S(1)}, f32[768,128]{1,0:T(8,128)S(1)}, u32[]{:S(2)}, u32[]{:S(2)}) collective-permute-start(f32[768,128]{1,0:T(8,128)S(1)} %get-tuple-element.42), channel_id=1, source_target_pairs={{1,2},{2,1},{5,6},{6,5},{9,10},{10,9},{13,14},{14,13},{17,18},{18,... | collective-permute-start | bytes 1179656 | tf_op jit(solution)/shard_map/ppermute | solution.py:326

commit v4 on v3

--- a/solution.py
+++ b/solution.py
@@ -9,7 +9,7 @@
 ACROSS = [(0, 2), (1, 3), (2, 0), (3, 1)]
 MIDDLE = [(1, 2), (2, 1)]
 ENDS = [(2, 3), (1, 0)]
-PIECES = (7, 6, 3)
+PIECES = (15, 13, 4)
 TILE = 512
 LAST_TILE = 256
 SMALL = pl.CostEstimate(flops=0, bytes_accessed=0, transcendentals=0)
@@ -43,27 +43,27 @@
 
 def cut_kernel(spans, panel, *refs):
     outs, sem = refs[:-1], refs[-1]
-    copies = [
-        pltpu.make_async_copy(panel.at[pl.ds(start, size), :], out, sem.at[i])
-        for i, ((start, size), out) in enumerate(zip(spans, outs))
-    ]
-    for copy in copies:
-        copy.start()
-    for copy in copies:
-        copy.wait()
+    for i, ((start, size), out) in enumerate(zip(spans, outs)):
+        for at in range(0, size, TILE):
+            step = min(TILE, size - at)
+            pltpu.make_async_copy(
+                panel.at[pl.ds(start + at, step), :], out.at[pl.ds(at, step), :], sem.at[i]
+            ).start()
+    for i, ((start, size), out) in enumerate(zip(spans, outs)):
+        pltpu.make_async_copy(panel.at[pl.ds(start, size), :], out, sem.at[i]).wait()
 
 
 def cut(panel, spans):
     return pl.pallas_call(
         lambda *refs: cut_kernel(spans, *refs),
         out_shape=tuple(jax.ShapeDtypeStruct((size, panel.shape[1]), panel.dtype) for _, size in spans),
-        in_specs=[HBM],
-        out_specs=tuple([VMEM] * len(spans)),
+        in_specs=[pl.BlockSpec(memory_space=pltpu.HBM)],
+        out_specs=tuple([HBM] * len(spans)),
         scratch_shapes=[pltpu.SemaphoreType.DMA((len(spans),))],
         compiler_params=pltpu.CompilerParams(vmem_limit_bytes=8 << 20),
         cost_estimate=SMALL,
         name="cut",
-    )(panel)
+    )(pltpu.with_memory_space_constraint(panel, pltpu.HBM))
 
 
 def pick_kernel(info, pivots, slab, send, keep, rows, sem, top_sem):
@@ -132,7 +132,7 @@
     )(info, pivots, slab)
 
 
-def upper_kernel(width, info, total, other, inverse, upper, terms):
+def upper_kernel(width, info, total, other, inverse, upper, terms, last_terms):
     block = upper.shape[0]
 
     def fill(picked):
@@ -146,8 +146,12 @@
     def _():
         fill(other)
 
-    for shard in range(block // width):
-        terms[pl.ds(shard * 3 * width, 3 * width), :] = right_terms(upper[pl.ds(shard * width, width), :])
+    for shard in range(4):
+        value = right_terms(upper[aligned((info[0] ^ shard) * width, width), :])
+        if shard < 3:
+            terms[pl.ds(shard * 3 * width, 3 * width), :] = value
+        else:
+            last_terms[...] = value
 
 
 def make_upper(info, total, other, inverse, width):
@@ -156,13 +160,14 @@
         lambda *refs: upper_kernel(width, *refs),
         out_shape=(
             jax.ShapeDtypeStruct((block, columns), total.dtype),
-            jax.ShapeDtypeStruct((3 * block, columns), jnp.bfloat16),
+            jax.ShapeDtypeStruct((9 * width, columns), jnp.bfloat16),
+            jax.ShapeDtypeStruct((3 * width, columns), jnp.bfloat16),
         ),
         grid_spec=pltpu.PrefetchScalarGridSpec(
             num_scalar_prefetch=1,
             grid=(),
             in_specs=[VMEM] * 3,
-            out_specs=(VMEM, VMEM),
+            out_specs=(VMEM, VMEM, VMEM),
         ),
         compiler_params=pltpu.CompilerParams(vmem_limit_bytes=24 << 20),
         cost_estimate=SMALL,
@@ -182,8 +187,8 @@
     loads = [pltpu.make_async_copy(a, b, panel_sem.at[i]) for i, (a, b) in enumerate(loads)]
     for load in loads:
         load.start()
-    column, place = info[0], info[1]
-    count, width = own_rows.shape
+    place = info[1]
+    count = own_rows.shape[0]
     block = upper.shape[0]
     first = place * count
     copy.wait()
@@ -213,8 +218,7 @@
     def _(t):
         part = aligned(t * tile, tile)
         left = [left_terms(panel[part, :]) for panel in (own_rows, near_rows, across_rows)]
-        right = [terms[aligned((column ^ shard) * 3 * width, 3 * width), :] for shard in range(3)]
-        out[part, :] = out[part, :] - dot(jnp.concatenate(left, axis=1), jnp.concatenate(right, axis=0))
+        out[part, :] = out[part, :] - dot(jnp.concatenate(left, axis=1), terms[...])
 
         @pl.when((place == 0) & (t < block // tile))
         def _():
@@ -240,45 +244,40 @@
     )(info, pivots, slab, total, other, own, near, *across, upper, terms)
 
 
-def last_kernel(first_row, block, tile, parts, info, base, terms, *refs):
+def last_kernel(first_row, block, tile, parts, base, terms, *refs):
     ends, middle = refs[:parts], refs[parts]
     out, result, sem = refs[-3:]
-    count, width = middle.shape
-    right = terms[aligned((info[0] ^ 3) * 3 * width, 3 * width), :]
-    copies = []
     at = 0
     for end in ends:
-        for inner in range(0, end.shape[0], tile):
-            part = pl.ds(at, tile)
-            delta = dot(left_terms(end[pl.ds(inner, tile), :] + middle[part, :]), right)
+        inner = 0
+        while inner < end.shape[0]:
+            size = min(tile, end.shape[0] - inner)
+            part = pl.ds(at, size)
             row = first_row + at
+            delta = dot(left_terms(end[pl.ds(inner, size), :] + middle[part, :]), terms[...])
             if row < block:
-                delta = jnp.where(info[1] == 0, 0.0, delta)
-            result[part, :] = base[pl.ds(row, tile), :] - delta
-            copies.append(pltpu.make_async_copy(result.at[part, :], out.at[pl.ds(row, tile), :], sem))
-            copies[-1].start()
-            at += tile
-    pltpu.make_async_copy(result, out.at[pl.ds(first_row, count), :], sem).wait()
-
-
-def last_update(info, base, terms, ends, middle, block, first_row, tile, done):
+                delta = jnp.where(lax.axis_index("prow") == 0, 0.0, delta)
+            result[part, :] = base[pl.ds(row, size), :] - delta
+            pltpu.make_async_copy(result.at[part, :], out.at[pl.ds(row, size), :], sem).start()
+            inner += size
+            at += size
+    pltpu.make_async_copy(result, out.at[pl.ds(first_row, at), :], sem).wait()
+
+
+def last_update(base, terms, ends, middle, block, first_row, done):
     columns = base.shape[1]
     count = middle.shape[0]
     return pl.pallas_call(
-        lambda *refs: last_kernel(first_row, block, tile, len(ends), *refs),
+        lambda *refs: last_kernel(first_row, block, min(LAST_TILE, block), len(ends), *refs),
         out_shape=jax.ShapeDtypeStruct(base.shape, base.dtype),
-        grid_spec=pltpu.PrefetchScalarGridSpec(
-            num_scalar_prefetch=1,
-            grid=(),
-            in_specs=[VMEM] * (3 + len(ends)) + [HBM] * len(done),
-            out_specs=HBM,
-            scratch_shapes=[pltpu.VMEM((count, columns), base.dtype), pltpu.SemaphoreType.DMA],
-        ),
-        input_output_aliases={4 + len(ends): 0} if done else {},
+        in_specs=[VMEM] * (3 + len(ends)) + [HBM] * len(done),
+        out_specs=HBM,
+        scratch_shapes=[pltpu.VMEM((count, columns), base.dtype), pltpu.SemaphoreType.DMA],
+        input_output_aliases={3 + len(ends): 0} if done else {},
         compiler_params=pltpu.CompilerParams(vmem_limit_bytes=24 << 20),
         cost_estimate=SMALL,
         name="last_update",
-    )(info, base, terms, *ends, middle, *done)
+    )(base, terms, *ends, middle, *done)
 
 
 def exchange(value, bit, count):
@@ -301,10 +300,9 @@
 
         first, second, last = (rows_here * part // sum(PIECES) for part in PIECES)
         early = first + second
+        near = lax.ppermute(panel, "pcol", SWAP)
         pieces = cut(panel, [(0, first), (first, second + last)])
         across = [lax.ppermute(piece, "pcol", ACROSS) for piece in pieces]
-        panel, _ = lax.optimization_barrier((panel, pieces))
-        near = lax.ppermute(panel, "pcol", SWAP)
 
         def gather_rows(slab, pivots):
             send, keep = pick(info, pivots, slab, block)
@@ -317,16 +315,17 @@
             return slab[:block], slab[:block]
 
         total, other = lax.cond(pivots[0] >= 0, gather_rows, no_rows, slab, pivots)
-        upper, terms = make_upper(info, total, other, diag_inverse, width)
+        upper, terms, last_terms = make_upper(info, total, other, diag_inverse, width)
         head, later, upper = lax.optimization_barrier((across[0], panel, upper))
         most, tail = cut(later, [(0, early), (early, last)])
-        ends = [lax.ppermute(piece, "pcol", ENDS) for piece in (head, across[1][:second], across[1][second:])]
+        rest, near = lax.optimization_barrier((across[1], near))
+        ends = [lax.ppermute(piece, "pcol", ENDS) for piece in (head, rest[:second], rest[second:])]
         middle = lax.ppermute(most, "pcol", MIDDLE)
-        tail, near = lax.optimization_barrier((tail, near))
+        tail, rest = lax.optimization_barrier((tail, rest))
         middle_tail = lax.ppermute(tail, "pcol", MIDDLE)
         base = main_update(info, pivots, slab, total, other, panel, near, across, upper, terms)
-        result = last_update(info, base, terms, ends[:2], middle, block, 0, LAST_TILE, [])
-        return last_update(info, base, terms, ends[2:], middle_tail, block, early, LAST_TILE, [result])
+        result = last_update(base, last_terms, ends[:2], middle, block, 0, [])
+        return last_update(base, last_terms, ends[2:], middle_tail, block, early, [result])
 
     in_specs = (P("prow", "pcol"), P("prow", "pcol"), P(), P())
     return jax.shard_map(

time: 145 us -> 207 us (1.43)
  Pallas kernels: 35.6 us -> 96.4 us
  starting transfers between devices: 16.8 us -> 19.7 us
  waiting for transfers between devices: 86.7 us -> 84.2 us
    pallas_call x2, Pallas kernels: 4.42 us -> 66.3 us  [cut(): pl.pallas_call(lambda *refs: cut_kernel(spans, *refs), out_shape=tuple((j...]
    ppermute x3, waiting for transfers between devices: 17.2 us -> 0.92 us  [shards(): lax.ppermute(piece, 'pcol', ENDS)]
    ppermute x1, waiting for transfers between devices: 0.36 us -> 14.5 us  [shards(): middle = lax.ppermute(most, 'pcol', MIDDLE)]
  transfers between devices with their start and end apart: 12 -> 12, of which waited for: 9 -> 8; matrix products, arithmetic and copies ran while one was open for 2% -> 1% of each run, Pallas kernels for 21% -> 46%
where the time goes in v4:
time: 207 us; the launch traced here: 205 us
  Pallas kernels  96.4 us (47%)
  waiting for transfers between devices  84.2 us (41%)
  starting transfers between devices  19.7 us (10%)
    pallas_call x2, Pallas kernels, cut(): pl.pallas_call(lambda *refs: cut_kernel(spans, *refs), out_shape=tuple((j...  66.3 us
    ppermute x4, waiting for transfers between devices, exchange(): lax.ppermute(value, 'prow', [(i, i ^ 1 << bit) for i in range(count)])  54.2 us
    pallas_call x1, Pallas kernels, main_update(): pl.pallas_call(lambda *refs: main_kernel(min(TILE, block), *refs), out_sh...  15.5 us
    ppermute x1, waiting for transfers between devices, shards(): middle = lax.ppermute(most, 'pcol', MIDDLE)  14.5 us
    ppermute x2, waiting for transfers between devices, shards(): across = [lax.ppermute(piece, 'pcol', ACROSS) for piece in pieces]  13.5 us
    pallas_call x1, Pallas kernels, pick(): pl.pallas_call(pick_kernel, out_shape=(shape, shape), grid_spec=pltpu.Pre...  6.75 us
    ppermute x3, starting transfers between devices, shards(): lax.ppermute(piece, 'pcol', ENDS)  5.69 us
    ppermute x1, starting transfers between devices, shards(): middle_tail = lax.ppermute(tail, 'pcol', MIDDLE)  4.67 us
  transfers between devices with their start and end apart: 12, of which 8 were waited for; matrix products, arithmetic and copies ran while one was open for 1% of the time, Pallas kernels for 46%

profile of v4, /device:TPU:14, one launch (start us, length us, event | category | flops | bytes accessed | tf_op | source)
XLA Modules:
  0.0 204.6 jit_solution(3384563558761227836)
XLA Ops:
  0.0 0.0 copy-start.2
  0.0 0.4 collective-permute-start.5
  0.5 64.6 %cut.2 = (f32[1920,128]{1,0:T(8,128)}, f32[2176,128]{1,0:T(8,128)}) custom-call(f32[4096,128]{1,0:T(8,128)} %refs_0_.2), custom_call_target="tpu_custom_call" | custom-call | tf_op jit(solution)/shard_map/cut/pallas_call | solution.py:57
  65.1 2.7 %collective-permute-start.6 = (f32[1920,128]{1,0:T(8,128)}, f32[1920,128]{1,0:T(8,128)}, u32[]{:S(2)}, u32[]{:S(2)}) collective-permute-start(f32[1920,128]{1,0:T(8,128)} %get-tuple-element.36), channel_id=1, source_target_pairs={{0,2},{1,3},{2,0},{3,1},{4,6},{5,7},{6,4},{7,5},{8,10},{9,11},{10,... | collective-permute-start | bytes 2949128 | tf_op jit(solution)/shard_map/ppermute | solution.py:305
  67.8 0.3 collective-permute-start.4
  68.1 0.0 copy-done.2
  68.1 0.5 slice.13
  69.3 0.1 pad_add_fusion.refs_0_
  69.4 63.8 %conditional.1 = (f32[512,512]{1,0:T(8,128)}, f32[512,512]{1,0:T(8,128)}) conditional(s32[]{:T(128)} %bitcast.2, f32[4096,512]{1,0:T(8,128)} %refs_2_.1, (s32[2]{0:T(128)S(1)}, s32[512]{0:T(512)S(1)}, f32[4096,512]{1,0:T(8,128)}) %tuple.22), branch_computations={%region_0.0_spmd, %region_1.0_spmd} | conditional | flops 786432 | bytes 26214576 | solution.py:317
  69.4 6.7 %pick.1 = (f32[512,512]{1,0:T(8,128)S(1)}, f32[512,512]{1,0:T(8,128)S(1)}) custom-call(s32[2]{0:T(128)S(1)} %get-tuple-element.12.info, s32[512]{0:T(512)S(1)} %get-tuple-element.13.pivots, f32[4096,512]{1,0:T(8,128)} %get-tuple-element.14.slab), custom_call_target="tpu_custom_call" | custom-call | tf_op jit(solution)/shard_map/cond/branch_1_fun/pick/pallas_call | solution.py:115
  76.1 0.1 collective-permute-start
  76.2 2.6 %collective-permute-done = f32[512,512]{1,0:T(8,128)S(1)} collective-permute-done((f32[512,512]{1,0:T(8,128)S(1)}, f32[512,512]{1,0:T(8,128)S(1)}, u32[]{:S(2)}, u32[]{:S(2)}) %collective-permute-start) | collective-permute-done | bytes 1048608 | tf_op jit(solution)/shard_map/cond/branch_1_fun/ppermute | solution.py:284
  78.8 0.2 add.6
  79.1 0.6 collective-permute-start.1
  79.7 24.7 %collective-permute-done.1 = f32[512,512]{1,0:T(8,128)S(1)} collective-permute-done((f32[512,512]{1,0:T(8,128)S(1)}, f32[512,512]{1,0:T(8,128)S(1)}, u32[]{:S(2)}, u32[]{:S(2)}) %collective-permute-start.1) | collective-permute-done | bytes 1048608 | tf_op jit(solution)/shard_map/cond/branch_1_fun/ppermute | solution.py:284
  104.3 0.2 add.7
  104.5 0.6 collective-permute-start.2
  105.1 23.9 %collective-permute-done.2 = f32[512,512]{1,0:T(8,128)S(1)} collective-permute-done((f32[512,512]{1,0:T(8,128)S(1)}, f32[512,512]{1,0:T(8,128)S(1)}, u32[]{:S(2)}, u32[]{:S(2)}) %collective-permute-start.2) | collective-permute-done | bytes 1048608 | tf_op jit(solution)/shard_map/cond/branch_1_fun/ppermute | solution.py:284
  129.0 1.2 add.8
  130.2 0.0 collective-permute-start.3
  130.2 3.0 %collective-permute-done.3 = f32[512,512]{1,0:T(8,128)} collective-permute-done((f32[512,512]{1,0:T(8,128)}, f32[512,512]{1,0:T(8,128)}, u32[]{:S(2)}, u32[]{:S(2)}) %collective-permute-start.3) | collective-permute-done | bytes 1048608 | tf_op jit(solution)/shard_map/cond/branch_1_fun/ppermute | solution.py:284
  133.2 0.0 copy-start.1
  133.2 1.2 copy-done.1
  134.4 3.2 %upper.1 = (f32[512,512]{1,0:T(8,128)S(1)}, bf16[1152,512]{1,0:T(8,128)(2,1)S(1)}, bf16[384,512]{1,0:T(8,128)(2,1)S(1)}) custom-call(s32[2]{0:T(128)S(1)} %pad_add_fusion.refs_0_, f32[512,512]{1,0:T(8,128)} %get-tuple-element.32.refs_1_.refs_3_, f32[512,512]{1,0:T(8,128)} %get-tuple-element.33.refs_2_.refs_4_, f32[512,512]{1,0:T(8,128)S(1)} %copy-done.1), custom_call_target="tpu_custom_call" | custom-call | tf_op jit(solution)/shard_map/upper/pallas_call | solution.py:159
  137.7 0.0 collective-permute-done.6.refs_7_
  137.7 0.0 copy-start
  137.7 1.7 cut.3
  139.3 4.6 %collective-permute-start.11 = (f32[3584,128]{1,0:T(8,128)S(1)}, f32[3584,128]{1,0:T(8,128)S(1)}, u32[]{:S(2)}, u32[]{:S(2)}) collective-permute-start(f32[3584,128]{1,0:T(8,128)S(1)} %get-tuple-element.46), channel_id=1, source_target_pairs={{1,2},{2,1},{5,6},{6,5},{9,10},{10,9},{13,14},{14,13},{17,18},{18,... | collective-permute-start | bytes 5505032 | tf_op jit(solution)/shard_map/ppermute | solution.py:323
  144.0 1.4 collective-permute-start.9
  145.3 13.5 %collective-permute-done.4.refs_8_ = f32[2176,128]{1,0:T(8,128)S(1)} collective-permute-done((f32[2176,128]{1,0:T(8,128)}, f32[2176,128]{1,0:T(8,128)S(1)}, u32[]{:S(2)}, u32[]{:S(2)}) %collective-permute-start.4) | collective-permute-done | bytes 1114144 | tf_op jit(solution)/shard_map/ppermute | solution.py:305
  158.8 0.0 collective-permute-done.5.refs_6_
  158.8 0.1 slice.15
  158.9 3.0 %collective-permute-start.10 = (f32[1664,128]{1,0:T(8,128)S(1)}, f32[1664,128]{1,0:T(8,128)S(1)}, u32[]{:S(2)}, u32[]{:S(2)}) collective-permute-start(f32[1664,128]{1,0:T(8,128)S(1)} %slice.15), channel_id=1, source_target_pairs={{2,3},{1,0},{6,7},{5,4},{10,11},{9,8},{14,15},{13,12},{18,19},{17,... | collective-permute-start | bytes 2555912 | tf_op jit(solution)/shard_map/ppermute | solution.py:322
  162.0 1.3 collective-permute-start.7
  163.3 4.7 %collective-permute-start.8 = (f32[512,128]{1,0:T(8,128)S(1)}, f32[512,128]{1,0:T(8,128)S(1)}, u32[]{:S(2)}, u32[]{:S(2)}) collective-permute-start(f32[512,128]{1,0:T(8,128)S(1)} %get-tuple-element.44), channel_id=1, source_target_pairs={{1,2},{2,1},{5,6},{6,5},{9,10},{10,9},{13,14},{14,13},{17,18},{18,... | collective-permute-start | bytes 786440 | tf_op jit(solution)/shard_map/ppermute | solution.py:325
  168.0 0.0 copy-done
  168.0 15.5 %main_update.1.refs_0_ = f32[4096,512]{1,0:T(8,128)S(1)} custom-call(s32[2]{0:T(128)S(1)} %pad_add_fusion.refs_0_, s32[512]{0:T(512)S(1)} %copy-done.2, f32[4096,512]{1,0:T(8,128)} %refs_2_.1, f32[512,512]{1,0:T(8,128)} %get-tuple-element.32.refs_1_.refs_3_, f32[512,512]{1,0:T(8,128)} %get-tuple-element.33.refs_2_.refs_4_, f32[4096,128]{1,0:T(8,128)S(1)} %copy-done, ...), custom_call_target="tpu_custom_call" | custom-call | tf_op jit(solution)/shard_map/main_update/pallas_call | solution.py:230
  183.5 0.0 collective-permute-done.9.refs_2_
  183.5 14.5 %collective-permute-done.11.refs_4_ = f32[3584,128]{1,0:T(8,128)S(1)} collective-permute-done((f32[3584,128]{1,0:T(8,128)S(1)}, f32[3584,128]{1,0:T(8,128)S(1)}, u32[]{:S(2)}, u32[]{:S(2)}) %collective-permute-start.11) | collective-permute-done | bytes 1835040 | tf_op jit(solution)/shard_map/ppermute | solution.py:323
  198.1 0.0 collective-permute-done.10.refs_3_
  198.1 3.3 %last_update.2.refs_4_ = f32[4096,512]{1,0:T(8,128)} custom-call(f32[4096,512]{1,0:T(8,128)S(1)} %main_update.1.refs_0_, bf16[384,512]{1,0:T(8,128)(2,1)S(1)} %get-tuple-element.40.refs_1_, f32[1920,128]{1,0:T(8,128)S(1)} %collective-permute-done.9.refs_2_, f32[1664,128]{1,0:T(8,128)S(1)} %collective-permute-done.10.refs_3_, ...), custom_call_target="tpu_custom_call" | custom-call | tf_op jit(solution)/shard_map/last_update/pallas_call | solution.py:270
  201.3 0.9 collective-permute-done.7.refs_2_
  202.2 1.1 collective-permute-done.8.refs_3_
  203.3 1.3 last_update.3
  (1 shorter events, 0.0 us)
Async XLA Ops:
  0.0 68.1 %copy-start.2 = (s32[512]{0:T(512)S(1)}, s32[512]{0:T(512)}, u32[]{:S(2)}) copy-start(s32[512]{0:T(512)} %refs_1_.1) | copy-start | bytes 6148
  0.0 158.8 %collective-permute-start.5 = (f32[4096,128]{1,0:T(8,128)}, f32[4096,128]{1,0:T(8,128)S(1)}, u32[]{:S(2)}, u32[]{:S(2)}) collective-permute-start(f32[4096,128]{1,0:T(8,128)} %refs_0_.2), channel_id=1, source_target_pairs={{0,1},{1,0},{2,3},{3,2},{4,5},{5,4},{6,7},{7,6},{8,9},{9,8},{10,11... | collective-permute-start | bytes 6291464 | tf_op jit(solution)/shard_map/ppermute | solution.py:303
  65.1 72.6 %collective-permute-start.6 = (f32[1920,128]{1,0:T(8,128)}, f32[1920,128]{1,0:T(8,128)}, u32[]{:S(2)}, u32[]{:S(2)}) collective-permute-start(f32[1920,128]{1,0:T(8,128)} %get-tuple-element.36), channel_id=1, source_target_pairs={{0,2},{1,3},{2,0},{3,1},{4,6},{5,7},{6,4},{7,5},{8,10},{9,11},{10,... | collective-permute-start | bytes 2949128 | tf_op jit(solution)/shard_map/ppermute | solution.py:305
  67.8 91.1 %collective-permute-start.4 = (f32[2176,128]{1,0:T(8,128)}, f32[2176,128]{1,0:T(8,128)S(1)}, u32[]{:S(2)}, u32[]{:S(2)}) collective-permute-start(f32[2176,128]{1,0:T(8,128)} %get-tuple-element.34), channel_id=1, source_target_pairs={{0,2},{1,3},{2,0},{3,1},{4,6},{5,7},{6,4},{7,5},{8,10},{9,11},{10,... | collective-permute-start | bytes 3342344 | tf_op jit(solution)/shard_map/ppermute | solution.py:305
  76.1 2.7 %collective-permute-start = (f32[512,512]{1,0:T(8,128)S(1)}, f32[512,512]{1,0:T(8,128)S(1)}, u32[]{:S(2)}, u32[]{:S(2)}) collective-permute-start(f32[512,512]{1,0:T(8,128)S(1)} %get-tuple-element.16), channel_id=1, source_target_pairs={{0,4},{4,0},{8,12},{12,8},{16,20},{20,16},{24,28},{28,24},{1,5},{5... | collective-permute-start | bytes 3145736 | tf_op jit(solution)/shard_map/cond/branch_1_fun/ppermute | solution.py:284
  79.1 25.3 %collective-permute-start.1 = (f32[512,512]{1,0:T(8,128)S(1)}, f32[512,512]{1,0:T(8,128)S(1)}, u32[]{:S(2)}, u32[]{:S(2)}) collective-permute-start(f32[512,512]{1,0:T(8,128)S(1)} %add.6), channel_id=1, source_target_pairs={{0,8},{4,12},{8,0},{12,4},{16,24},{20,28},{24,16},{28,20},{1,9},{5... | collective-permute-start | bytes 3145736 | tf_op jit(solution)/shard_map/cond/branch_1_fun/ppermute | solution.py:284
  104.5 24.4 %collective-permute-start.2 = (f32[512,512]{1,0:T(8,128)S(1)}, f32[512,512]{1,0:T(8,128)S(1)}, u32[]{:S(2)}, u32[]{:S(2)}) collective-permute-start(f32[512,512]{1,0:T(8,128)S(1)} %add.7), channel_id=1, source_target_pairs={{0,16},{4,20},{8,24},{12,28},{16,0},{20,4},{24,8},{28,12},{1,17},{... | collective-permute-start | bytes 3145736 | tf_op jit(solution)/shard_map/cond/branch_1_fun/ppermute | solution.py:284
  130.2 3.0 %collective-permute-start.3 = (f32[512,512]{1,0:T(8,128)}, f32[512,512]{1,0:T(8,128)}, u32[]{:S(2)}, u32[]{:S(2)}) collective-permute-start(f32[512,512]{1,0:T(8,128)} %add.8), channel_id=1, source_target_pairs={{0,4},{4,0},{8,12},{12,8},{16,20},{20,16},{24,28},{28,24},{1,5},{5... | collective-permute-start | bytes 3145736 | tf_op jit(solution)/shard_map/cond/branch_1_fun/ppermute | solution.py:284
  133.2 1.2 copy-start.1
  137.7 30.3 %copy-start = (f32[4096,128]{1,0:T(8,128)S(1)}, f32[4096,128]{1,0:T(8,128)}, u32[]{:S(2)}) copy-start(f32[4096,128]{1,0:T(8,128)} %refs_0_.2) | copy-start | bytes 6291460
  139.3 58.7 %collective-permute-start.11 = (f32[3584,128]{1,0:T(8,128)S(1)}, f32[3584,128]{1,0:T(8,128)S(1)}, u32[]{:S(2)}, u32[]{:S(2)}) collective-permute-start(f32[3584,128]{1,0:T(8,128)S(1)} %get-tuple-element.46), channel_id=1, source_target_pairs={{1,2},{2,1},{5,6},{6,5},{9,10},{10,9},{13,14},{14,13},{17,18},{18,... | collective-permute-start | bytes 5505032 | tf_op jit(solution)/shard_map/ppermute | solution.py:323
  144.0 39.5 %collective-permute-start.9 = (f32[1920,128]{1,0:T(8,128)}, f32[1920,128]{1,0:T(8,128)S(1)}, u32[]{:S(2)}, u32[]{:S(2)}) collective-permute-start(f32[1920,128]{1,0:T(8,128)} %collective-permute-done.6.refs_7_), channel_id=1, source_target_pairs={{2,3},{1,0},{6,7},{5,4},{10,11},{9,8},{14,15},{13,12},{18,19},{17,... | collective-permute-start | bytes 2949128 | tf_op jit(solution)/shard_map/ppermute | solution.py:322
  158.9 39.2 %collective-permute-start.10 = (f32[1664,128]{1,0:T(8,128)S(1)}, f32[1664,128]{1,0:T(8,128)S(1)}, u32[]{:S(2)}, u32[]{:S(2)}) collective-permute-start(f32[1664,128]{1,0:T(8,128)S(1)} %slice.15), channel_id=1, source_target_pairs={{2,3},{1,0},{6,7},{5,4},{10,11},{9,8},{14,15},{13,12},{18,19},{17,... | collective-permute-start | bytes 2555912 | tf_op jit(solution)/shard_map/ppermute | solution.py:322
  162.0 40.3 %collective-permute-start.7 = (f32[512,128]{1,0:T(8,128)S(1)}, f32[512,128]{1,0:T(8,128)S(1)}, u32[]{:S(2)}, u32[]{:S(2)}) collective-permute-start(f32[512,128]{1,0:T(8,128)S(1)} %slice.14), channel_id=1, source_target_pairs={{2,3},{1,0},{6,7},{5,4},{10,11},{9,8},{14,15},{13,12},{18,19},{17,... | collective-permute-start | bytes 786440 | tf_op jit(solution)/shard_map/ppermute | solution.py:322
  163.3 40.0 %collective-permute-start.8 = (f32[512,128]{1,0:T(8,128)S(1)}, f32[512,128]{1,0:T(8,128)S(1)}, u32[]{:S(2)}, u32[]{:S(2)}) collective-permute-start(f32[512,128]{1,0:T(8,128)S(1)} %get-tuple-element.44), channel_id=1, source_target_pairs={{1,2},{2,1},{5,6},{6,5},{9,10},{10,9},{13,14},{14,13},{17,18},{18,... | collective-permute-start | bytes 786440 | tf_op jit(solution)/shard_map/ppermute | solution.py:325

commit v5 on v4

--- a/solution.py
+++ b/solution.py
@@ -41,25 +41,64 @@
     return pl.ds(pl.multiple_of(start, size), size)
 
 
+def load_kernel(spans, panel, *refs):
+    outs, sem = refs[:-1], refs[-1]
+    copies = [
+        pltpu.make_async_copy(panel.at[pl.ds(start, size), :], out, sem.at[i])
+        for i, ((start, size), out) in enumerate(zip(spans, outs))
+    ]
+    for copy in copies:
+        copy.start()
+    for copy in copies:
+        copy.wait()
+
+
+def load_pieces(panel, spans):
+    return pl.pallas_call(
+        lambda *refs: load_kernel(spans, *refs),
+        out_shape=tuple(jax.ShapeDtypeStruct((size, panel.shape[1]), panel.dtype) for _, size in spans),
+        in_specs=[pl.BlockSpec(memory_space=pltpu.HBM)],
+        out_specs=tuple([VMEM] * len(spans)),
+        scratch_shapes=[pltpu.SemaphoreType.DMA((len(spans),))],
+        compiler_params=pltpu.CompilerParams(vmem_limit_bytes=8 << 20),
+        cost_estimate=SMALL,
+        name="load_pieces",
+    )(pltpu.with_memory_space_constraint(panel, pltpu.HBM))
+
+
 def cut_kernel(spans, panel, *refs):
-    outs, sem = refs[:-1], refs[-1]
-    for i, ((start, size), out) in enumerate(zip(spans, outs)):
+    outs, (rows, sem, out_sem) = refs[:-3], refs[-3:]
+    steps = []
+    for i, (start, size) in enumerate(spans):
         for at in range(0, size, TILE):
-            step = min(TILE, size - at)
-            pltpu.make_async_copy(
-                panel.at[pl.ds(start + at, step), :], out.at[pl.ds(at, step), :], sem.at[i]
-            ).start()
-    for i, ((start, size), out) in enumerate(zip(spans, outs)):
-        pltpu.make_async_copy(panel.at[pl.ds(start, size), :], out, sem.at[i]).wait()
+            steps.append((i, start + at, at, min(TILE, size - at)))
+
+    def load(number):
+        _, row, _, size = steps[number]
+        part = pl.ds(row, size)
+        return pltpu.make_async_copy(panel.at[part, :], rows.at[part, :], sem.at[number])
+
+    for number in range(len(steps)):
+        load(number).start()
+    for number, (i, row, at, size) in enumerate(steps):
+        load(number).wait()
+        pltpu.make_async_copy(rows.at[pl.ds(row, size), :], outs[i].at[pl.ds(at, size), :], out_sem.at[i]).start()
+    for i, (start, size) in enumerate(spans):
+        pltpu.make_async_copy(rows.at[pl.ds(start, size), :], outs[i], out_sem.at[i]).wait()
 
 
 def cut(panel, spans):
+    count = sum(-(-size // TILE) for _, size in spans)
     return pl.pallas_call(
         lambda *refs: cut_kernel(spans, *refs),
         out_shape=tuple(jax.ShapeDtypeStruct((size, panel.shape[1]), panel.dtype) for _, size in spans),
         in_specs=[pl.BlockSpec(memory_space=pltpu.HBM)],
         out_specs=tuple([HBM] * len(spans)),
-        scratch_shapes=[pltpu.SemaphoreType.DMA((len(spans),))],
+        scratch_shapes=[
+            pltpu.VMEM(panel.shape, panel.dtype),
+            pltpu.SemaphoreType.DMA((count,)),
+            pltpu.SemaphoreType.DMA((len(spans),)),
+        ],
         compiler_params=pltpu.CompilerParams(vmem_limit_bytes=8 << 20),
         cost_estimate=SMALL,
         name="cut",
@@ -317,7 +356,7 @@
         total, other = lax.cond(pivots[0] >= 0, gather_rows, no_rows, slab, pivots)
         upper, terms, last_terms = make_upper(info, total, other, diag_inverse, width)
         head, later, upper = lax.optimization_barrier((across[0], panel, upper))
-        most, tail = cut(later, [(0, early), (early, last)])
+        most, tail = load_pieces(later, [(0, early), (early, last)])
         rest, near = lax.optimization_barrier((across[1], near))
         ends = [lax.ppermute(piece, "pcol", ENDS) for piece in (head, rest[:second], rest[second:])]
         middle = lax.ppermute(most, "pcol", MIDDLE)

time: 207 us -> 143 us (0.69)
  Pallas kernels: 96.4 us -> 34.1 us
    pallas_call x2 -> x1, Pallas kernels: 66.3 us -> 2.37 us  [cut(): pl.pallas_call(lambda *refs: cut_kernel(spans, *refs), out_shape=tuple((j...]
  transfers between devices with their start and end apart: 12 -> 12, of which waited for: 8 -> 7; matrix products, arithmetic and copies ran while one was open for 1% -> 2% of each run, Pallas kernels for 46% -> 23%
where the time goes in v5:
time: 143 us; the launch traced here: 142 us
  waiting for transfers between devices  84.4 us (59%)
  Pallas kernels  34.1 us (24%)
  starting transfers between devices  19.7 us (14%)
  local copies, waits for them, and re-layouts  1.85 us (1%)
  other arithmetic  1.69 us (1%)
    ppermute x4, waiting for transfers between devices, exchange(): lax.ppermute(value, 'prow', [(i, i ^ 1 << bit) for i in range(count)])  54.2 us
    pallas_call x1, Pallas kernels, main_update(): pl.pallas_call(lambda *refs: main_kernel(min(TILE, block), *refs), out_sh...  15.5 us
    ppermute x1, waiting for transfers between devices, shards(): middle = lax.ppermute(most, 'pcol', MIDDLE)  15.5 us
    ppermute x2, waiting for transfers between devices, shards(): across = [lax.ppermute(piece, 'pcol', ACROSS) for piece in pieces]  13.8 us
    ppermute x3, starting transfers between devices, shards(): lax.ppermute(piece, 'pcol', ENDS)  6.88 us
    pallas_call x1, Pallas kernels, pick(): pl.pallas_call(pick_kernel, out_shape=(shape, shape), grid_spec=pltpu.Pre...  6.75 us
    ppermute x1, starting transfers between devices, shards(): middle = lax.ppermute(most, 'pcol', MIDDLE)  4.61 us
    pallas_call x2, Pallas kernels, last_update(): pl.pallas_call(lambda *refs: last_kernel(first_row, block, min(LAST_TILE,...  4.53 us
  transfers between devices with their start and end apart: 12, of which 7 were waited for; matrix products, arithmetic and copies ran while one was open for 2% of the time, Pallas kernels for 23%

profile of v5, /device:TPU:14, one launch (start us, length us, event | category | flops | bytes accessed | tf_op | source)
XLA Modules:
  0.0 142.5 jit_solution(1796199170585706290)
XLA Ops:
  0.0 0.0 copy-start.2
  0.0 0.4 collective-permute-start.5
  0.5 2.4 %cut.1 = (f32[1920,128]{1,0:T(8,128)}, f32[2176,128]{1,0:T(8,128)}) custom-call(f32[4096,128]{1,0:T(8,128)} %refs_0_.2), custom_call_target="tpu_custom_call" | custom-call | tf_op jit(solution)/shard_map/cut/pallas_call | solution.py:92
  2.8 2.7 %collective-permute-start.6 = (f32[1920,128]{1,0:T(8,128)}, f32[1920,128]{1,0:T(8,128)}, u32[]{:S(2)}, u32[]{:S(2)}) collective-permute-start(f32[1920,128]{1,0:T(8,128)} %get-tuple-element.36), channel_id=1, source_target_pairs={{0,2},{1,3},{2,0},{3,1},{4,6},{5,7},{6,4},{7,5},{8,10},{9,11},{10,... | collective-permute-start | bytes 2949128 | tf_op jit(solution)/shard_map/ppermute | solution.py:344
  5.5 0.3 collective-permute-start.4
  5.8 0.0 copy-done.2
  5.8 0.5 slice.13
  7.0 0.1 pad_add_fusion.refs_0_
  7.1 63.8 %conditional.1 = (f32[512,512]{1,0:T(8,128)}, f32[512,512]{1,0:T(8,128)}) conditional(s32[]{:T(128)} %bitcast.2, f32[4096,512]{1,0:T(8,128)} %refs_2_.1, (s32[2]{0:T(128)S(1)}, s32[512]{0:T(512)S(1)}, f32[4096,512]{1,0:T(8,128)}) %tuple.22), branch_computations={%region_0.0_spmd, %region_1.0_spmd} | conditional | flops 786432 | bytes 26214576 | solution.py:356
  7.1 6.7 %pick.1 = (f32[512,512]{1,0:T(8,128)S(1)}, f32[512,512]{1,0:T(8,128)S(1)}) custom-call(s32[2]{0:T(128)S(1)} %get-tuple-element.12.info, s32[512]{0:T(512)S(1)} %get-tuple-element.13.pivots, f32[4096,512]{1,0:T(8,128)} %get-tuple-element.14.slab), custom_call_target="tpu_custom_call" | custom-call | tf_op jit(solution)/shard_map/cond/branch_1_fun/pick/pallas_call | solution.py:154
  13.8 0.1 collective-permute-start
  13.9 2.6 %collective-permute-done = f32[512,512]{1,0:T(8,128)S(1)} collective-permute-done((f32[512,512]{1,0:T(8,128)S(1)}, f32[512,512]{1,0:T(8,128)S(1)}, u32[]{:S(2)}, u32[]{:S(2)}) %collective-permute-start) | collective-permute-done | bytes 1048608 | tf_op jit(solution)/shard_map/cond/branch_1_fun/ppermute | solution.py:323
  16.6 0.2 add.6
  16.8 0.6 collective-permute-start.1
  17.4 24.7 %collective-permute-done.1 = f32[512,512]{1,0:T(8,128)S(1)} collective-permute-done((f32[512,512]{1,0:T(8,128)S(1)}, f32[512,512]{1,0:T(8,128)S(1)}, u32[]{:S(2)}, u32[]{:S(2)}) %collective-permute-start.1) | collective-permute-done | bytes 1048608 | tf_op jit(solution)/shard_map/cond/branch_1_fun/ppermute | solution.py:323
  42.0 0.2 add.7
  42.3 0.6 collective-permute-start.2
  42.8 23.9 %collective-permute-done.2 = f32[512,512]{1,0:T(8,128)S(1)} collective-permute-done((f32[512,512]{1,0:T(8,128)S(1)}, f32[512,512]{1,0:T(8,128)S(1)}, u32[]{:S(2)}, u32[]{:S(2)}) %collective-permute-start.2) | collective-permute-done | bytes 1048608 | tf_op jit(solution)/shard_map/cond/branch_1_fun/ppermute | solution.py:323
  66.7 1.2 add.8
  67.9 0.0 collective-permute-start.3
  67.9 3.0 %collective-permute-done.3 = f32[512,512]{1,0:T(8,128)} collective-permute-done((f32[512,512]{1,0:T(8,128)}, f32[512,512]{1,0:T(8,128)}, u32[]{:S(2)}, u32[]{:S(2)}) %collective-permute-start.3) | collective-permute-done | bytes 1048608 | tf_op jit(solution)/shard_map/cond/branch_1_fun/ppermute | solution.py:323
  70.9 0.0 copy-start.1
  70.9 1.2 copy-done.1
  72.1 3.2 %upper.1 = (f32[512,512]{1,0:T(8,128)S(1)}, bf16[1152,512]{1,0:T(8,128)(2,1)S(1)}, bf16[384,512]{1,0:T(8,128)(2,1)S(1)}) custom-call(s32[2]{0:T(128)S(1)} %pad_add_fusion.refs_0_, f32[512,512]{1,0:T(8,128)} %get-tuple-element.32.refs_1_.refs_3_, f32[512,512]{1,0:T(8,128)} %get-tuple-element.33.refs_2_.refs_4_, f32[512,512]{1,0:T(8,128)S(1)} %copy-done.1), custom_call_target="tpu_custom_call" | custom-call | tf_op jit(solution)/shard_map/upper/pallas_call | solution.py:198
  75.4 0.0 collective-permute-done.6.refs_7_
  75.4 0.0 copy-start
  75.4 1.7 %load_pieces.1 = (f32[3584,128]{1,0:T(8,128)S(1)}, f32[512,128]{1,0:T(8,128)S(1)}) custom-call(f32[4096,128]{1,0:T(8,128)} %refs_0_.2), custom_call_target="tpu_custom_call" | custom-call | tf_op jit(solution)/shard_map/load_pieces/pallas_call | solution.py:57
  77.1 4.6 %collective-permute-start.11 = (f32[3584,128]{1,0:T(8,128)S(1)}, f32[3584,128]{1,0:T(8,128)S(1)}, u32[]{:S(2)}, u32[]{:S(2)}) collective-permute-start(f32[3584,128]{1,0:T(8,128)S(1)} %get-tuple-element.46), channel_id=1, source_target_pairs={{1,2},{2,1},{5,6},{6,5},{9,10},{10,9},{13,14},{14,13},{17,18},{18,... | collective-permute-start | bytes 5505032 | tf_op jit(solution)/shard_map/ppermute | solution.py:362
  81.7 1.4 collective-permute-start.9
  83.1 13.8 %collective-permute-done.4.refs_8_ = f32[2176,128]{1,0:T(8,128)S(1)} collective-permute-done((f32[2176,128]{1,0:T(8,128)}, f32[2176,128]{1,0:T(8,128)S(1)}, u32[]{:S(2)}, u32[]{:S(2)}) %collective-permute-start.4) | collective-permute-done | bytes 1114144 | tf_op jit(solution)/shard_map/ppermute | solution.py:344
  96.9 0.0 collective-permute-done.5.refs_6_
  96.9 0.1 slice.15
  96.9 4.2 %collective-permute-start.10 = (f32[1664,128]{1,0:T(8,128)S(1)}, f32[1664,128]{1,0:T(8,128)S(1)}, u32[]{:S(2)}, u32[]{:S(2)}) collective-permute-start(f32[1664,128]{1,0:T(8,128)S(1)} %slice.15), channel_id=1, source_target_pairs={{2,3},{1,0},{6,7},{5,4},{10,11},{9,8},{14,15},{13,12},{18,19},{17,... | collective-permute-start | bytes 2555912 | tf_op jit(solution)/shard_map/ppermute | solution.py:361
  101.2 1.3 collective-permute-start.7
  102.5 3.5 %collective-permute-start.8 = (f32[512,128]{1,0:T(8,128)S(1)}, f32[512,128]{1,0:T(8,128)S(1)}, u32[]{:S(2)}, u32[]{:S(2)}) collective-permute-start(f32[512,128]{1,0:T(8,128)S(1)} %get-tuple-element.44), channel_id=1, source_target_pairs={{1,2},{2,1},{5,6},{6,5},{9,10},{10,9},{13,14},{14,13},{17,18},{18,... | collective-permute-start | bytes 786440 | tf_op jit(solution)/shard_map/ppermute | solution.py:364
  106.0 0.0 copy-done
  106.0 15.5 %main_update.1.refs_0_ = f32[4096,512]{1,0:T(8,128)S(1)} custom-call(s32[2]{0:T(128)S(1)} %pad_add_fusion.refs_0_, s32[512]{0:T(512)S(1)} %copy-done.2, f32[4096,512]{1,0:T(8,128)} %refs_2_.1, f32[512,512]{1,0:T(8,128)} %get-tuple-element.32.refs_1_.refs_3_, f32[512,512]{1,0:T(8,128)} %get-tuple-element.33.refs_2_.refs_4_, f32[4096,128]{1,0:T(8,128)S(1)} %copy-done, ...), custom_call_target="tpu_custom_call" | custom-call | tf_op jit(solution)/shard_map/main_update/pallas_call | solution.py:269
  121.5 0.0 collective-permute-done.9.refs_2_
  121.5 15.5 %collective-permute-done.11.refs_4_ = f32[3584,128]{1,0:T(8,128)S(1)} collective-permute-done((f32[3584,128]{1,0:T(8,128)S(1)}, f32[3584,128]{1,0:T(8,128)S(1)}, u32[]{:S(2)}, u32[]{:S(2)}) %collective-permute-start.11) | collective-permute-done | bytes 1835040 | tf_op jit(solution)/shard_map/ppermute | solution.py:362
  137.0 0.0 collective-permute-done.10.refs_3_
  137.0 3.3 %last_update.2.refs_4_ = f32[4096,512]{1,0:T(8,128)} custom-call(f32[4096,512]{1,0:T(8,128)S(1)} %main_update.1.refs_0_, bf16[384,512]{1,0:T(8,128)(2,1)S(1)} %get-tuple-element.40.refs_1_, f32[1920,128]{1,0:T(8,128)S(1)} %collective-permute-done.9.refs_2_, f32[1664,128]{1,0:T(8,128)S(1)} %collective-permute-done.10.refs_3_, ...), custom_call_target="tpu_custom_call" | custom-call | tf_op jit(solution)/shard_map/last_update/pallas_call | solution.py:309
  140.3 0.0 collective-permute-done.7.refs_2_
  140.3 0.9 collective-permute-done.8.refs_3_
  141.2 1.3 last_update.3
  (1 shorter events, 0.0 us)
Async XLA Ops:
  0.0 5.8 %copy-start.2 = (s32[512]{0:T(512)S(1)}, s32[512]{0:T(512)}, u32[]{:S(2)}) copy-start(s32[512]{0:T(512)} %refs_1_.1) | copy-start | bytes 6148
  0.0 96.9 %collective-permute-start.5 = (f32[4096,128]{1,0:T(8,128)}, f32[4096,128]{1,0:T(8,128)S(1)}, u32[]{:S(2)}, u32[]{:S(2)}) collective-permute-start(f32[4096,128]{1,0:T(8,128)} %refs_0_.2), channel_id=1, source_target_pairs={{0,1},{1,0},{2,3},{3,2},{4,5},{5,4},{6,7},{7,6},{8,9},{9,8},{10,11... | collective-permute-start | bytes 6291464 | tf_op jit(solution)/shard_map/ppermute | solution.py:342
  2.8 72.6 %collective-permute-start.6 = (f32[1920,128]{1,0:T(8,128)}, f32[1920,128]{1,0:T(8,128)}, u32[]{:S(2)}, u32[]{:S(2)}) collective-permute-start(f32[1920,128]{1,0:T(8,128)} %get-tuple-element.36), channel_id=1, source_target_pairs={{0,2},{1,3},{2,0},{3,1},{4,6},{5,7},{6,4},{7,5},{8,10},{9,11},{10,... | collective-permute-start | bytes 2949128 | tf_op jit(solution)/shard_map/ppermute | solution.py:344
  5.5 91.4 %collective-permute-start.4 = (f32[2176,128]{1,0:T(8,128)}, f32[2176,128]{1,0:T(8,128)S(1)}, u32[]{:S(2)}, u32[]{:S(2)}) collective-permute-start(f32[2176,128]{1,0:T(8,128)} %get-tuple-element.34), channel_id=1, source_target_pairs={{0,2},{1,3},{2,0},{3,1},{4,6},{5,7},{6,4},{7,5},{8,10},{9,11},{10,... | collective-permute-start | bytes 3342344 | tf_op jit(solution)/shard_map/ppermute | solution.py:344
  13.8 2.7 %collective-permute-start = (f32[512,512]{1,0:T(8,128)S(1)}, f32[512,512]{1,0:T(8,128)S(1)}, u32[]{:S(2)}, u32[]{:S(2)}) collective-permute-start(f32[512,512]{1,0:T(8,128)S(1)} %get-tuple-element.16), channel_id=1, source_target_pairs={{0,4},{4,0},{8,12},{12,8},{16,20},{20,16},{24,28},{28,24},{1,5},{5... | collective-permute-start | bytes 3145736 | tf_op jit(solution)/shard_map/cond/branch_1_fun/ppermute | solution.py:323
  16.8 25.3 %collective-permute-start.1 = (f32[512,512]{1,0:T(8,128)S(1)}, f32[512,512]{1,0:T(8,128)S(1)}, u32[]{:S(2)}, u32[]{:S(2)}) collective-permute-start(f32[512,512]{1,0:T(8,128)S(1)} %add.6), channel_id=1, source_target_pairs={{0,8},{4,12},{8,0},{12,4},{16,24},{20,28},{24,16},{28,20},{1,9},{5... | collective-permute-start | bytes 3145736 | tf_op jit(solution)/shard_map/cond/branch_1_fun/ppermute | solution.py:323
  42.3 24.4 %collective-permute-start.2 = (f32[512,512]{1,0:T(8,128)S(1)}, f32[512,512]{1,0:T(8,128)S(1)}, u32[]{:S(2)}, u32[]{:S(2)}) collective-permute-start(f32[512,512]{1,0:T(8,128)S(1)} %add.7), channel_id=1, source_target_pairs={{0,16},{4,20},{8,24},{12,28},{16,0},{20,4},{24,8},{28,12},{1,17},{... | collective-permute-start | bytes 3145736 | tf_op jit(solution)/shard_map/cond/branch_1_fun/ppermute | solution.py:323
  67.9 3.0 %collective-permute-start.3 = (f32[512,512]{1,0:T(8,128)}, f32[512,512]{1,0:T(8,128)}, u32[]{:S(2)}, u32[]{:S(2)}) collective-permute-start(f32[512,512]{1,0:T(8,128)} %add.8), channel_id=1, source_target_pairs={{0,4},{4,0},{8,12},{12,8},{16,20},{20,16},{24,28},{28,24},{1,5},{5... | collective-permute-start | bytes 3145736 | tf_op jit(solution)/shard_map/cond/branch_1_fun/ppermute | solution.py:323
  70.9 1.2 copy-start.1
  75.4 30.6 %copy-start = (f32[4096,128]{1,0:T(8,128)S(1)}, f32[4096,128]{1,0:T(8,128)}, u32[]{:S(2)}) copy-start(f32[4096,128]{1,0:T(8,128)} %refs_0_.2) | copy-start | bytes 6291460
  77.1 59.9 %collective-permute-start.11 = (f32[3584,128]{1,0:T(8,128)S(1)}, f32[3584,128]{1,0:T(8,128)S(1)}, u32[]{:S(2)}, u32[]{:S(2)}) collective-permute-start(f32[3584,128]{1,0:T(8,128)S(1)} %get-tuple-element.46), channel_id=1, source_target_pairs={{1,2},{2,1},{5,6},{6,5},{9,10},{10,9},{13,14},{14,13},{17,18},{18,... | collective-permute-start | bytes 5505032 | tf_op jit(solution)/shard_map/ppermute | solution.py:362
  81.7 39.8 %collective-permute-start.9 = (f32[1920,128]{1,0:T(8,128)}, f32[1920,128]{1,0:T(8,128)S(1)}, u32[]{:S(2)}, u32[]{:S(2)}) collective-permute-start(f32[1920,128]{1,0:T(8,128)} %collective-permute-done.6.refs_7_), channel_id=1, source_target_pairs={{2,3},{1,0},{6,7},{5,4},{10,11},{9,8},{14,15},{13,12},{18,19},{17,... | collective-permute-start | bytes 2949128 | tf_op jit(solution)/shard_map/ppermute | solution.py:361
  96.9 40.1 %collective-permute-start.10 = (f32[1664,128]{1,0:T(8,128)S(1)}, f32[1664,128]{1,0:T(8,128)S(1)}, u32[]{:S(2)}, u32[]{:S(2)}) collective-permute-start(f32[1664,128]{1,0:T(8,128)S(1)} %slice.15), channel_id=1, source_target_pairs={{2,3},{1,0},{6,7},{5,4},{10,11},{9,8},{14,15},{13,12},{18,19},{17,... | collective-permute-start | bytes 2555912 | tf_op jit(solution)/shard_map/ppermute | solution.py:361
  101.2 39.1 %collective-permute-start.7 = (f32[512,128]{1,0:T(8,128)S(1)}, f32[512,128]{1,0:T(8,128)S(1)}, u32[]{:S(2)}, u32[]{:S(2)}) collective-permute-start(f32[512,128]{1,0:T(8,128)S(1)} %slice.14), channel_id=1, source_target_pairs={{2,3},{1,0},{6,7},{5,4},{10,11},{9,8},{14,15},{13,12},{18,19},{17,... | collective-permute-start | bytes 786440 | tf_op jit(solution)/shard_map/ppermute | solution.py:361
  102.5 38.7 %collective-permute-start.8 = (f32[512,128]{1,0:T(8,128)S(1)}, f32[512,128]{1,0:T(8,128)S(1)}, u32[]{:S(2)}, u32[]{:S(2)}) collective-permute-start(f32[512,128]{1,0:T(8,128)S(1)} %get-tuple-element.44), channel_id=1, source_target_pairs={{1,2},{2,1},{5,6},{6,5},{9,10},{10,9},{13,14},{14,13},{17,18},{18,... | collective-permute-start | bytes 786440 | tf_op jit(solution)/shard_map/ppermute | solution.py:364

commit v6 on v5

--- a/solution.py
+++ b/solution.py
@@ -9,7 +9,7 @@
 ACROSS = [(0, 2), (1, 3), (2, 0), (3, 1)]
 MIDDLE = [(1, 2), (2, 1)]
 ENDS = [(2, 3), (1, 0)]
-PIECES = (15, 13, 4)
+PIECES = (4, 12, 12, 4)
 TILE = 512
 LAST_TILE = 256
 SMALL = pl.CostEstimate(flops=0, bytes_accessed=0, transcendentals=0)
@@ -337,10 +337,13 @@
         column = lax.axis_index("pcol")
         info = jnp.stack([column, place]).astype(jnp.int32)
 
-        first, second, last = (rows_here * part // sum(PIECES) for part in PIECES)
-        early = first + second
+        small, first, second, last = (rows_here * part // sum(PIECES) for part in PIECES)
+        early = small + first + second
         near = lax.ppermute(panel, "pcol", SWAP)
-        pieces = cut(panel, [(0, first), (first, second + last)])
+        start = panel[:small]
+        begun = lax.ppermute(start, "pcol", ACROSS)
+        later, _ = lax.optimization_barrier((panel, start))
+        pieces = cut(later, [(small, first), (small + first, second + last)])
         across = [lax.ppermute(piece, "pcol", ACROSS) for piece in pieces]
 
         def gather_rows(slab, pivots):
@@ -355,14 +358,16 @@
 
         total, other = lax.cond(pivots[0] >= 0, gather_rows, no_rows, slab, pivots)
         upper, terms, last_terms = make_upper(info, total, other, diag_inverse, width)
-        head, later, upper = lax.optimization_barrier((across[0], panel, upper))
+        begun, later, upper = lax.optimization_barrier((begun, panel, upper))
+        head, upper = lax.optimization_barrier((across[0], upper))
+        head = jnp.concatenate([begun, head], axis=0)
         most, tail = load_pieces(later, [(0, early), (early, last)])
         rest, near = lax.optimization_barrier((across[1], near))
         ends = [lax.ppermute(piece, "pcol", ENDS) for piece in (head, rest[:second], rest[second:])]
         middle = lax.ppermute(most, "pcol", MIDDLE)
         tail, rest = lax.optimization_barrier((tail, rest))
         middle_tail = lax.ppermute(tail, "pcol", MIDDLE)
-        base = main_update(info, pivots, slab, total, other, panel, near, across, upper, terms)
+        base = main_update(info, pivots, slab, total, other, panel, near, [head, rest], upper, terms)
         result = last_update(base, last_terms, ends[:2], middle, block, 0, [])
         return last_update(base, last_terms, ends[2:], middle_tail, block, early, [result])
 

time: 143 us -> 142 us (level)
  waiting for transfers between devices: 84.4 us -> 79.8 us
  local copies, waits for them, and re-layouts: 1.85 us -> 4.78 us
    ppermute x2, waiting for transfers between devices: 13.8 us -> 9.27 us  [shards(): across = [lax.ppermute(piece, 'pcol', ACROSS) for piece in pieces]]
    ppermute x0 -> x1, starting transfers between devices: none -> 2.59 us  [shards(): begun = lax.ppermute(start, 'pcol', ACROSS)]
    ppermute x1, starting transfers between devices: 4.61 us -> 2.49 us  [shards(): middle = lax.ppermute(most, 'pcol', MIDDLE)]
    slice x0 -> x1, local copies, waits for them, and re-layouts: none -> 1.69 us  [shards(): start = panel[:small]]
  transfers between devices with their start and end apart: 12 -> 13, of which waited for: 7 -> 7; matrix products, arithmetic and copies ran while one was open for 2% -> 4% of each run, Pallas kernels for 23% -> 23%
where the time goes in v6:
time: 142 us
  waiting for transfers between devices  79.8 us (56%)
  Pallas kernels  33.8 us (24%)
  starting transfers between devices  20.7 us (15%)
  local copies, waits for them, and re-layouts  4.78 us (3%)
  other arithmetic  1.67 us (1%)
    ppermute x4, waiting for transfers between devices, exchange(): lax.ppermute(value, 'prow', [(i, i ^ 1 << bit) for i in range(count)])  54.2 us
    pallas_call x1, Pallas kernels, main_update(): pl.pallas_call(lambda *refs: main_kernel(min(TILE, block), *refs), out_sh...  15.5 us
    ppermute x1, waiting for transfers between devices, shards(): middle = lax.ppermute(most, 'pcol', MIDDLE)  15 us
    ppermute x2, waiting for transfers between devices, shards(): across = [lax.ppermute(piece, 'pcol', ACROSS) for piece in pieces]  9.27 us
    ppermute x3, starting transfers between devices, shards(): lax.ppermute(piece, 'pcol', ENDS)  6.99 us
    pallas_call x1, Pallas kernels, pick(): pl.pallas_call(pick_kernel, out_shape=(shape, shape), grid_spec=pltpu.Pre...  6.75 us
    pallas_call x2, Pallas kernels, last_update(): pl.pallas_call(lambda *refs: last_kernel(first_row, block, min(LAST_TILE,...  4.54 us
    ppermute x1, starting transfers between devices, shards(): middle_tail = lax.ppermute(tail, 'pcol', MIDDLE)  3.98 us
  transfers between devices with their start and end apart: 13, of which 7 were waited for; matrix products, arithmetic and copies ran while one was open for 4% of the time, Pallas kernels for 23%

profile of v6, /device:TPU:14, one launch (start us, length us, event | category | flops | bytes accessed | tf_op | source)
XLA Modules:
  0.0 141.7 jit_solution(1726681278648972166)
XLA Ops:
  0.0 0.0 copy-start.2
  0.0 0.4 collective-permute-start.5
  0.5 1.7 %slice.17 = f32[512,128]{1,0:T(8,128)} slice(f32[4096,128]{1,0:T(8,128)} %refs_5_.1), slice={[0:512], [0:128]} | slice | bytes 524288 | tf_op jit(solution)/shard_map/slice | solution.py:343
  2.1 2.6 %collective-permute-start.6 = (f32[512,128]{1,0:T(8,128)}, f32[512,128]{1,0:T(8,128)S(1)}, u32[]{:S(2)}, u32[]{:S(2)}) collective-permute-start(f32[512,128]{1,0:T(8,128)} %slice.17), channel_id=1, source_target_pairs={{0,2},{1,3},{2,0},{3,1},{4,6},{5,7},{6,4},{7,5},{8,10},{9,11},{10,... | collective-permute-start | bytes 786440 | tf_op jit(solution)/shard_map/ppermute | solution.py:344
  4.7 2.2 %cut.1 = (f32[1536,128]{1,0:T(8,128)}, f32[2048,128]{1,0:T(8,128)}) custom-call(f32[4096,128]{1,0:T(8,128)} %refs_5_.1), custom_call_target="tpu_custom_call" | custom-call | tf_op jit(solution)/shard_map/cut/pallas_call | solution.py:92
  7.0 0.4 collective-permute-start.7
  7.4 2.6 %collective-permute-start.4 = (f32[2048,128]{1,0:T(8,128)}, f32[2048,128]{1,0:T(8,128)S(1)}, u32[]{:S(2)}, u32[]{:S(2)}) collective-permute-start(f32[2048,128]{1,0:T(8,128)} %get-tuple-element.39), channel_id=1, source_target_pairs={{0,2},{1,3},{2,0},{3,1},{4,6},{5,7},{6,4},{7,5},{8,10},{9,11},{10,... | collective-permute-start | bytes 3145736 | tf_op jit(solution)/shard_map/ppermute | solution.py:347
  10.0 0.0 copy-done.2
  10.0 0.6 slice.16
  11.2 0.1 pad_add_fusion.refs_0_
  11.3 63.8 %conditional.1 = (f32[512,512]{1,0:T(8,128)}, f32[512,512]{1,0:T(8,128)}) conditional(s32[]{:T(128)} %bitcast.2, f32[4096,512]{1,0:T(8,128)} %refs_2_.1, (s32[2]{0:T(128)S(1)}, s32[512]{0:T(512)S(1)}, f32[4096,512]{1,0:T(8,128)}) %tuple.26), branch_computations={%region_0.0_spmd, %region_1.0_spmd} | conditional | flops 786432 | bytes 26214576 | solution.py:359
  11.3 6.7 %pick.1 = (f32[512,512]{1,0:T(8,128)S(1)}, f32[512,512]{1,0:T(8,128)S(1)}) custom-call(s32[2]{0:T(128)S(1)} %get-tuple-element.12.info, s32[512]{0:T(512)S(1)} %get-tuple-element.13.pivots, f32[4096,512]{1,0:T(8,128)} %get-tuple-element.14.slab), custom_call_target="tpu_custom_call" | custom-call | tf_op jit(solution)/shard_map/cond/branch_1_fun/pick/pallas_call | solution.py:154
  18.1 0.1 collective-permute-start
  18.2 2.6 %collective-permute-done = f32[512,512]{1,0:T(8,128)S(1)} collective-permute-done((f32[512,512]{1,0:T(8,128)S(1)}, f32[512,512]{1,0:T(8,128)S(1)}, u32[]{:S(2)}, u32[]{:S(2)}) %collective-permute-start) | collective-permute-done | bytes 1048608 | tf_op jit(solution)/shard_map/cond/branch_1_fun/ppermute | solution.py:323
  20.8 0.2 add.6
  21.0 0.6 collective-permute-start.1
  21.6 24.7 %collective-permute-done.1 = f32[512,512]{1,0:T(8,128)S(1)} collective-permute-done((f32[512,512]{1,0:T(8,128)S(1)}, f32[512,512]{1,0:T(8,128)S(1)}, u32[]{:S(2)}, u32[]{:S(2)}) %collective-permute-start.1) | collective-permute-done | bytes 1048608 | tf_op jit(solution)/shard_map/cond/branch_1_fun/ppermute | solution.py:323
  46.3 0.2 add.7
  46.5 0.6 collective-permute-start.2
  47.1 23.9 %collective-permute-done.2 = f32[512,512]{1,0:T(8,128)S(1)} collective-permute-done((f32[512,512]{1,0:T(8,128)S(1)}, f32[512,512]{1,0:T(8,128)S(1)}, u32[]{:S(2)}, u32[]{:S(2)}) %collective-permute-start.2) | collective-permute-done | bytes 1048608 | tf_op jit(solution)/shard_map/cond/branch_1_fun/ppermute | solution.py:323
  70.9 1.2 add.8
  72.1 0.0 collective-permute-start.3
  72.1 3.0 %collective-permute-done.3 = f32[512,512]{1,0:T(8,128)} collective-permute-done((f32[512,512]{1,0:T(8,128)}, f32[512,512]{1,0:T(8,128)}, u32[]{:S(2)}, u32[]{:S(2)}) %collective-permute-start.3) | collective-permute-done | bytes 1048608 | tf_op jit(solution)/shard_map/cond/branch_1_fun/ppermute | solution.py:323
  75.1 0.0 copy-start.1
  75.1 1.2 copy-done.1
  76.3 3.2 %upper.1 = (f32[512,512]{1,0:T(8,128)S(1)}, bf16[1152,512]{1,0:T(8,128)(2,1)S(1)}, bf16[384,512]{1,0:T(8,128)(2,1)S(1)}) custom-call(s32[2]{0:T(128)S(1)} %pad_add_fusion.refs_0_, f32[512,512]{1,0:T(8,128)} %get-tuple-element.36.refs_1_.refs_3_, f32[512,512]{1,0:T(8,128)} %get-tuple-element.37.refs_2_.refs_4_, f32[512,512]{1,0:T(8,128)S(1)} %copy-done.1), custom_call_target="tpu_custom_call" | custom-call | tf_op jit(solution)/shard_map/upper/pallas_call | solution.py:198
  79.6 0.0 collective-permute-done.6
  79.6 1.5 %load_pieces.1 = (f32[3584,128]{1,0:T(8,128)S(1)}, f32[512,128]{1,0:T(8,128)S(1)}) custom-call(f32[4096,128]{1,0:T(8,128)} %refs_5_.1), custom_call_target="tpu_custom_call" | custom-call | tf_op jit(solution)/shard_map/load_pieces/pallas_call | solution.py:57
  81.1 0.0 copy-start
  81.1 2.5 %collective-permute-start.12 = (f32[3584,128]{1,0:T(8,128)S(1)}, f32[3584,128]{1,0:T(8,128)S(1)}, u32[]{:S(2)}, u32[]{:S(2)}) collective-permute-start(f32[3584,128]{1,0:T(8,128)S(1)} %get-tuple-element.54), channel_id=1, source_target_pairs={{1,2},{2,1},{5,6},{6,5},{9,10},{10,9},{13,14},{14,13},{17,18},{18,... | collective-permute-start | bytes 5505032 | tf_op jit(solution)/shard_map/ppermute | solution.py:367
  83.7 0.0 collective-permute-done.7
  83.7 1.2 constant_dynamic-update-slice_fusion.refs_7_
  84.9 2.0 %collective-permute-start.10 = (f32[2048,128]{1,0:T(8,128)S(1)}, f32[2048,128]{1,0:T(8,128)S(1)}, u32[]{:S(2)}, u32[]{:S(2)}) collective-permute-start(f32[2048,128]{1,0:T(8,128)S(1)} %constant_dynamic-update-slice_fusion.refs_7_), channel_id=1, source_target_pairs={{2,3},{1,0},{6,7},{5,4},{10,11},{9,8},{14,15},{13,12},{18,19},{17,... | collective-permute-start | bytes 3145736 | tf_op jit(solution)/shard_map/ppermute | solution.py:366
  86.8 9.3 %collective-permute-done.4.refs_8_ = f32[2048,128]{1,0:T(8,128)S(1)} collective-permute-done((f32[2048,128]{1,0:T(8,128)}, f32[2048,128]{1,0:T(8,128)S(1)}, u32[]{:S(2)}, u32[]{:S(2)}) %collective-permute-start.4) | collective-permute-done | bytes 1048608 | tf_op jit(solution)/shard_map/ppermute | solution.py:347
  96.1 0.0 collective-permute-done.5.refs_6_
  96.1 0.1 slice.19
  96.2 3.7 %collective-permute-start.11 = (f32[1536,128]{1,0:T(8,128)S(1)}, f32[1536,128]{1,0:T(8,128)S(1)}, u32[]{:S(2)}, u32[]{:S(2)}) collective-permute-start(f32[1536,128]{1,0:T(8,128)S(1)} %slice.19), channel_id=1, source_target_pairs={{2,3},{1,0},{6,7},{5,4},{10,11},{9,8},{14,15},{13,12},{18,19},{17,... | collective-permute-start | bytes 2359304 | tf_op jit(solution)/shard_map/ppermute | solution.py:366
  99.9 1.3 collective-permute-start.8
  101.2 4.0 %collective-permute-start.9 = (f32[512,128]{1,0:T(8,128)S(1)}, f32[512,128]{1,0:T(8,128)S(1)}, u32[]{:S(2)}, u32[]{:S(2)}) collective-permute-start(f32[512,128]{1,0:T(8,128)S(1)} %get-tuple-element.53), channel_id=1, source_target_pairs={{1,2},{2,1},{5,6},{6,5},{9,10},{10,9},{13,14},{14,13},{17,18},{18,... | collective-permute-start | bytes 786440 | tf_op jit(solution)/shard_map/ppermute | solution.py:369
  105.2 0.0 copy-done
  105.2 15.5 %main_update.1.refs_0_ = f32[4096,512]{1,0:T(8,128)S(1)} custom-call(s32[2]{0:T(128)S(1)} %pad_add_fusion.refs_0_, s32[512]{0:T(512)S(1)} %copy-done.2, f32[4096,512]{1,0:T(8,128)} %refs_2_.1, f32[512,512]{1,0:T(8,128)} %get-tuple-element.36.refs_1_.refs_3_, f32[512,512]{1,0:T(8,128)} %get-tuple-element.37.refs_2_.refs_4_, f32[4096,128]{1,0:T(8,128)S(1)} %copy-done, ...), custom_call_target="tpu_custom_call" | custom-call | tf_op jit(solution)/shard_map/main_update/pallas_call | solution.py:269
  120.8 0.0 collective-permute-done.10.refs_2_
  120.8 15.0 %collective-permute-done.12.refs_4_ = f32[3584,128]{1,0:T(8,128)S(1)} collective-permute-done((f32[3584,128]{1,0:T(8,128)S(1)}, f32[3584,128]{1,0:T(8,128)S(1)}, u32[]{:S(2)}, u32[]{:S(2)}) %collective-permute-start.12) | collective-permute-done | bytes 1835040 | tf_op jit(solution)/shard_map/ppermute | solution.py:367
  135.7 0.0 collective-permute-done.11.refs_3_
  135.7 3.3 %last_update.2.refs_4_ = f32[4096,512]{1,0:T(8,128)} custom-call(f32[4096,512]{1,0:T(8,128)S(1)} %main_update.1.refs_0_, bf16[384,512]{1,0:T(8,128)(2,1)S(1)} %get-tuple-element.52.refs_1_, f32[2048,128]{1,0:T(8,128)S(1)} %collective-permute-done.10.refs_2_, f32[1536,128]{1,0:T(8,128)S(1)} %collective-permute-done.11.refs_3_, ...), custom_call_target="tpu_custom_call" | custom-call | tf_op jit(solution)/shard_map/last_update/pallas_call | solution.py:309
  139.0 0.0 collective-permute-done.8.refs_2_
  139.0 1.4 collective-permute-done.9.refs_3_
  140.4 1.3 last_update.3
  (2 shorter events, 0.0 us)
Async XLA Ops:
  0.0 10.0 %copy-start.2 = (s32[512]{0:T(512)S(1)}, s32[512]{0:T(512)}, u32[]{:S(2)}) copy-start(s32[512]{0:T(512)} %refs_1_.1) | copy-start | bytes 6148
  0.0 96.1 %collective-permute-start.5 = (f32[4096,128]{1,0:T(8,128)}, f32[4096,128]{1,0:T(8,128)S(1)}, u32[]{:S(2)}, u32[]{:S(2)}) collective-permute-start(f32[4096,128]{1,0:T(8,128)} %refs_5_.1), channel_id=1, source_target_pairs={{0,1},{1,0},{2,3},{3,2},{4,5},{5,4},{6,7},{7,6},{8,9},{9,8},{10,11... | collective-permute-start | bytes 6291464 | tf_op jit(solution)/shard_map/ppermute | solution.py:342
  2.1 77.4 %collective-permute-start.6 = (f32[512,128]{1,0:T(8,128)}, f32[512,128]{1,0:T(8,128)S(1)}, u32[]{:S(2)}, u32[]{:S(2)}) collective-permute-start(f32[512,128]{1,0:T(8,128)} %slice.17), channel_id=1, source_target_pairs={{0,2},{1,3},{2,0},{3,1},{4,6},{5,7},{6,4},{7,5},{8,10},{9,11},{10,... | collective-permute-start | bytes 786440 | tf_op jit(solution)/shard_map/ppermute | solution.py:344
  7.0 76.7 %collective-permute-start.7 = (f32[1536,128]{1,0:T(8,128)}, f32[1536,128]{1,0:T(8,128)}, u32[]{:S(2)}, u32[]{:S(2)}) collective-permute-start(f32[1536,128]{1,0:T(8,128)} %get-tuple-element.43), channel_id=1, source_target_pairs={{0,2},{1,3},{2,0},{3,1},{4,6},{5,7},{6,4},{7,5},{8,10},{9,11},{10,... | collective-permute-start | bytes 2359304 | tf_op jit(solution)/shard_map/ppermute | solution.py:347
  7.4 88.7 %collective-permute-start.4 = (f32[2048,128]{1,0:T(8,128)}, f32[2048,128]{1,0:T(8,128)S(1)}, u32[]{:S(2)}, u32[]{:S(2)}) collective-permute-start(f32[2048,128]{1,0:T(8,128)} %get-tuple-element.39), channel_id=1, source_target_pairs={{0,2},{1,3},{2,0},{3,1},{4,6},{5,7},{6,4},{7,5},{8,10},{9,11},{10,... | collective-permute-start | bytes 3145736 | tf_op jit(solution)/shard_map/ppermute | solution.py:347
  18.1 2.7 %collective-permute-start = (f32[512,512]{1,0:T(8,128)S(1)}, f32[512,512]{1,0:T(8,128)S(1)}, u32[]{:S(2)}, u32[]{:S(2)}) collective-permute-start(f32[512,512]{1,0:T(8,128)S(1)} %get-tuple-element.16), channel_id=1, source_target_pairs={{0,4},{4,0},{8,12},{12,8},{16,20},{20,16},{24,28},{28,24},{1,5},{5... | collective-permute-start | bytes 3145736 | tf_op jit(solution)/shard_map/cond/branch_1_fun/ppermute | solution.py:323
  21.0 25.3 %collective-permute-start.1 = (f32[512,512]{1,0:T(8,128)S(1)}, f32[512,512]{1,0:T(8,128)S(1)}, u32[]{:S(2)}, u32[]{:S(2)}) collective-permute-start(f32[512,512]{1,0:T(8,128)S(1)} %add.6), channel_id=1, source_target_pairs={{0,8},{4,12},{8,0},{12,4},{16,24},{20,28},{24,16},{28,20},{1,9},{5... | collective-permute-start | bytes 3145736 | tf_op jit(solution)/shard_map/cond/branch_1_fun/ppermute | solution.py:323
  46.5 24.4 %collective-permute-start.2 = (f32[512,512]{1,0:T(8,128)S(1)}, f32[512,512]{1,0:T(8,128)S(1)}, u32[]{:S(2)}, u32[]{:S(2)}) collective-permute-start(f32[512,512]{1,0:T(8,128)S(1)} %add.7), channel_id=1, source_target_pairs={{0,16},{4,20},{8,24},{12,28},{16,0},{20,4},{24,8},{28,12},{1,17},{... | collective-permute-start | bytes 3145736 | tf_op jit(solution)/shard_map/cond/branch_1_fun/ppermute | solution.py:323
  72.1 3.0 %collective-permute-start.3 = (f32[512,512]{1,0:T(8,128)}, f32[512,512]{1,0:T(8,128)}, u32[]{:S(2)}, u32[]{:S(2)}) collective-permute-start(f32[512,512]{1,0:T(8,128)} %add.8), channel_id=1, source_target_pairs={{0,4},{4,0},{8,12},{12,8},{16,20},{20,16},{24,28},{28,24},{1,5},{5... | collective-permute-start | bytes 3145736 | tf_op jit(solution)/shard_map/cond/branch_1_fun/ppermute | solution.py:323
  75.1 1.2 copy-start.1
  81.1 24.1 %copy-start = (f32[4096,128]{1,0:T(8,128)S(1)}, f32[4096,128]{1,0:T(8,128)}, u32[]{:S(2)}) copy-start(f32[4096,128]{1,0:T(8,128)} %refs_5_.1) | copy-start | bytes 6291460
  81.1 54.6 %collective-permute-start.12 = (f32[3584,128]{1,0:T(8,128)S(1)}, f32[3584,128]{1,0:T(8,128)S(1)}, u32[]{:S(2)}, u32[]{:S(2)}) collective-permute-start(f32[3584,128]{1,0:T(8,128)S(1)} %get-tuple-element.54), channel_id=1, source_target_pairs={{1,2},{2,1},{5,6},{6,5},{9,10},{10,9},{13,14},{14,13},{17,18},{18,... | collective-permute-start | bytes 5505032 | tf_op jit(solution)/shard_map/ppermute | solution.py:367
  84.9 35.9 %collective-permute-start.10 = (f32[2048,128]{1,0:T(8,128)S(1)}, f32[2048,128]{1,0:T(8,128)S(1)}, u32[]{:S(2)}, u32[]{:S(2)}) collective-permute-start(f32[2048,128]{1,0:T(8,128)S(1)} %constant_dynamic-update-slice_fusion.refs_7_), channel_id=1, source_target_pairs={{2,3},{1,0},{6,7},{5,4},{10,11},{9,8},{14,15},{13,12},{18,19},{17,... | collective-permute-start | bytes 3145736 | tf_op jit(solution)/shard_map/ppermute | solution.py:366
  96.2 39.6 %collective-permute-start.11 = (f32[1536,128]{1,0:T(8,128)S(1)}, f32[1536,128]{1,0:T(8,128)S(1)}, u32[]{:S(2)}, u32[]{:S(2)}) collective-permute-start(f32[1536,128]{1,0:T(8,128)S(1)} %slice.19), channel_id=1, source_target_pairs={{2,3},{1,0},{6,7},{5,4},{10,11},{9,8},{14,15},{13,12},{18,19},{17,... | collective-permute-start | bytes 2359304 | tf_op jit(solution)/shard_map/ppermute | solution.py:366
  99.9 39.1 %collective-permute-start.8 = (f32[512,128]{1,0:T(8,128)S(1)}, f32[512,128]{1,0:T(8,128)S(1)}, u32[]{:S(2)}, u32[]{:S(2)}) collective-permute-start(f32[512,128]{1,0:T(8,128)S(1)} %slice.18), channel_id=1, source_target_pairs={{2,3},{1,0},{6,7},{5,4},{10,11},{9,8},{14,15},{13,12},{18,19},{17,... | collective-permute-start | bytes 786440 | tf_op jit(solution)/shard_map/ppermute | solution.py:366
  101.2 39.2 %collective-permute-start.9 = (f32[512,128]{1,0:T(8,128)S(1)}, f32[512,128]{1,0:T(8,128)S(1)}, u32[]{:S(2)}, u32[]{:S(2)}) collective-permute-start(f32[512,128]{1,0:T(8,128)S(1)} %get-tuple-element.53), channel_id=1, source_target_pairs={{1,2},{2,1},{5,6},{6,5},{9,10},{10,9},{13,14},{14,13},{17,18},{18,... | collective-permute-start | bytes 786440 | tf_op jit(solution)/shard_map/ppermute | solution.py:369

commit v7 on v5

--- a/solution.py
+++ b/solution.py
@@ -9,7 +9,8 @@
 ACROSS = [(0, 2), (1, 3), (2, 0), (3, 1)]
 MIDDLE = [(1, 2), (2, 1)]
 ENDS = [(2, 3), (1, 0)]
-PIECES = (15, 13, 4)
+FAR = [(0, 2), (3, 1)]
+PIECES = (57, 53, 18)
 TILE = 512
 LAST_TILE = 256
 SMALL = pl.CostEstimate(flops=0, bytes_accessed=0, transcendentals=0)
@@ -171,7 +172,7 @@
     )(info, pivots, slab)
 
 
-def upper_kernel(width, info, total, other, inverse, upper, terms, last_terms):
+def upper_kernel(width, info, total, other, inverse, upper, terms, across_terms, last_terms):
     block = upper.shape[0]
 
     def fill(picked):
@@ -187,6 +188,8 @@
 
     for shard in range(4):
         value = right_terms(upper[aligned((info[0] ^ shard) * width, width), :])
+        if shard == 2:
+            across_terms[...] = value
         if shard < 3:
             terms[pl.ds(shard * 3 * width, 3 * width), :] = value
         else:
@@ -200,13 +203,14 @@
         out_shape=(
             jax.ShapeDtypeStruct((block, columns), total.dtype),
             jax.ShapeDtypeStruct((9 * width, columns), jnp.bfloat16),
+            jax.ShapeDtypeStruct((3 * width, columns), jnp.bfloat16),
             jax.ShapeDtypeStruct((3 * width, columns), jnp.bfloat16),
         ),
         grid_spec=pltpu.PrefetchScalarGridSpec(
             num_scalar_prefetch=1,
             grid=(),
             in_specs=[VMEM] * 3,
-            out_specs=(VMEM, VMEM, VMEM),
+            out_specs=(VMEM, VMEM, VMEM, VMEM),
         ),
         compiler_params=pltpu.CompilerParams(vmem_limit_bytes=24 << 20),
         cost_estimate=SMALL,
@@ -253,15 +257,22 @@
     for load in loads:
         load.wait()
 
-    @pl.loop(0, count // tile)
+    def subtract(part, panels):
+        left = jnp.concatenate([left_terms(panel[part, :]) for panel in panels], axis=1)
+        out[part, :] = out[part, :] - dot(left, terms[pl.ds(0, left.shape[1]), :])
+
+    @pl.loop(0, at // tile)
     def _(t):
         part = aligned(t * tile, tile)
-        left = [left_terms(panel[part, :]) for panel in (own_rows, near_rows, across_rows)]
-        out[part, :] = out[part, :] - dot(jnp.concatenate(left, axis=1), terms[...])
+        subtract(part, (own_rows, near_rows, across_rows))
 
         @pl.when((place == 0) & (t < block // tile))
         def _():
             out[part, :] = upper[aligned(jnp.minimum(t * tile, block - tile), tile), :]
+
+    if at % tile:
+        subtract(pl.ds(at - at % tile, at % tile), (own_rows, near_rows, across_rows))
+    subtract(pl.ds(at, count - at), (own_rows, near_rows))
 
 
 def main_update(info, pivots, slab, total, other, own, near, across, upper, terms):
@@ -274,7 +285,8 @@
             grid=(),
             in_specs=[HBM, VMEM, VMEM, HBM, HBM] + [HBM] * len(across) + [VMEM, VMEM],
             out_specs=VMEM,
-            scratch_shapes=[pltpu.VMEM(own.shape, own.dtype)] * 3
+            scratch_shapes=[pltpu.VMEM(own.shape, own.dtype)] * 2
+            + [pltpu.VMEM((sum(piece.shape[0] for piece in across), own.shape[1]), own.dtype)]
             + [pltpu.SemaphoreType.DMA, pltpu.SemaphoreType.DMA((2 + len(across),))],
         ),
         compiler_params=pltpu.CompilerParams(vmem_limit_bytes=32 << 20),
@@ -283,40 +295,44 @@
     )(info, pivots, slab, total, other, own, near, *across, upper, terms)
 
 
-def last_kernel(first_row, block, tile, parts, base, terms, *refs):
-    ends, middle = refs[:parts], refs[parts]
+def last_kernel(first_row, block, tile, groups, base, *refs):
     out, result, sem = refs[-3:]
+    count = result.shape[0]
+    blocks = []
     at = 0
-    for end in ends:
-        inner = 0
-        while inner < end.shape[0]:
-            size = min(tile, end.shape[0] - inner)
-            part = pl.ds(at, size)
-            row = first_row + at
-            delta = dot(left_terms(end[pl.ds(inner, size), :] + middle[part, :]), terms[...])
-            if row < block:
-                delta = jnp.where(lax.axis_index("prow") == 0, 0.0, delta)
-            result[part, :] = base[pl.ds(row, size), :] - delta
-            pltpu.make_async_copy(result.at[part, :], out.at[pl.ds(row, size), :], sem).start()
-            inner += size
-            at += size
-    pltpu.make_async_copy(result, out.at[pl.ds(first_row, at), :], sem).wait()
-
-
-def last_update(base, terms, ends, middle, block, first_row, done):
-    columns = base.shape[1]
-    count = middle.shape[0]
-    return pl.pallas_call(
-        lambda *refs: last_kernel(first_row, block, min(LAST_TILE, block), len(ends), *refs),
+    for offsets in groups:
+        blocks.append((refs[at], list(zip(refs[at + 1 : at + 1 + len(offsets)], offsets))))
+        at += 1 + len(offsets)
+    for at in range(0, count, tile):
+        size = min(tile, count - at)
+        part = pl.ds(at, size)
+        row = first_row + at
+        delta = None
+        for terms, pieces in blocks:
+            left = sum(piece[pl.ds(offset + at, size), :] for piece, offset in pieces)
+            change = dot(left_terms(left), terms[...])
+            delta = change if delta is None else delta + change
+        if row < block:
+            delta = jnp.where(lax.axis_index("prow") == 0, 0.0, delta)
+        result[part, :] = base[pl.ds(row, size), :] - delta
+        pltpu.make_async_copy(result.at[part, :], out.at[pl.ds(row, size), :], sem).start()
+    pltpu.make_async_copy(result, out.at[pl.ds(first_row, count), :], sem).wait()
+
+
+def last_update(base, groups, count, block, first_row, done):
+    offsets = [[offset for _, offset in pieces] for _, pieces in groups]
+    arrays = [array for terms, pieces in groups for array in (terms, *(piece for piece, _ in pieces))]
+    return pl.pallas_call(
+        lambda *refs: last_kernel(first_row, block, min(LAST_TILE, block), offsets, *refs),
         out_shape=jax.ShapeDtypeStruct(base.shape, base.dtype),
-        in_specs=[VMEM] * (3 + len(ends)) + [HBM] * len(done),
+        in_specs=[VMEM] * (1 + len(arrays)) + [HBM] * len(done),
         out_specs=HBM,
-        scratch_shapes=[pltpu.VMEM((count, columns), base.dtype), pltpu.SemaphoreType.DMA],
-        input_output_aliases={3 + len(ends): 0} if done else {},
+        scratch_shapes=[pltpu.VMEM((count, base.shape[1]), base.dtype), pltpu.SemaphoreType.DMA],
+        input_output_aliases={1 + len(arrays): 0} if done else {},
         compiler_params=pltpu.CompilerParams(vmem_limit_bytes=24 << 20),
         cost_estimate=SMALL,
         name="last_update",
-    )(base, terms, *ends, middle, *done)
+    )(base, *arrays, *done)
 
 
 def exchange(value, bit, count):
@@ -339,9 +355,11 @@
 
         first, second, last = (rows_here * part // sum(PIECES) for part in PIECES)
         early = first + second
+        spans = [(0, first), (first, second), (early, last)]
         near = lax.ppermute(panel, "pcol", SWAP)
-        pieces = cut(panel, [(0, first), (first, second + last)])
+        *pieces, tail = cut(panel, spans)
         across = [lax.ppermute(piece, "pcol", ACROSS) for piece in pieces]
+        far = lax.ppermute(tail, "pcol", FAR)
 
         def gather_rows(slab, pivots):
             send, keep = pick(info, pivots, slab, block)
@@ -354,17 +372,24 @@
             return slab[:block], slab[:block]
 
         total, other = lax.cond(pivots[0] >= 0, gather_rows, no_rows, slab, pivots)
-        upper, terms, last_terms = make_upper(info, total, other, diag_inverse, width)
-        head, later, upper = lax.optimization_barrier((across[0], panel, upper))
-        most, tail = load_pieces(later, [(0, early), (early, last)])
-        rest, near = lax.optimization_barrier((across[1], near))
-        ends = [lax.ppermute(piece, "pcol", ENDS) for piece in (head, rest[:second], rest[second:])]
-        middle = lax.ppermute(most, "pcol", MIDDLE)
-        tail, rest = lax.optimization_barrier((tail, rest))
-        middle_tail = lax.ppermute(tail, "pcol", MIDDLE)
-        base = main_update(info, pivots, slab, total, other, panel, near, across, upper, terms)
-        result = last_update(base, last_terms, ends[:2], middle, block, 0, [])
-        return last_update(base, last_terms, ends[2:], middle_tail, block, early, [result])
+        upper, terms, across_terms, last_terms = make_upper(info, total, other, diag_inverse, width)
+        far, later, upper = lax.optimization_barrier((far, panel, upper))
+        head, upper = lax.optimization_barrier((across[0], upper))
+        head_mid, rest_mid, tail_mid = load_pieces(later, spans)
+        tail_mid = lax.ppermute(tail_mid, "pcol", MIDDLE)
+        head_mid = lax.ppermute(head_mid, "pcol", MIDDLE)
+        head_end = lax.ppermute(head, "pcol", ENDS)
+        rest, rest_mid, near = lax.optimization_barrier((across[1], rest_mid, near))
+        rest_end = lax.ppermute(rest, "pcol", ENDS)
+        rest_mid = lax.ppermute(rest_mid, "pcol", MIDDLE)
+        both, rest = lax.optimization_barrier((jnp.concatenate([far, tail_mid], axis=0), rest))
+        both = lax.ppermute(both, "pcol", ENDS)
+
+        base = main_update(info, pivots, slab, total, other, panel, near, [head, rest], upper, terms)
+        result = last_update(base, [(last_terms, [(head_end, 0), (head_mid, 0)])], first, block, 0, [])
+        result = last_update(base, [(last_terms, [(rest_end, 0), (rest_mid, 0)])], second, block, first, [result])
+        groups = [(across_terms, [(far, 0), (both, last)]), (last_terms, [(tail_mid, 0), (both, 0)])]
+        return last_update(base, groups, last, block, early, [result])
 
     in_specs = (P("prow", "pcol"), P("prow", "pcol"), P(), P())
     return jax.shard_map(

time: 143 us -> 158 us (1.10)
  the two profiles are of different devices: /device:TPU:14 before, /device:TPU:0 now
where the time goes in v7:
time: 158 us
  waiting for transfers between devices  98.7 us (62%)
  Pallas kernels  35.4 us (22%)
  starting transfers between devices  19.7 us (12%)
  other arithmetic  1.71 us (1%)
    ppermute x4, waiting for transfers between devices, exchange(): lax.ppermute(value, 'prow', [(i, i ^ 1 << bit) for i in range(count)])  52.3 us
    ppermute x1, waiting for transfers between devices, shards(): rest_end = lax.ppermute(rest, 'pcol', ENDS)  16.4 us
    pallas_call x1, Pallas kernels, main_update(): pl.pallas_call(lambda *refs: main_kernel(min(TILE, block), *refs), out_sh...  15.3 us
    ppermute x1, waiting for transfers between devices, shards(): head_end = lax.ppermute(head, 'pcol', ENDS)  10.9 us
    ppermute x1, waiting for transfers between devices, shards(): far = lax.ppermute(tail, 'pcol', FAR)  10.7 us
    ppermute x1, waiting for transfers between devices, shards(): both = lax.ppermute(both, 'pcol', ENDS)  8.22 us
    pallas_call x1, Pallas kernels, pick(): pl.pallas_call(pick_kernel, out_shape=(shape, shape), grid_spec=pltpu.Pre...  7.12 us
    pallas_call x3, Pallas kernels, last_update(): pl.pallas_call(lambda *refs: last_kernel(first_row, block, min(LAST_TILE,...  5.76 us
  transfers between devices with their start and end apart: 14, of which 8 were waited for; matrix products, arithmetic and copies ran while one was open for 2% of the time, Pallas kernels for 21%

profile of v7, /device:TPU:0, one launch (start us, length us, event | category | flops | bytes accessed | tf_op | source)
XLA Modules:
  0.0 157.5 jit_solution(11545205804484771929)
XLA Ops:
  0.0 3.0 %collective-permute-start.6 = (f32[4096,128]{1,0:T(8,128)}, f32[4096,128]{1,0:T(8,128)}, u32[]{:S(2)}, u32[]{:S(2)}) collective-permute-start(f32[4096,128]{1,0:T(8,128)} %refs_5_.1), channel_id=1, source_target_pairs={{0,1},{1,0},{2,3},{3,2},{4,5},{5,4},{6,7},{7,6},{8,9},{9,8},{10,11... | collective-permute-start | bytes 6291464 | tf_op jit(solution)/shard_map/ppermute | solution.py:359
  3.0 2.4 %cut.1 = (f32[1824,128]{1,0:T(8,128)}, f32[1696,128]{1,0:T(8,128)}, f32[576,128]{1,0:T(8,128)}) custom-call(f32[4096,128]{1,0:T(8,128)} %refs_5_.1), custom_call_target="tpu_custom_call" | custom-call | tf_op jit(solution)/shard_map/cut/pallas_call | solution.py:93
  5.5 2.7 %collective-permute-start.7 = (f32[1824,128]{1,0:T(8,128)}, f32[1824,128]{1,0:T(8,128)}, u32[]{:S(2)}, u32[]{:S(2)}) collective-permute-start(f32[1824,128]{1,0:T(8,128)} %get-tuple-element.47), channel_id=1, source_target_pairs={{0,2},{1,3},{2,0},{3,1},{4,6},{5,7},{6,4},{7,5},{8,10},{9,11},{10,... | collective-permute-start | bytes 2801672 | tf_op jit(solution)/shard_map/ppermute | solution.py:361
  8.1 0.3 collective-permute-start.4
  8.4 4.5 %collective-permute-start.5 = (f32[576,128]{1,0:T(8,128)}, f32[576,128]{1,0:T(8,128)S(1)}, u32[]{:S(2)}, u32[]{:S(2)}) collective-permute-start(f32[576,128]{1,0:T(8,128)} %get-tuple-element.42), channel_id=1, source_target_pairs={{0,2},{3,1},{4,6},{7,5},{8,10},{11,9},{12,14},{15,13},{16,18},{19,... | collective-permute-start | bytes 884744 | tf_op jit(solution)/shard_map/ppermute | solution.py:362
  13.0 1.2 slice.7
  14.8 0.1 pad_add_fusion.refs_0_
  14.9 0.0 copy-start.1
  14.9 0.0 copy-start
  14.9 64.3 %conditional.1 = (f32[512,512]{1,0:T(8,128)}, f32[512,512]{1,0:T(8,128)}) conditional(s32[]{:T(128)} %bitcast.2, f32[4096,512]{1,0:T(8,128)} %refs_2_.1, (s32[2]{0:T(128)S(1)}, s32[512]{0:T(512)}, f32[4096,512]{1,0:T(8,128)}) %tuple.17), branch_computations={%region_0.0_spmd, %region_1.0_spmd} | conditional | flops 786432 | bytes 26214576 | solution.py:374
  14.9 7.1 %pick.1 = (f32[512,512]{1,0:T(8,128)S(1)}, f32[512,512]{1,0:T(8,128)S(1)}) custom-call(s32[2]{0:T(128)S(1)} %get-tuple-element.12.info, s32[512]{0:T(512)} %get-tuple-element.13.pivots, f32[4096,512]{1,0:T(8,128)} %get-tuple-element.14.slab), custom_call_target="tpu_custom_call" | custom-call | tf_op jit(solution)/shard_map/cond/branch_1_fun/pick/pallas_call | solution.py:155
  22.0 0.1 collective-permute-start
  22.1 2.6 %collective-permute-done = f32[512,512]{1,0:T(8,128)S(1)} collective-permute-done((f32[512,512]{1,0:T(8,128)S(1)}, f32[512,512]{1,0:T(8,128)S(1)}, u32[]{:S(2)}, u32[]{:S(2)}) %collective-permute-start) | collective-permute-done | bytes 1048608 | tf_op jit(solution)/shard_map/cond/branch_1_fun/ppermute | solution.py:339
  24.7 0.2 add.6
  24.9 1.6 collective-permute-start.1
  26.5 23.7 %collective-permute-done.1 = f32[512,512]{1,0:T(8,128)S(1)} collective-permute-done((f32[512,512]{1,0:T(8,128)S(1)}, f32[512,512]{1,0:T(8,128)S(1)}, u32[]{:S(2)}, u32[]{:S(2)}) %collective-permute-start.1) | collective-permute-done | bytes 1048608 | tf_op jit(solution)/shard_map/cond/branch_1_fun/ppermute | solution.py:339
  50.2 0.2 add.7
  50.4 1.6 %collective-permute-start.2 = (f32[512,512]{1,0:T(8,128)S(1)}, f32[512,512]{1,0:T(8,128)S(1)}, u32[]{:S(2)}, u32[]{:S(2)}) collective-permute-start(f32[512,512]{1,0:T(8,128)S(1)} %add.7), channel_id=1, source_target_pairs={{0,16},{4,20},{8,24},{12,28},{16,0},{20,4},{24,8},{28,12},{1,17},{... | collective-permute-start | bytes 3145736 | tf_op jit(solution)/shard_map/cond/branch_1_fun/ppermute | solution.py:339
  52.0 23.0 %collective-permute-done.2 = f32[512,512]{1,0:T(8,128)S(1)} collective-permute-done((f32[512,512]{1,0:T(8,128)S(1)}, f32[512,512]{1,0:T(8,128)S(1)}, u32[]{:S(2)}, u32[]{:S(2)}) %collective-permute-start.2) | collective-permute-done | bytes 1048608 | tf_op jit(solution)/shard_map/cond/branch_1_fun/ppermute | solution.py:339
  75.0 1.2 add.8
  76.1 0.0 collective-permute-start.3
  76.2 3.0 %collective-permute-done.3 = f32[512,512]{1,0:T(8,128)} collective-permute-done((f32[512,512]{1,0:T(8,128)}, f32[512,512]{1,0:T(8,128)}, u32[]{:S(2)}, u32[]{:S(2)}) %collective-permute-start.3) | collective-permute-done | bytes 1048608 | tf_op jit(solution)/shard_map/cond/branch_1_fun/ppermute | solution.py:339
  79.2 0.0 copy-done.1
  79.2 3.3 %upper.1 = (f32[512,512]{1,0:T(8,128)S(1)}, bf16[1152,512]{1,0:T(8,128)(2,1)S(1)}, bf16[384,512]{1,0:T(8,128)(2,1)S(1)}, bf16[384,512]{1,0:T(8,128)(2,1)S(1)}) custom-call(s32[2]{0:T(128)S(1)} %pad_add_fusion.refs_0_, f32[512,512]{1,0:T(8,128)} %get-tuple-element.39.refs_1_.refs_3_, f32[512,512]{1,0:T(8,128)} %get-tuple-element.40.refs_2_.refs_4_, ...), custom_call_target="tpu_custom_call" | custom-call | tf_op jit(solution)/shard_map/upper/pallas_call | solution.py:201
  82.4 10.7 %collective-permute-done.5.refs_2_ = f32[576,128]{1,0:T(8,128)S(1)} collective-permute-done((f32[576,128]{1,0:T(8,128)}, f32[576,128]{1,0:T(8,128)S(1)}, u32[]{:S(2)}, u32[]{:S(2)}) %collective-permute-start.5) | collective-permute-done | bytes 294944 | tf_op jit(solution)/shard_map/ppermute | solution.py:362
  93.2 1.5 load_pieces.1
  94.7 0.7 collective-permute-start.8
  95.4 0.7 collective-permute-start.13
  96.1 0.0 collective-permute-done.7.refs_7_
  96.1 1.3 collective-permute-start.12
  97.4 0.0 collective-permute-done.4.refs_8_
  97.4 0.0 collective-permute-done.6.refs_6_
  97.5 0.7 collective-permute-start.11
  98.2 1.3 collective-permute-start.10
  99.5 0.0 collective-permute-done.8.refs_5_
  99.5 1.3 collective-permute-start.9
  100.8 0.0 copy-done
  100.8 15.3 %main_update.1.refs_0_ = f32[4096,512]{1,0:T(8,128)S(1)} custom-call(s32[2]{0:T(128)S(1)} %pad_add_fusion.refs_0_, s32[512]{0:T(512)} %refs_1_.1, f32[4096,512]{1,0:T(8,128)} %refs_2_.1, f32[512,512]{1,0:T(8,128)} %get-tuple-element.39.refs_1_.refs_3_, f32[512,512]{1,0:T(8,128)} %get-tuple-element.40.refs_2_.refs_4_, f32[4096,128]{1,0:T(8,128)S(1)} %copy-done, ...), custom_call_target="tpu_custom_call" | custom-call | tf_op jit(solution)/shard_map/main_update/pallas_call | solution.py:280
  116.1 0.0 collective-permute-done.13.refs_3_
  116.1 10.9 %collective-permute-done.12.refs_2_ = f32[1824,128]{1,0:T(8,128)S(1)} collective-permute-done((f32[1824,128]{1,0:T(8,128)}, f32[1824,128]{1,0:T(8,128)S(1)}, u32[]{:S(2)}, u32[]{:S(2)}) %collective-permute-start.12) | collective-permute-done | bytes 933920 | tf_op jit(solution)/shard_map/ppermute | solution.py:381
  127.1 2.1 %last_update.3.refs_4_ = f32[4096,512]{1,0:T(8,128)} custom-call(f32[4096,512]{1,0:T(8,128)S(1)} %main_update.1.refs_0_, bf16[384,512]{1,0:T(8,128)(2,1)S(1)} %get-tuple-element.58.refs_1_.refs_4_, f32[1824,128]{1,0:T(8,128)S(1)} %collective-permute-done.12.refs_2_, f32[1824,128]{1,0:T(8,128)S(1)} %collective-permute-done.13.refs_3_), custom_call_target="tpu_custom_call" | custom-call | tf_op jit(solution)/shard_map/last_update/pallas_call | solution.py:325
  129.2 0.0 collective-permute-done.11.refs_3_
  129.2 16.4 %collective-permute-done.10.refs_2_ = f32[1696,128]{1,0:T(8,128)S(1)} collective-permute-done((f32[1696,128]{1,0:T(8,128)}, f32[1696,128]{1,0:T(8,128)S(1)}, u32[]{:S(2)}, u32[]{:S(2)}) %collective-permute-start.10) | collective-permute-done | bytes 868384 | tf_op jit(solution)/shard_map/ppermute | solution.py:383
  145.7 2.1 %last_update.4.refs_7_ = f32[4096,512]{1,0:T(8,128)} custom-call(f32[4096,512]{1,0:T(8,128)S(1)} %main_update.1.refs_0_, bf16[384,512]{1,0:T(8,128)(2,1)S(1)} %get-tuple-element.58.refs_1_.refs_4_, f32[1696,128]{1,0:T(8,128)S(1)} %collective-permute-done.10.refs_2_, f32[1696,128]{1,0:T(8,128)S(1)} %collective-permute-done.11.refs_3_, ...), custom_call_target="tpu_custom_call", output_to_operand_aliasing={{}: (4, {})} | custom-call | tf_op jit(solution)/shard_map/last_update/pallas_call | solution.py:325
  147.7 8.2 %collective-permute-done.9.refs_3_.refs_6_ = f32[1152,128]{1,0:T(8,128)S(1)} collective-permute-done((f32[1152,128]{1,0:T(8,128)S(1)}, f32[1152,128]{1,0:T(8,128)S(1)}, u32[]{:S(2)}, u32[]{:S(2)}) %collective-permute-start.9) | collective-permute-done | bytes 589856 | tf_op jit(solution)/shard_map/ppermute | solution.py:386
  156.0 1.6 last_update.5
  (1 shorter events, 0.0 us)
Async XLA Ops:
  0.0 97.4 %collective-permute-start.6 = (f32[4096,128]{1,0:T(8,128)}, f32[4096,128]{1,0:T(8,128)}, u32[]{:S(2)}, u32[]{:S(2)}) collective-permute-start(f32[4096,128]{1,0:T(8,128)} %refs_5_.1), channel_id=1, source_target_pairs={{0,1},{1,0},{2,3},{3,2},{4,5},{5,4},{6,7},{7,6},{8,9},{9,8},{10,11... | collective-permute-start | bytes 6291464 | tf_op jit(solution)/shard_map/ppermute | solution.py:359
  5.5 90.7 %collective-permute-start.7 = (f32[1824,128]{1,0:T(8,128)}, f32[1824,128]{1,0:T(8,128)}, u32[]{:S(2)}, u32[]{:S(2)}) collective-permute-start(f32[1824,128]{1,0:T(8,128)} %get-tuple-element.47), channel_id=1, source_target_pairs={{0,2},{1,3},{2,0},{3,1},{4,6},{5,7},{6,4},{7,5},{8,10},{9,11},{10,... | collective-permute-start | bytes 2801672 | tf_op jit(solution)/shard_map/ppermute | solution.py:361
  8.1 89.3 %collective-permute-start.4 = (f32[1696,128]{1,0:T(8,128)}, f32[1696,128]{1,0:T(8,128)}, u32[]{:S(2)}, u32[]{:S(2)}) collective-permute-start(f32[1696,128]{1,0:T(8,128)} %get-tuple-element.41), channel_id=1, source_target_pairs={{0,2},{1,3},{2,0},{3,1},{4,6},{5,7},{6,4},{7,5},{8,10},{9,11},{10,... | collective-permute-start | bytes 2605064 | tf_op jit(solution)/shard_map/ppermute | solution.py:361
  8.4 84.7 %collective-permute-start.5 = (f32[576,128]{1,0:T(8,128)}, f32[576,128]{1,0:T(8,128)S(1)}, u32[]{:S(2)}, u32[]{:S(2)}) collective-permute-start(f32[576,128]{1,0:T(8,128)} %get-tuple-element.42), channel_id=1, source_target_pairs={{0,2},{3,1},{4,6},{7,5},{8,10},{11,9},{12,14},{15,13},{16,18},{19,... | collective-permute-start | bytes 884744 | tf_op jit(solution)/shard_map/ppermute | solution.py:362
  14.9 64.3 %copy-start.1 = (f32[512,512]{1,0:T(8,128)S(1)}, f32[512,512]{1,0:T(8,128)}, u32[]{:S(2)}) copy-start(f32[512,512]{1,0:T(8,128)} %refs_3_.1) | copy-start | bytes 3145732
  14.9 86.0 %copy-start = (f32[4096,128]{1,0:T(8,128)S(1)}, f32[4096,128]{1,0:T(8,128)}, u32[]{:S(2)}) copy-start(f32[4096,128]{1,0:T(8,128)} %refs_5_.1) | copy-start | bytes 6291460
  22.0 2.7 %collective-permute-start = (f32[512,512]{1,0:T(8,128)S(1)}, f32[512,512]{1,0:T(8,128)S(1)}, u32[]{:S(2)}, u32[]{:S(2)}) collective-permute-start(f32[512,512]{1,0:T(8,128)S(1)} %get-tuple-element.16), channel_id=1, source_target_pairs={{0,4},{4,0},{8,12},{12,8},{16,20},{20,16},{24,28},{28,24},{1,5},{5... | collective-permute-start | bytes 3145736 | tf_op jit(solution)/shard_map/cond/branch_1_fun/ppermute | solution.py:339
  24.9 25.3 %collective-permute-start.1 = (f32[512,512]{1,0:T(8,128)S(1)}, f32[512,512]{1,0:T(8,128)S(1)}, u32[]{:S(2)}, u32[]{:S(2)}) collective-permute-start(f32[512,512]{1,0:T(8,128)S(1)} %add.6), channel_id=1, source_target_pairs={{0,8},{4,12},{8,0},{12,4},{16,24},{20,28},{24,16},{28,20},{1,9},{5... | collective-permute-start | bytes 3145736 | tf_op jit(solution)/shard_map/cond/branch_1_fun/ppermute | solution.py:339
  50.4 24.5 %collective-permute-start.2 = (f32[512,512]{1,0:T(8,128)S(1)}, f32[512,512]{1,0:T(8,128)S(1)}, u32[]{:S(2)}, u32[]{:S(2)}) collective-permute-start(f32[512,512]{1,0:T(8,128)S(1)} %add.7), channel_id=1, source_target_pairs={{0,16},{4,20},{8,24},{12,28},{16,0},{20,4},{24,8},{28,12},{1,17},{... | collective-permute-start | bytes 3145736 | tf_op jit(solution)/shard_map/cond/branch_1_fun/ppermute | solution.py:339
  76.1 3.0 %collective-permute-start.3 = (f32[512,512]{1,0:T(8,128)}, f32[512,512]{1,0:T(8,128)}, u32[]{:S(2)}, u32[]{:S(2)}) collective-permute-start(f32[512,512]{1,0:T(8,128)} %add.8), channel_id=1, source_target_pairs={{0,4},{4,0},{8,12},{12,8},{16,20},{20,16},{24,28},{28,24},{1,5},{5... | collective-permute-start | bytes 3145736 | tf_op jit(solution)/shard_map/cond/branch_1_fun/ppermute | solution.py:339
  94.7 4.8 %collective-permute-start.8 = (f32[576,128]{1,0:T(8,128)S(1)}, f32[576,128]{1,0:T(8,128)S(1)}, u32[]{:S(2)}, u32[]{:S(2)}) collective-permute-start(f32[576,128]{1,0:T(8,128)S(1)} %get-tuple-element.51), channel_id=1, source_target_pairs={{1,2},{2,1},{5,6},{6,5},{9,10},{10,9},{13,14},{14,13},{17,18},{18,... | collective-permute-start | bytes 884744 | tf_op jit(solution)/shard_map/ppermute | solution.py:379
  95.4 20.7 %collective-permute-start.13 = (f32[1824,128]{1,0:T(8,128)S(1)}, f32[1824,128]{1,0:T(8,128)S(1)}, u32[]{:S(2)}, u32[]{:S(2)}) collective-permute-start(f32[1824,128]{1,0:T(8,128)S(1)} %get-tuple-element.60), channel_id=1, source_target_pairs={{1,2},{2,1},{5,6},{6,5},{9,10},{10,9},{13,14},{14,13},{17,18},{18,... | collective-permute-start | bytes 2801672 | tf_op jit(solution)/shard_map/ppermute | solution.py:380
  96.1 30.9 %collective-permute-start.12 = (f32[1824,128]{1,0:T(8,128)}, f32[1824,128]{1,0:T(8,128)S(1)}, u32[]{:S(2)}, u32[]{:S(2)}) collective-permute-start(f32[1824,128]{1,0:T(8,128)} %collective-permute-done.7.refs_7_), channel_id=1, source_target_pairs={{2,3},{1,0},{6,7},{5,4},{10,11},{9,8},{14,15},{13,12},{18,19},{17,... | collective-permute-start | bytes 2801672 | tf_op jit(solution)/shard_map/ppermute | solution.py:381
  97.5 31.8 %collective-permute-start.11 = (f32[1696,128]{1,0:T(8,128)S(1)}, f32[1696,128]{1,0:T(8,128)S(1)}, u32[]{:S(2)}, u32[]{:S(2)}) collective-permute-start(f32[1696,128]{1,0:T(8,128)S(1)} %get-tuple-element.59), channel_id=1, source_target_pairs={{1,2},{2,1},{5,6},{6,5},{9,10},{10,9},{13,14},{14,13},{17,18},{18,... | collective-permute-start | bytes 2605064 | tf_op jit(solution)/shard_map/ppermute | solution.py:384
  98.2 47.5 %collective-permute-start.10 = (f32[1696,128]{1,0:T(8,128)}, f32[1696,128]{1,0:T(8,128)S(1)}, u32[]{:S(2)}, u32[]{:S(2)}) collective-permute-start(f32[1696,128]{1,0:T(8,128)} %collective-permute-done.4.refs_8_), channel_id=1, source_target_pairs={{2,3},{1,0},{6,7},{5,4},{10,11},{9,8},{14,15},{13,12},{18,19},{17,... | collective-permute-start | bytes 2605064 | tf_op jit(solution)/shard_map/ppermute | solution.py:383
  99.5 56.4 %collective-permute-start.9 = (f32[1152,128]{1,0:T(8,128)S(1)}, f32[1152,128]{1,0:T(8,128)S(1)}, u32[]{:S(2)}, u32[]{:S(2)}) collective-permute-start(f32[1152,128]{1,0:T(8,128)S(1)} %pad_maximum_fusion), channel_id=1, source_target_pairs={{2,3},{1,0},{6,7},{5,4},{10,11},{9,8},{14,15},{13,12},{18,19},{17,... | collective-permute-start | bytes 1769480 | tf_op jit(solution)/shard_map/ppermute | solution.py:386

commit v8 on v7

--- a/solution.py
+++ b/solution.py
@@ -10,7 +10,8 @@
 MIDDLE = [(1, 2), (2, 1)]
 ENDS = [(2, 3), (1, 0)]
 FAR = [(0, 2), (3, 1)]
-PIECES = (57, 53, 18)
+PIECES = (64, 46, 18)
+MIDDLE_PIECES = (58, 52, 18)
 TILE = 512
 LAST_TILE = 256
 SMALL = pl.CostEstimate(flops=0, bytes_accessed=0, transcendentals=0)
@@ -295,35 +296,31 @@
     )(info, pivots, slab, total, other, own, near, *across, upper, terms)
 
 
-def last_kernel(first_row, block, tile, groups, base, *refs):
+def last_kernel(first_row, block, tile, segments, base, *refs):
     out, result, sem = refs[-3:]
-    count = result.shape[0]
-    blocks = []
     at = 0
-    for offsets in groups:
-        blocks.append((refs[at], list(zip(refs[at + 1 : at + 1 + len(offsets)], offsets))))
-        at += 1 + len(offsets)
-    for at in range(0, count, tile):
-        size = min(tile, count - at)
-        part = pl.ds(at, size)
-        row = first_row + at
-        delta = None
-        for terms, pieces in blocks:
-            left = sum(piece[pl.ds(offset + at, size), :] for piece, offset in pieces)
-            change = dot(left_terms(left), terms[...])
-            delta = change if delta is None else delta + change
-        if row < block:
-            delta = jnp.where(lax.axis_index("prow") == 0, 0.0, delta)
-        result[part, :] = base[pl.ds(row, size), :] - delta
-        pltpu.make_async_copy(result.at[part, :], out.at[pl.ds(row, size), :], sem).start()
-    pltpu.make_async_copy(result, out.at[pl.ds(first_row, count), :], sem).wait()
-
-
-def last_update(base, groups, count, block, first_row, done):
-    offsets = [[offset for _, offset in pieces] for _, pieces in groups]
-    arrays = [array for terms, pieces in groups for array in (terms, *(piece for piece, _ in pieces))]
-    return pl.pallas_call(
-        lambda *refs: last_kernel(first_row, block, min(LAST_TILE, block), offsets, *refs),
+    for count, groups in segments:
+        for inner in range(0, count, tile):
+            size = min(tile, count - inner)
+            part = pl.ds(at, size)
+            row = first_row + at
+            delta = None
+            for terms, pieces in groups:
+                left = sum(refs[piece][pl.ds(offset + inner, size), :] for piece, offset in pieces)
+                change = dot(left_terms(left), refs[terms][...])
+                delta = change if delta is None else delta + change
+            if row < block:
+                delta = jnp.where(lax.axis_index("prow") == 0, 0.0, delta)
+            result[part, :] = base[pl.ds(row, size), :] - delta
+            pltpu.make_async_copy(result.at[part, :], out.at[pl.ds(row, size), :], sem).start()
+            at += size
+    pltpu.make_async_copy(result, out.at[pl.ds(first_row, at), :], sem).wait()
+
+
+def last_update(base, arrays, segments, block, first_row, done):
+    count = sum(size for size, _ in segments)
+    return pl.pallas_call(
+        lambda *refs: last_kernel(first_row, block, min(LAST_TILE, block), segments, *refs),
         out_shape=jax.ShapeDtypeStruct(base.shape, base.dtype),
         in_specs=[VMEM] * (1 + len(arrays)) + [HBM] * len(done),
         out_specs=HBM,
@@ -354,10 +351,10 @@
         info = jnp.stack([column, place]).astype(jnp.int32)
 
         first, second, last = (rows_here * part // sum(PIECES) for part in PIECES)
+        first_mid, second_mid, _ = (rows_here * part // sum(PIECES) for part in MIDDLE_PIECES)
         early = first + second
-        spans = [(0, first), (first, second), (early, last)]
         near = lax.ppermute(panel, "pcol", SWAP)
-        *pieces, tail = cut(panel, spans)
+        *pieces, tail = cut(panel, [(0, first), (first, second), (early, last)])
         across = [lax.ppermute(piece, "pcol", ACROSS) for piece in pieces]
         far = lax.ppermute(tail, "pcol", FAR)
 
@@ -373,23 +370,34 @@
 
         total, other = lax.cond(pivots[0] >= 0, gather_rows, no_rows, slab, pivots)
         upper, terms, across_terms, last_terms = make_upper(info, total, other, diag_inverse, width)
-        far, later, upper = lax.optimization_barrier((far, panel, upper))
+        later, upper = lax.optimization_barrier((panel, upper))
         head, upper = lax.optimization_barrier((across[0], upper))
-        head_mid, rest_mid, tail_mid = load_pieces(later, spans)
+        head_mid, rest_mid, tail_mid = load_pieces(
+            later, [(0, first_mid), (first_mid, second_mid), (early, last)]
+        )
         tail_mid = lax.ppermute(tail_mid, "pcol", MIDDLE)
+        head_end = lax.ppermute(head, "pcol", ENDS)
+        rest, head_mid, rest_mid, near, far = lax.optimization_barrier(
+            (across[1], head_mid, rest_mid, near, far)
+        )
         head_mid = lax.ppermute(head_mid, "pcol", MIDDLE)
-        head_end = lax.ppermute(head, "pcol", ENDS)
-        rest, rest_mid, near = lax.optimization_barrier((across[1], rest_mid, near))
+        rest_mid = lax.ppermute(rest_mid, "pcol", MIDDLE)
         rest_end = lax.ppermute(rest, "pcol", ENDS)
-        rest_mid = lax.ppermute(rest_mid, "pcol", MIDDLE)
         both, rest = lax.optimization_barrier((jnp.concatenate([far, tail_mid], axis=0), rest))
         both = lax.ppermute(both, "pcol", ENDS)
 
         base = main_update(info, pivots, slab, total, other, panel, near, [head, rest], upper, terms)
-        result = last_update(base, [(last_terms, [(head_end, 0), (head_mid, 0)])], first, block, 0, [])
-        result = last_update(base, [(last_terms, [(rest_end, 0), (rest_mid, 0)])], second, block, first, [result])
-        groups = [(across_terms, [(far, 0), (both, last)]), (last_terms, [(tail_mid, 0), (both, 0)])]
-        return last_update(base, groups, last, block, early, [result])
+        segments = [(first_mid, [(0, [(1, 0), (2, 0)])])]
+        result = last_update(base, [last_terms, head_end, head_mid], segments, block, 0, [])
+        segments = [
+            (first - first_mid, [(0, [(1, first_mid), (3, 0)])]),
+            (second, [(0, [(2, 0), (3, first - first_mid)])]),
+        ]
+        arrays = [last_terms, head_end, rest_end, rest_mid]
+        result = last_update(base, arrays, segments, block, first_mid, [result])
+        segments = [(last, [(0, [(2, 0), (4, last)]), (1, [(3, 0), (4, 0)])])]
+        arrays = [across_terms, last_terms, far, tail_mid, both]
+        return last_update(base, arrays, segments, block, early, [result])
 
     in_specs = (P("prow", "pcol"), P("prow", "pcol"), P(), P())
     return jax.shard_map(

time: 158 us -> 144 us (0.911)
  the two profiles are of different devices: /device:TPU:0 before, /device:TPU:14 now
where the time goes in v8:
time: 144 us; the launch traced here: 142 us
  waiting for transfers between devices  80 us (56%)
  Pallas kernels  35.2 us (24%)
  starting transfers between devices  21.9 us (15%)
  local copies, waits for them, and re-layouts  2.44 us (2%)
  other arithmetic  1.71 us (1%)
    ppermute x4, waiting for transfers between devices, exchange(): lax.ppermute(value, 'prow', [(i, i ^ 1 << bit) for i in range(count)])  54.3 us
    pallas_call x1, Pallas kernels, main_update(): pl.pallas_call(lambda *refs: main_kernel(min(TILE, block), *refs), out_sh...  15.2 us
    ppermute x1, waiting for transfers between devices, shards(): rest_mid = lax.ppermute(rest_mid, 'pcol', MIDDLE)  12 us
    pallas_call x1, Pallas kernels, pick(): pl.pallas_call(pick_kernel, out_shape=(shape, shape), grid_spec=pltpu.Pre...  7.02 us
    ppermute x1, waiting for transfers between devices, shards(): far = lax.ppermute(tail, 'pcol', FAR)  6.86 us
    pallas_call x3, Pallas kernels, last_update(): pl.pallas_call(lambda *refs: last_kernel(first_row, block, min(LAST_TILE,...  5.74 us
    ppermute x1, starting transfers between devices, shards(): tail_mid = lax.ppermute(tail_mid, 'pcol', MIDDLE)  4.61 us
    ppermute x1, waiting for transfers between devices, shards(): rest_end = lax.ppermute(rest, 'pcol', ENDS)  4.04 us
  transfers between devices with their start and end apart: 14, of which 8 were waited for; matrix products, arithmetic and copies ran while one was open for 2% of the time, Pallas kernels for 24%

profile of v8, /device:TPU:14, one launch (start us, length us, event | category | flops | bytes accessed | tf_op | source)
XLA Modules:
  0.0 142.1 jit_solution(202289066631099991)
XLA Ops:
  0.0 0.4 collective-permute-start.5
  0.5 2.4 %cut.1 = (f32[2048,128]{1,0:T(8,128)}, f32[1472,128]{1,0:T(8,128)}, f32[576,128]{1,0:T(8,128)}) custom-call(f32[4096,128]{1,0:T(8,128)} %refs_5_.1), custom_call_target="tpu_custom_call" | custom-call | tf_op jit(solution)/shard_map/cut/pallas_call | solution.py:94
  2.9 2.7 %collective-permute-start.7 = (f32[2048,128]{1,0:T(8,128)}, f32[2048,128]{1,0:T(8,128)S(1)}, u32[]{:S(2)}, u32[]{:S(2)}) collective-permute-start(f32[2048,128]{1,0:T(8,128)} %get-tuple-element.49), channel_id=1, source_target_pairs={{0,2},{1,3},{2,0},{3,1},{4,6},{5,7},{6,4},{7,5},{8,10},{9,11},{10,... | collective-permute-start | bytes 3145736 | tf_op jit(solution)/shard_map/ppermute | solution.py:358
  5.6 0.3 collective-permute-start.4
  5.9 1.3 collective-permute-start.6
  7.2 1.2 slice.7
  9.0 0.1 pad_add_fusion.refs_0_
  9.1 0.0 copy-start
  9.1 64.2 %conditional.1 = (f32[512,512]{1,0:T(8,128)}, f32[512,512]{1,0:T(8,128)}) conditional(s32[]{:T(128)} %bitcast.2, f32[4096,512]{1,0:T(8,128)} %refs_2_.1, (s32[2]{0:T(128)S(1)}, s32[512]{0:T(512)}, f32[4096,512]{1,0:T(8,128)}) %tuple.17), branch_computations={%region_0.0_spmd, %region_1.0_spmd} | conditional | flops 786432 | bytes 26214576 | solution.py:371
  9.1 7.0 %pick.1 = (f32[512,512]{1,0:T(8,128)S(1)}, f32[512,512]{1,0:T(8,128)S(1)}) custom-call(s32[2]{0:T(128)S(1)} %get-tuple-element.12.info, s32[512]{0:T(512)} %get-tuple-element.13.pivots, f32[4096,512]{1,0:T(8,128)} %get-tuple-element.14.slab), custom_call_target="tpu_custom_call" | custom-call | tf_op jit(solution)/shard_map/cond/branch_1_fun/pick/pallas_call | solution.py:156
  16.1 0.1 collective-permute-start
  16.2 2.6 %collective-permute-done = f32[512,512]{1,0:T(8,128)S(1)} collective-permute-done((f32[512,512]{1,0:T(8,128)S(1)}, f32[512,512]{1,0:T(8,128)S(1)}, u32[]{:S(2)}, u32[]{:S(2)}) %collective-permute-start) | collective-permute-done | bytes 1048608 | tf_op jit(solution)/shard_map/cond/branch_1_fun/ppermute | solution.py:336
  18.9 0.2 add.6
  19.1 0.6 collective-permute-start.1
  19.7 24.7 %collective-permute-done.1 = f32[512,512]{1,0:T(8,128)S(1)} collective-permute-done((f32[512,512]{1,0:T(8,128)S(1)}, f32[512,512]{1,0:T(8,128)S(1)}, u32[]{:S(2)}, u32[]{:S(2)}) %collective-permute-start.1) | collective-permute-done | bytes 1048608 | tf_op jit(solution)/shard_map/cond/branch_1_fun/ppermute | solution.py:336
  44.3 0.2 add.7
  44.5 0.6 collective-permute-start.2
  45.1 24.0 %collective-permute-done.2 = f32[512,512]{1,0:T(8,128)S(1)} collective-permute-done((f32[512,512]{1,0:T(8,128)S(1)}, f32[512,512]{1,0:T(8,128)S(1)}, u32[]{:S(2)}, u32[]{:S(2)}) %collective-permute-start.2) | collective-permute-done | bytes 1048608 | tf_op jit(solution)/shard_map/cond/branch_1_fun/ppermute | solution.py:336
  69.1 1.2 add.8
  70.3 0.0 collective-permute-start.3
  70.3 3.0 %collective-permute-done.3 = f32[512,512]{1,0:T(8,128)} collective-permute-done((f32[512,512]{1,0:T(8,128)}, f32[512,512]{1,0:T(8,128)}, u32[]{:S(2)}, u32[]{:S(2)}) %collective-permute-start.3) | collective-permute-done | bytes 1048608 | tf_op jit(solution)/shard_map/cond/branch_1_fun/ppermute | solution.py:336
  73.3 0.0 copy-start.1
  73.3 1.2 copy-done.1
  74.5 3.3 %upper.1 = (f32[512,512]{1,0:T(8,128)S(1)}, bf16[1152,512]{1,0:T(8,128)(2,1)S(1)}, bf16[384,512]{1,0:T(8,128)(2,1)S(1)}, bf16[384,512]{1,0:T(8,128)(2,1)S(1)}) custom-call(s32[2]{0:T(128)S(1)} %pad_add_fusion.refs_0_, f32[512,512]{1,0:T(8,128)} %get-tuple-element.40.refs_1_.refs_3_, f32[512,512]{1,0:T(8,128)} %get-tuple-element.41.refs_2_.refs_4_, ...), custom_call_target="tpu_custom_call" | custom-call | tf_op jit(solution)/shard_map/upper/pallas_call | solution.py:202
  77.8 1.5 %load_pieces.1 = (f32[1856,128]{1,0:T(8,128)S(1)}, f32[1664,128]{1,0:T(8,128)S(1)}, f32[576,128]{1,0:T(8,128)S(1)}) custom-call(f32[4096,128]{1,0:T(8,128)} %refs_5_.1), custom_call_target="tpu_custom_call" | custom-call | tf_op jit(solution)/shard_map/load_pieces/pallas_call | solution.py:59
  79.3 4.6 %collective-permute-start.8 = (f32[576,128]{1,0:T(8,128)S(1)}, f32[576,128]{1,0:T(8,128)S(1)}, u32[]{:S(2)}, u32[]{:S(2)}) collective-permute-start(f32[576,128]{1,0:T(8,128)S(1)} %get-tuple-element.53), channel_id=1, source_target_pairs={{1,2},{2,1},{5,6},{6,5},{9,10},{10,9},{13,14},{14,13},{17,18},{18,... | collective-permute-start | bytes 884744 | tf_op jit(solution)/shard_map/ppermute | solution.py:378
  83.9 0.0 collective-permute-done.7.refs_7_
  83.9 2.8 %collective-permute-start.10 = (f32[2048,128]{1,0:T(8,128)S(1)}, f32[2048,128]{1,0:T(8,128)S(1)}, u32[]{:S(2)}, u32[]{:S(2)}) collective-permute-start(f32[2048,128]{1,0:T(8,128)S(1)} %collective-permute-done.7.refs_7_), channel_id=1, source_target_pairs={{2,3},{1,0},{6,7},{5,4},{10,11},{9,8},{14,15},{13,12},{18,19},{17,... | collective-permute-start | bytes 3145736 | tf_op jit(solution)/shard_map/ppermute | solution.py:379
  86.8 6.9 %collective-permute-done.6.refs_3_ = f32[576,128]{1,0:T(8,128)S(1)} collective-permute-done((f32[576,128]{1,0:T(8,128)}, f32[576,128]{1,0:T(8,128)S(1)}, u32[]{:S(2)}, u32[]{:S(2)}) %collective-permute-start.6) | collective-permute-done | bytes 294944 | tf_op jit(solution)/shard_map/ppermute | solution.py:359
  93.6 0.0 collective-permute-done.4.refs_8_
  93.6 0.0 collective-permute-done.5.refs_6_
  93.6 2.3 %collective-permute-start.13 = (f32[1856,128]{1,0:T(8,128)S(1)}, f32[1856,128]{1,0:T(8,128)S(1)}, u32[]{:S(2)}, u32[]{:S(2)}) collective-permute-start(f32[1856,128]{1,0:T(8,128)S(1)} %get-tuple-element.62), channel_id=1, source_target_pairs={{1,2},{2,1},{5,6},{6,5},{9,10},{10,9},{13,14},{14,13},{17,18},{18,... | collective-permute-start | bytes 2850824 | tf_op jit(solution)/shard_map/ppermute | solution.py:383
  96.0 3.5 %collective-permute-start.12 = (f32[1664,128]{1,0:T(8,128)S(1)}, f32[1664,128]{1,0:T(8,128)S(1)}, u32[]{:S(2)}, u32[]{:S(2)}) collective-permute-start(f32[1664,128]{1,0:T(8,128)S(1)} %get-tuple-element.61), channel_id=1, source_target_pairs={{1,2},{2,1},{5,6},{6,5},{9,10},{10,9},{13,14},{14,13},{17,18},{18,... | collective-permute-start | bytes 2555912 | tf_op jit(solution)/shard_map/ppermute | solution.py:384
  99.5 1.3 collective-permute-start.11
  100.8 0.0 collective-permute-done.8.refs_4_
  100.9 1.3 collective-permute-start.9
  102.2 0.0 copy-done
  102.2 15.2 %main_update.1.refs_0_ = f32[4096,512]{1,0:T(8,128)S(1)} custom-call(s32[2]{0:T(128)S(1)} %pad_add_fusion.refs_0_, s32[512]{0:T(512)} %refs_1_.1, f32[4096,512]{1,0:T(8,128)} %refs_2_.1, f32[512,512]{1,0:T(8,128)} %get-tuple-element.40.refs_1_.refs_3_, f32[512,512]{1,0:T(8,128)} %get-tuple-element.41.refs_2_.refs_4_, f32[4096,128]{1,0:T(8,128)S(1)} %copy-done, ...), custom_call_target="tpu_custom_call" | custom-call | tf_op jit(solution)/shard_map/main_update/pallas_call | solution.py:281
  117.4 0.0 collective-permute-done.10.refs_2_
  117.5 2.8 %collective-permute-done.13.refs_3_ = f32[1856,128]{1,0:T(8,128)S(1)} collective-permute-done((f32[1856,128]{1,0:T(8,128)S(1)}, f32[1856,128]{1,0:T(8,128)S(1)}, u32[]{:S(2)}, u32[]{:S(2)}) %collective-permute-start.13) | collective-permute-done | bytes 950304 | tf_op jit(solution)/shard_map/ppermute | solution.py:383
  120.3 2.2 %last_update.3.refs_5_ = f32[4096,512]{1,0:T(8,128)} custom-call(f32[4096,512]{1,0:T(8,128)S(1)} %main_update.1.refs_0_, bf16[384,512]{1,0:T(8,128)(2,1)S(1)} %get-tuple-element.59.refs_1_.refs_2_, f32[2048,128]{1,0:T(8,128)S(1)} %collective-permute-done.10.refs_2_, f32[1856,128]{1,0:T(8,128)S(1)} %collective-permute-done.13.refs_3_), custom_call_target="tpu_custom_call" | custom-call | tf_op jit(solution)/shard_map/last_update/pallas_call | solution.py:322
  122.4 4.0 %collective-permute-done.11.refs_3_ = f32[1472,128]{1,0:T(8,128)S(1)} collective-permute-done((f32[1472,128]{1,0:T(8,128)}, f32[1472,128]{1,0:T(8,128)S(1)}, u32[]{:S(2)}, u32[]{:S(2)}) %collective-permute-start.11) | collective-permute-done | bytes 753696 | tf_op jit(solution)/shard_map/ppermute | solution.py:385
  126.5 12.0 %collective-permute-done.12.refs_4_ = f32[1664,128]{1,0:T(8,128)S(1)} collective-permute-done((f32[1664,128]{1,0:T(8,128)S(1)}, f32[1664,128]{1,0:T(8,128)S(1)}, u32[]{:S(2)}, u32[]{:S(2)}) %collective-permute-start.12) | collective-permute-done | bytes 852000 | tf_op jit(solution)/shard_map/ppermute | solution.py:384
  138.5 2.0 %last_update.4.refs_6_ = f32[4096,512]{1,0:T(8,128)} custom-call(f32[4096,512]{1,0:T(8,128)S(1)} %main_update.1.refs_0_, bf16[384,512]{1,0:T(8,128)(2,1)S(1)} %get-tuple-element.59.refs_1_.refs_2_, f32[2048,128]{1,0:T(8,128)S(1)} %collective-permute-done.10.refs_2_, f32[1472,128]{1,0:T(8,128)S(1)} %collective-permute-done.11.refs_3_, ...), custom_call_target="tpu_custom_call", output_to_operand_aliasing={{}: (5, {})} | custom-call | tf_op jit(solution)/shard_map/last_update/pallas_call | solution.py:322
  140.5 0.0 collective-permute-done.9.refs_5_
  140.5 1.6 %last_update.5 = f32[4096,512]{1,0:T(8,128)} custom-call(f32[4096,512]{1,0:T(8,128)S(1)} %main_update.1.refs_0_, bf16[384,512]{1,0:T(8,128)(2,1)S(1)} %get-tuple-element.58.refs_1_, bf16[384,512]{1,0:T(8,128)(2,1)S(1)} %get-tuple-element.59.refs_1_.refs_2_, f32[576,128]{1,0:T(8,128)S(1)} %collective-permute-done.6.refs_3_, ...), custom_call_target="tpu_custom_call", output_to_operand_aliasing={{}: (6, {})} | custom-call | tf_op jit(solution)/shard_map/last_update/pallas_call | solution.py:322
  (1 shorter events, 0.0 us)
Async XLA Ops:
  0.0 93.6 %collective-permute-start.5 = (f32[4096,128]{1,0:T(8,128)}, f32[4096,128]{1,0:T(8,128)}, u32[]{:S(2)}, u32[]{:S(2)}) collective-permute-start(f32[4096,128]{1,0:T(8,128)} %refs_5_.1), channel_id=1, source_target_pairs={{0,1},{1,0},{2,3},{3,2},{4,5},{5,4},{6,7},{7,6},{8,9},{9,8},{10,11... | collective-permute-start | bytes 6291464 | tf_op jit(solution)/shard_map/ppermute | solution.py:356
  2.9 81.0 %collective-permute-start.7 = (f32[2048,128]{1,0:T(8,128)}, f32[2048,128]{1,0:T(8,128)S(1)}, u32[]{:S(2)}, u32[]{:S(2)}) collective-permute-start(f32[2048,128]{1,0:T(8,128)} %get-tuple-element.49), channel_id=1, source_target_pairs={{0,2},{1,3},{2,0},{3,1},{4,6},{5,7},{6,4},{7,5},{8,10},{9,11},{10,... | collective-permute-start | bytes 3145736 | tf_op jit(solution)/shard_map/ppermute | solution.py:358
  5.6 88.1 %collective-permute-start.4 = (f32[1472,128]{1,0:T(8,128)}, f32[1472,128]{1,0:T(8,128)}, u32[]{:S(2)}, u32[]{:S(2)}) collective-permute-start(f32[1472,128]{1,0:T(8,128)} %get-tuple-element.42), channel_id=1, source_target_pairs={{0,2},{1,3},{2,0},{3,1},{4,6},{5,7},{6,4},{7,5},{8,10},{9,11},{10,... | collective-permute-start | bytes 2261000 | tf_op jit(solution)/shard_map/ppermute | solution.py:358
  5.9 87.7 %collective-permute-start.6 = (f32[576,128]{1,0:T(8,128)}, f32[576,128]{1,0:T(8,128)S(1)}, u32[]{:S(2)}, u32[]{:S(2)}) collective-permute-start(f32[576,128]{1,0:T(8,128)} %get-tuple-element.47), channel_id=1, source_target_pairs={{0,2},{3,1},{4,6},{7,5},{8,10},{11,9},{12,14},{15,13},{16,18},{19,... | collective-permute-start | bytes 884744 | tf_op jit(solution)/shard_map/ppermute | solution.py:359
  9.1 93.1 %copy-start = (f32[4096,128]{1,0:T(8,128)S(1)}, f32[4096,128]{1,0:T(8,128)}, u32[]{:S(2)}) copy-start(f32[4096,128]{1,0:T(8,128)} %refs_5_.1) | copy-start | bytes 6291460
  16.1 2.7 %collective-permute-start = (f32[512,512]{1,0:T(8,128)S(1)}, f32[512,512]{1,0:T(8,128)S(1)}, u32[]{:S(2)}, u32[]{:S(2)}) collective-permute-start(f32[512,512]{1,0:T(8,128)S(1)} %get-tuple-element.16), channel_id=1, source_target_pairs={{0,4},{4,0},{8,12},{12,8},{16,20},{20,16},{24,28},{28,24},{1,5},{5... | collective-permute-start | bytes 3145736 | tf_op jit(solution)/shard_map/cond/branch_1_fun/ppermute | solution.py:336
  19.1 25.3 %collective-permute-start.1 = (f32[512,512]{1,0:T(8,128)S(1)}, f32[512,512]{1,0:T(8,128)S(1)}, u32[]{:S(2)}, u32[]{:S(2)}) collective-permute-start(f32[512,512]{1,0:T(8,128)S(1)} %add.6), channel_id=1, source_target_pairs={{0,8},{4,12},{8,0},{12,4},{16,24},{20,28},{24,16},{28,20},{1,9},{5... | collective-permute-start | bytes 3145736 | tf_op jit(solution)/shard_map/cond/branch_1_fun/ppermute | solution.py:336
  44.5 24.5 %collective-permute-start.2 = (f32[512,512]{1,0:T(8,128)S(1)}, f32[512,512]{1,0:T(8,128)S(1)}, u32[]{:S(2)}, u32[]{:S(2)}) collective-permute-start(f32[512,512]{1,0:T(8,128)S(1)} %add.7), channel_id=1, source_target_pairs={{0,16},{4,20},{8,24},{12,28},{16,0},{20,4},{24,8},{28,12},{1,17},{... | collective-permute-start | bytes 3145736 | tf_op jit(solution)/shard_map/cond/branch_1_fun/ppermute | solution.py:336
  70.3 3.0 %collective-permute-start.3 = (f32[512,512]{1,0:T(8,128)}, f32[512,512]{1,0:T(8,128)}, u32[]{:S(2)}, u32[]{:S(2)}) collective-permute-start(f32[512,512]{1,0:T(8,128)} %add.8), channel_id=1, source_target_pairs={{0,4},{4,0},{8,12},{12,8},{16,20},{20,16},{24,28},{28,24},{1,5},{5... | collective-permute-start | bytes 3145736 | tf_op jit(solution)/shard_map/cond/branch_1_fun/ppermute | solution.py:336
  73.3 1.2 copy-start.1
  79.3 21.5 %collective-permute-start.8 = (f32[576,128]{1,0:T(8,128)S(1)}, f32[576,128]{1,0:T(8,128)S(1)}, u32[]{:S(2)}, u32[]{:S(2)}) collective-permute-start(f32[576,128]{1,0:T(8,128)S(1)} %get-tuple-element.53), channel_id=1, source_target_pairs={{1,2},{2,1},{5,6},{6,5},{9,10},{10,9},{13,14},{14,13},{17,18},{18,... | collective-permute-start | bytes 884744 | tf_op jit(solution)/shard_map/ppermute | solution.py:378
  83.9 33.5 %collective-permute-start.10 = (f32[2048,128]{1,0:T(8,128)S(1)}, f32[2048,128]{1,0:T(8,128)S(1)}, u32[]{:S(2)}, u32[]{:S(2)}) collective-permute-start(f32[2048,128]{1,0:T(8,128)S(1)} %collective-permute-done.7.refs_7_), channel_id=1, source_target_pairs={{2,3},{1,0},{6,7},{5,4},{10,11},{9,8},{14,15},{13,12},{18,19},{17,... | collective-permute-start | bytes 3145736 | tf_op jit(solution)/shard_map/ppermute | solution.py:379
  93.6 26.6 %collective-permute-start.13 = (f32[1856,128]{1,0:T(8,128)S(1)}, f32[1856,128]{1,0:T(8,128)S(1)}, u32[]{:S(2)}, u32[]{:S(2)}) collective-permute-start(f32[1856,128]{1,0:T(8,128)S(1)} %get-tuple-element.62), channel_id=1, source_target_pairs={{1,2},{2,1},{5,6},{6,5},{9,10},{10,9},{13,14},{14,13},{17,18},{18,... | collective-permute-start | bytes 2850824 | tf_op jit(solution)/shard_map/ppermute | solution.py:383
  96.0 42.5 %collective-permute-start.12 = (f32[1664,128]{1,0:T(8,128)S(1)}, f32[1664,128]{1,0:T(8,128)S(1)}, u32[]{:S(2)}, u32[]{:S(2)}) collective-permute-start(f32[1664,128]{1,0:T(8,128)S(1)} %get-tuple-element.61), channel_id=1, source_target_pairs={{1,2},{2,1},{5,6},{6,5},{9,10},{10,9},{13,14},{14,13},{17,18},{18,... | collective-permute-start | bytes 2555912 | tf_op jit(solution)/shard_map/ppermute | solution.py:384
  99.5 27.0 %collective-permute-start.11 = (f32[1472,128]{1,0:T(8,128)}, f32[1472,128]{1,0:T(8,128)S(1)}, u32[]{:S(2)}, u32[]{:S(2)}) collective-permute-start(f32[1472,128]{1,0:T(8,128)} %collective-permute-done.4.refs_8_), channel_id=1, source_target_pairs={{2,3},{1,0},{6,7},{5,4},{10,11},{9,8},{14,15},{13,12},{18,19},{17,... | collective-permute-start | bytes 2261000 | tf_op jit(solution)/shard_map/ppermute | solution.py:385
  100.9 39.6 %collective-permute-start.9 = (f32[1152,128]{1,0:T(8,128)S(1)}, f32[1152,128]{1,0:T(8,128)S(1)}, u32[]{:S(2)}, u32[]{:S(2)}) collective-permute-start(f32[1152,128]{1,0:T(8,128)S(1)} %pad_maximum_fusion), channel_id=1, source_target_pairs={{2,3},{1,0},{6,7},{5,4},{10,11},{9,8},{14,15},{13,12},{18,19},{17,... | collective-permute-start | bytes 1769480 | tf_op jit(solution)/shard_map/ppermute | solution.py:387

commit v9 on v8

--- a/solution.py
+++ b/solution.py
@@ -361,8 +361,12 @@
         def gather_rows(slab, pivots):
             send, keep = pick(info, pivots, slab, block)
             total = keep + exchange(send, 0, row_parts)
-            for bit in range(1, bits):
-                total = total + exchange(total, bit, row_parts)
+            halves = [total[: block // 2], total[block // 2 :]]
+            orders = [list(range(1, bits)), list(range(1, bits))[::-1]]
+            for step in range(bits - 1):
+                other = [exchange(half, order[step], row_parts) for half, order in zip(halves, orders)]
+                halves = [half + part for half, part in zip(halves, other)]
+            total = jnp.concatenate(halves, axis=0)
             return total, exchange(total, 0, row_parts)
 
         def no_rows(slab, pivots):
@@ -377,9 +381,8 @@
         )
         tail_mid = lax.ppermute(tail_mid, "pcol", MIDDLE)
         head_end = lax.ppermute(head, "pcol", ENDS)
-        rest, head_mid, rest_mid, near, far = lax.optimization_barrier(
-            (across[1], head_mid, rest_mid, near, far)
-        )
+        rest, head_mid, near = lax.optimization_barrier((across[1], head_mid, near))
+        rest_mid, far, near = lax.optimization_barrier((rest_mid, far, near))
         head_mid = lax.ppermute(head_mid, "pcol", MIDDLE)
         rest_mid = lax.ppermute(rest_mid, "pcol", MIDDLE)
         rest_end = lax.ppermute(rest, "pcol", ENDS)

time: 144 us -> 143 us (level)
    ppermute x2, waiting for transfers between devices: 0.01 us -> 25.6 us  [shards(): across = [lax.ppermute(piece, 'pcol', ACROSS) for piece in pieces]]
    ppermute x4 -> x6, waiting for transfers between devices: 54.3 us -> 30.2 us  [exchange(): lax.ppermute(value, 'prow', [(i, i ^ 1 << bit) for i in range(count)])]
    ppermute x1, waiting for transfers between devices: 6.86 us -> 2.71 us  [shards(): far = lax.ppermute(tail, 'pcol', FAR)]
    ppermute x1, waiting for transfers between devices: 0.01 us -> 2.57 us  [shards(): tail_mid = lax.ppermute(tail_mid, 'pcol', MIDDLE)]
    ppermute x1, waiting for transfers between devices: 4.04 us -> 1.6 us  [shards(): rest_end = lax.ppermute(rest, 'pcol', ENDS)]
    ppermute x1, waiting for transfers between devices: 12 us -> 14.4 us  [shards(): rest_mid = lax.ppermute(rest_mid, 'pcol', MIDDLE)]
    ppermute x4 -> x6, starting transfers between devices: 1.25 us -> 2.98 us  [exchange(): lax.ppermute(value, 'prow', [(i, i ^ 1 << bit) for i in range(count)])]
    ppermute x1, starting transfers between devices: 2.83 us -> 1.34 us  [shards(): head_end = lax.ppermute(head, 'pcol', ENDS)]
  transfers between devices with their start and end apart: 14 -> 16, of which waited for: 8 -> 13; matrix products, arithmetic and copies ran while one was open for 2% -> 2% of each run, Pallas kernels for 24% -> 23%
where the time goes in v9:
time: 143 us; the launch traced here: 142 us
  waiting for transfers between devices  81.3 us (57%)
  Pallas kernels  34.7 us (24%)
  starting transfers between devices  21 us (15%)
  local copies, waits for them, and re-layouts  2.5 us (2%)
  other arithmetic  1.74 us (1%)
    ppermute x6, waiting for transfers between devices, exchange(): lax.ppermute(value, 'prow', [(i, i ^ 1 << bit) for i in range(count)])  30.2 us
    ppermute x2, waiting for transfers between devices, shards(): across = [lax.ppermute(piece, 'pcol', ACROSS) for piece in pieces]  25.6 us
    pallas_call x1, Pallas kernels, main_update(): pl.pallas_call(lambda *refs: main_kernel(min(TILE, block), *refs), out_sh...  14.8 us
    ppermute x1, waiting for transfers between devices, shards(): rest_mid = lax.ppermute(rest_mid, 'pcol', MIDDLE)  14.4 us
    pallas_call x1, Pallas kernels, pick(): pl.pallas_call(pick_kernel, out_shape=(shape, shape), grid_spec=pltpu.Pre...  7.02 us
    pallas_call x3, Pallas kernels, last_update(): pl.pallas_call(lambda *refs: last_kernel(first_row, block, min(LAST_TILE,...  5.74 us
    ppermute x1, starting transfers between devices, shards(): tail_mid = lax.ppermute(tail_mid, 'pcol', MIDDLE)  4.61 us
    ppermute x1, waiting for transfers between devices, shards(): head_mid = lax.ppermute(head_mid, 'pcol', MIDDLE)  4.18 us
  transfers between devices with their start and end apart: 16, of which 13 were waited for; matrix products, arithmetic and copies ran while one was open for 2% of the time, Pallas kernels for 23%

profile of v9, /device:TPU:14, one launch (start us, length us, event | category | flops | bytes accessed | tf_op | source)
XLA Modules:
  0.0 142.1 jit_solution(15921590190681463209)
XLA Ops:
  0.0 0.4 collective-permute-start.8
  0.5 2.4 %cut.1 = (f32[2048,128]{1,0:T(8,128)}, f32[1472,128]{1,0:T(8,128)}, f32[576,128]{1,0:T(8,128)S(1)}) custom-call(f32[4096,128]{1,0:T(8,128)} %refs_5_.1), custom_call_target="tpu_custom_call" | custom-call | tf_op jit(solution)/shard_map/cut/pallas_call | solution.py:94
  2.8 2.7 %collective-permute-start.9 = (f32[2048,128]{1,0:T(8,128)}, f32[2048,128]{1,0:T(8,128)S(1)}, u32[]{:S(2)}, u32[]{:S(2)}) collective-permute-start(f32[2048,128]{1,0:T(8,128)} %get-tuple-element.51), channel_id=1, source_target_pairs={{0,2},{1,3},{2,0},{3,1},{4,6},{5,7},{6,4},{7,5},{8,10},{9,11},{10,... | collective-permute-start | bytes 3145736 | tf_op jit(solution)/shard_map/ppermute | solution.py:358
  5.5 0.3 collective-permute-start.7
  5.8 1.2 slice.13
  7.7 0.1 pad_add_fusion.refs_0_
  7.7 0.0 copy-start
  7.7 42.0 %conditional.1 = (f32[512,512]{1,0:T(8,128)}, f32[512,512]{1,0:T(8,128)}) conditional(s32[]{:T(128)} %bitcast.2, f32[4096,512]{1,0:T(8,128)} %refs_2_.1, (s32[2]{0:T(128)S(1)}, s32[512]{0:T(512)}, f32[4096,512]{1,0:T(8,128)}) %tuple.18), branch_computations={%region_0.0_spmd, %region_1.0_spmd} | conditional | flops 1048576 | bytes 30408960 | solution.py:375
  7.7 7.0 %pick.1 = (f32[512,512]{1,0:T(8,128)S(1)}, f32[512,512]{1,0:T(8,128)S(1)}) custom-call(s32[2]{0:T(128)S(1)} %get-tuple-element.12.info, s32[512]{0:T(512)} %get-tuple-element.13.pivots, f32[4096,512]{1,0:T(8,128)} %get-tuple-element.14.slab), custom_call_target="tpu_custom_call" | custom-call | tf_op jit(solution)/shard_map/cond/branch_1_fun/pick/pallas_call | solution.py:156
  14.8 0.1 collective-permute-start
  14.8 2.6 %collective-permute-done = f32[512,512]{1,0:T(8,128)S(1)} collective-permute-done((f32[512,512]{1,0:T(8,128)S(1)}, f32[512,512]{1,0:T(8,128)S(1)}, u32[]{:S(2)}, u32[]{:S(2)}) %collective-permute-start) | collective-permute-done | bytes 1048608 | tf_op jit(solution)/shard_map/cond/branch_1_fun/ppermute | solution.py:336
  17.5 0.2 add.10
  17.7 0.1 fusion
  17.8 0.6 collective-permute-start.1
  18.4 0.2 collective-permute-start.3
  18.6 13.2 %collective-permute-done.1 = f32[256,512]{1,0:T(8,128)S(1)} collective-permute-done((f32[256,512]{1,0:T(8,128)S(1)}, f32[256,512]{1,0:T(8,128)S(1)}, u32[]{:S(2)}, u32[]{:S(2)}) %collective-permute-start.1) | collective-permute-done | bytes 524320 | tf_op jit(solution)/shard_map/cond/branch_1_fun/ppermute | solution.py:336
  31.8 0.3 collective-permute-done.3
  32.1 0.2 slice_add_fusion.1
  32.3 0.4 collective-permute-start.2
  32.7 1.7 %collective-permute-start.4 = (f32[256,512]{1,0:T(8,128)S(1)}, f32[256,512]{1,0:T(8,128)S(1)}, u32[]{:S(2)}, u32[]{:S(2)}) collective-permute-start(f32[256,512]{1,0:T(8,128)S(1)} %get-tuple-element.66), channel_id=1, source_target_pairs={{0,8},{4,12},{8,0},{12,4},{16,24},{20,28},{24,16},{28,20},{1,9},{5... | collective-permute-start | bytes 1572872 | tf_op jit(solution)/shard_map/cond/branch_1_fun/ppermute | solution.py:336
  34.3 11.0 %collective-permute-done.2 = f32[256,512]{1,0:T(8,128)S(1)} collective-permute-done((f32[256,512]{1,0:T(8,128)S(1)}, f32[256,512]{1,0:T(8,128)S(1)}, u32[]{:S(2)}, u32[]{:S(2)}) %collective-permute-start.2) | collective-permute-done | bytes 524320 | tf_op jit(solution)/shard_map/cond/branch_1_fun/ppermute | solution.py:336
  45.3 0.1 add.12
  45.4 0.1 collective-permute-done.4
  45.6 0.1 add.14
  45.6 1.0 pad_maximum_fusion
  46.7 0.0 collective-permute-start.5
  46.7 3.0 %collective-permute-done.5 = f32[512,512]{1,0:T(8,128)} collective-permute-done((f32[512,512]{1,0:T(8,128)}, f32[512,512]{1,0:T(8,128)}, u32[]{:S(2)}, u32[]{:S(2)}) %collective-permute-start.5) | collective-permute-done | bytes 1048608 | tf_op jit(solution)/shard_map/cond/branch_1_fun/ppermute | solution.py:336
  49.7 1.3 collective-permute-start.6
  51.0 0.0 copy-start.1
  51.0 1.2 copy-done.1
  52.2 3.3 %upper.1 = (f32[512,512]{1,0:T(8,128)S(1)}, bf16[1152,512]{1,0:T(8,128)(2,1)S(1)}, bf16[384,512]{1,0:T(8,128)(2,1)S(1)}, bf16[384,512]{1,0:T(8,128)(2,1)S(1)}) custom-call(s32[2]{0:T(128)S(1)} %pad_add_fusion.refs_0_, f32[512,512]{1,0:T(8,128)} %get-tuple-element.41.refs_1_.refs_3_, f32[512,512]{1,0:T(8,128)} %get-tuple-element.42.refs_2_.refs_4_, ...), custom_call_target="tpu_custom_call" | custom-call | tf_op jit(solution)/shard_map/upper/pallas_call | solution.py:202
  55.5 1.5 %load_pieces.1 = (f32[1856,128]{1,0:T(8,128)S(1)}, f32[1664,128]{1,0:T(8,128)S(1)}, f32[576,128]{1,0:T(8,128)S(1)}) custom-call(f32[4096,128]{1,0:T(8,128)} %refs_5_.1), custom_call_target="tpu_custom_call" | custom-call | tf_op jit(solution)/shard_map/load_pieces/pallas_call | solution.py:59
  57.0 4.6 %collective-permute-start.10 = (f32[576,128]{1,0:T(8,128)S(1)}, f32[576,128]{1,0:T(8,128)S(1)}, u32[]{:S(2)}, u32[]{:S(2)}) collective-permute-start(f32[576,128]{1,0:T(8,128)S(1)} %get-tuple-element.55), channel_id=1, source_target_pairs={{1,2},{2,1},{5,6},{6,5},{9,10},{10,9},{13,14},{14,13},{17,18},{18,... | collective-permute-start | bytes 884744 | tf_op jit(solution)/shard_map/ppermute | solution.py:382
  61.6 10.7 %collective-permute-done.9.refs_7_ = f32[2048,128]{1,0:T(8,128)S(1)} collective-permute-done((f32[2048,128]{1,0:T(8,128)}, f32[2048,128]{1,0:T(8,128)S(1)}, u32[]{:S(2)}, u32[]{:S(2)}) %collective-permute-start.9) | collective-permute-done | bytes 1048608 | tf_op jit(solution)/shard_map/ppermute | solution.py:358
  72.3 1.3 collective-permute-start.12
  73.7 14.9 %collective-permute-done.7.refs_8_ = f32[1472,128]{1,0:T(8,128)} collective-permute-done((f32[1472,128]{1,0:T(8,128)}, f32[1472,128]{1,0:T(8,128)}, u32[]{:S(2)}, u32[]{:S(2)}) %collective-permute-start.7) | collective-permute-done | bytes 753696 | tf_op jit(solution)/shard_map/ppermute | solution.py:358
  88.6 0.0 collective-permute-done.8.refs_6_
  88.6 2.3 %collective-permute-start.15 = (f32[1856,128]{1,0:T(8,128)S(1)}, f32[1856,128]{1,0:T(8,128)S(1)}, u32[]{:S(2)}, u32[]{:S(2)}) collective-permute-start(f32[1856,128]{1,0:T(8,128)S(1)} %get-tuple-element.64), channel_id=1, source_target_pairs={{1,2},{2,1},{5,6},{6,5},{9,10},{10,9},{13,14},{14,13},{17,18},{18,... | collective-permute-start | bytes 2850824 | tf_op jit(solution)/shard_map/ppermute | solution.py:386
  90.9 2.7 %collective-permute-done.6.refs_3_ = f32[576,128]{1,0:T(8,128)S(1)} collective-permute-done((f32[576,128]{1,0:T(8,128)S(1)}, f32[576,128]{1,0:T(8,128)S(1)}, u32[]{:S(2)}, u32[]{:S(2)}) %collective-permute-start.6) | collective-permute-done | bytes 294944 | tf_op jit(solution)/shard_map/ppermute | solution.py:359
  93.6 2.3 %collective-permute-start.14 = (f32[1664,128]{1,0:T(8,128)S(1)}, f32[1664,128]{1,0:T(8,128)S(1)}, u32[]{:S(2)}, u32[]{:S(2)}) collective-permute-start(f32[1664,128]{1,0:T(8,128)S(1)} %get-tuple-element.63), channel_id=1, source_target_pairs={{1,2},{2,1},{5,6},{6,5},{9,10},{10,9},{13,14},{14,13},{17,18},{18,... | collective-permute-start | bytes 2555912 | tf_op jit(solution)/shard_map/ppermute | solution.py:387
  96.0 1.3 collective-permute-start.13
  97.3 2.6 %collective-permute-done.10.refs_4_ = f32[576,128]{1,0:T(8,128)S(1)} collective-permute-done((f32[576,128]{1,0:T(8,128)S(1)}, f32[576,128]{1,0:T(8,128)S(1)}, u32[]{:S(2)}, u32[]{:S(2)}) %collective-permute-start.10) | collective-permute-done | bytes 294944 | tf_op jit(solution)/shard_map/ppermute | solution.py:382
  99.9 1.3 collective-permute-start.11
  101.3 0.0 copy-done
  101.3 14.8 %main_update.1.refs_0_ = f32[4096,512]{1,0:T(8,128)S(1)} custom-call(s32[2]{0:T(128)S(1)} %pad_add_fusion.refs_0_, s32[512]{0:T(512)} %refs_1_.1, f32[4096,512]{1,0:T(8,128)} %refs_2_.1, f32[512,512]{1,0:T(8,128)} %get-tuple-element.41.refs_1_.refs_3_, f32[512,512]{1,0:T(8,128)} %get-tuple-element.42.refs_2_.refs_4_, f32[4096,128]{1,0:T(8,128)S(1)} %copy-done, ...), custom_call_target="tpu_custom_call" | custom-call | tf_op jit(solution)/shard_map/main_update/pallas_call | solution.py:281
  116.1 0.0 collective-permute-done.12.refs_2_
  116.1 4.2 %collective-permute-done.15.refs_3_ = f32[1856,128]{1,0:T(8,128)S(1)} collective-permute-done((f32[1856,128]{1,0:T(8,128)S(1)}, f32[1856,128]{1,0:T(8,128)S(1)}, u32[]{:S(2)}, u32[]{:S(2)}) %collective-permute-start.15) | collective-permute-done | bytes 950304 | tf_op jit(solution)/shard_map/ppermute | solution.py:386
  120.3 2.2 %last_update.3.refs_5_ = f32[4096,512]{1,0:T(8,128)} custom-call(f32[4096,512]{1,0:T(8,128)S(1)} %main_update.1.refs_0_, bf16[384,512]{1,0:T(8,128)(2,1)S(1)} %get-tuple-element.61.refs_1_.refs_2_, f32[2048,128]{1,0:T(8,128)S(1)} %collective-permute-done.12.refs_2_, f32[1856,128]{1,0:T(8,128)S(1)} %collective-permute-done.15.refs_3_), custom_call_target="tpu_custom_call" | custom-call | tf_op jit(solution)/shard_map/last_update/pallas_call | solution.py:322
  122.4 1.6 %collective-permute-done.13.refs_3_ = f32[1472,128]{1,0:T(8,128)S(1)} collective-permute-done((f32[1472,128]{1,0:T(8,128)}, f32[1472,128]{1,0:T(8,128)S(1)}, u32[]{:S(2)}, u32[]{:S(2)}) %collective-permute-start.13) | collective-permute-done | bytes 753696 | tf_op jit(solution)/shard_map/ppermute | solution.py:388
  124.0 14.4 %collective-permute-done.14.refs_4_ = f32[1664,128]{1,0:T(8,128)S(1)} collective-permute-done((f32[1664,128]{1,0:T(8,128)S(1)}, f32[1664,128]{1,0:T(8,128)S(1)}, u32[]{:S(2)}, u32[]{:S(2)}) %collective-permute-start.14) | collective-permute-done | bytes 852000 | tf_op jit(solution)/shard_map/ppermute | solution.py:387
  138.5 2.0 %last_update.4.refs_6_ = f32[4096,512]{1,0:T(8,128)} custom-call(f32[4096,512]{1,0:T(8,128)S(1)} %main_update.1.refs_0_, bf16[384,512]{1,0:T(8,128)(2,1)S(1)} %get-tuple-element.61.refs_1_.refs_2_, f32[2048,128]{1,0:T(8,128)S(1)} %collective-permute-done.12.refs_2_, f32[1472,128]{1,0:T(8,128)S(1)} %collective-permute-done.13.refs_3_, ...), custom_call_target="tpu_custom_call", output_to_operand_aliasing={{}: (5, {})} | custom-call | tf_op jit(solution)/shard_map/last_update/pallas_call | solution.py:322
  140.5 0.0 collective-permute-done.11.refs_5_
  140.5 1.6 %last_update.5 = f32[4096,512]{1,0:T(8,128)} custom-call(f32[4096,512]{1,0:T(8,128)S(1)} %main_update.1.refs_0_, bf16[384,512]{1,0:T(8,128)(2,1)S(1)} %get-tuple-element.60.refs_1_, bf16[384,512]{1,0:T(8,128)(2,1)S(1)} %get-tuple-element.61.refs_1_.refs_2_, f32[576,128]{1,0:T(8,128)S(1)} %collective-permute-done.6.refs_3_, ...), custom_call_target="tpu_custom_call", output_to_operand_aliasing={{}: (6, {})} | custom-call | tf_op jit(solution)/shard_map/last_update/pallas_call | solution.py:322
  (1 shorter events, 0.0 us)
Async XLA Ops:
  0.0 88.6 %collective-permute-start.8 = (f32[4096,128]{1,0:T(8,128)}, f32[4096,128]{1,0:T(8,128)}, u32[]{:S(2)}, u32[]{:S(2)}) collective-permute-start(f32[4096,128]{1,0:T(8,128)} %refs_5_.1), channel_id=1, source_target_pairs={{0,1},{1,0},{2,3},{3,2},{4,5},{5,4},{6,7},{7,6},{8,9},{9,8},{10,11... | collective-permute-start | bytes 6291464 | tf_op jit(solution)/shard_map/ppermute | solution.py:356
  2.8 69.5 %collective-permute-start.9 = (f32[2048,128]{1,0:T(8,128)}, f32[2048,128]{1,0:T(8,128)S(1)}, u32[]{:S(2)}, u32[]{:S(2)}) collective-permute-start(f32[2048,128]{1,0:T(8,128)} %get-tuple-element.51), channel_id=1, source_target_pairs={{0,2},{1,3},{2,0},{3,1},{4,6},{5,7},{6,4},{7,5},{8,10},{9,11},{10,... | collective-permute-start | bytes 3145736 | tf_op jit(solution)/shard_map/ppermute | solution.py:358
  5.5 83.1 %collective-permute-start.7 = (f32[1472,128]{1,0:T(8,128)}, f32[1472,128]{1,0:T(8,128)}, u32[]{:S(2)}, u32[]{:S(2)}) collective-permute-start(f32[1472,128]{1,0:T(8,128)} %get-tuple-element.47), channel_id=1, source_target_pairs={{0,2},{1,3},{2,0},{3,1},{4,6},{5,7},{6,4},{7,5},{8,10},{9,11},{10,... | collective-permute-start | bytes 2261000 | tf_op jit(solution)/shard_map/ppermute | solution.py:358
  7.7 93.5 %copy-start = (f32[4096,128]{1,0:T(8,128)S(1)}, f32[4096,128]{1,0:T(8,128)}, u32[]{:S(2)}) copy-start(f32[4096,128]{1,0:T(8,128)} %refs_5_.1) | copy-start | bytes 6291460
  14.8 2.7 %collective-permute-start = (f32[512,512]{1,0:T(8,128)S(1)}, f32[512,512]{1,0:T(8,128)S(1)}, u32[]{:S(2)}, u32[]{:S(2)}) collective-permute-start(f32[512,512]{1,0:T(8,128)S(1)} %get-tuple-element.16), channel_id=1, source_target_pairs={{0,4},{4,0},{8,12},{12,8},{16,20},{20,16},{24,28},{28,24},{1,5},{5... | collective-permute-start | bytes 3145736 | tf_op jit(solution)/shard_map/cond/branch_1_fun/ppermute | solution.py:336
  17.8 14.0 %collective-permute-start.1 = (f32[256,512]{1,0:T(8,128)S(1)}, f32[256,512]{1,0:T(8,128)S(1)}, u32[]{:S(2)}, u32[]{:S(2)}) collective-permute-start(f32[256,512]{1,0:T(8,128)S(1)} %get-tuple-element.67), channel_id=1, source_target_pairs={{0,8},{4,12},{8,0},{12,4},{16,24},{20,28},{24,16},{28,20},{1,9},{5... | collective-permute-start | bytes 1572872 | tf_op jit(solution)/shard_map/cond/branch_1_fun/ppermute | solution.py:336
  18.4 13.7 %collective-permute-start.3 = (f32[256,512]{1,0:T(8,128)S(1)}, f32[256,512]{1,0:T(8,128)S(1)}, u32[]{:S(2)}, u32[]{:S(2)}) collective-permute-start(f32[256,512]{1,0:T(8,128)S(1)} %get-tuple-element.68), channel_id=1, source_target_pairs={{0,16},{4,20},{8,24},{12,28},{16,0},{20,4},{24,8},{28,12},{1,17},{... | collective-permute-start | bytes 1572872 | tf_op jit(solution)/shard_map/cond/branch_1_fun/ppermute | solution.py:336
  32.3 13.1 %collective-permute-start.2 = (f32[256,512]{1,0:T(8,128)S(1)}, f32[256,512]{1,0:T(8,128)S(1)}, u32[]{:S(2)}, u32[]{:S(2)}) collective-permute-start(f32[256,512]{1,0:T(8,128)S(1)} %get-tuple-element.65), channel_id=1, source_target_pairs={{0,16},{4,20},{8,24},{12,28},{16,0},{20,4},{24,8},{28,12},{1,17},{... | collective-permute-start | bytes 1572872 | tf_op jit(solution)/shard_map/cond/branch_1_fun/ppermute | solution.py:336
  32.7 12.9 %collective-permute-start.4 = (f32[256,512]{1,0:T(8,128)S(1)}, f32[256,512]{1,0:T(8,128)S(1)}, u32[]{:S(2)}, u32[]{:S(2)}) collective-permute-start(f32[256,512]{1,0:T(8,128)S(1)} %get-tuple-element.66), channel_id=1, source_target_pairs={{0,8},{4,12},{8,0},{12,4},{16,24},{20,28},{24,16},{28,20},{1,9},{5... | collective-permute-start | bytes 1572872 | tf_op jit(solution)/shard_map/cond/branch_1_fun/ppermute | solution.py:336
  46.7 3.0 %collective-permute-start.5 = (f32[512,512]{1,0:T(8,128)}, f32[512,512]{1,0:T(8,128)}, u32[]{:S(2)}, u32[]{:S(2)}) collective-permute-start(f32[512,512]{1,0:T(8,128)} %pad_maximum_fusion), channel_id=1, source_target_pairs={{0,4},{4,0},{8,12},{12,8},{16,20},{20,16},{24,28},{28,24},{1,5},{5... | collective-permute-start | bytes 3145736 | tf_op jit(solution)/shard_map/cond/branch_1_fun/ppermute | solution.py:336
  49.7 43.9 %collective-permute-start.6 = (f32[576,128]{1,0:T(8,128)S(1)}, f32[576,128]{1,0:T(8,128)S(1)}, u32[]{:S(2)}, u32[]{:S(2)}) collective-permute-start(f32[576,128]{1,0:T(8,128)S(1)} %get-tuple-element.46), channel_id=1, source_target_pairs={{0,2},{3,1},{4,6},{7,5},{8,10},{11,9},{12,14},{15,13},{16,18},{19,... | collective-permute-start | bytes 884744 | tf_op jit(solution)/shard_map/ppermute | solution.py:359
  51.0 1.2 copy-start.1
  57.0 42.9 %collective-permute-start.10 = (f32[576,128]{1,0:T(8,128)S(1)}, f32[576,128]{1,0:T(8,128)S(1)}, u32[]{:S(2)}, u32[]{:S(2)}) collective-permute-start(f32[576,128]{1,0:T(8,128)S(1)} %get-tuple-element.55), channel_id=1, source_target_pairs={{1,2},{2,1},{5,6},{6,5},{9,10},{10,9},{13,14},{14,13},{17,18},{18,... | collective-permute-start | bytes 884744 | tf_op jit(solution)/shard_map/ppermute | solution.py:382
  72.3 43.8 %collective-permute-start.12 = (f32[2048,128]{1,0:T(8,128)S(1)}, f32[2048,128]{1,0:T(8,128)S(1)}, u32[]{:S(2)}, u32[]{:S(2)}) collective-permute-start(f32[2048,128]{1,0:T(8,128)S(1)} %collective-permute-done.9.refs_7_), channel_id=1, source_target_pairs={{2,3},{1,0},{6,7},{5,4},{10,11},{9,8},{14,15},{13,12},{18,19},{17,... | collective-permute-start | bytes 3145736 | tf_op jit(solution)/shard_map/ppermute | solution.py:383
  88.6 31.7 %collective-permute-start.15 = (f32[1856,128]{1,0:T(8,128)S(1)}, f32[1856,128]{1,0:T(8,128)S(1)}, u32[]{:S(2)}, u32[]{:S(2)}) collective-permute-start(f32[1856,128]{1,0:T(8,128)S(1)} %get-tuple-element.64), channel_id=1, source_target_pairs={{1,2},{2,1},{5,6},{6,5},{9,10},{10,9},{13,14},{14,13},{17,18},{18,... | collective-permute-start | bytes 2850824 | tf_op jit(solution)/shard_map/ppermute | solution.py:386
  93.6 44.8 %collective-permute-start.14 = (f32[1664,128]{1,0:T(8,128)S(1)}, f32[1664,128]{1,0:T(8,128)S(1)}, u32[]{:S(2)}, u32[]{:S(2)}) collective-permute-start(f32[1664,128]{1,0:T(8,128)S(1)} %get-tuple-element.63), channel_id=1, source_target_pairs={{1,2},{2,1},{5,6},{6,5},{9,10},{10,9},{13,14},{14,13},{17,18},{18,... | collective-permute-start | bytes 2555912 | tf_op jit(solution)/shard_map/ppermute | solution.py:387
  96.0 28.1 %collective-permute-start.13 = (f32[1472,128]{1,0:T(8,128)}, f32[1472,128]{1,0:T(8,128)S(1)}, u32[]{:S(2)}, u32[]{:S(2)}) collective-permute-start(f32[1472,128]{1,0:T(8,128)} %collective-permute-done.7.refs_8_), channel_id=1, source_target_pairs={{2,3},{1,0},{6,7},{5,4},{10,11},{9,8},{14,15},{13,12},{18,19},{17,... | collective-permute-start | bytes 2261000 | tf_op jit(solution)/shard_map/ppermute | solution.py:388
  99.9 40.6 %collective-permute-start.11 = (f32[1152,128]{1,0:T(8,128)S(1)}, f32[1152,128]{1,0:T(8,128)S(1)}, u32[]{:S(2)}, u32[]{:S(2)}) collective-permute-start(f32[1152,128]{1,0:T(8,128)S(1)} %pad_maximum_fusion.1), channel_id=1, source_target_pairs={{2,3},{1,0},{6,7},{5,4},{10,11},{9,8},{14,15},{13,12},{18,19},{17,... | collective-permute-start | bytes 1769480 | tf_op jit(solution)/shard_map/ppermute | solution.py:390

commit v10 on v9

--- a/solution.py
+++ b/solution.py
@@ -10,8 +10,8 @@
 MIDDLE = [(1, 2), (2, 1)]
 ENDS = [(2, 3), (1, 0)]
 FAR = [(0, 2), (3, 1)]
-PIECES = (64, 46, 18)
-MIDDLE_PIECES = (58, 52, 18)
+PIECES = (88, 12, 28)
+MIDDLE_PIECES = (84, 16, 28)
 TILE = 512
 LAST_TILE = 256
 SMALL = pl.CostEstimate(flops=0, bytes_accessed=0, transcendentals=0)
@@ -392,15 +392,15 @@
         base = main_update(info, pivots, slab, total, other, panel, near, [head, rest], upper, terms)
         segments = [(first_mid, [(0, [(1, 0), (2, 0)])])]
         result = last_update(base, [last_terms, head_end, head_mid], segments, block, 0, [])
+        segments = [(last, [(0, [(2, 0), (4, last)]), (1, [(3, 0), (4, 0)])])]
+        arrays = [across_terms, last_terms, far, tail_mid, both]
+        result = last_update(base, arrays, segments, block, early, [result])
         segments = [
             (first - first_mid, [(0, [(1, first_mid), (3, 0)])]),
             (second, [(0, [(2, 0), (3, first - first_mid)])]),
         ]
         arrays = [last_terms, head_end, rest_end, rest_mid]
-        result = last_update(base, arrays, segments, block, first_mid, [result])
-        segments = [(last, [(0, [(2, 0), (4, last)]), (1, [(3, 0), (4, 0)])])]
-        arrays = [across_terms, last_terms, far, tail_mid, both]
-        return last_update(base, arrays, segments, block, early, [result])
+        return last_update(base, arrays, segments, block, first_mid, [result])
 
     in_specs = (P("prow", "pcol"), P("prow", "pcol"), P(), P())
     return jax.shard_map(

time: 143 us -> 147 us (1.028)
  waiting for transfers between devices: 81.3 us -> 84.2 us
  starting transfers between devices: 21 us -> 23.3 us
    ppermute x2, waiting for transfers between devices: 25.6 us -> 44.3 us  [shards(): across = [lax.ppermute(piece, 'pcol', ACROSS) for piece in pieces]]
    ppermute x1, waiting for transfers between devices: 14.4 us -> 0.09 us  [shards(): rest_mid = lax.ppermute(rest_mid, 'pcol', MIDDLE)]
    ppermute x1, waiting for transfers between devices: 4.18 us -> 9.97 us  [shards(): head_mid = lax.ppermute(head_mid, 'pcol', MIDDLE)]
    ppermute x1, waiting for transfers between devices: 2.71 us -> 0.01 us  [shards(): far = lax.ppermute(tail, 'pcol', FAR)]
    ppermute x1, waiting for transfers between devices: 2.57 us -> 0.01 us  [shards(): tail_mid = lax.ppermute(tail_mid, 'pcol', MIDDLE)]
    ppermute x1, starting transfers between devices: 4.61 us -> 2.36 us  [shards(): tail_mid = lax.ppermute(tail_mid, 'pcol', MIDDLE)]
    ppermute x2, starting transfers between devices: 2.99 us -> 4.72 us  [shards(): across = [lax.ppermute(piece, 'pcol', ACROSS) for piece in pieces]]
    ppermute x1, waiting for transfers between devices: 1.6 us -> 0.01 us  [shards(): rest_end = lax.ppermute(rest, 'pcol', ENDS)]
  transfers between devices with their start and end apart: 16 -> 16, of which waited for: 13 -> 10; matrix products, arithmetic and copies ran while one was open for 2% -> 2% of each run, Pallas kernels for 23% -> 23%
where the time goes in v10:
time: 147 us; the launch traced here: 146 us
  waiting for transfers between devices  84.2 us (57%)
  Pallas kernels  34.6 us (24%)
  starting transfers between devices  23.3 us (16%)
  other arithmetic  1.79 us (1%)
  local copies, waits for them, and re-layouts  1.78 us (1%)
    ppermute x2, waiting for transfers between devices, shards(): across = [lax.ppermute(piece, 'pcol', ACROSS) for piece in pieces]  44.3 us
    ppermute x6, waiting for transfers between devices, exchange(): lax.ppermute(value, 'prow', [(i, i ^ 1 << bit) for i in range(count)])  29.9 us
    pallas_call x1, Pallas kernels, main_update(): pl.pallas_call(lambda *refs: main_kernel(min(TILE, block), *refs), out_sh...  14.9 us
    ppermute x1, waiting for transfers between devices, shards(): head_mid = lax.ppermute(head_mid, 'pcol', MIDDLE)  9.97 us
    pallas_call x1, Pallas kernels, pick(): pl.pallas_call(pick_kernel, out_shape=(shape, shape), grid_spec=pltpu.Pre...  6.75 us
    pallas_call x3, Pallas kernels, last_update(): pl.pallas_call(lambda *refs: last_kernel(first_row, block, min(LAST_TILE,...  5.82 us
    ppermute x2, starting transfers between devices, shards(): across = [lax.ppermute(piece, 'pcol', ACROSS) for piece in pieces]  4.72 us
    ppermute x1, starting transfers between devices, shards(): head_mid = lax.ppermute(head_mid, 'pcol', MIDDLE)  3.47 us
  transfers between devices with their start and end apart: 16, of which 10 were waited for; matrix products, arithmetic and copies ran while one was open for 2% of the time, Pallas kernels for 23%

profile of v10, /device:TPU:14, one launch (start us, length us, event | category | flops | bytes accessed | tf_op | source)
XLA Modules:
  0.0 146.5 jit_solution(11784096200507021437)
XLA Ops:
  0.0 0.0 copy-start.2
  0.0 0.4 collective-permute-start.8
  0.5 2.2 %cut.1 = (f32[2816,128]{1,0:T(8,128)}, f32[384,128]{1,0:T(8,128)S(1)}, f32[896,128]{1,0:T(8,128)S(1)}) custom-call(f32[4096,128]{1,0:T(8,128)} %refs_5_.1), custom_call_target="tpu_custom_call" | custom-call | tf_op jit(solution)/shard_map/cut/pallas_call | solution.py:94
  2.6 2.7 %collective-permute-start.9 = (f32[2816,128]{1,0:T(8,128)}, f32[2816,128]{1,0:T(8,128)}, u32[]{:S(2)}, u32[]{:S(2)}) collective-permute-start(f32[2816,128]{1,0:T(8,128)} %get-tuple-element.51), channel_id=1, source_target_pairs={{0,2},{1,3},{2,0},{3,1},{4,6},{5,7},{6,4},{7,5},{8,10},{9,11},{10,... | collective-permute-start | bytes 4325384 | tf_op jit(solution)/shard_map/ppermute | solution.py:358
  5.3 1.3 collective-permute-start.6
  6.6 0.0 copy-done.2
  6.6 0.5 slice.13
  7.6 0.1 pad_add_fusion.refs_0_
  7.7 41.6 %conditional.1 = (f32[512,512]{1,0:T(8,128)}, f32[512,512]{1,0:T(8,128)}) conditional(s32[]{:T(128)} %bitcast.2, f32[4096,512]{1,0:T(8,128)} %refs_2_.1, (s32[2]{0:T(128)S(1)}, s32[512]{0:T(512)S(1)}, f32[4096,512]{1,0:T(8,128)}) %tuple.28), branch_computations={%region_0.0_spmd, %region_1.0_spmd} | conditional | flops 1048576 | bytes 30408960 | solution.py:375
  7.7 6.7 %pick.1 = (f32[512,512]{1,0:T(8,128)S(1)}, f32[512,512]{1,0:T(8,128)S(1)}) custom-call(s32[2]{0:T(128)S(1)} %get-tuple-element.12.info, s32[512]{0:T(512)S(1)} %get-tuple-element.13.pivots, f32[4096,512]{1,0:T(8,128)} %get-tuple-element.14.slab), custom_call_target="tpu_custom_call" | custom-call | tf_op jit(solution)/shard_map/cond/branch_1_fun/pick/pallas_call | solution.py:156
  14.5 0.1 collective-permute-start
  14.5 2.6 %collective-permute-done = f32[512,512]{1,0:T(8,128)S(1)} collective-permute-done((f32[512,512]{1,0:T(8,128)S(1)}, f32[512,512]{1,0:T(8,128)S(1)}, u32[]{:S(2)}, u32[]{:S(2)}) %collective-permute-start) | collective-permute-done | bytes 1048608 | tf_op jit(solution)/shard_map/cond/branch_1_fun/ppermute | solution.py:336
  17.2 0.2 add.10
  17.4 0.1 fusion
  17.5 0.6 collective-permute-start.1
  18.1 0.5 collective-permute-start.3
  18.6 12.9 %collective-permute-done.1 = f32[256,512]{1,0:T(8,128)S(1)} collective-permute-done((f32[256,512]{1,0:T(8,128)S(1)}, f32[256,512]{1,0:T(8,128)S(1)}, u32[]{:S(2)}, u32[]{:S(2)}) %collective-permute-start.1) | collective-permute-done | bytes 524320 | tf_op jit(solution)/shard_map/cond/branch_1_fun/ppermute | solution.py:336
  31.5 0.3 collective-permute-done.3
  31.8 0.2 slice_add_fusion.1
  32.0 0.6 collective-permute-start.2
  32.5 1.5 %collective-permute-start.4 = (f32[256,512]{1,0:T(8,128)S(1)}, f32[256,512]{1,0:T(8,128)S(1)}, u32[]{:S(2)}, u32[]{:S(2)}) collective-permute-start(f32[256,512]{1,0:T(8,128)S(1)} %get-tuple-element.66), channel_id=1, source_target_pairs={{0,8},{4,12},{8,0},{12,4},{16,24},{20,28},{24,16},{28,20},{1,9},{5... | collective-permute-start | bytes 1572872 | tf_op jit(solution)/shard_map/cond/branch_1_fun/ppermute | solution.py:336
  34.0 10.9 %collective-permute-done.2 = f32[256,512]{1,0:T(8,128)S(1)} collective-permute-done((f32[256,512]{1,0:T(8,128)S(1)}, f32[256,512]{1,0:T(8,128)S(1)}, u32[]{:S(2)}, u32[]{:S(2)}) %collective-permute-start.2) | collective-permute-done | bytes 524320 | tf_op jit(solution)/shard_map/cond/branch_1_fun/ppermute | solution.py:336
  44.9 0.1 add.12
  45.0 0.1 collective-permute-done.4
  45.2 0.1 add.14
  45.2 1.1 pad_maximum_fusion
  46.3 0.0 collective-permute-start.5
  46.3 3.0 %collective-permute-done.5 = f32[512,512]{1,0:T(8,128)} collective-permute-done((f32[512,512]{1,0:T(8,128)}, f32[512,512]{1,0:T(8,128)}, u32[]{:S(2)}, u32[]{:S(2)}) %collective-permute-start.5) | collective-permute-done | bytes 1048608 | tf_op jit(solution)/shard_map/cond/branch_1_fun/ppermute | solution.py:336
  49.3 0.0 copy-start.1
  49.3 1.2 copy-done.1
  50.5 3.3 %upper.1 = (f32[512,512]{1,0:T(8,128)S(1)}, bf16[1152,512]{1,0:T(8,128)(2,1)S(1)}, bf16[384,512]{1,0:T(8,128)(2,1)S(1)}, bf16[384,512]{1,0:T(8,128)(2,1)S(1)}) custom-call(s32[2]{0:T(128)S(1)} %pad_add_fusion.refs_0_, f32[512,512]{1,0:T(8,128)} %get-tuple-element.41.refs_1_.refs_3_, f32[512,512]{1,0:T(8,128)} %get-tuple-element.42.refs_2_.refs_4_, ...), custom_call_target="tpu_custom_call" | custom-call | tf_op jit(solution)/shard_map/upper/pallas_call | solution.py:202
  53.8 0.0 copy-start
  53.8 1.7 %load_pieces.1 = (f32[2688,128]{1,0:T(8,128)S(1)}, f32[512,128]{1,0:T(8,128)S(1)}, f32[896,128]{1,0:T(8,128)S(1)}) custom-call(f32[4096,128]{1,0:T(8,128)} %refs_5_.1), custom_call_target="tpu_custom_call" | custom-call | tf_op jit(solution)/shard_map/load_pieces/pallas_call | solution.py:59
  55.5 2.4 %collective-permute-start.10 = (f32[896,128]{1,0:T(8,128)S(1)}, f32[896,128]{1,0:T(8,128)S(1)}, u32[]{:S(2)}, u32[]{:S(2)}) collective-permute-start(f32[896,128]{1,0:T(8,128)S(1)} %get-tuple-element.55), channel_id=1, source_target_pairs={{1,2},{2,1},{5,6},{6,5},{9,10},{10,9},{13,14},{14,13},{17,18},{18,... | collective-permute-start | bytes 1376264 | tf_op jit(solution)/shard_map/ppermute | solution.py:382
  57.9 2.1 %collective-permute-start.7 = (f32[384,128]{1,0:T(8,128)S(1)}, f32[384,128]{1,0:T(8,128)S(1)}, u32[]{:S(2)}, u32[]{:S(2)}) collective-permute-start(f32[384,128]{1,0:T(8,128)S(1)} %get-tuple-element.47), channel_id=1, source_target_pairs={{0,2},{1,3},{2,0},{3,1},{4,6},{5,7},{6,4},{7,5},{8,10},{9,11},{10,... | collective-permute-start | bytes 589832 | tf_op jit(solution)/shard_map/ppermute | solution.py:358
  59.9 20.9 %collective-permute-done.9.refs_7_ = f32[2816,128]{1,0:T(8,128)} collective-permute-done((f32[2816,128]{1,0:T(8,128)}, f32[2816,128]{1,0:T(8,128)}, u32[]{:S(2)}, u32[]{:S(2)}) %collective-permute-start.9) | collective-permute-done | bytes 1441824 | tf_op jit(solution)/shard_map/ppermute | solution.py:358
  80.8 1.4 collective-permute-start.11
  82.2 23.4 %collective-permute-done.7.refs_8_ = f32[384,128]{1,0:T(8,128)S(1)} collective-permute-done((f32[384,128]{1,0:T(8,128)S(1)}, f32[384,128]{1,0:T(8,128)S(1)}, u32[]{:S(2)}, u32[]{:S(2)}) %collective-permute-start.7) | collective-permute-done | bytes 196640 | tf_op jit(solution)/shard_map/ppermute | solution.py:358
  105.6 0.0 collective-permute-done.8.refs_6_
  105.6 3.5 %collective-permute-start.15 = (f32[2688,128]{1,0:T(8,128)S(1)}, f32[2688,128]{1,0:T(8,128)S(1)}, u32[]{:S(2)}, u32[]{:S(2)}) collective-permute-start(f32[2688,128]{1,0:T(8,128)S(1)} %get-tuple-element.64), channel_id=1, source_target_pairs={{1,2},{2,1},{5,6},{6,5},{9,10},{10,9},{13,14},{14,13},{17,18},{18,... | collective-permute-start | bytes 4128776 | tf_op jit(solution)/shard_map/ppermute | solution.py:386
  109.1 0.0 collective-permute-done.6.refs_3_
  109.1 0.0 collective-permute-done.10.refs_4_
  109.1 0.1 pad_maximum_fusion.1
  109.2 2.8 %collective-permute-start.14 = (f32[1792,128]{1,0:T(8,128)S(1)}, f32[1792,128]{1,0:T(8,128)S(1)}, u32[]{:S(2)}, u32[]{:S(2)}) collective-permute-start(f32[1792,128]{1,0:T(8,128)S(1)} %pad_maximum_fusion.1), channel_id=1, source_target_pairs={{2,3},{1,0},{6,7},{5,4},{10,11},{9,8},{14,15},{13,12},{18,19},{17,... | collective-permute-start | bytes 2752520 | tf_op jit(solution)/shard_map/ppermute | solution.py:390
  112.0 2.4 %collective-permute-start.13 = (f32[512,128]{1,0:T(8,128)S(1)}, f32[512,128]{1,0:T(8,128)S(1)}, u32[]{:S(2)}, u32[]{:S(2)}) collective-permute-start(f32[512,128]{1,0:T(8,128)S(1)} %get-tuple-element.61), channel_id=1, source_target_pairs={{1,2},{2,1},{5,6},{6,5},{9,10},{10,9},{13,14},{14,13},{17,18},{18,... | collective-permute-start | bytes 786440 | tf_op jit(solution)/shard_map/ppermute | solution.py:387
  114.3 1.3 collective-permute-start.12
  115.6 0.0 copy-done
  115.6 14.9 %main_update.1.refs_0_ = f32[4096,512]{1,0:T(8,128)S(1)} custom-call(s32[2]{0:T(128)S(1)} %pad_add_fusion.refs_0_, s32[512]{0:T(512)S(1)} %copy-done.2, f32[4096,512]{1,0:T(8,128)} %refs_2_.1, f32[512,512]{1,0:T(8,128)} %get-tuple-element.41.refs_1_.refs_3_, f32[512,512]{1,0:T(8,128)} %get-tuple-element.42.refs_2_.refs_4_, f32[4096,128]{1,0:T(8,128)S(1)} %copy-done, ...), custom_call_target="tpu_custom_call" | custom-call | tf_op jit(solution)/shard_map/main_update/pallas_call | solution.py:281
  130.5 0.0 collective-permute-done.11.refs_2_
  130.6 10.0 %collective-permute-done.15.refs_3_ = f32[2688,128]{1,0:T(8,128)S(1)} collective-permute-done((f32[2688,128]{1,0:T(8,128)S(1)}, f32[2688,128]{1,0:T(8,128)S(1)}, u32[]{:S(2)}, u32[]{:S(2)}) %collective-permute-start.15) | collective-permute-done | bytes 1376288 | tf_op jit(solution)/shard_map/ppermute | solution.py:386
  140.5 2.7 %last_update.3.refs_6_ = f32[4096,512]{1,0:T(8,128)} custom-call(f32[4096,512]{1,0:T(8,128)S(1)} %main_update.1.refs_0_, bf16[384,512]{1,0:T(8,128)(2,1)S(1)} %get-tuple-element.60.refs_1_.refs_2_, f32[2816,128]{1,0:T(8,128)S(1)} %collective-permute-done.11.refs_2_, f32[2688,128]{1,0:T(8,128)S(1)} %collective-permute-done.15.refs_3_), custom_call_target="tpu_custom_call" | custom-call | tf_op jit(solution)/shard_map/last_update/pallas_call | solution.py:322
  143.2 0.0 collective-permute-done.14.refs_5_
  143.2 1.9 %last_update.4.refs_5_ = f32[4096,512]{1,0:T(8,128)} custom-call(f32[4096,512]{1,0:T(8,128)S(1)} %main_update.1.refs_0_, bf16[384,512]{1,0:T(8,128)(2,1)S(1)} %get-tuple-element.62.refs_1_, bf16[384,512]{1,0:T(8,128)(2,1)S(1)} %get-tuple-element.60.refs_1_.refs_2_, f32[896,128]{1,0:T(8,128)S(1)} %collective-permute-done.6.refs_3_, ...), custom_call_target="tpu_custom_call", output_to_operand_aliasing={{}: (6, {})} | custom-call | tf_op jit(solution)/shard_map/last_update/pallas_call | solution.py:322
  145.1 0.0 collective-permute-done.12.refs_3_
  145.1 0.1 collective-permute-done.13.refs_4_
  145.2 1.3 last_update.5
Async XLA Ops:
  0.0 6.6 %copy-start.2 = (s32[512]{0:T(512)S(1)}, s32[512]{0:T(512)}, u32[]{:S(2)}) copy-start(s32[512]{0:T(512)} %refs_1_.1) | copy-start | bytes 6148
  0.0 105.6 %collective-permute-start.8 = (f32[4096,128]{1,0:T(8,128)}, f32[4096,128]{1,0:T(8,128)S(1)}, u32[]{:S(2)}, u32[]{:S(2)}) collective-permute-start(f32[4096,128]{1,0:T(8,128)} %refs_5_.1), channel_id=1, source_target_pairs={{0,1},{1,0},{2,3},{3,2},{4,5},{5,4},{6,7},{7,6},{8,9},{9,8},{10,11... | collective-permute-start | bytes 6291464 | tf_op jit(solution)/shard_map/ppermute | solution.py:356
  2.6 78.2 %collective-permute-start.9 = (f32[2816,128]{1,0:T(8,128)}, f32[2816,128]{1,0:T(8,128)}, u32[]{:S(2)}, u32[]{:S(2)}) collective-permute-start(f32[2816,128]{1,0:T(8,128)} %get-tuple-element.51), channel_id=1, source_target_pairs={{0,2},{1,3},{2,0},{3,1},{4,6},{5,7},{6,4},{7,5},{8,10},{9,11},{10,... | collective-permute-start | bytes 4325384 | tf_op jit(solution)/shard_map/ppermute | solution.py:358
  5.3 103.8 %collective-permute-start.6 = (f32[896,128]{1,0:T(8,128)S(1)}, f32[896,128]{1,0:T(8,128)S(1)}, u32[]{:S(2)}, u32[]{:S(2)}) collective-permute-start(f32[896,128]{1,0:T(8,128)S(1)} %get-tuple-element.46), channel_id=1, source_target_pairs={{0,2},{3,1},{4,6},{7,5},{8,10},{11,9},{12,14},{15,13},{16,18},{19,... | collective-permute-start | bytes 1376264 | tf_op jit(solution)/shard_map/ppermute | solution.py:359
  14.5 2.7 %collective-permute-start = (f32[512,512]{1,0:T(8,128)S(1)}, f32[512,512]{1,0:T(8,128)S(1)}, u32[]{:S(2)}, u32[]{:S(2)}) collective-permute-start(f32[512,512]{1,0:T(8,128)S(1)} %get-tuple-element.16), channel_id=1, source_target_pairs={{0,4},{4,0},{8,12},{12,8},{16,20},{20,16},{24,28},{28,24},{1,5},{5... | collective-permute-start | bytes 3145736 | tf_op jit(solution)/shard_map/cond/branch_1_fun/ppermute | solution.py:336
  17.5 14.0 %collective-permute-start.1 = (f32[256,512]{1,0:T(8,128)S(1)}, f32[256,512]{1,0:T(8,128)S(1)}, u32[]{:S(2)}, u32[]{:S(2)}) collective-permute-start(f32[256,512]{1,0:T(8,128)S(1)} %get-tuple-element.67), channel_id=1, source_target_pairs={{0,8},{4,12},{8,0},{12,4},{16,24},{20,28},{24,16},{28,20},{1,9},{5... | collective-permute-start | bytes 1572872 | tf_op jit(solution)/shard_map/cond/branch_1_fun/ppermute | solution.py:336
  18.1 13.7 %collective-permute-start.3 = (f32[256,512]{1,0:T(8,128)S(1)}, f32[256,512]{1,0:T(8,128)S(1)}, u32[]{:S(2)}, u32[]{:S(2)}) collective-permute-start(f32[256,512]{1,0:T(8,128)S(1)} %get-tuple-element.68), channel_id=1, source_target_pairs={{0,16},{4,20},{8,24},{12,28},{16,0},{20,4},{24,8},{28,12},{1,17},{... | collective-permute-start | bytes 1572872 | tf_op jit(solution)/shard_map/cond/branch_1_fun/ppermute | solution.py:336
  32.0 13.0 %collective-permute-start.2 = (f32[256,512]{1,0:T(8,128)S(1)}, f32[256,512]{1,0:T(8,128)S(1)}, u32[]{:S(2)}, u32[]{:S(2)}) collective-permute-start(f32[256,512]{1,0:T(8,128)S(1)} %get-tuple-element.65), channel_id=1, source_target_pairs={{0,16},{4,20},{8,24},{12,28},{16,0},{20,4},{24,8},{28,12},{1,17},{... | collective-permute-start | bytes 1572872 | tf_op jit(solution)/shard_map/cond/branch_1_fun/ppermute | solution.py:336
  32.5 12.6 %collective-permute-start.4 = (f32[256,512]{1,0:T(8,128)S(1)}, f32[256,512]{1,0:T(8,128)S(1)}, u32[]{:S(2)}, u32[]{:S(2)}) collective-permute-start(f32[256,512]{1,0:T(8,128)S(1)} %get-tuple-element.66), channel_id=1, source_target_pairs={{0,8},{4,12},{8,0},{12,4},{16,24},{20,28},{24,16},{28,20},{1,9},{5... | collective-permute-start | bytes 1572872 | tf_op jit(solution)/shard_map/cond/branch_1_fun/ppermute | solution.py:336
  46.3 3.0 %collective-permute-start.5 = (f32[512,512]{1,0:T(8,128)}, f32[512,512]{1,0:T(8,128)}, u32[]{:S(2)}, u32[]{:S(2)}) collective-permute-start(f32[512,512]{1,0:T(8,128)} %pad_maximum_fusion), channel_id=1, source_target_pairs={{0,4},{4,0},{8,12},{12,8},{16,20},{20,16},{24,28},{28,24},{1,5},{5... | collective-permute-start | bytes 3145736 | tf_op jit(solution)/shard_map/cond/branch_1_fun/ppermute | solution.py:336
  49.3 1.2 copy-start.1
  53.8 61.8 %copy-start = (f32[4096,128]{1,0:T(8,128)S(1)}, f32[4096,128]{1,0:T(8,128)}, u32[]{:S(2)}) copy-start(f32[4096,128]{1,0:T(8,128)} %refs_5_.1) | copy-start | bytes 6291460
  55.5 53.6 %collective-permute-start.10 = (f32[896,128]{1,0:T(8,128)S(1)}, f32[896,128]{1,0:T(8,128)S(1)}, u32[]{:S(2)}, u32[]{:S(2)}) collective-permute-start(f32[896,128]{1,0:T(8,128)S(1)} %get-tuple-element.55), channel_id=1, source_target_pairs={{1,2},{2,1},{5,6},{6,5},{9,10},{10,9},{13,14},{14,13},{17,18},{18,... | collective-permute-start | bytes 1376264 | tf_op jit(solution)/shard_map/ppermute | solution.py:382
  57.9 47.7 %collective-permute-start.7 = (f32[384,128]{1,0:T(8,128)S(1)}, f32[384,128]{1,0:T(8,128)S(1)}, u32[]{:S(2)}, u32[]{:S(2)}) collective-permute-start(f32[384,128]{1,0:T(8,128)S(1)} %get-tuple-element.47), channel_id=1, source_target_pairs={{0,2},{1,3},{2,0},{3,1},{4,6},{5,7},{6,4},{7,5},{8,10},{9,11},{10,... | collective-permute-start | bytes 589832 | tf_op jit(solution)/shard_map/ppermute | solution.py:358
  80.8 49.7 %collective-permute-start.11 = (f32[2816,128]{1,0:T(8,128)}, f32[2816,128]{1,0:T(8,128)S(1)}, u32[]{:S(2)}, u32[]{:S(2)}) collective-permute-start(f32[2816,128]{1,0:T(8,128)} %collective-permute-done.9.refs_7_), channel_id=1, source_target_pairs={{2,3},{1,0},{6,7},{5,4},{10,11},{9,8},{14,15},{13,12},{18,19},{17,... | collective-permute-start | bytes 4325384 | tf_op jit(solution)/shard_map/ppermute | solution.py:383
  105.6 34.9 %collective-permute-start.15 = (f32[2688,128]{1,0:T(8,128)S(1)}, f32[2688,128]{1,0:T(8,128)S(1)}, u32[]{:S(2)}, u32[]{:S(2)}) collective-permute-start(f32[2688,128]{1,0:T(8,128)S(1)} %get-tuple-element.64), channel_id=1, source_target_pairs={{1,2},{2,1},{5,6},{6,5},{9,10},{10,9},{13,14},{14,13},{17,18},{18,... | collective-permute-start | bytes 4128776 | tf_op jit(solution)/shard_map/ppermute | solution.py:386
  109.2 34.1 %collective-permute-start.14 = (f32[1792,128]{1,0:T(8,128)S(1)}, f32[1792,128]{1,0:T(8,128)S(1)}, u32[]{:S(2)}, u32[]{:S(2)}) collective-permute-start(f32[1792,128]{1,0:T(8,128)S(1)} %pad_maximum_fusion.1), channel_id=1, source_target_pairs={{2,3},{1,0},{6,7},{5,4},{10,11},{9,8},{14,15},{13,12},{18,19},{17,... | collective-permute-start | bytes 2752520 | tf_op jit(solution)/shard_map/ppermute | solution.py:390
  112.0 33.3 %collective-permute-start.13 = (f32[512,128]{1,0:T(8,128)S(1)}, f32[512,128]{1,0:T(8,128)S(1)}, u32[]{:S(2)}, u32[]{:S(2)}) collective-permute-start(f32[512,128]{1,0:T(8,128)S(1)} %get-tuple-element.61), channel_id=1, source_target_pairs={{1,2},{2,1},{5,6},{6,5},{9,10},{10,9},{13,14},{14,13},{17,18},{18,... | collective-permute-start | bytes 786440 | tf_op jit(solution)/shard_map/ppermute | solution.py:387
  114.3 30.8 %collective-permute-start.12 = (f32[384,128]{1,0:T(8,128)S(1)}, f32[384,128]{1,0:T(8,128)S(1)}, u32[]{:S(2)}, u32[]{:S(2)}) collective-permute-start(f32[384,128]{1,0:T(8,128)S(1)} %collective-permute-done.7.refs_8_), channel_id=1, source_target_pairs={{2,3},{1,0},{6,7},{5,4},{10,11},{9,8},{14,15},{13,12},{18,19},{17,... | collective-permute-start | bytes 589832 | tf_op jit(solution)/shard_map/ppermute | solution.py:388

commit v11 on v10

--- a/solution.py
+++ b/solution.py
@@ -10,8 +10,8 @@
 MIDDLE = [(1, 2), (2, 1)]
 ENDS = [(2, 3), (1, 0)]
 FAR = [(0, 2), (3, 1)]
-PIECES = (88, 12, 28)
-MIDDLE_PIECES = (84, 16, 28)
+PIECES = (76, 28, 24)
+MIDDLE_PIECES = (72, 32, 24)
 TILE = 512
 LAST_TILE = 256
 SMALL = pl.CostEstimate(flops=0, bytes_accessed=0, transcendentals=0)

time: 147 us -> 141 us (0.959)
  waiting for transfers between devices: 84.2 us -> 79.5 us
  starting transfers between devices: 23.3 us -> 21 us
    ppermute x2, waiting for transfers between devices: 44.3 us -> 23.7 us  [shards(): across = [lax.ppermute(piece, 'pcol', ACROSS) for piece in pieces]]
    ppermute x1, waiting for transfers between devices: 0.01 us -> 8.37 us  [shards(): tail_mid = lax.ppermute(tail_mid, 'pcol', MIDDLE)]
    ppermute x1, waiting for transfers between devices: 0.01 us -> 4.82 us  [shards(): far = lax.ppermute(tail, 'pcol', FAR)]
    ppermute x1, waiting for transfers between devices: 9.97 us -> 5.59 us  [shards(): head_mid = lax.ppermute(head_mid, 'pcol', MIDDLE)]
    ppermute x1, waiting for transfers between devices: 0.01 us -> 3.96 us  [shards(): rest_end = lax.ppermute(rest, 'pcol', ENDS)]
    ppermute x1, waiting for transfers between devices: 0.09 us -> 2.94 us  [shards(): rest_mid = lax.ppermute(rest_mid, 'pcol', MIDDLE)]
    ppermute x1, starting transfers between devices: 2.36 us -> 4.61 us  [shards(): tail_mid = lax.ppermute(tail_mid, 'pcol', MIDDLE)]
    ppermute x2, starting transfers between devices: 4.72 us -> 2.92 us  [shards(): across = [lax.ppermute(piece, 'pcol', ACROSS) for piece in pieces]]
  transfers between devices with their start and end apart: 16 -> 16, of which waited for: 10 -> 13; matrix products, arithmetic and copies ran while one was open for 2% -> 2% of each run, Pallas kernels for 23% -> 23%
where the time goes in v11:
time: 141 us; the launch traced here: 140 us
  waiting for transfers between devices  79.5 us (56%)
  Pallas kernels  34.3 us (24%)
  starting transfers between devices  21 us (15%)
  local copies, waits for them, and re-layouts  2.6 us (2%)
  other arithmetic  1.79 us (1%)
    ppermute x6, waiting for transfers between devices, exchange(): lax.ppermute(value, 'prow', [(i, i ^ 1 << bit) for i in range(count)])  30.2 us
    ppermute x2, waiting for transfers between devices, shards(): across = [lax.ppermute(piece, 'pcol', ACROSS) for piece in pieces]  23.7 us
    pallas_call x1, Pallas kernels, main_update(): pl.pallas_call(lambda *refs: main_kernel(min(TILE, block), *refs), out_sh...  14.5 us
    ppermute x1, waiting for transfers between devices, shards(): tail_mid = lax.ppermute(tail_mid, 'pcol', MIDDLE)  8.37 us
    pallas_call x1, Pallas kernels, pick(): pl.pallas_call(pick_kernel, out_shape=(shape, shape), grid_spec=pltpu.Pre...  6.75 us
    pallas_call x3, Pallas kernels, last_update(): pl.pallas_call(lambda *refs: last_kernel(first_row, block, min(LAST_TILE,...  5.86 us
    ppermute x1, waiting for transfers between devices, shards(): head_mid = lax.ppermute(head_mid, 'pcol', MIDDLE)  5.59 us
    ppermute x1, waiting for transfers between devices, shards(): far = lax.ppermute(tail, 'pcol', FAR)  4.82 us
  transfers between devices with their start and end apart: 16, of which 13 were waited for; matrix products, arithmetic and copies ran while one was open for 2% of the time, Pallas kernels for 23%

profile of v11, /device:TPU:14, one launch (start us, length us, event | category | flops | bytes accessed | tf_op | source)
XLA Modules:
  0.0 140.1 jit_solution(17390209557104599309)
XLA Ops:
  0.0 0.0 copy-start.3
  0.0 0.4 collective-permute-start.8
  0.5 2.2 %cut.1 = (f32[2432,128]{1,0:T(8,128)}, f32[896,128]{1,0:T(8,128)}, f32[768,128]{1,0:T(8,128)S(1)}) custom-call(f32[4096,128]{1,0:T(8,128)} %refs_5_.1), custom_call_target="tpu_custom_call" | custom-call | tf_op jit(solution)/shard_map/cut/pallas_call | solution.py:94
  2.7 0.0 copy-start.2
  2.7 0.8 copy-done.2
  3.5 2.6 %collective-permute-start.9 = (f32[2432,128]{1,0:T(8,128)}, f32[2432,128]{1,0:T(8,128)S(1)}, u32[]{:S(2)}, u32[]{:S(2)}) collective-permute-start(f32[2432,128]{1,0:T(8,128)} %get-tuple-element.51), channel_id=1, source_target_pairs={{0,2},{1,3},{2,0},{3,1},{4,6},{5,7},{6,4},{7,5},{8,10},{9,11},{10,... | collective-permute-start | bytes 3735560 | tf_op jit(solution)/shard_map/ppermute | solution.py:358
  6.1 0.3 collective-permute-start.7
  6.4 0.0 copy-done.3
  6.4 0.5 slice.13
  7.6 0.1 pad_add_fusion.refs_0_
  7.7 41.6 %conditional.1 = (f32[512,512]{1,0:T(8,128)}, f32[512,512]{1,0:T(8,128)}) conditional(s32[]{:T(128)} %bitcast.2, f32[4096,512]{1,0:T(8,128)} %refs_2_.1, (s32[2]{0:T(128)S(1)}, s32[512]{0:T(512)S(1)}, f32[4096,512]{1,0:T(8,128)}) %tuple.28), branch_computations={%region_0.0_spmd, %region_1.0_spmd} | conditional | flops 1048576 | bytes 30408960 | solution.py:375
  7.7 6.7 %pick.1 = (f32[512,512]{1,0:T(8,128)S(1)}, f32[512,512]{1,0:T(8,128)S(1)}) custom-call(s32[2]{0:T(128)S(1)} %get-tuple-element.12.info, s32[512]{0:T(512)S(1)} %get-tuple-element.13.pivots, f32[4096,512]{1,0:T(8,128)} %get-tuple-element.14.slab), custom_call_target="tpu_custom_call" | custom-call | tf_op jit(solution)/shard_map/cond/branch_1_fun/pick/pallas_call | solution.py:156
  14.4 0.1 collective-permute-start
  14.5 2.6 %collective-permute-done = f32[512,512]{1,0:T(8,128)S(1)} collective-permute-done((f32[512,512]{1,0:T(8,128)S(1)}, f32[512,512]{1,0:T(8,128)S(1)}, u32[]{:S(2)}, u32[]{:S(2)}) %collective-permute-start) | collective-permute-done | bytes 1048608 | tf_op jit(solution)/shard_map/cond/branch_1_fun/ppermute | solution.py:336
  17.2 0.2 add.10
  17.4 0.1 fusion
  17.4 0.6 collective-permute-start.1
  18.0 0.2 collective-permute-start.3
  18.2 13.2 %collective-permute-done.1 = f32[256,512]{1,0:T(8,128)S(1)} collective-permute-done((f32[256,512]{1,0:T(8,128)S(1)}, f32[256,512]{1,0:T(8,128)S(1)}, u32[]{:S(2)}, u32[]{:S(2)}) %collective-permute-start.1) | collective-permute-done | bytes 524320 | tf_op jit(solution)/shard_map/cond/branch_1_fun/ppermute | solution.py:336
  31.5 0.3 collective-permute-done.3
  31.7 0.2 slice_add_fusion.1
  31.9 0.4 collective-permute-start.2
  32.3 1.7 %collective-permute-start.4 = (f32[256,512]{1,0:T(8,128)S(1)}, f32[256,512]{1,0:T(8,128)S(1)}, u32[]{:S(2)}, u32[]{:S(2)}) collective-permute-start(f32[256,512]{1,0:T(8,128)S(1)} %get-tuple-element.66), channel_id=1, source_target_pairs={{0,8},{4,12},{8,0},{12,4},{16,24},{20,28},{24,16},{28,20},{1,9},{5... | collective-permute-start | bytes 1572872 | tf_op jit(solution)/shard_map/cond/branch_1_fun/ppermute | solution.py:336
  34.0 10.9 %collective-permute-done.2 = f32[256,512]{1,0:T(8,128)S(1)} collective-permute-done((f32[256,512]{1,0:T(8,128)S(1)}, f32[256,512]{1,0:T(8,128)S(1)}, u32[]{:S(2)}, u32[]{:S(2)}) %collective-permute-start.2) | collective-permute-done | bytes 524320 | tf_op jit(solution)/shard_map/cond/branch_1_fun/ppermute | solution.py:336
  44.9 0.1 add.12
  45.0 0.1 collective-permute-done.4
  45.1 0.1 add.14
  45.2 1.1 pad_maximum_fusion
  46.3 0.0 collective-permute-start.5
  46.3 3.0 %collective-permute-done.5 = f32[512,512]{1,0:T(8,128)} collective-permute-done((f32[512,512]{1,0:T(8,128)}, f32[512,512]{1,0:T(8,128)}, u32[]{:S(2)}, u32[]{:S(2)}) %collective-permute-start.5) | collective-permute-done | bytes 1048608 | tf_op jit(solution)/shard_map/cond/branch_1_fun/ppermute | solution.py:336
  49.3 1.3 collective-permute-start.6
  50.6 0.0 copy-start.1
  50.6 1.2 copy-done.1
  51.8 3.3 %upper.1 = (f32[512,512]{1,0:T(8,128)S(1)}, bf16[1152,512]{1,0:T(8,128)(2,1)S(1)}, bf16[384,512]{1,0:T(8,128)(2,1)S(1)}, bf16[384,512]{1,0:T(8,128)(2,1)S(1)}) custom-call(s32[2]{0:T(128)S(1)} %pad_add_fusion.refs_0_, f32[512,512]{1,0:T(8,128)} %get-tuple-element.41.refs_1_.refs_3_, f32[512,512]{1,0:T(8,128)} %get-tuple-element.42.refs_2_.refs_4_, ...), custom_call_target="tpu_custom_call" | custom-call | tf_op jit(solution)/shard_map/upper/pallas_call | solution.py:202
  55.1 0.0 copy-start
  55.1 1.7 %load_pieces.1 = (f32[2304,128]{1,0:T(8,128)S(1)}, f32[1024,128]{1,0:T(8,128)S(1)}, f32[768,128]{1,0:T(8,128)S(1)}) custom-call(f32[4096,128]{1,0:T(8,128)} %refs_5_.1), custom_call_target="tpu_custom_call" | custom-call | tf_op jit(solution)/shard_map/load_pieces/pallas_call | solution.py:59
  56.8 4.6 %collective-permute-start.10 = (f32[768,128]{1,0:T(8,128)S(1)}, f32[768,128]{1,0:T(8,128)S(1)}, u32[]{:S(2)}, u32[]{:S(2)}) collective-permute-start(f32[768,128]{1,0:T(8,128)S(1)} %get-tuple-element.55), channel_id=1, source_target_pairs={{1,2},{2,1},{5,6},{6,5},{9,10},{10,9},{13,14},{14,13},{17,18},{18,... | collective-permute-start | bytes 1179656 | tf_op jit(solution)/shard_map/ppermute | solution.py:382
  61.4 15.1 %collective-permute-done.9.refs_7_ = f32[2432,128]{1,0:T(8,128)S(1)} collective-permute-done((f32[2432,128]{1,0:T(8,128)}, f32[2432,128]{1,0:T(8,128)S(1)}, u32[]{:S(2)}, u32[]{:S(2)}) %collective-permute-start.9) | collective-permute-done | bytes 1245216 | tf_op jit(solution)/shard_map/ppermute | solution.py:358
  76.5 1.4 collective-permute-start.11
  77.9 8.6 %collective-permute-done.7.refs_8_ = f32[896,128]{1,0:T(8,128)} collective-permute-done((f32[896,128]{1,0:T(8,128)}, f32[896,128]{1,0:T(8,128)}, u32[]{:S(2)}, u32[]{:S(2)}) %collective-permute-start.7) | collective-permute-done | bytes 458784 | tf_op jit(solution)/shard_map/ppermute | solution.py:358
  86.5 0.0 collective-permute-done.8.refs_6_
  86.5 2.3 %collective-permute-start.15 = (f32[2304,128]{1,0:T(8,128)S(1)}, f32[2304,128]{1,0:T(8,128)S(1)}, u32[]{:S(2)}, u32[]{:S(2)}) collective-permute-start(f32[2304,128]{1,0:T(8,128)S(1)} %get-tuple-element.64), channel_id=1, source_target_pairs={{1,2},{2,1},{5,6},{6,5},{9,10},{10,9},{13,14},{14,13},{17,18},{18,... | collective-permute-start | bytes 3538952 | tf_op jit(solution)/shard_map/ppermute | solution.py:386
  88.8 4.8 %collective-permute-done.6.refs_3_ = f32[768,128]{1,0:T(8,128)S(1)} collective-permute-done((f32[768,128]{1,0:T(8,128)}, f32[768,128]{1,0:T(8,128)S(1)}, u32[]{:S(2)}, u32[]{:S(2)}) %collective-permute-start.6) | collective-permute-done | bytes 393248 | tf_op jit(solution)/shard_map/ppermute | solution.py:359
  93.6 8.4 %collective-permute-done.10.refs_4_ = f32[768,128]{1,0:T(8,128)S(1)} collective-permute-done((f32[768,128]{1,0:T(8,128)S(1)}, f32[768,128]{1,0:T(8,128)S(1)}, u32[]{:S(2)}, u32[]{:S(2)}) %collective-permute-start.10) | collective-permute-done | bytes 393248 | tf_op jit(solution)/shard_map/ppermute | solution.py:382
  102.0 0.1 pad_maximum_fusion.1
  102.1 1.3 collective-permute-start.14
  103.4 2.4 %collective-permute-start.13 = (f32[1024,128]{1,0:T(8,128)S(1)}, f32[1024,128]{1,0:T(8,128)S(1)}, u32[]{:S(2)}, u32[]{:S(2)}) collective-permute-start(f32[1024,128]{1,0:T(8,128)S(1)} %get-tuple-element.61), channel_id=1, source_target_pairs={{1,2},{2,1},{5,6},{6,5},{9,10},{10,9},{13,14},{14,13},{17,18},{18,... | collective-permute-start | bytes 1572872 | tf_op jit(solution)/shard_map/ppermute | solution.py:387
  105.8 1.3 collective-permute-start.12
  107.1 0.0 copy-done
  107.1 14.5 %main_update.1.refs_0_ = f32[4096,512]{1,0:T(8,128)S(1)} custom-call(s32[2]{0:T(128)S(1)} %pad_add_fusion.refs_0_, s32[512]{0:T(512)S(1)} %copy-done.3, f32[4096,512]{1,0:T(8,128)} %refs_2_.1, f32[512,512]{1,0:T(8,128)} %get-tuple-element.41.refs_1_.refs_3_, f32[512,512]{1,0:T(8,128)} %get-tuple-element.42.refs_2_.refs_4_, f32[4096,128]{1,0:T(8,128)S(1)} %copy-done, ...), custom_call_target="tpu_custom_call" | custom-call | tf_op jit(solution)/shard_map/main_update/pallas_call | solution.py:281
  121.7 0.0 collective-permute-done.11.refs_2_
  121.7 5.6 %collective-permute-done.15.refs_3_ = f32[2304,128]{1,0:T(8,128)S(1)} collective-permute-done((f32[2304,128]{1,0:T(8,128)S(1)}, f32[2304,128]{1,0:T(8,128)S(1)}, u32[]{:S(2)}, u32[]{:S(2)}) %collective-permute-start.15) | collective-permute-done | bytes 1179680 | tf_op jit(solution)/shard_map/ppermute | solution.py:386
  127.3 2.5 %last_update.3.refs_6_ = f32[4096,512]{1,0:T(8,128)} custom-call(f32[4096,512]{1,0:T(8,128)S(1)} %main_update.1.refs_0_, bf16[384,512]{1,0:T(8,128)(2,1)S(1)} %get-tuple-element.60.refs_1_.refs_2_, f32[2432,128]{1,0:T(8,128)S(1)} %collective-permute-done.11.refs_2_, f32[2304,128]{1,0:T(8,128)S(1)} %collective-permute-done.15.refs_3_), custom_call_target="tpu_custom_call" | custom-call | tf_op jit(solution)/shard_map/last_update/pallas_call | solution.py:322
  129.8 0.0 collective-permute-done.14.refs_5_
  129.8 1.8 %last_update.4.refs_5_ = f32[4096,512]{1,0:T(8,128)} custom-call(f32[4096,512]{1,0:T(8,128)S(1)} %main_update.1.refs_0_, bf16[384,512]{1,0:T(8,128)(2,1)S(1)} %get-tuple-element.62.refs_1_, bf16[384,512]{1,0:T(8,128)(2,1)S(1)} %get-tuple-element.60.refs_1_.refs_2_, f32[768,128]{1,0:T(8,128)S(1)} %collective-permute-done.6.refs_3_, ...), custom_call_target="tpu_custom_call", output_to_operand_aliasing={{}: (6, {})} | custom-call | tf_op jit(solution)/shard_map/last_update/pallas_call | solution.py:322
  131.6 4.0 %collective-permute-done.12.refs_3_ = f32[896,128]{1,0:T(8,128)S(1)} collective-permute-done((f32[896,128]{1,0:T(8,128)}, f32[896,128]{1,0:T(8,128)S(1)}, u32[]{:S(2)}, u32[]{:S(2)}) %collective-permute-start.12) | collective-permute-done | bytes 458784 | tf_op jit(solution)/shard_map/ppermute | solution.py:388
  135.5 2.9 %collective-permute-done.13.refs_4_ = f32[1024,128]{1,0:T(8,128)S(1)} collective-permute-done((f32[1024,128]{1,0:T(8,128)S(1)}, f32[1024,128]{1,0:T(8,128)S(1)}, u32[]{:S(2)}, u32[]{:S(2)}) %collective-permute-start.13) | collective-permute-done | bytes 524320 | tf_op jit(solution)/shard_map/ppermute | solution.py:387
  138.5 1.6 %last_update.5 = f32[4096,512]{1,0:T(8,128)} custom-call(f32[4096,512]{1,0:T(8,128)S(1)} %main_update.1.refs_0_, bf16[384,512]{1,0:T(8,128)(2,1)S(1)} %get-tuple-element.60.refs_1_.refs_2_, f32[2432,128]{1,0:T(8,128)S(1)} %collective-permute-done.11.refs_2_, f32[896,128]{1,0:T(8,128)S(1)} %collective-permute-done.12.refs_3_, ...), custom_call_target="tpu_custom_call", output_to_operand_aliasing={{}: (5, {})} | custom-call | tf_op jit(solution)/shard_map/last_update/pallas_call | solution.py:322
Async XLA Ops:
  0.0 6.4 %copy-start.3 = (s32[512]{0:T(512)S(1)}, s32[512]{0:T(512)}, u32[]{:S(2)}) copy-start(s32[512]{0:T(512)} %refs_1_.1) | copy-start | bytes 6148
  0.0 86.5 %collective-permute-start.8 = (f32[4096,128]{1,0:T(8,128)}, f32[4096,128]{1,0:T(8,128)S(1)}, u32[]{:S(2)}, u32[]{:S(2)}) collective-permute-start(f32[4096,128]{1,0:T(8,128)} %refs_5_.1), channel_id=1, source_target_pairs={{0,1},{1,0},{2,3},{3,2},{4,5},{5,4},{6,7},{7,6},{8,9},{9,8},{10,11... | collective-permute-start | bytes 6291464 | tf_op jit(solution)/shard_map/ppermute | solution.py:356
  2.7 0.8 copy-start.2
  3.5 73.0 %collective-permute-start.9 = (f32[2432,128]{1,0:T(8,128)}, f32[2432,128]{1,0:T(8,128)S(1)}, u32[]{:S(2)}, u32[]{:S(2)}) collective-permute-start(f32[2432,128]{1,0:T(8,128)} %get-tuple-element.51), channel_id=1, source_target_pairs={{0,2},{1,3},{2,0},{3,1},{4,6},{5,7},{6,4},{7,5},{8,10},{9,11},{10,... | collective-permute-start | bytes 3735560 | tf_op jit(solution)/shard_map/ppermute | solution.py:358
  6.1 80.4 %collective-permute-start.7 = (f32[896,128]{1,0:T(8,128)}, f32[896,128]{1,0:T(8,128)}, u32[]{:S(2)}, u32[]{:S(2)}) collective-permute-start(f32[896,128]{1,0:T(8,128)} %get-tuple-element.47), channel_id=1, source_target_pairs={{0,2},{1,3},{2,0},{3,1},{4,6},{5,7},{6,4},{7,5},{8,10},{9,11},{10,... | collective-permute-start | bytes 1376264 | tf_op jit(solution)/shard_map/ppermute | solution.py:358
  14.4 2.7 %collective-permute-start = (f32[512,512]{1,0:T(8,128)S(1)}, f32[512,512]{1,0:T(8,128)S(1)}, u32[]{:S(2)}, u32[]{:S(2)}) collective-permute-start(f32[512,512]{1,0:T(8,128)S(1)} %get-tuple-element.16), channel_id=1, source_target_pairs={{0,4},{4,0},{8,12},{12,8},{16,20},{20,16},{24,28},{28,24},{1,5},{5... | collective-permute-start | bytes 3145736 | tf_op jit(solution)/shard_map/cond/branch_1_fun/ppermute | solution.py:336
  17.4 14.0 %collective-permute-start.1 = (f32[256,512]{1,0:T(8,128)S(1)}, f32[256,512]{1,0:T(8,128)S(1)}, u32[]{:S(2)}, u32[]{:S(2)}) collective-permute-start(f32[256,512]{1,0:T(8,128)S(1)} %get-tuple-element.67), channel_id=1, source_target_pairs={{0,8},{4,12},{8,0},{12,4},{16,24},{20,28},{24,16},{28,20},{1,9},{5... | collective-permute-start | bytes 1572872 | tf_op jit(solution)/shard_map/cond/branch_1_fun/ppermute | solution.py:336
  18.0 13.7 %collective-permute-start.3 = (f32[256,512]{1,0:T(8,128)S(1)}, f32[256,512]{1,0:T(8,128)S(1)}, u32[]{:S(2)}, u32[]{:S(2)}) collective-permute-start(f32[256,512]{1,0:T(8,128)S(1)} %get-tuple-element.68), channel_id=1, source_target_pairs={{0,16},{4,20},{8,24},{12,28},{16,0},{20,4},{24,8},{28,12},{1,17},{... | collective-permute-start | bytes 1572872 | tf_op jit(solution)/shard_map/cond/branch_1_fun/ppermute | solution.py:336
  31.9 13.0 %collective-permute-start.2 = (f32[256,512]{1,0:T(8,128)S(1)}, f32[256,512]{1,0:T(8,128)S(1)}, u32[]{:S(2)}, u32[]{:S(2)}) collective-permute-start(f32[256,512]{1,0:T(8,128)S(1)} %get-tuple-element.65), channel_id=1, source_target_pairs={{0,16},{4,20},{8,24},{12,28},{16,0},{20,4},{24,8},{28,12},{1,17},{... | collective-permute-start | bytes 1572872 | tf_op jit(solution)/shard_map/cond/branch_1_fun/ppermute | solution.py:336
  32.3 12.8 %collective-permute-start.4 = (f32[256,512]{1,0:T(8,128)S(1)}, f32[256,512]{1,0:T(8,128)S(1)}, u32[]{:S(2)}, u32[]{:S(2)}) collective-permute-start(f32[256,512]{1,0:T(8,128)S(1)} %get-tuple-element.66), channel_id=1, source_target_pairs={{0,8},{4,12},{8,0},{12,4},{16,24},{20,28},{24,16},{28,20},{1,9},{5... | collective-permute-start | bytes 1572872 | tf_op jit(solution)/shard_map/cond/branch_1_fun/ppermute | solution.py:336
  46.3 3.0 %collective-permute-start.5 = (f32[512,512]{1,0:T(8,128)}, f32[512,512]{1,0:T(8,128)}, u32[]{:S(2)}, u32[]{:S(2)}) collective-permute-start(f32[512,512]{1,0:T(8,128)} %pad_maximum_fusion), channel_id=1, source_target_pairs={{0,4},{4,0},{8,12},{12,8},{16,20},{20,16},{24,28},{28,24},{1,5},{5... | collective-permute-start | bytes 3145736 | tf_op jit(solution)/shard_map/cond/branch_1_fun/ppermute | solution.py:336
  49.3 44.4 %collective-permute-start.6 = (f32[768,128]{1,0:T(8,128)}, f32[768,128]{1,0:T(8,128)S(1)}, u32[]{:S(2)}, u32[]{:S(2)}) collective-permute-start(f32[768,128]{1,0:T(8,128)} %copy-done.2), channel_id=1, source_target_pairs={{0,2},{3,1},{4,6},{7,5},{8,10},{11,9},{12,14},{15,13},{16,18},{19,... | collective-permute-start | bytes 1179656 | tf_op jit(solution)/shard_map/ppermute | solution.py:359
  50.6 1.2 copy-start.1
  55.1 52.1 %copy-start = (f32[4096,128]{1,0:T(8,128)S(1)}, f32[4096,128]{1,0:T(8,128)}, u32[]{:S(2)}) copy-start(f32[4096,128]{1,0:T(8,128)} %refs_5_.1) | copy-start | bytes 6291460
  56.8 45.2 %collective-permute-start.10 = (f32[768,128]{1,0:T(8,128)S(1)}, f32[768,128]{1,0:T(8,128)S(1)}, u32[]{:S(2)}, u32[]{:S(2)}) collective-permute-start(f32[768,128]{1,0:T(8,128)S(1)} %get-tuple-element.55), channel_id=1, source_target_pairs={{1,2},{2,1},{5,6},{6,5},{9,10},{10,9},{13,14},{14,13},{17,18},{18,... | collective-permute-start | bytes 1179656 | tf_op jit(solution)/shard_map/ppermute | solution.py:382
  76.5 45.2 %collective-permute-start.11 = (f32[2432,128]{1,0:T(8,128)S(1)}, f32[2432,128]{1,0:T(8,128)S(1)}, u32[]{:S(2)}, u32[]{:S(2)}) collective-permute-start(f32[2432,128]{1,0:T(8,128)S(1)} %collective-permute-done.9.refs_7_), channel_id=1, source_target_pairs={{2,3},{1,0},{6,7},{5,4},{10,11},{9,8},{14,15},{13,12},{18,19},{17,... | collective-permute-start | bytes 3735560 | tf_op jit(solution)/shard_map/ppermute | solution.py:383
  86.5 40.8 %collective-permute-start.15 = (f32[2304,128]{1,0:T(8,128)S(1)}, f32[2304,128]{1,0:T(8,128)S(1)}, u32[]{:S(2)}, u32[]{:S(2)}) collective-permute-start(f32[2304,128]{1,0:T(8,128)S(1)} %get-tuple-element.64), channel_id=1, source_target_pairs={{1,2},{2,1},{5,6},{6,5},{9,10},{10,9},{13,14},{14,13},{17,18},{18,... | collective-permute-start | bytes 3538952 | tf_op jit(solution)/shard_map/ppermute | solution.py:386
  102.1 27.7 %collective-permute-start.14 = (f32[1536,128]{1,0:T(8,128)S(1)}, f32[1536,128]{1,0:T(8,128)S(1)}, u32[]{:S(2)}, u32[]{:S(2)}) collective-permute-start(f32[1536,128]{1,0:T(8,128)S(1)} %pad_maximum_fusion.1), channel_id=1, source_target_pairs={{2,3},{1,0},{6,7},{5,4},{10,11},{9,8},{14,15},{13,12},{18,19},{17,... | collective-permute-start | bytes 2359304 | tf_op jit(solution)/shard_map/ppermute | solution.py:390
  103.4 35.1 %collective-permute-start.13 = (f32[1024,128]{1,0:T(8,128)S(1)}, f32[1024,128]{1,0:T(8,128)S(1)}, u32[]{:S(2)}, u32[]{:S(2)}) collective-permute-start(f32[1024,128]{1,0:T(8,128)S(1)} %get-tuple-element.61), channel_id=1, source_target_pairs={{1,2},{2,1},{5,6},{6,5},{9,10},{10,9},{13,14},{14,13},{17,18},{18,... | collective-permute-start | bytes 1572872 | tf_op jit(solution)/shard_map/ppermute | solution.py:387
  105.8 29.7 %collective-permute-start.12 = (f32[896,128]{1,0:T(8,128)}, f32[896,128]{1,0:T(8,128)S(1)}, u32[]{:S(2)}, u32[]{:S(2)}) collective-permute-start(f32[896,128]{1,0:T(8,128)} %collective-permute-done.7.refs_8_), channel_id=1, source_target_pairs={{2,3},{1,0},{6,7},{5,4},{10,11},{9,8},{14,15},{13,12},{18,19},{17,... | collective-permute-start | bytes 1376264 | tf_op jit(solution)/shard_map/ppermute | solution.py:388

commit v12 on v11

--- a/solution.py
+++ b/solution.py
@@ -10,8 +10,8 @@
 MIDDLE = [(1, 2), (2, 1)]
 ENDS = [(2, 3), (1, 0)]
 FAR = [(0, 2), (3, 1)]
-PIECES = (76, 28, 24)
-MIDDLE_PIECES = (72, 32, 24)
+PIECES = (86, 16, 26)
+MIDDLE_PIECES = (80, 22, 26)
 TILE = 512
 LAST_TILE = 256
 SMALL = pl.CostEstimate(flops=0, bytes_accessed=0, transcendentals=0)
@@ -336,6 +336,12 @@
     return lax.ppermute(value, "prow", [(i, i ^ (1 << bit)) for i in range(count)])
 
 
+def on_rows(value, rows, pairs):
+    return lax.ppermute(
+        value, ("prow", "pcol"), [(4 * row + a, 4 * row + b) for row in rows for a, b in pairs]
+    )
+
+
 def solution(mesh):
     row_parts, column_parts = mesh.shape["prow"], mesh.shape["pcol"]
     bits = row_parts.bit_length() - 1
@@ -353,10 +359,12 @@
         first, second, last = (rows_here * part // sum(PIECES) for part in PIECES)
         first_mid, second_mid, _ = (rows_here * part // sum(PIECES) for part in MIDDLE_PIECES)
         early = first + second
+        if second > block or second % min(LAST_TILE, block):
+            raise ValueError("unsupported sizes")
+        below = [row for row in range(row_parts) if row]
         near = lax.ppermute(panel, "pcol", SWAP)
-        *pieces, tail = cut(panel, [(0, first), (first, second), (early, last)])
-        across = [lax.ppermute(piece, "pcol", ACROSS) for piece in pieces]
-        far = lax.ppermute(tail, "pcol", FAR)
+        pieces = cut(panel, [(second, first), (0, second)])
+        across = [lax.ppermute(pieces[0], "pcol", ACROSS), on_rows(pieces[1], below, ACROSS)]
 
         def gather_rows(slab, pivots):
             send, keep = pick(info, pivots, slab, block)
@@ -376,31 +384,33 @@
         upper, terms, across_terms, last_terms = make_upper(info, total, other, diag_inverse, width)
         later, upper = lax.optimization_barrier((panel, upper))
         head, upper = lax.optimization_barrier((across[0], upper))
-        head_mid, rest_mid, tail_mid = load_pieces(
-            later, [(0, first_mid), (first_mid, second_mid), (early, last)]
+        head_mid, rest_mid, tail = load_pieces(
+            later, [(second_mid, first_mid), (0, second_mid), (early, last)]
         )
-        tail_mid = lax.ppermute(tail_mid, "pcol", MIDDLE)
+        tail_mid = lax.ppermute(tail, "pcol", MIDDLE)
+        far = lax.ppermute(tail, "pcol", FAR)
         head_end = lax.ppermute(head, "pcol", ENDS)
         rest, head_mid, near = lax.optimization_barrier((across[1], head_mid, near))
         rest_mid, far, near = lax.optimization_barrier((rest_mid, far, near))
         head_mid = lax.ppermute(head_mid, "pcol", MIDDLE)
         rest_mid = lax.ppermute(rest_mid, "pcol", MIDDLE)
-        rest_end = lax.ppermute(rest, "pcol", ENDS)
+        rest_end = on_rows(rest, below, ENDS)
         both, rest = lax.optimization_barrier((jnp.concatenate([far, tail_mid], axis=0), rest))
         both = lax.ppermute(both, "pcol", ENDS)
 
-        base = main_update(info, pivots, slab, total, other, panel, near, [head, rest], upper, terms)
-        segments = [(first_mid, [(0, [(1, 0), (2, 0)])])]
-        result = last_update(base, [last_terms, head_end, head_mid], segments, block, 0, [])
+        base = main_update(info, pivots, slab, total, other, panel, near, [rest, head], upper, terms)
+        segments = [(first_mid, [(0, [(1, second_mid - second), (2, 0)])])]
+        arrays = [last_terms, head_end, head_mid]
+        result = last_update(base, arrays, segments, block, second_mid, [])
         segments = [(last, [(0, [(2, 0), (4, last)]), (1, [(3, 0), (4, 0)])])]
         arrays = [across_terms, last_terms, far, tail_mid, both]
         result = last_update(base, arrays, segments, block, early, [result])
         segments = [
-            (first - first_mid, [(0, [(1, first_mid), (3, 0)])]),
-            (second, [(0, [(2, 0), (3, first - first_mid)])]),
+            (second_mid - second, [(0, [(1, 0), (3, second)])]),
+            (second, [(0, [(2, 0), (3, 0)])]),
         ]
         arrays = [last_terms, head_end, rest_end, rest_mid]
-        return last_update(base, arrays, segments, block, first_mid, [result])
+        return last_update(base, arrays, segments[::-1], block, 0, [result])
 
     in_specs = (P("prow", "pcol"), P("prow", "pcol"), P(), P())
     return jax.shard_map(

time: 141 us -> 141 us (level)
  starting transfers between devices: 21 us -> 22.8 us
    ppermute x4, waiting for transfers between devices: 36 us -> 31.1 us  [the longest x1 17.4 us: shards(): lax.ppermute(pieces[0], 'pcol', ACROSS)]
    ppermute x1, waiting for transfers between devices: 5.59 us -> 8.42 us  [shards(): head_mid = lax.ppermute(head_mid, 'pcol', MIDDLE)]
    ppermute x4, starting transfers between devices: 8.85 us -> 10.8 us  [the longest x1 4.61 us: shards(): tail_mid = lax.ppermute(tail, 'pcol', MIDDLE)]
  transfers between devices with their start and end apart: 16 -> 16, of which waited for: 13 -> 13; matrix products, arithmetic and copies ran while one was open for 2% -> 2% of each run, Pallas kernels for 23% -> 24%
where the time goes in v12:
time: 141 us; the launch traced here: 140 us
  waiting for transfers between devices  78.4 us (56%)
  Pallas kernels  34.3 us (24%)
  starting transfers between devices  22.8 us (16%)
  local copies, waits for them, and re-layouts  1.82 us (1%)
  other arithmetic  1.8 us (1%)
    ppermute x6, waiting for transfers between devices, exchange(): lax.ppermute(value, 'prow', [(i, i ^ 1 << bit) for i in range(count)])  30.4 us
    ppermute x1, waiting for transfers between devices, shards(): lax.ppermute(pieces[0], 'pcol', ACROSS)  17.4 us
    pallas_call x1, Pallas kernels, main_update(): pl.pallas_call(lambda *refs: main_kernel(min(TILE, block), *refs), out_sh...  14.5 us
    ppermute x1, waiting for transfers between devices, shards(): tail_mid = lax.ppermute(tail, 'pcol', MIDDLE)  9.07 us
    ppermute x1, waiting for transfers between devices, shards(): head_mid = lax.ppermute(head_mid, 'pcol', MIDDLE)  8.42 us
    pallas_call x1, Pallas kernels, pick(): pl.pallas_call(pick_kernel, out_shape=(shape, shape), grid_spec=pltpu.Pre...  6.75 us
    pallas_call x3, Pallas kernels, last_update(): pl.pallas_call(lambda *refs: last_kernel(first_row, block, min(LAST_TILE,...  5.85 us
    ppermute x1, waiting for transfers between devices, shards(): far = lax.ppermute(tail, 'pcol', FAR)  5.52 us
  transfers between devices with their start and end apart: 16, of which 13 were waited for; matrix products, arithmetic and copies ran while one was open for 2% of the time, Pallas kernels for 24%

profile of v12, /device:TPU:14, one launch (start us, length us, event | category | flops | bytes accessed | tf_op | source)
XLA Modules:
  0.0 139.9 jit_solution(14662624182720191942)
XLA Ops:
  0.0 0.0 copy-start.2
  0.0 0.4 collective-permute-start.8
  0.5 2.2 %cut.1 = (f32[2752,128]{1,0:T(8,128)}, f32[512,128]{1,0:T(8,128)}) custom-call(f32[4096,128]{1,0:T(8,128)} %refs_5_.1), custom_call_target="tpu_custom_call" | custom-call | tf_op jit(solution)/shard_map/cut/pallas_call | solution.py:94
  2.7 2.7 %collective-permute-start.10 = (f32[2752,128]{1,0:T(8,128)}, f32[2752,128]{1,0:T(8,128)S(1)}, u32[]{:S(2)}, u32[]{:S(2)}) collective-permute-start(f32[2752,128]{1,0:T(8,128)} %get-tuple-element.53), channel_id=1, source_target_pairs={{0,2},{1,3},{2,0},{3,1},{4,6},{5,7},{6,4},{7,5},{8,10},{9,11},{10,... | collective-permute-start | bytes 4227080 | tf_op jit(solution)/shard_map/ppermute | solution.py:367
  5.3 2.2 %collective-permute-start.7 = (f32[512,128]{1,0:T(8,128)}, f32[512,128]{1,0:T(8,128)}, u32[]{:S(2)}, u32[]{:S(2)}) collective-permute-start(f32[512,128]{1,0:T(8,128)} %get-tuple-element.46), channel_id=1, source_target_pairs={{4,6},{5,7},{6,4},{7,5},{8,10},{9,11},{10,8},{11,9},{12,14},{13,15... | collective-permute-start | bytes 786440 | tf_op jit(solution)/shard_map/ppermute | solution.py:340
  7.6 0.1 pad_add_fusion.refs_0_
  7.7 0.0 copy-done.2
  7.7 0.5 slice.13
  8.8 41.7 %conditional.1 = (f32[512,512]{1,0:T(8,128)}, f32[512,512]{1,0:T(8,128)}) conditional(s32[]{:T(128)} %bitcast.2, f32[4096,512]{1,0:T(8,128)} %refs_2_.1, (s32[2]{0:T(128)S(1)}, s32[512]{0:T(512)S(1)}, f32[4096,512]{1,0:T(8,128)}) %tuple.28), branch_computations={%region_0.0_spmd, %region_1.0_spmd} | conditional | flops 1048576 | bytes 30408960 | solution.py:383
  8.8 6.8 %pick.1 = (f32[512,512]{1,0:T(8,128)S(1)}, f32[512,512]{1,0:T(8,128)S(1)}) custom-call(s32[2]{0:T(128)S(1)} %get-tuple-element.12.info, s32[512]{0:T(512)S(1)} %get-tuple-element.13.pivots, f32[4096,512]{1,0:T(8,128)} %get-tuple-element.14.slab), custom_call_target="tpu_custom_call" | custom-call | tf_op jit(solution)/shard_map/cond/branch_1_fun/pick/pallas_call | solution.py:156
  15.5 0.1 collective-permute-start
  15.6 2.6 %collective-permute-done = f32[512,512]{1,0:T(8,128)S(1)} collective-permute-done((f32[512,512]{1,0:T(8,128)S(1)}, f32[512,512]{1,0:T(8,128)S(1)}, u32[]{:S(2)}, u32[]{:S(2)}) %collective-permute-start) | collective-permute-done | bytes 1048608 | tf_op jit(solution)/shard_map/cond/branch_1_fun/ppermute | solution.py:336
  18.3 0.2 add.10
  18.5 0.1 fusion
  18.5 0.6 collective-permute-start.1
  19.1 0.1 collective-permute-start.3
  19.2 13.4 %collective-permute-done.1 = f32[256,512]{1,0:T(8,128)S(1)} collective-permute-done((f32[256,512]{1,0:T(8,128)S(1)}, f32[256,512]{1,0:T(8,128)S(1)}, u32[]{:S(2)}, u32[]{:S(2)}) %collective-permute-start.1) | collective-permute-done | bytes 524320 | tf_op jit(solution)/shard_map/cond/branch_1_fun/ppermute | solution.py:336
  32.6 0.3 collective-permute-done.3
  32.8 0.2 slice_add_fusion.1
  33.0 0.4 collective-permute-start.2
  33.4 1.7 %collective-permute-start.4 = (f32[256,512]{1,0:T(8,128)S(1)}, f32[256,512]{1,0:T(8,128)S(1)}, u32[]{:S(2)}, u32[]{:S(2)}) collective-permute-start(f32[256,512]{1,0:T(8,128)S(1)} %get-tuple-element.64), channel_id=1, source_target_pairs={{0,8},{4,12},{8,0},{12,4},{16,24},{20,28},{24,16},{28,20},{1,9},{5... | collective-permute-start | bytes 1572872 | tf_op jit(solution)/shard_map/cond/branch_1_fun/ppermute | solution.py:336
  35.1 10.9 %collective-permute-done.2 = f32[256,512]{1,0:T(8,128)S(1)} collective-permute-done((f32[256,512]{1,0:T(8,128)S(1)}, f32[256,512]{1,0:T(8,128)S(1)}, u32[]{:S(2)}, u32[]{:S(2)}) %collective-permute-start.2) | collective-permute-done | bytes 524320 | tf_op jit(solution)/shard_map/cond/branch_1_fun/ppermute | solution.py:336
  46.0 0.1 add.12
  46.1 0.2 collective-permute-done.4
  46.3 0.1 add.14
  46.4 1.1 pad_maximum_fusion
  47.5 0.0 collective-permute-start.5
  47.5 3.0 %collective-permute-done.5 = f32[512,512]{1,0:T(8,128)} collective-permute-done((f32[512,512]{1,0:T(8,128)}, f32[512,512]{1,0:T(8,128)}, u32[]{:S(2)}, u32[]{:S(2)}) %collective-permute-start.5) | collective-permute-done | bytes 1048608 | tf_op jit(solution)/shard_map/cond/branch_1_fun/ppermute | solution.py:336
  50.5 0.0 copy-start.1
  50.5 1.2 copy-done.1
  51.7 3.3 %upper.1 = (f32[512,512]{1,0:T(8,128)S(1)}, bf16[1152,512]{1,0:T(8,128)(2,1)S(1)}, bf16[384,512]{1,0:T(8,128)(2,1)S(1)}, bf16[384,512]{1,0:T(8,128)(2,1)S(1)}) custom-call(s32[2]{0:T(128)S(1)} %pad_add_fusion.refs_0_, f32[512,512]{1,0:T(8,128)} %get-tuple-element.40.refs_1_.refs_3_, f32[512,512]{1,0:T(8,128)} %get-tuple-element.41.refs_2_.refs_4_, ...), custom_call_target="tpu_custom_call" | custom-call | tf_op jit(solution)/shard_map/upper/pallas_call | solution.py:202
  55.0 0.0 copy-start
  55.0 1.7 %load_pieces.1 = (f32[2560,128]{1,0:T(8,128)S(1)}, f32[704,128]{1,0:T(8,128)S(1)}, f32[832,128]{1,0:T(8,128)S(1)}) custom-call(f32[4096,128]{1,0:T(8,128)} %refs_5_.1), custom_call_target="tpu_custom_call" | custom-call | tf_op jit(solution)/shard_map/load_pieces/pallas_call | solution.py:59
  56.7 1.3 collective-permute-start.6
  58.0 4.6 %collective-permute-start.9 = (f32[832,128]{1,0:T(8,128)S(1)}, f32[832,128]{1,0:T(8,128)S(1)}, u32[]{:S(2)}, u32[]{:S(2)}) collective-permute-start(f32[832,128]{1,0:T(8,128)S(1)} %get-tuple-element.45), channel_id=1, source_target_pairs={{1,2},{2,1},{5,6},{6,5},{9,10},{10,9},{13,14},{14,13},{17,18},{18,... | collective-permute-start | bytes 1277960 | tf_op jit(solution)/shard_map/ppermute | solution.py:390
  62.6 17.4 %collective-permute-done.10.refs_8_ = f32[2752,128]{1,0:T(8,128)S(1)} collective-permute-done((f32[2752,128]{1,0:T(8,128)}, f32[2752,128]{1,0:T(8,128)S(1)}, u32[]{:S(2)}, u32[]{:S(2)}) %collective-permute-start.10) | collective-permute-done | bytes 1409056 | tf_op jit(solution)/shard_map/ppermute | solution.py:367
  80.0 1.4 collective-permute-start.11
  81.4 4.3 %collective-permute-done.7.refs_7_ = f32[512,128]{1,0:T(8,128)} collective-permute-done((f32[512,128]{1,0:T(8,128)}, f32[512,128]{1,0:T(8,128)}, u32[]{:S(2)}, u32[]{:S(2)}) %collective-permute-start.7) | collective-permute-done | bytes 262176 | tf_op jit(solution)/shard_map/ppermute | solution.py:340
  85.8 0.0 collective-permute-done.8.refs_6_
  85.8 2.3 %collective-permute-start.15 = (f32[2560,128]{1,0:T(8,128)S(1)}, f32[2560,128]{1,0:T(8,128)S(1)}, u32[]{:S(2)}, u32[]{:S(2)}) collective-permute-start(f32[2560,128]{1,0:T(8,128)S(1)} %get-tuple-element.62), channel_id=1, source_target_pairs={{1,2},{2,1},{5,6},{6,5},{9,10},{10,9},{13,14},{14,13},{17,18},{18,... | collective-permute-start | bytes 3932168 | tf_op jit(solution)/shard_map/ppermute | solution.py:395
  88.1 5.5 %collective-permute-done.6.refs_3_ = f32[832,128]{1,0:T(8,128)S(1)} collective-permute-done((f32[832,128]{1,0:T(8,128)S(1)}, f32[832,128]{1,0:T(8,128)S(1)}, u32[]{:S(2)}, u32[]{:S(2)}) %collective-permute-start.6) | collective-permute-done | bytes 426016 | tf_op jit(solution)/shard_map/ppermute | solution.py:391
  93.6 9.1 %collective-permute-done.9.refs_4_ = f32[832,128]{1,0:T(8,128)S(1)} collective-permute-done((f32[832,128]{1,0:T(8,128)S(1)}, f32[832,128]{1,0:T(8,128)S(1)}, u32[]{:S(2)}, u32[]{:S(2)}) %collective-permute-start.9) | collective-permute-done | bytes 426016 | tf_op jit(solution)/shard_map/ppermute | solution.py:390
  102.7 0.1 pad_maximum_fusion.1
  102.8 1.3 collective-permute-start.14
  104.1 2.4 %collective-permute-start.13 = (f32[704,128]{1,0:T(8,128)S(1)}, f32[704,128]{1,0:T(8,128)S(1)}, u32[]{:S(2)}, u32[]{:S(2)}) collective-permute-start(f32[704,128]{1,0:T(8,128)S(1)} %get-tuple-element.59), channel_id=1, source_target_pairs={{1,2},{2,1},{5,6},{6,5},{9,10},{10,9},{13,14},{14,13},{17,18},{18,... | collective-permute-start | bytes 1081352 | tf_op jit(solution)/shard_map/ppermute | solution.py:396
  106.5 1.3 collective-permute-start.12
  107.8 0.0 copy-done
  107.8 14.5 %main_update.1.refs_0_ = f32[4096,512]{1,0:T(8,128)S(1)} custom-call(s32[2]{0:T(128)S(1)} %pad_add_fusion.refs_0_, s32[512]{0:T(512)S(1)} %copy-done.2, f32[4096,512]{1,0:T(8,128)} %refs_2_.1, f32[512,512]{1,0:T(8,128)} %get-tuple-element.40.refs_1_.refs_3_, f32[512,512]{1,0:T(8,128)} %get-tuple-element.41.refs_2_.refs_4_, f32[4096,128]{1,0:T(8,128)S(1)} %copy-done, ...), custom_call_target="tpu_custom_call" | custom-call | tf_op jit(solution)/shard_map/main_update/pallas_call | solution.py:281
  122.4 0.0 collective-permute-done.11.refs_2_
  122.4 8.4 %collective-permute-done.15.refs_3_ = f32[2560,128]{1,0:T(8,128)S(1)} collective-permute-done((f32[2560,128]{1,0:T(8,128)S(1)}, f32[2560,128]{1,0:T(8,128)S(1)}, u32[]{:S(2)}, u32[]{:S(2)}) %collective-permute-start.15) | collective-permute-done | bytes 1310752 | tf_op jit(solution)/shard_map/ppermute | solution.py:395
  130.8 2.6 %last_update.3.refs_6_ = f32[4096,512]{1,0:T(8,128)} custom-call(f32[4096,512]{1,0:T(8,128)S(1)} %main_update.1.refs_0_, bf16[384,512]{1,0:T(8,128)(2,1)S(1)} %get-tuple-element.58.refs_1_.refs_2_, f32[2752,128]{1,0:T(8,128)S(1)} %collective-permute-done.11.refs_2_, f32[2560,128]{1,0:T(8,128)S(1)} %collective-permute-done.15.refs_3_), custom_call_target="tpu_custom_call" | custom-call | tf_op jit(solution)/shard_map/last_update/pallas_call | solution.py:322
  133.4 0.0 collective-permute-done.14.refs_5_
  133.5 1.8 %last_update.4.refs_5_ = f32[4096,512]{1,0:T(8,128)} custom-call(f32[4096,512]{1,0:T(8,128)S(1)} %main_update.1.refs_0_, bf16[384,512]{1,0:T(8,128)(2,1)S(1)} %get-tuple-element.60.refs_1_, bf16[384,512]{1,0:T(8,128)(2,1)S(1)} %get-tuple-element.58.refs_1_.refs_2_, f32[832,128]{1,0:T(8,128)S(1)} %collective-permute-done.6.refs_3_, ...), custom_call_target="tpu_custom_call", output_to_operand_aliasing={{}: (6, {})} | custom-call | tf_op jit(solution)/shard_map/last_update/pallas_call | solution.py:322
  135.3 0.2 collective-permute-done.12.refs_3_
  135.5 2.9 %collective-permute-done.13.refs_4_ = f32[704,128]{1,0:T(8,128)S(1)} collective-permute-done((f32[704,128]{1,0:T(8,128)S(1)}, f32[704,128]{1,0:T(8,128)S(1)}, u32[]{:S(2)}, u32[]{:S(2)}) %collective-permute-start.13) | collective-permute-done | bytes 360480 | tf_op jit(solution)/shard_map/ppermute | solution.py:396
  138.5 1.4 last_update.5
Async XLA Ops:
  0.0 7.7 %copy-start.2 = (s32[512]{0:T(512)S(1)}, s32[512]{0:T(512)}, u32[]{:S(2)}) copy-start(s32[512]{0:T(512)} %refs_1_.1) | copy-start | bytes 6148
  0.0 85.8 %collective-permute-start.8 = (f32[4096,128]{1,0:T(8,128)}, f32[4096,128]{1,0:T(8,128)S(1)}, u32[]{:S(2)}, u32[]{:S(2)}) collective-permute-start(f32[4096,128]{1,0:T(8,128)} %refs_5_.1), channel_id=1, source_target_pairs={{0,1},{1,0},{2,3},{3,2},{4,5},{5,4},{6,7},{7,6},{8,9},{9,8},{10,11... | collective-permute-start | bytes 6291464 | tf_op jit(solution)/shard_map/ppermute | solution.py:365
  2.7 77.4 %collective-permute-start.10 = (f32[2752,128]{1,0:T(8,128)}, f32[2752,128]{1,0:T(8,128)S(1)}, u32[]{:S(2)}, u32[]{:S(2)}) collective-permute-start(f32[2752,128]{1,0:T(8,128)} %get-tuple-element.53), channel_id=1, source_target_pairs={{0,2},{1,3},{2,0},{3,1},{4,6},{5,7},{6,4},{7,5},{8,10},{9,11},{10,... | collective-permute-start | bytes 4227080 | tf_op jit(solution)/shard_map/ppermute | solution.py:367
  5.3 80.4 %collective-permute-start.7 = (f32[512,128]{1,0:T(8,128)}, f32[512,128]{1,0:T(8,128)}, u32[]{:S(2)}, u32[]{:S(2)}) collective-permute-start(f32[512,128]{1,0:T(8,128)} %get-tuple-element.46), channel_id=1, source_target_pairs={{4,6},{5,7},{6,4},{7,5},{8,10},{9,11},{10,8},{11,9},{12,14},{13,15... | collective-permute-start | bytes 786440 | tf_op jit(solution)/shard_map/ppermute | solution.py:340
  15.5 2.7 %collective-permute-start = (f32[512,512]{1,0:T(8,128)S(1)}, f32[512,512]{1,0:T(8,128)S(1)}, u32[]{:S(2)}, u32[]{:S(2)}) collective-permute-start(f32[512,512]{1,0:T(8,128)S(1)} %get-tuple-element.16), channel_id=1, source_target_pairs={{0,4},{4,0},{8,12},{12,8},{16,20},{20,16},{24,28},{28,24},{1,5},{5... | collective-permute-start | bytes 3145736 | tf_op jit(solution)/shard_map/cond/branch_1_fun/ppermute | solution.py:336
  18.5 14.0 %collective-permute-start.1 = (f32[256,512]{1,0:T(8,128)S(1)}, f32[256,512]{1,0:T(8,128)S(1)}, u32[]{:S(2)}, u32[]{:S(2)}) collective-permute-start(f32[256,512]{1,0:T(8,128)S(1)} %get-tuple-element.65), channel_id=1, source_target_pairs={{0,8},{4,12},{8,0},{12,4},{16,24},{20,28},{24,16},{28,20},{1,9},{5... | collective-permute-start | bytes 1572872 | tf_op jit(solution)/shard_map/cond/branch_1_fun/ppermute | solution.py:336
  19.1 13.7 %collective-permute-start.3 = (f32[256,512]{1,0:T(8,128)S(1)}, f32[256,512]{1,0:T(8,128)S(1)}, u32[]{:S(2)}, u32[]{:S(2)}) collective-permute-start(f32[256,512]{1,0:T(8,128)S(1)} %get-tuple-element.66), channel_id=1, source_target_pairs={{0,16},{4,20},{8,24},{12,28},{16,0},{20,4},{24,8},{28,12},{1,17},{... | collective-permute-start | bytes 1572872 | tf_op jit(solution)/shard_map/cond/branch_1_fun/ppermute | solution.py:336
  33.0 13.0 %collective-permute-start.2 = (f32[256,512]{1,0:T(8,128)S(1)}, f32[256,512]{1,0:T(8,128)S(1)}, u32[]{:S(2)}, u32[]{:S(2)}) collective-permute-start(f32[256,512]{1,0:T(8,128)S(1)} %get-tuple-element.63), channel_id=1, source_target_pairs={{0,16},{4,20},{8,24},{12,28},{16,0},{20,4},{24,8},{28,12},{1,17},{... | collective-permute-start | bytes 1572872 | tf_op jit(solution)/shard_map/cond/branch_1_fun/ppermute | solution.py:336
  33.4 12.9 %collective-permute-start.4 = (f32[256,512]{1,0:T(8,128)S(1)}, f32[256,512]{1,0:T(8,128)S(1)}, u32[]{:S(2)}, u32[]{:S(2)}) collective-permute-start(f32[256,512]{1,0:T(8,128)S(1)} %get-tuple-element.64), channel_id=1, source_target_pairs={{0,8},{4,12},{8,0},{12,4},{16,24},{20,28},{24,16},{28,20},{1,9},{5... | collective-permute-start | bytes 1572872 | tf_op jit(solution)/shard_map/cond/branch_1_fun/ppermute | solution.py:336
  47.5 3.0 %collective-permute-start.5 = (f32[512,512]{1,0:T(8,128)}, f32[512,512]{1,0:T(8,128)}, u32[]{:S(2)}, u32[]{:S(2)}) collective-permute-start(f32[512,512]{1,0:T(8,128)} %pad_maximum_fusion), channel_id=1, source_target_pairs={{0,4},{4,0},{8,12},{12,8},{16,20},{20,16},{24,28},{28,24},{1,5},{5... | collective-permute-start | bytes 3145736 | tf_op jit(solution)/shard_map/cond/branch_1_fun/ppermute | solution.py:336
  50.5 1.2 copy-start.1
  55.0 52.9 %copy-start = (f32[4096,128]{1,0:T(8,128)S(1)}, f32[4096,128]{1,0:T(8,128)}, u32[]{:S(2)}) copy-start(f32[4096,128]{1,0:T(8,128)} %refs_5_.1) | copy-start | bytes 6291460
  56.7 37.0 %collective-permute-start.6 = (f32[832,128]{1,0:T(8,128)S(1)}, f32[832,128]{1,0:T(8,128)S(1)}, u32[]{:S(2)}, u32[]{:S(2)}) collective-permute-start(f32[832,128]{1,0:T(8,128)S(1)} %get-tuple-element.45), channel_id=1, source_target_pairs={{0,2},{3,1},{4,6},{7,5},{8,10},{11,9},{12,14},{15,13},{16,18},{19,... | collective-permute-start | bytes 1277960 | tf_op jit(solution)/shard_map/ppermute | solution.py:391
  58.0 44.7 %collective-permute-start.9 = (f32[832,128]{1,0:T(8,128)S(1)}, f32[832,128]{1,0:T(8,128)S(1)}, u32[]{:S(2)}, u32[]{:S(2)}) collective-permute-start(f32[832,128]{1,0:T(8,128)S(1)} %get-tuple-element.45), channel_id=1, source_target_pairs={{1,2},{2,1},{5,6},{6,5},{9,10},{10,9},{13,14},{14,13},{17,18},{18,... | collective-permute-start | bytes 1277960 | tf_op jit(solution)/shard_map/ppermute | solution.py:390
  80.0 42.3 %collective-permute-start.11 = (f32[2752,128]{1,0:T(8,128)S(1)}, f32[2752,128]{1,0:T(8,128)S(1)}, u32[]{:S(2)}, u32[]{:S(2)}) collective-permute-start(f32[2752,128]{1,0:T(8,128)S(1)} %collective-permute-done.10.refs_8_), channel_id=1, source_target_pairs={{2,3},{1,0},{6,7},{5,4},{10,11},{9,8},{14,15},{13,12},{18,19},{17,... | collective-permute-start | bytes 4227080 | tf_op jit(solution)/shard_map/ppermute | solution.py:392
  85.8 45.0 %collective-permute-start.15 = (f32[2560,128]{1,0:T(8,128)S(1)}, f32[2560,128]{1,0:T(8,128)S(1)}, u32[]{:S(2)}, u32[]{:S(2)}) collective-permute-start(f32[2560,128]{1,0:T(8,128)S(1)} %get-tuple-element.62), channel_id=1, source_target_pairs={{1,2},{2,1},{5,6},{6,5},{9,10},{10,9},{13,14},{14,13},{17,18},{18,... | collective-permute-start | bytes 3932168 | tf_op jit(solution)/shard_map/ppermute | solution.py:395
  102.8 30.7 %collective-permute-start.14 = (f32[1664,128]{1,0:T(8,128)S(1)}, f32[1664,128]{1,0:T(8,128)S(1)}, u32[]{:S(2)}, u32[]{:S(2)}) collective-permute-start(f32[1664,128]{1,0:T(8,128)S(1)} %pad_maximum_fusion.1), channel_id=1, source_target_pairs={{2,3},{1,0},{6,7},{5,4},{10,11},{9,8},{14,15},{13,12},{18,19},{17,... | collective-permute-start | bytes 2555912 | tf_op jit(solution)/shard_map/ppermute | solution.py:399
  104.1 34.4 %collective-permute-start.13 = (f32[704,128]{1,0:T(8,128)S(1)}, f32[704,128]{1,0:T(8,128)S(1)}, u32[]{:S(2)}, u32[]{:S(2)}) collective-permute-start(f32[704,128]{1,0:T(8,128)S(1)} %get-tuple-element.59), channel_id=1, source_target_pairs={{1,2},{2,1},{5,6},{6,5},{9,10},{10,9},{13,14},{14,13},{17,18},{18,... | collective-permute-start | bytes 1081352 | tf_op jit(solution)/shard_map/ppermute | solution.py:396
  106.5 29.0 %collective-permute-start.12 = (f32[512,128]{1,0:T(8,128)}, f32[512,128]{1,0:T(8,128)S(1)}, u32[]{:S(2)}, u32[]{:S(2)}) collective-permute-start(f32[512,128]{1,0:T(8,128)} %collective-permute-done.7.refs_7_), channel_id=1, source_target_pairs={{6,7},{5,4},{10,11},{9,8},{14,15},{13,12},{18,19},{17,16},{22,23},... | collective-permute-start | bytes 786440 | tf_op jit(solution)/shard_map/ppermute | solution.py:340

commit v13 on v12

--- a/solution.py
+++ b/solution.py
@@ -365,6 +365,7 @@
         near = lax.ppermute(panel, "pcol", SWAP)
         pieces = cut(panel, [(second, first), (0, second)])
         across = [lax.ppermute(pieces[0], "pcol", ACROSS), on_rows(pieces[1], below, ACROSS)]
+        tail_mid = lax.ppermute(panel[early:], "pcol", MIDDLE)
 
         def gather_rows(slab, pivots):
             send, keep = pick(info, pivots, slab, block)
@@ -383,11 +384,10 @@
         total, other = lax.cond(pivots[0] >= 0, gather_rows, no_rows, slab, pivots)
         upper, terms, across_terms, last_terms = make_upper(info, total, other, diag_inverse, width)
         later, upper = lax.optimization_barrier((panel, upper))
-        head, upper = lax.optimization_barrier((across[0], upper))
+        head, tail_mid, upper = lax.optimization_barrier((across[0], tail_mid, upper))
         head_mid, rest_mid, tail = load_pieces(
             later, [(second_mid, first_mid), (0, second_mid), (early, last)]
         )
-        tail_mid = lax.ppermute(tail, "pcol", MIDDLE)
         far = lax.ppermute(tail, "pcol", FAR)
         head_end = lax.ppermute(head, "pcol", ENDS)
         rest, head_mid, near = lax.optimization_barrier((across[1], head_mid, near))

time: 141 us -> 143 us (1.014)
    ppermute x2, waiting for transfers between devices: 4.59 us -> 16.7 us  [on_rows(): lax.ppermute(value, ('prow', 'pcol'), [(4 * row + a, 4 * row + b) for row...]
    ppermute x1, waiting for transfers between devices: 9.07 us -> 0.01 us  [shards(): tail_mid = lax.ppermute(panel[early:], 'pcol', MIDDLE)]
    ppermute x1, waiting for transfers between devices: 5.52 us -> 0.01 us  [shards(): far = lax.ppermute(tail, 'pcol', FAR)]
    ppermute x1, waiting for transfers between devices: 0.01 us -> 3.18 us  [shards(): both = lax.ppermute(both, 'pcol', ENDS)]
    ppermute x1, waiting for transfers between devices: 2.94 us -> 0.01 us  [shards(): rest_mid = lax.ppermute(rest_mid, 'pcol', MIDDLE)]
    ppermute x1, starting transfers between devices: 4.61 us -> 2.36 us  [shards(): tail_mid = lax.ppermute(panel[early:], 'pcol', MIDDLE)]
    ppermute x1, waiting for transfers between devices: 17.4 us -> 19.2 us  [shards(): lax.ppermute(pieces[0], 'pcol', ACROSS)]
  transfers between devices with their start and end apart: 16 -> 16, of which waited for: 13 -> 11; matrix products, arithmetic and copies ran while one was open for 2% -> 2% of each run, Pallas kernels for 24% -> 24%
where the time goes in v13:
time: 143 us; the launch traced here: 141 us
  waiting for transfers between devices  77.4 us (54%)
  Pallas kernels  34.6 us (24%)
  starting transfers between devices  23.2 us (16%)
  local copies, waits for them, and re-layouts  2.9 us (2%)
  other arithmetic  1.79 us (1%)
    ppermute x6, waiting for transfers between devices, exchange(): lax.ppermute(value, 'prow', [(i, i ^ 1 << bit) for i in range(count)])  29.9 us
    ppermute x1, waiting for transfers between devices, shards(): lax.ppermute(pieces[0], 'pcol', ACROSS)  19.2 us
    ppermute x2, waiting for transfers between devices, on_rows(): lax.ppermute(value, ('prow', 'pcol'), [(4 * row + a, 4 * row + b) for row...  16.7 us
    pallas_call x1, Pallas kernels, main_update(): pl.pallas_call(lambda *refs: main_kernel(min(TILE, block), *refs), out_sh...  14.9 us
    ppermute x1, waiting for transfers between devices, shards(): head_mid = lax.ppermute(head_mid, 'pcol', MIDDLE)  8.58 us
    pallas_call x1, Pallas kernels, pick(): pl.pallas_call(pick_kernel, out_shape=(shape, shape), grid_spec=pltpu.Pre...  6.75 us
    pallas_call x3, Pallas kernels, last_update(): pl.pallas_call(lambda *refs: last_kernel(first_row, block, min(LAST_TILE,...  5.86 us
    ppermute x1, starting transfers between devices, shards(): head_mid = lax.ppermute(head_mid, 'pcol', MIDDLE)  3.47 us
  transfers between devices with their start and end apart: 16, of which 11 were waited for; matrix products, arithmetic and copies ran while one was open for 2% of the time, Pallas kernels for 24%

profile of v13, /device:TPU:14, one launch (start us, length us, event | category | flops | bytes accessed | tf_op | source)
XLA Modules:
  0.0 140.8 jit_solution(14822638884395474479)
XLA Ops:
  0.0 0.0 copy-start.2
  0.0 0.4 collective-permute-start.8
  0.5 2.1 %cut.1 = (f32[2752,128]{1,0:T(8,128)}, f32[512,128]{1,0:T(8,128)S(1)}) custom-call(f32[4096,128]{1,0:T(8,128)} %refs_5_.1), custom_call_target="tpu_custom_call" | custom-call | tf_op jit(solution)/shard_map/cut/pallas_call | solution.py:94
  2.6 2.7 %collective-permute-start.9 = (f32[2752,128]{1,0:T(8,128)}, f32[2752,128]{1,0:T(8,128)}, u32[]{:S(2)}, u32[]{:S(2)}) collective-permute-start(f32[2752,128]{1,0:T(8,128)} %get-tuple-element.52), channel_id=1, source_target_pairs={{0,2},{1,3},{2,0},{3,1},{4,6},{5,7},{6,4},{7,5},{8,10},{9,11},{10,... | collective-permute-start | bytes 4227080 | tf_op jit(solution)/shard_map/ppermute | solution.py:367
  5.2 1.0 slice.17
  6.3 2.4 %collective-permute-start.10 = (f32[832,128]{1,0:T(8,128)S(1)}, f32[832,128]{1,0:T(8,128)S(1)}, u32[]{:S(2)}, u32[]{:S(2)}) collective-permute-start(f32[832,128]{1,0:T(8,128)S(1)} %slice.17), channel_id=1, source_target_pairs={{1,2},{2,1},{5,6},{6,5},{9,10},{10,9},{13,14},{14,13},{17,18},{18,... | collective-permute-start | bytes 1277960 | tf_op jit(solution)/shard_map/ppermute | solution.py:368
  8.7 0.0 copy-done.2
  8.7 0.6 slice.16
  9.9 0.1 pad_add_fusion.refs_0_
  9.9 41.6 %conditional.1 = (f32[512,512]{1,0:T(8,128)}, f32[512,512]{1,0:T(8,128)}) conditional(s32[]{:T(128)} %bitcast.2, f32[4096,512]{1,0:T(8,128)} %refs_2_.1, (s32[2]{0:T(128)S(1)}, s32[512]{0:T(512)S(1)}, f32[4096,512]{1,0:T(8,128)}) %tuple.28), branch_computations={%region_0.0_spmd, %region_1.0_spmd} | conditional | flops 1048576 | bytes 30408960 | solution.py:384
  9.9 6.7 %pick.1 = (f32[512,512]{1,0:T(8,128)S(1)}, f32[512,512]{1,0:T(8,128)S(1)}) custom-call(s32[2]{0:T(128)S(1)} %get-tuple-element.12.info, s32[512]{0:T(512)S(1)} %get-tuple-element.13.pivots, f32[4096,512]{1,0:T(8,128)} %get-tuple-element.14.slab), custom_call_target="tpu_custom_call" | custom-call | tf_op jit(solution)/shard_map/cond/branch_1_fun/pick/pallas_call | solution.py:156
  16.7 0.1 collective-permute-start
  16.8 2.6 %collective-permute-done = f32[512,512]{1,0:T(8,128)S(1)} collective-permute-done((f32[512,512]{1,0:T(8,128)S(1)}, f32[512,512]{1,0:T(8,128)S(1)}, u32[]{:S(2)}, u32[]{:S(2)}) %collective-permute-start) | collective-permute-done | bytes 1048608 | tf_op jit(solution)/shard_map/cond/branch_1_fun/ppermute | solution.py:336
  19.4 0.2 add.10
  19.6 0.1 fusion
  19.7 0.6 collective-permute-start.1
  20.3 0.5 collective-permute-start.3
  20.8 12.9 %collective-permute-done.1 = f32[256,512]{1,0:T(8,128)S(1)} collective-permute-done((f32[256,512]{1,0:T(8,128)S(1)}, f32[256,512]{1,0:T(8,128)S(1)}, u32[]{:S(2)}, u32[]{:S(2)}) %collective-permute-start.1) | collective-permute-done | bytes 524320 | tf_op jit(solution)/shard_map/cond/branch_1_fun/ppermute | solution.py:336
  33.7 0.3 collective-permute-done.3
  34.0 0.2 slice_add_fusion.1
  34.2 0.6 collective-permute-start.2
  34.8 1.5 %collective-permute-start.4 = (f32[256,512]{1,0:T(8,128)S(1)}, f32[256,512]{1,0:T(8,128)S(1)}, u32[]{:S(2)}, u32[]{:S(2)}) collective-permute-start(f32[256,512]{1,0:T(8,128)S(1)} %get-tuple-element.66), channel_id=1, source_target_pairs={{0,8},{4,12},{8,0},{12,4},{16,24},{20,28},{24,16},{28,20},{1,9},{5... | collective-permute-start | bytes 1572872 | tf_op jit(solution)/shard_map/cond/branch_1_fun/ppermute | solution.py:336
  36.3 10.9 %collective-permute-done.2 = f32[256,512]{1,0:T(8,128)S(1)} collective-permute-done((f32[256,512]{1,0:T(8,128)S(1)}, f32[256,512]{1,0:T(8,128)S(1)}, u32[]{:S(2)}, u32[]{:S(2)}) %collective-permute-start.2) | collective-permute-done | bytes 524320 | tf_op jit(solution)/shard_map/cond/branch_1_fun/ppermute | solution.py:336
  47.2 0.1 add.12
  47.2 0.1 collective-permute-done.4
  47.4 0.1 add.14
  47.5 1.1 pad_maximum_fusion
  48.5 0.0 collective-permute-start.5
  48.5 3.0 %collective-permute-done.5 = f32[512,512]{1,0:T(8,128)} collective-permute-done((f32[512,512]{1,0:T(8,128)}, f32[512,512]{1,0:T(8,128)}, u32[]{:S(2)}, u32[]{:S(2)}) %collective-permute-start.5) | collective-permute-done | bytes 1048608 | tf_op jit(solution)/shard_map/cond/branch_1_fun/ppermute | solution.py:336
  51.6 1.9 %collective-permute-start.7 = (f32[512,128]{1,0:T(8,128)S(1)}, f32[512,128]{1,0:T(8,128)S(1)}, u32[]{:S(2)}, u32[]{:S(2)}) collective-permute-start(f32[512,128]{1,0:T(8,128)S(1)} %get-tuple-element.47), channel_id=1, source_target_pairs={{4,6},{5,7},{6,4},{7,5},{8,10},{9,11},{10,8},{11,9},{12,14},{13,15... | collective-permute-start | bytes 786440 | tf_op jit(solution)/shard_map/ppermute | solution.py:340
  53.5 0.0 copy-start.1
  53.5 1.2 copy-done.1
  54.7 3.3 %upper.1 = (f32[512,512]{1,0:T(8,128)S(1)}, bf16[1152,512]{1,0:T(8,128)(2,1)S(1)}, bf16[384,512]{1,0:T(8,128)(2,1)S(1)}, bf16[384,512]{1,0:T(8,128)(2,1)S(1)}) custom-call(s32[2]{0:T(128)S(1)} %pad_add_fusion.refs_0_, f32[512,512]{1,0:T(8,128)} %get-tuple-element.41.refs_1_.refs_3_, f32[512,512]{1,0:T(8,128)} %get-tuple-element.42.refs_2_.refs_4_, ...), custom_call_target="tpu_custom_call" | custom-call | tf_op jit(solution)/shard_map/upper/pallas_call | solution.py:202
  58.0 0.0 copy-start
  58.0 1.7 %load_pieces.1 = (f32[2560,128]{1,0:T(8,128)S(1)}, f32[704,128]{1,0:T(8,128)S(1)}, f32[832,128]{1,0:T(8,128)S(1)}) custom-call(f32[4096,128]{1,0:T(8,128)} %refs_5_.1), custom_call_target="tpu_custom_call" | custom-call | tf_op jit(solution)/shard_map/load_pieces/pallas_call | solution.py:59
  59.7 1.3 collective-permute-start.6
  61.0 0.0 collective-permute-done.10.refs_4_
  61.0 19.2 %collective-permute-done.9.refs_8_ = f32[2752,128]{1,0:T(8,128)} collective-permute-done((f32[2752,128]{1,0:T(8,128)}, f32[2752,128]{1,0:T(8,128)}, u32[]{:S(2)}, u32[]{:S(2)}) %collective-permute-start.9) | collective-permute-done | bytes 1409056 | tf_op jit(solution)/shard_map/ppermute | solution.py:367
  80.1 1.4 collective-permute-start.11
  81.5 15.7 %collective-permute-done.7.refs_7_ = f32[512,128]{1,0:T(8,128)S(1)} collective-permute-done((f32[512,128]{1,0:T(8,128)S(1)}, f32[512,128]{1,0:T(8,128)S(1)}, u32[]{:S(2)}, u32[]{:S(2)}) %collective-permute-start.7) | collective-permute-done | bytes 262176 | tf_op jit(solution)/shard_map/ppermute | solution.py:340
  97.2 0.0 collective-permute-done.8.refs_6_
  97.2 3.5 %collective-permute-start.15 = (f32[2560,128]{1,0:T(8,128)S(1)}, f32[2560,128]{1,0:T(8,128)S(1)}, u32[]{:S(2)}, u32[]{:S(2)}) collective-permute-start(f32[2560,128]{1,0:T(8,128)S(1)} %get-tuple-element.64), channel_id=1, source_target_pairs={{1,2},{2,1},{5,6},{6,5},{9,10},{10,9},{13,14},{14,13},{17,18},{18,... | collective-permute-start | bytes 3932168 | tf_op jit(solution)/shard_map/ppermute | solution.py:395
  100.7 0.0 collective-permute-done.6.refs_3_
  100.7 0.1 pad_maximum_fusion.1
  100.8 2.7 %collective-permute-start.14 = (f32[1664,128]{1,0:T(8,128)S(1)}, f32[1664,128]{1,0:T(8,128)S(1)}, u32[]{:S(2)}, u32[]{:S(2)}) collective-permute-start(f32[1664,128]{1,0:T(8,128)S(1)} %pad_maximum_fusion.1), channel_id=1, source_target_pairs={{2,3},{1,0},{6,7},{5,4},{10,11},{9,8},{14,15},{13,12},{18,19},{17,... | collective-permute-start | bytes 2555912 | tf_op jit(solution)/shard_map/ppermute | solution.py:399
  103.5 2.4 %collective-permute-start.13 = (f32[704,128]{1,0:T(8,128)S(1)}, f32[704,128]{1,0:T(8,128)S(1)}, u32[]{:S(2)}, u32[]{:S(2)}) collective-permute-start(f32[704,128]{1,0:T(8,128)S(1)} %get-tuple-element.61), channel_id=1, source_target_pairs={{1,2},{2,1},{5,6},{6,5},{9,10},{10,9},{13,14},{14,13},{17,18},{18,... | collective-permute-start | bytes 1081352 | tf_op jit(solution)/shard_map/ppermute | solution.py:396
  105.9 1.3 collective-permute-start.12
  107.2 0.0 copy-done
  107.2 14.9 %main_update.1.refs_0_ = f32[4096,512]{1,0:T(8,128)S(1)} custom-call(s32[2]{0:T(128)S(1)} %pad_add_fusion.refs_0_, s32[512]{0:T(512)S(1)} %copy-done.2, f32[4096,512]{1,0:T(8,128)} %refs_2_.1, f32[512,512]{1,0:T(8,128)} %get-tuple-element.41.refs_1_.refs_3_, f32[512,512]{1,0:T(8,128)} %get-tuple-element.42.refs_2_.refs_4_, f32[4096,128]{1,0:T(8,128)S(1)} %copy-done, ...), custom_call_target="tpu_custom_call" | custom-call | tf_op jit(solution)/shard_map/main_update/pallas_call | solution.py:281
  122.1 0.0 collective-permute-done.11.refs_2_
  122.1 8.6 %collective-permute-done.15.refs_3_ = f32[2560,128]{1,0:T(8,128)S(1)} collective-permute-done((f32[2560,128]{1,0:T(8,128)S(1)}, f32[2560,128]{1,0:T(8,128)S(1)}, u32[]{:S(2)}, u32[]{:S(2)}) %collective-permute-start.15) | collective-permute-done | bytes 1310752 | tf_op jit(solution)/shard_map/ppermute | solution.py:395
  130.7 2.6 %last_update.3.refs_6_ = f32[4096,512]{1,0:T(8,128)} custom-call(f32[4096,512]{1,0:T(8,128)S(1)} %main_update.1.refs_0_, bf16[384,512]{1,0:T(8,128)(2,1)S(1)} %get-tuple-element.60.refs_1_.refs_2_, f32[2752,128]{1,0:T(8,128)S(1)} %collective-permute-done.11.refs_2_, f32[2560,128]{1,0:T(8,128)S(1)} %collective-permute-done.15.refs_3_), custom_call_target="tpu_custom_call" | custom-call | tf_op jit(solution)/shard_map/last_update/pallas_call | solution.py:322
  133.4 3.2 %collective-permute-done.14.refs_5_ = f32[1664,128]{1,0:T(8,128)S(1)} collective-permute-done((f32[1664,128]{1,0:T(8,128)S(1)}, f32[1664,128]{1,0:T(8,128)S(1)}, u32[]{:S(2)}, u32[]{:S(2)}) %collective-permute-start.14) | collective-permute-done | bytes 852000 | tf_op jit(solution)/shard_map/ppermute | solution.py:399
  136.6 1.8 %last_update.4.refs_5_ = f32[4096,512]{1,0:T(8,128)} custom-call(f32[4096,512]{1,0:T(8,128)S(1)} %main_update.1.refs_0_, bf16[384,512]{1,0:T(8,128)(2,1)S(1)} %get-tuple-element.62.refs_1_, bf16[384,512]{1,0:T(8,128)(2,1)S(1)} %get-tuple-element.60.refs_1_.refs_2_, f32[832,128]{1,0:T(8,128)S(1)} %collective-permute-done.6.refs_3_, ...), custom_call_target="tpu_custom_call", output_to_operand_aliasing={{}: (6, {})} | custom-call | tf_op jit(solution)/shard_map/last_update/pallas_call | solution.py:322
  138.4 1.0 collective-permute-done.12.refs_3_
  139.4 0.0 collective-permute-done.13.refs_4_
  139.4 1.4 last_update.5
Async XLA Ops:
  0.0 8.7 %copy-start.2 = (s32[512]{0:T(512)S(1)}, s32[512]{0:T(512)}, u32[]{:S(2)}) copy-start(s32[512]{0:T(512)} %refs_1_.1) | copy-start | bytes 6148
  0.0 97.2 %collective-permute-start.8 = (f32[4096,128]{1,0:T(8,128)}, f32[4096,128]{1,0:T(8,128)S(1)}, u32[]{:S(2)}, u32[]{:S(2)}) collective-permute-start(f32[4096,128]{1,0:T(8,128)} %refs_5_.1), channel_id=1, source_target_pairs={{0,1},{1,0},{2,3},{3,2},{4,5},{5,4},{6,7},{7,6},{8,9},{9,8},{10,11... | collective-permute-start | bytes 6291464 | tf_op jit(solution)/shard_map/ppermute | solution.py:365
  2.6 77.5 %collective-permute-start.9 = (f32[2752,128]{1,0:T(8,128)}, f32[2752,128]{1,0:T(8,128)}, u32[]{:S(2)}, u32[]{:S(2)}) collective-permute-start(f32[2752,128]{1,0:T(8,128)} %get-tuple-element.52), channel_id=1, source_target_pairs={{0,2},{1,3},{2,0},{3,1},{4,6},{5,7},{6,4},{7,5},{8,10},{9,11},{10,... | collective-permute-start | bytes 4227080 | tf_op jit(solution)/shard_map/ppermute | solution.py:367
  6.3 54.7 %collective-permute-start.10 = (f32[832,128]{1,0:T(8,128)S(1)}, f32[832,128]{1,0:T(8,128)S(1)}, u32[]{:S(2)}, u32[]{:S(2)}) collective-permute-start(f32[832,128]{1,0:T(8,128)S(1)} %slice.17), channel_id=1, source_target_pairs={{1,2},{2,1},{5,6},{6,5},{9,10},{10,9},{13,14},{14,13},{17,18},{18,... | collective-permute-start | bytes 1277960 | tf_op jit(solution)/shard_map/ppermute | solution.py:368
  16.7 2.7 %collective-permute-start = (f32[512,512]{1,0:T(8,128)S(1)}, f32[512,512]{1,0:T(8,128)S(1)}, u32[]{:S(2)}, u32[]{:S(2)}) collective-permute-start(f32[512,512]{1,0:T(8,128)S(1)} %get-tuple-element.16), channel_id=1, source_target_pairs={{0,4},{4,0},{8,12},{12,8},{16,20},{20,16},{24,28},{28,24},{1,5},{5... | collective-permute-start | bytes 3145736 | tf_op jit(solution)/shard_map/cond/branch_1_fun/ppermute | solution.py:336
  19.7 14.0 %collective-permute-start.1 = (f32[256,512]{1,0:T(8,128)S(1)}, f32[256,512]{1,0:T(8,128)S(1)}, u32[]{:S(2)}, u32[]{:S(2)}) collective-permute-start(f32[256,512]{1,0:T(8,128)S(1)} %get-tuple-element.67), channel_id=1, source_target_pairs={{0,8},{4,12},{8,0},{12,4},{16,24},{20,28},{24,16},{28,20},{1,9},{5... | collective-permute-start | bytes 1572872 | tf_op jit(solution)/shard_map/cond/branch_1_fun/ppermute | solution.py:336
  20.3 13.7 %collective-permute-start.3 = (f32[256,512]{1,0:T(8,128)S(1)}, f32[256,512]{1,0:T(8,128)S(1)}, u32[]{:S(2)}, u32[]{:S(2)}) collective-permute-start(f32[256,512]{1,0:T(8,128)S(1)} %get-tuple-element.68), channel_id=1, source_target_pairs={{0,16},{4,20},{8,24},{12,28},{16,0},{20,4},{24,8},{28,12},{1,17},{... | collective-permute-start | bytes 1572872 | tf_op jit(solution)/shard_map/cond/branch_1_fun/ppermute | solution.py:336
  34.2 13.0 %collective-permute-start.2 = (f32[256,512]{1,0:T(8,128)S(1)}, f32[256,512]{1,0:T(8,128)S(1)}, u32[]{:S(2)}, u32[]{:S(2)}) collective-permute-start(f32[256,512]{1,0:T(8,128)S(1)} %get-tuple-element.65), channel_id=1, source_target_pairs={{0,16},{4,20},{8,24},{12,28},{16,0},{20,4},{24,8},{28,12},{1,17},{... | collective-permute-start | bytes 1572872 | tf_op jit(solution)/shard_map/cond/branch_1_fun/ppermute | solution.py:336
  34.8 12.6 %collective-permute-start.4 = (f32[256,512]{1,0:T(8,128)S(1)}, f32[256,512]{1,0:T(8,128)S(1)}, u32[]{:S(2)}, u32[]{:S(2)}) collective-permute-start(f32[256,512]{1,0:T(8,128)S(1)} %get-tuple-element.66), channel_id=1, source_target_pairs={{0,8},{4,12},{8,0},{12,4},{16,24},{20,28},{24,16},{28,20},{1,9},{5... | collective-permute-start | bytes 1572872 | tf_op jit(solution)/shard_map/cond/branch_1_fun/ppermute | solution.py:336
  48.5 3.0 %collective-permute-start.5 = (f32[512,512]{1,0:T(8,128)}, f32[512,512]{1,0:T(8,128)}, u32[]{:S(2)}, u32[]{:S(2)}) collective-permute-start(f32[512,512]{1,0:T(8,128)} %pad_maximum_fusion), channel_id=1, source_target_pairs={{0,4},{4,0},{8,12},{12,8},{16,20},{20,16},{24,28},{28,24},{1,5},{5... | collective-permute-start | bytes 3145736 | tf_op jit(solution)/shard_map/cond/branch_1_fun/ppermute | solution.py:336
  51.6 45.7 %collective-permute-start.7 = (f32[512,128]{1,0:T(8,128)S(1)}, f32[512,128]{1,0:T(8,128)S(1)}, u32[]{:S(2)}, u32[]{:S(2)}) collective-permute-start(f32[512,128]{1,0:T(8,128)S(1)} %get-tuple-element.47), channel_id=1, source_target_pairs={{4,6},{5,7},{6,4},{7,5},{8,10},{9,11},{10,8},{11,9},{12,14},{13,15... | collective-permute-start | bytes 786440 | tf_op jit(solution)/shard_map/ppermute | solution.py:340
  53.5 1.2 copy-start.1
  58.0 49.2 %copy-start = (f32[4096,128]{1,0:T(8,128)S(1)}, f32[4096,128]{1,0:T(8,128)}, u32[]{:S(2)}) copy-start(f32[4096,128]{1,0:T(8,128)} %refs_5_.1) | copy-start | bytes 6291460
  59.7 41.0 %collective-permute-start.6 = (f32[832,128]{1,0:T(8,128)S(1)}, f32[832,128]{1,0:T(8,128)S(1)}, u32[]{:S(2)}, u32[]{:S(2)}) collective-permute-start(f32[832,128]{1,0:T(8,128)S(1)} %get-tuple-element.46), channel_id=1, source_target_pairs={{0,2},{3,1},{4,6},{7,5},{8,10},{11,9},{12,14},{15,13},{16,18},{19,... | collective-permute-start | bytes 1277960 | tf_op jit(solution)/shard_map/ppermute | solution.py:391
  80.1 42.0 %collective-permute-start.11 = (f32[2752,128]{1,0:T(8,128)}, f32[2752,128]{1,0:T(8,128)S(1)}, u32[]{:S(2)}, u32[]{:S(2)}) collective-permute-start(f32[2752,128]{1,0:T(8,128)} %collective-permute-done.9.refs_8_), channel_id=1, source_target_pairs={{2,3},{1,0},{6,7},{5,4},{10,11},{9,8},{14,15},{13,12},{18,19},{17,... | collective-permute-start | bytes 4227080 | tf_op jit(solution)/shard_map/ppermute | solution.py:392
  97.2 33.5 %collective-permute-start.15 = (f32[2560,128]{1,0:T(8,128)S(1)}, f32[2560,128]{1,0:T(8,128)S(1)}, u32[]{:S(2)}, u32[]{:S(2)}) collective-permute-start(f32[2560,128]{1,0:T(8,128)S(1)} %get-tuple-element.64), channel_id=1, source_target_pairs={{1,2},{2,1},{5,6},{6,5},{9,10},{10,9},{13,14},{14,13},{17,18},{18,... | collective-permute-start | bytes 3932168 | tf_op jit(solution)/shard_map/ppermute | solution.py:395
  100.8 35.8 %collective-permute-start.14 = (f32[1664,128]{1,0:T(8,128)S(1)}, f32[1664,128]{1,0:T(8,128)S(1)}, u32[]{:S(2)}, u32[]{:S(2)}) collective-permute-start(f32[1664,128]{1,0:T(8,128)S(1)} %pad_maximum_fusion.1), channel_id=1, source_target_pairs={{2,3},{1,0},{6,7},{5,4},{10,11},{9,8},{14,15},{13,12},{18,19},{17,... | collective-permute-start | bytes 2555912 | tf_op jit(solution)/shard_map/ppermute | solution.py:399
  103.5 35.9 %collective-permute-start.13 = (f32[704,128]{1,0:T(8,128)S(1)}, f32[704,128]{1,0:T(8,128)S(1)}, u32[]{:S(2)}, u32[]{:S(2)}) collective-permute-start(f32[704,128]{1,0:T(8,128)S(1)} %get-tuple-element.61), channel_id=1, source_target_pairs={{1,2},{2,1},{5,6},{6,5},{9,10},{10,9},{13,14},{14,13},{17,18},{18,... | collective-permute-start | bytes 1081352 | tf_op jit(solution)/shard_map/ppermute | solution.py:396
  105.9 33.5 %collective-permute-start.12 = (f32[512,128]{1,0:T(8,128)S(1)}, f32[512,128]{1,0:T(8,128)S(1)}, u32[]{:S(2)}, u32[]{:S(2)}) collective-permute-start(f32[512,128]{1,0:T(8,128)S(1)} %collective-permute-done.7.refs_7_), channel_id=1, source_target_pairs={{6,7},{5,4},{10,11},{9,8},{14,15},{13,12},{18,19},{17,16},{22,23},... | collective-permute-start | bytes 786440 | tf_op jit(solution)/shard_map/ppermute | solution.py:340

commit v14 on v12

--- a/solution.py
+++ b/solution.py
@@ -10,8 +10,8 @@
 MIDDLE = [(1, 2), (2, 1)]
 ENDS = [(2, 3), (1, 0)]
 FAR = [(0, 2), (3, 1)]
-PIECES = (86, 16, 26)
-MIDDLE_PIECES = (80, 22, 26)
+PIECES = (85, 16, 27)
+MIDDLE_PIECES = (83, 18, 27)
 TILE = 512
 LAST_TILE = 256
 SMALL = pl.CostEstimate(flops=0, bytes_accessed=0, transcendentals=0)

time: 141 us -> 140 us (level)
  transfers between devices with their start and end apart: 16 -> 16, of which waited for: 13 -> 12; matrix products, arithmetic and copies ran while one was open for 2% -> 2% of each run, Pallas kernels for 24% -> 24%
where the time goes in v14:
time: 140 us
  waiting for transfers between devices  78.3 us (56%)
  Pallas kernels  34.3 us (24%)
  starting transfers between devices  22.8 us (16%)
  local copies, waits for them, and re-layouts  1.82 us (1%)
  other arithmetic  1.8 us (1%)
    ppermute x6, waiting for transfers between devices, exchange(): lax.ppermute(value, 'prow', [(i, i ^ 1 << bit) for i in range(count)])  30.4 us
    ppermute x1, waiting for transfers between devices, shards(): lax.ppermute(pieces[0], 'pcol', ACROSS)  17.1 us
    pallas_call x1, Pallas kernels, main_update(): pl.pallas_call(lambda *refs: main_kernel(min(TILE, block), *refs), out_sh...  14.5 us
    ppermute x1, waiting for transfers between devices, shards(): head_mid = lax.ppermute(head_mid, 'pcol', MIDDLE)  9.45 us
    ppermute x1, waiting for transfers between devices, shards(): tail_mid = lax.ppermute(tail, 'pcol', MIDDLE)  9.42 us
    pallas_call x1, Pallas kernels, pick(): pl.pallas_call(pick_kernel, out_shape=(shape, shape), grid_spec=pltpu.Pre...  6.75 us
    ppermute x1, waiting for transfers between devices, shards(): far = lax.ppermute(tail, 'pcol', FAR)  5.87 us
    pallas_call x3, Pallas kernels, last_update(): pl.pallas_call(lambda *refs: last_kernel(first_row, block, min(LAST_TILE,...  5.84 us
  transfers between devices with their start and end apart: 16, of which 12 were waited for; matrix products, arithmetic and copies ran while one was open for 2% of the time, Pallas kernels for 24%

profile of v14, /device:TPU:14, one launch (start us, length us, event | category | flops | bytes accessed | tf_op | source)
XLA Modules:
  0.0 139.8 jit_solution(183944091945164707)
XLA Ops:
  0.0 0.0 copy-start.2
  0.0 0.4 collective-permute-start.8
  0.5 2.2 %cut.1 = (f32[2720,128]{1,0:T(8,128)}, f32[512,128]{1,0:T(8,128)}) custom-call(f32[4096,128]{1,0:T(8,128)} %refs_5_.1), custom_call_target="tpu_custom_call" | custom-call | tf_op jit(solution)/shard_map/cut/pallas_call | solution.py:94
  2.7 2.7 %collective-permute-start.10 = (f32[2720,128]{1,0:T(8,128)}, f32[2720,128]{1,0:T(8,128)S(1)}, u32[]{:S(2)}, u32[]{:S(2)}) collective-permute-start(f32[2720,128]{1,0:T(8,128)} %get-tuple-element.53), channel_id=1, source_target_pairs={{0,2},{1,3},{2,0},{3,1},{4,6},{5,7},{6,4},{7,5},{8,10},{9,11},{10,... | collective-permute-start | bytes 4177928 | tf_op jit(solution)/shard_map/ppermute | solution.py:367
  5.3 2.2 %collective-permute-start.7 = (f32[512,128]{1,0:T(8,128)}, f32[512,128]{1,0:T(8,128)}, u32[]{:S(2)}, u32[]{:S(2)}) collective-permute-start(f32[512,128]{1,0:T(8,128)} %get-tuple-element.46), channel_id=1, source_target_pairs={{4,6},{5,7},{6,4},{7,5},{8,10},{9,11},{10,8},{11,9},{12,14},{13,15... | collective-permute-start | bytes 786440 | tf_op jit(solution)/shard_map/ppermute | solution.py:340
  7.6 0.1 pad_add_fusion.refs_0_
  7.7 0.0 copy-done.2
  7.7 0.5 slice.13
  8.7 41.7 %conditional.1 = (f32[512,512]{1,0:T(8,128)}, f32[512,512]{1,0:T(8,128)}) conditional(s32[]{:T(128)} %bitcast.2, f32[4096,512]{1,0:T(8,128)} %refs_2_.1, (s32[2]{0:T(128)S(1)}, s32[512]{0:T(512)S(1)}, f32[4096,512]{1,0:T(8,128)}) %tuple.28), branch_computations={%region_0.0_spmd, %region_1.0_spmd} | conditional | flops 1048576 | bytes 30408960 | solution.py:383
  8.8 6.8 %pick.1 = (f32[512,512]{1,0:T(8,128)S(1)}, f32[512,512]{1,0:T(8,128)S(1)}) custom-call(s32[2]{0:T(128)S(1)} %get-tuple-element.12.info, s32[512]{0:T(512)S(1)} %get-tuple-element.13.pivots, f32[4096,512]{1,0:T(8,128)} %get-tuple-element.14.slab), custom_call_target="tpu_custom_call" | custom-call | tf_op jit(solution)/shard_map/cond/branch_1_fun/pick/pallas_call | solution.py:156
  15.5 0.1 collective-permute-start
  15.6 2.6 %collective-permute-done = f32[512,512]{1,0:T(8,128)S(1)} collective-permute-done((f32[512,512]{1,0:T(8,128)S(1)}, f32[512,512]{1,0:T(8,128)S(1)}, u32[]{:S(2)}, u32[]{:S(2)}) %collective-permute-start) | collective-permute-done | bytes 1048608 | tf_op jit(solution)/shard_map/cond/branch_1_fun/ppermute | solution.py:336
  18.3 0.2 add.10
  18.5 0.1 fusion
  18.5 0.6 collective-permute-start.1
  19.1 0.1 collective-permute-start.3
  19.2 13.4 %collective-permute-done.1 = f32[256,512]{1,0:T(8,128)S(1)} collective-permute-done((f32[256,512]{1,0:T(8,128)S(1)}, f32[256,512]{1,0:T(8,128)S(1)}, u32[]{:S(2)}, u32[]{:S(2)}) %collective-permute-start.1) | collective-permute-done | bytes 524320 | tf_op jit(solution)/shard_map/cond/branch_1_fun/ppermute | solution.py:336
  32.6 0.3 collective-permute-done.3
  32.8 0.2 slice_add_fusion.1
  33.0 0.4 collective-permute-start.2
  33.4 1.7 %collective-permute-start.4 = (f32[256,512]{1,0:T(8,128)S(1)}, f32[256,512]{1,0:T(8,128)S(1)}, u32[]{:S(2)}, u32[]{:S(2)}) collective-permute-start(f32[256,512]{1,0:T(8,128)S(1)} %get-tuple-element.64), channel_id=1, source_target_pairs={{0,8},{4,12},{8,0},{12,4},{16,24},{20,28},{24,16},{28,20},{1,9},{5... | collective-permute-start | bytes 1572872 | tf_op jit(solution)/shard_map/cond/branch_1_fun/ppermute | solution.py:336
  35.1 10.9 %collective-permute-done.2 = f32[256,512]{1,0:T(8,128)S(1)} collective-permute-done((f32[256,512]{1,0:T(8,128)S(1)}, f32[256,512]{1,0:T(8,128)S(1)}, u32[]{:S(2)}, u32[]{:S(2)}) %collective-permute-start.2) | collective-permute-done | bytes 524320 | tf_op jit(solution)/shard_map/cond/branch_1_fun/ppermute | solution.py:336
  46.0 0.1 add.12
  46.1 0.2 collective-permute-done.4
  46.3 0.1 add.14
  46.4 1.1 pad_maximum_fusion
  47.5 0.0 collective-permute-start.5
  47.5 3.0 %collective-permute-done.5 = f32[512,512]{1,0:T(8,128)} collective-permute-done((f32[512,512]{1,0:T(8,128)}, f32[512,512]{1,0:T(8,128)}, u32[]{:S(2)}, u32[]{:S(2)}) %collective-permute-start.5) | collective-permute-done | bytes 1048608 | tf_op jit(solution)/shard_map/cond/branch_1_fun/ppermute | solution.py:336
  50.5 0.0 copy-start.1
  50.5 1.2 copy-done.1
  51.7 3.3 %upper.1 = (f32[512,512]{1,0:T(8,128)S(1)}, bf16[1152,512]{1,0:T(8,128)(2,1)S(1)}, bf16[384,512]{1,0:T(8,128)(2,1)S(1)}, bf16[384,512]{1,0:T(8,128)(2,1)S(1)}) custom-call(s32[2]{0:T(128)S(1)} %pad_add_fusion.refs_0_, f32[512,512]{1,0:T(8,128)} %get-tuple-element.40.refs_1_.refs_3_, f32[512,512]{1,0:T(8,128)} %get-tuple-element.41.refs_2_.refs_4_, ...), custom_call_target="tpu_custom_call" | custom-call | tf_op jit(solution)/shard_map/upper/pallas_call | solution.py:202
  55.0 0.0 copy-start
  55.0 1.7 %load_pieces.1 = (f32[2656,128]{1,0:T(8,128)S(1)}, f32[576,128]{1,0:T(8,128)S(1)}, f32[864,128]{1,0:T(8,128)S(1)}) custom-call(f32[4096,128]{1,0:T(8,128)} %refs_5_.1), custom_call_target="tpu_custom_call" | custom-call | tf_op jit(solution)/shard_map/load_pieces/pallas_call | solution.py:59
  56.7 1.3 collective-permute-start.6
  58.0 4.6 %collective-permute-start.9 = (f32[864,128]{1,0:T(8,128)S(1)}, f32[864,128]{1,0:T(8,128)S(1)}, u32[]{:S(2)}, u32[]{:S(2)}) collective-permute-start(f32[864,128]{1,0:T(8,128)S(1)} %get-tuple-element.45), channel_id=1, source_target_pairs={{1,2},{2,1},{5,6},{6,5},{9,10},{10,9},{13,14},{14,13},{17,18},{18,... | collective-permute-start | bytes 1327112 | tf_op jit(solution)/shard_map/ppermute | solution.py:390
  62.6 17.1 %collective-permute-done.10.refs_8_ = f32[2720,128]{1,0:T(8,128)S(1)} collective-permute-done((f32[2720,128]{1,0:T(8,128)}, f32[2720,128]{1,0:T(8,128)S(1)}, u32[]{:S(2)}, u32[]{:S(2)}) %collective-permute-start.10) | collective-permute-done | bytes 1392672 | tf_op jit(solution)/shard_map/ppermute | solution.py:367
  79.7 1.4 collective-permute-start.11
  81.1 4.3 %collective-permute-done.7.refs_7_ = f32[512,128]{1,0:T(8,128)} collective-permute-done((f32[512,128]{1,0:T(8,128)}, f32[512,128]{1,0:T(8,128)}, u32[]{:S(2)}, u32[]{:S(2)}) %collective-permute-start.7) | collective-permute-done | bytes 262176 | tf_op jit(solution)/shard_map/ppermute | solution.py:340
  85.4 0.0 collective-permute-done.8.refs_6_
  85.4 2.3 %collective-permute-start.15 = (f32[2656,128]{1,0:T(8,128)S(1)}, f32[2656,128]{1,0:T(8,128)S(1)}, u32[]{:S(2)}, u32[]{:S(2)}) collective-permute-start(f32[2656,128]{1,0:T(8,128)S(1)} %get-tuple-element.62), channel_id=1, source_target_pairs={{1,2},{2,1},{5,6},{6,5},{9,10},{10,9},{13,14},{14,13},{17,18},{18,... | collective-permute-start | bytes 4079624 | tf_op jit(solution)/shard_map/ppermute | solution.py:395
  87.8 5.9 %collective-permute-done.6.refs_3_ = f32[864,128]{1,0:T(8,128)S(1)} collective-permute-done((f32[864,128]{1,0:T(8,128)S(1)}, f32[864,128]{1,0:T(8,128)S(1)}, u32[]{:S(2)}, u32[]{:S(2)}) %collective-permute-start.6) | collective-permute-done | bytes 442400 | tf_op jit(solution)/shard_map/ppermute | solution.py:391
  93.6 9.4 %collective-permute-done.9.refs_4_ = f32[864,128]{1,0:T(8,128)S(1)} collective-permute-done((f32[864,128]{1,0:T(8,128)S(1)}, f32[864,128]{1,0:T(8,128)S(1)}, u32[]{:S(2)}, u32[]{:S(2)}) %collective-permute-start.9) | collective-permute-done | bytes 442400 | tf_op jit(solution)/shard_map/ppermute | solution.py:390
  103.1 0.1 pad_maximum_fusion.1
  103.1 1.3 collective-permute-start.14
  104.5 2.4 %collective-permute-start.13 = (f32[576,128]{1,0:T(8,128)S(1)}, f32[576,128]{1,0:T(8,128)S(1)}, u32[]{:S(2)}, u32[]{:S(2)}) collective-permute-start(f32[576,128]{1,0:T(8,128)S(1)} %get-tuple-element.59), channel_id=1, source_target_pairs={{1,2},{2,1},{5,6},{6,5},{9,10},{10,9},{13,14},{14,13},{17,18},{18,... | collective-permute-start | bytes 884744 | tf_op jit(solution)/shard_map/ppermute | solution.py:396
  106.9 1.3 collective-permute-start.12
  108.2 0.0 copy-done
  108.2 14.5 %main_update.1.refs_0_ = f32[4096,512]{1,0:T(8,128)S(1)} custom-call(s32[2]{0:T(128)S(1)} %pad_add_fusion.refs_0_, s32[512]{0:T(512)S(1)} %copy-done.2, f32[4096,512]{1,0:T(8,128)} %refs_2_.1, f32[512,512]{1,0:T(8,128)} %get-tuple-element.40.refs_1_.refs_3_, f32[512,512]{1,0:T(8,128)} %get-tuple-element.41.refs_2_.refs_4_, f32[4096,128]{1,0:T(8,128)S(1)} %copy-done, ...), custom_call_target="tpu_custom_call" | custom-call | tf_op jit(solution)/shard_map/main_update/pallas_call | solution.py:281
  122.7 0.0 collective-permute-done.11.refs_2_
  122.8 9.5 %collective-permute-done.15.refs_3_ = f32[2656,128]{1,0:T(8,128)S(1)} collective-permute-done((f32[2656,128]{1,0:T(8,128)S(1)}, f32[2656,128]{1,0:T(8,128)S(1)}, u32[]{:S(2)}, u32[]{:S(2)}) %collective-permute-start.15) | collective-permute-done | bytes 1359904 | tf_op jit(solution)/shard_map/ppermute | solution.py:395
  132.2 2.7 %last_update.3.refs_6_ = f32[4096,512]{1,0:T(8,128)} custom-call(f32[4096,512]{1,0:T(8,128)S(1)} %main_update.1.refs_0_, bf16[384,512]{1,0:T(8,128)(2,1)S(1)} %get-tuple-element.58.refs_1_.refs_2_, f32[2720,128]{1,0:T(8,128)S(1)} %collective-permute-done.11.refs_2_, f32[2656,128]{1,0:T(8,128)S(1)} %collective-permute-done.15.refs_3_), custom_call_target="tpu_custom_call" | custom-call | tf_op jit(solution)/shard_map/last_update/pallas_call | solution.py:322
  134.9 0.0 collective-permute-done.14.refs_5_
  134.9 1.9 %last_update.4.refs_5_ = f32[4096,512]{1,0:T(8,128)} custom-call(f32[4096,512]{1,0:T(8,128)S(1)} %main_update.1.refs_0_, bf16[384,512]{1,0:T(8,128)(2,1)S(1)} %get-tuple-element.60.refs_1_, bf16[384,512]{1,0:T(8,128)(2,1)S(1)} %get-tuple-element.58.refs_1_.refs_2_, f32[864,128]{1,0:T(8,128)S(1)} %collective-permute-done.6.refs_3_, ...), custom_call_target="tpu_custom_call", output_to_operand_aliasing={{}: (6, {})} | custom-call | tf_op jit(solution)/shard_map/last_update/pallas_call | solution.py:322
  136.8 0.0 collective-permute-done.12.refs_3_
  136.8 1.7 %collective-permute-done.13.refs_4_ = f32[576,128]{1,0:T(8,128)S(1)} collective-permute-done((f32[576,128]{1,0:T(8,128)S(1)}, f32[576,128]{1,0:T(8,128)S(1)}, u32[]{:S(2)}, u32[]{:S(2)}) %collective-permute-start.13) | collective-permute-done | bytes 294944 | tf_op jit(solution)/shard_map/ppermute | solution.py:396
  138.5 1.3 last_update.5
Async XLA Ops:
  0.0 7.7 %copy-start.2 = (s32[512]{0:T(512)S(1)}, s32[512]{0:T(512)}, u32[]{:S(2)}) copy-start(s32[512]{0:T(512)} %refs_1_.1) | copy-start | bytes 6148
  0.0 85.4 %collective-permute-start.8 = (f32[4096,128]{1,0:T(8,128)}, f32[4096,128]{1,0:T(8,128)S(1)}, u32[]{:S(2)}, u32[]{:S(2)}) collective-permute-start(f32[4096,128]{1,0:T(8,128)} %refs_5_.1), channel_id=1, source_target_pairs={{0,1},{1,0},{2,3},{3,2},{4,5},{5,4},{6,7},{7,6},{8,9},{9,8},{10,11... | collective-permute-start | bytes 6291464 | tf_op jit(solution)/shard_map/ppermute | solution.py:365
  2.7 77.0 %collective-permute-start.10 = (f32[2720,128]{1,0:T(8,128)}, f32[2720,128]{1,0:T(8,128)S(1)}, u32[]{:S(2)}, u32[]{:S(2)}) collective-permute-start(f32[2720,128]{1,0:T(8,128)} %get-tuple-element.53), channel_id=1, source_target_pairs={{0,2},{1,3},{2,0},{3,1},{4,6},{5,7},{6,4},{7,5},{8,10},{9,11},{10,... | collective-permute-start | bytes 4177928 | tf_op jit(solution)/shard_map/ppermute | solution.py:367
  5.3 80.1 %collective-permute-start.7 = (f32[512,128]{1,0:T(8,128)}, f32[512,128]{1,0:T(8,128)}, u32[]{:S(2)}, u32[]{:S(2)}) collective-permute-start(f32[512,128]{1,0:T(8,128)} %get-tuple-element.46), channel_id=1, source_target_pairs={{4,6},{5,7},{6,4},{7,5},{8,10},{9,11},{10,8},{11,9},{12,14},{13,15... | collective-permute-start | bytes 786440 | tf_op jit(solution)/shard_map/ppermute | solution.py:340
  15.5 2.7 %collective-permute-start = (f32[512,512]{1,0:T(8,128)S(1)}, f32[512,512]{1,0:T(8,128)S(1)}, u32[]{:S(2)}, u32[]{:S(2)}) collective-permute-start(f32[512,512]{1,0:T(8,128)S(1)} %get-tuple-element.16), channel_id=1, source_target_pairs={{0,4},{4,0},{8,12},{12,8},{16,20},{20,16},{24,28},{28,24},{1,5},{5... | collective-permute-start | bytes 3145736 | tf_op jit(solution)/shard_map/cond/branch_1_fun/ppermute | solution.py:336
  18.5 14.0 %collective-permute-start.1 = (f32[256,512]{1,0:T(8,128)S(1)}, f32[256,512]{1,0:T(8,128)S(1)}, u32[]{:S(2)}, u32[]{:S(2)}) collective-permute-start(f32[256,512]{1,0:T(8,128)S(1)} %get-tuple-element.65), channel_id=1, source_target_pairs={{0,8},{4,12},{8,0},{12,4},{16,24},{20,28},{24,16},{28,20},{1,9},{5... | collective-permute-start | bytes 1572872 | tf_op jit(solution)/shard_map/cond/branch_1_fun/ppermute | solution.py:336
  19.1 13.7 %collective-permute-start.3 = (f32[256,512]{1,0:T(8,128)S(1)}, f32[256,512]{1,0:T(8,128)S(1)}, u32[]{:S(2)}, u32[]{:S(2)}) collective-permute-start(f32[256,512]{1,0:T(8,128)S(1)} %get-tuple-element.66), channel_id=1, source_target_pairs={{0,16},{4,20},{8,24},{12,28},{16,0},{20,4},{24,8},{28,12},{1,17},{... | collective-permute-start | bytes 1572872 | tf_op jit(solution)/shard_map/cond/branch_1_fun/ppermute | solution.py:336
  33.0 13.0 %collective-permute-start.2 = (f32[256,512]{1,0:T(8,128)S(1)}, f32[256,512]{1,0:T(8,128)S(1)}, u32[]{:S(2)}, u32[]{:S(2)}) collective-permute-start(f32[256,512]{1,0:T(8,128)S(1)} %get-tuple-element.63), channel_id=1, source_target_pairs={{0,16},{4,20},{8,24},{12,28},{16,0},{20,4},{24,8},{28,12},{1,17},{... | collective-permute-start | bytes 1572872 | tf_op jit(solution)/shard_map/cond/branch_1_fun/ppermute | solution.py:336
  33.4 12.9 %collective-permute-start.4 = (f32[256,512]{1,0:T(8,128)S(1)}, f32[256,512]{1,0:T(8,128)S(1)}, u32[]{:S(2)}, u32[]{:S(2)}) collective-permute-start(f32[256,512]{1,0:T(8,128)S(1)} %get-tuple-element.64), channel_id=1, source_target_pairs={{0,8},{4,12},{8,0},{12,4},{16,24},{20,28},{24,16},{28,20},{1,9},{5... | collective-permute-start | bytes 1572872 | tf_op jit(solution)/shard_map/cond/branch_1_fun/ppermute | solution.py:336
  47.5 3.0 %collective-permute-start.5 = (f32[512,512]{1,0:T(8,128)}, f32[512,512]{1,0:T(8,128)}, u32[]{:S(2)}, u32[]{:S(2)}) collective-permute-start(f32[512,512]{1,0:T(8,128)} %pad_maximum_fusion), channel_id=1, source_target_pairs={{0,4},{4,0},{8,12},{12,8},{16,20},{20,16},{24,28},{28,24},{1,5},{5... | collective-permute-start | bytes 3145736 | tf_op jit(solution)/shard_map/cond/branch_1_fun/ppermute | solution.py:336
  50.5 1.2 copy-start.1
  55.0 53.2 %copy-start = (f32[4096,128]{1,0:T(8,128)S(1)}, f32[4096,128]{1,0:T(8,128)}, u32[]{:S(2)}) copy-start(f32[4096,128]{1,0:T(8,128)} %refs_5_.1) | copy-start | bytes 6291460
  56.7 37.0 %collective-permute-start.6 = (f32[864,128]{1,0:T(8,128)S(1)}, f32[864,128]{1,0:T(8,128)S(1)}, u32[]{:S(2)}, u32[]{:S(2)}) collective-permute-start(f32[864,128]{1,0:T(8,128)S(1)} %get-tuple-element.45), channel_id=1, source_target_pairs={{0,2},{3,1},{4,6},{7,5},{8,10},{11,9},{12,14},{15,13},{16,18},{19,... | collective-permute-start | bytes 1327112 | tf_op jit(solution)/shard_map/ppermute | solution.py:391
  58.0 45.1 %collective-permute-start.9 = (f32[864,128]{1,0:T(8,128)S(1)}, f32[864,128]{1,0:T(8,128)S(1)}, u32[]{:S(2)}, u32[]{:S(2)}) collective-permute-start(f32[864,128]{1,0:T(8,128)S(1)} %get-tuple-element.45), channel_id=1, source_target_pairs={{1,2},{2,1},{5,6},{6,5},{9,10},{10,9},{13,14},{14,13},{17,18},{18,... | collective-permute-start | bytes 1327112 | tf_op jit(solution)/shard_map/ppermute | solution.py:390
  79.7 43.1 %collective-permute-start.11 = (f32[2720,128]{1,0:T(8,128)S(1)}, f32[2720,128]{1,0:T(8,128)S(1)}, u32[]{:S(2)}, u32[]{:S(2)}) collective-permute-start(f32[2720,128]{1,0:T(8,128)S(1)} %collective-permute-done.10.refs_8_), channel_id=1, source_target_pairs={{2,3},{1,0},{6,7},{5,4},{10,11},{9,8},{14,15},{13,12},{18,19},{17,... | collective-permute-start | bytes 4177928 | tf_op jit(solution)/shard_map/ppermute | solution.py:392
  85.4 46.8 %collective-permute-start.15 = (f32[2656,128]{1,0:T(8,128)S(1)}, f32[2656,128]{1,0:T(8,128)S(1)}, u32[]{:S(2)}, u32[]{:S(2)}) collective-permute-start(f32[2656,128]{1,0:T(8,128)S(1)} %get-tuple-element.62), channel_id=1, source_target_pairs={{1,2},{2,1},{5,6},{6,5},{9,10},{10,9},{13,14},{14,13},{17,18},{18,... | collective-permute-start | bytes 4079624 | tf_op jit(solution)/shard_map/ppermute | solution.py:395
  103.1 31.8 %collective-permute-start.14 = (f32[1728,128]{1,0:T(8,128)S(1)}, f32[1728,128]{1,0:T(8,128)S(1)}, u32[]{:S(2)}, u32[]{:S(2)}) collective-permute-start(f32[1728,128]{1,0:T(8,128)S(1)} %pad_maximum_fusion.1), channel_id=1, source_target_pairs={{2,3},{1,0},{6,7},{5,4},{10,11},{9,8},{14,15},{13,12},{18,19},{17,... | collective-permute-start | bytes 2654216 | tf_op jit(solution)/shard_map/ppermute | solution.py:399
  104.5 34.0 %collective-permute-start.13 = (f32[576,128]{1,0:T(8,128)S(1)}, f32[576,128]{1,0:T(8,128)S(1)}, u32[]{:S(2)}, u32[]{:S(2)}) collective-permute-start(f32[576,128]{1,0:T(8,128)S(1)} %get-tuple-element.59), channel_id=1, source_target_pairs={{1,2},{2,1},{5,6},{6,5},{9,10},{10,9},{13,14},{14,13},{17,18},{18,... | collective-permute-start | bytes 884744 | tf_op jit(solution)/shard_map/ppermute | solution.py:396
  106.9 29.9 %collective-permute-start.12 = (f32[512,128]{1,0:T(8,128)}, f32[512,128]{1,0:T(8,128)S(1)}, u32[]{:S(2)}, u32[]{:S(2)}) collective-permute-start(f32[512,128]{1,0:T(8,128)} %collective-permute-done.7.refs_7_), channel_id=1, source_target_pairs={{6,7},{5,4},{10,11},{9,8},{14,15},{13,12},{18,19},{17,16},{22,23},... | collective-permute-start | bytes 786440 | tf_op jit(solution)/shard_map/ppermute | solution.py:340

commit v15 on v14

--- a/solution.py
+++ b/solution.py
@@ -365,30 +365,26 @@
         near = lax.ppermute(panel, "pcol", SWAP)
         pieces = cut(panel, [(second, first), (0, second)])
         across = [lax.ppermute(pieces[0], "pcol", ACROSS), on_rows(pieces[1], below, ACROSS)]
+        tail = panel[early:]
+        tail_mid = lax.ppermute(tail, "pcol", MIDDLE)
 
         def gather_rows(slab, pivots):
             send, keep = pick(info, pivots, slab, block)
             total = keep + exchange(send, 0, row_parts)
-            halves = [total[: block // 2], total[block // 2 :]]
-            orders = [list(range(1, bits)), list(range(1, bits))[::-1]]
-            for step in range(bits - 1):
-                other = [exchange(half, order[step], row_parts) for half, order in zip(halves, orders)]
-                halves = [half + part for half, part in zip(halves, other)]
-            total = jnp.concatenate(halves, axis=0)
+            for bit in range(1, bits):
+                total = total + exchange(total, bit, row_parts)
             return total, exchange(total, 0, row_parts)
 
         def no_rows(slab, pivots):
             return slab[:block], slab[:block]
 
         total, other = lax.cond(pivots[0] >= 0, gather_rows, no_rows, slab, pivots)
+        tail, total = lax.optimization_barrier((tail, total))
+        far = lax.ppermute(tail, "pcol", FAR)
+        head, tail_mid, total = lax.optimization_barrier((across[0], tail_mid, total))
         upper, terms, across_terms, last_terms = make_upper(info, total, other, diag_inverse, width)
         later, upper = lax.optimization_barrier((panel, upper))
-        head, upper = lax.optimization_barrier((across[0], upper))
-        head_mid, rest_mid, tail = load_pieces(
-            later, [(second_mid, first_mid), (0, second_mid), (early, last)]
-        )
-        tail_mid = lax.ppermute(tail, "pcol", MIDDLE)
-        far = lax.ppermute(tail, "pcol", FAR)
+        head_mid, rest_mid = load_pieces(later, [(second_mid, first_mid), (0, second_mid)])
         head_end = lax.ppermute(head, "pcol", ENDS)
         rest, head_mid, near = lax.optimization_barrier((across[1], head_mid, near))
         rest_mid, far, near = lax.optimization_barrier((rest_mid, far, near))

time: 140 us -> 143 us (1.021); the launches traced: 140 us -> 141 us
    ppermute x6 -> x4, waiting for transfers between devices: 30.4 us -> 54.2 us  [exchange(): lax.ppermute(value, 'prow', [(i, i ^ 1 << bit) for i in range(count)])]
    ppermute x1, waiting for transfers between devices: 17.1 us -> 2.83 us  [shards(): lax.ppermute(pieces[0], 'pcol', ACROSS)]
    ppermute x1, waiting for transfers between devices: 9.42 us -> 0.01 us  [shards(): tail_mid = lax.ppermute(tail, 'pcol', MIDDLE)]
    ppermute x1, waiting for transfers between devices: 5.87 us -> 0.01 us  [shards(): far = lax.ppermute(tail, 'pcol', FAR)]
    ppermute x2, waiting for transfers between devices: 4.35 us -> 9.03 us  [on_rows(): lax.ppermute(value, ('prow', 'pcol'), [(4 * row + a, 4 * row + b) for row...]
    ppermute x1, waiting for transfers between devices: 0.01 us -> 2.53 us  [shards(): both = lax.ppermute(both, 'pcol', ENDS)]
    ppermute x1, starting transfers between devices: 4.61 us -> 2.36 us  [shards(): tail_mid = lax.ppermute(tail, 'pcol', MIDDLE)]
    ppermute x1, waiting for transfers between devices: 1.7 us -> 0.01 us  [shards(): rest_mid = lax.ppermute(rest_mid, 'pcol', MIDDLE)]
  transfers between devices with their start and end apart: 16 -> 14, of which waited for: 12 -> 9; matrix products, arithmetic and copies ran while one was open for 2% -> 2% of each run, Pallas kernels for 24% -> 24%
where the time goes in v15:
time: 143 us; the launch traced here: 141 us
  waiting for transfers between devices  78.3 us (55%)
  Pallas kernels  34.4 us (24%)
  starting transfers between devices  22.7 us (16%)
  local copies, waits for them, and re-layouts  2.81 us (2%)
  other arithmetic  1.73 us (1%)
    ppermute x4, waiting for transfers between devices, exchange(): lax.ppermute(value, 'prow', [(i, i ^ 1 << bit) for i in range(count)])  54.2 us
    pallas_call x1, Pallas kernels, main_update(): pl.pallas_call(lambda *refs: main_kernel(min(TILE, block), *refs), out_sh...  14.9 us
    ppermute x1, waiting for transfers between devices, shards(): head_mid = lax.ppermute(head_mid, 'pcol', MIDDLE)  9.69 us
    ppermute x2, waiting for transfers between devices, on_rows(): lax.ppermute(value, ('prow', 'pcol'), [(4 * row + a, 4 * row + b) for row...  9.03 us
    pallas_call x1, Pallas kernels, pick(): pl.pallas_call(pick_kernel, out_shape=(shape, shape), grid_spec=pltpu.Pre...  6.75 us
    pallas_call x3, Pallas kernels, last_update(): pl.pallas_call(lambda *refs: last_kernel(first_row, block, min(LAST_TILE,...  5.83 us
    ppermute x1, starting transfers between devices, shards(): rest_mid = lax.ppermute(rest_mid, 'pcol', MIDDLE)  3.48 us
    pallas_call x1, Pallas kernels, make_upper(): pl.pallas_call(lambda *refs: upper_kernel(width, *refs), out_shape=(jax.S...  3.26 us
  transfers between devices with their start and end apart: 14, of which 9 were waited for; matrix products, arithmetic and copies ran while one was open for 2% of the time, Pallas kernels for 24%

profile of v15, /device:TPU:14, one launch (start us, length us, event | category | flops | bytes accessed | tf_op | source)
XLA Modules:
  0.0 140.8 jit_solution(8210404071499690309)
XLA Ops:
  0.0 0.0 copy-start.2
  0.0 0.4 collective-permute-start.8
  0.5 2.1 %cut.1 = (f32[2720,128]{1,0:T(8,128)}, f32[512,128]{1,0:T(8,128)S(1)}) custom-call(f32[4096,128]{1,0:T(8,128)} %refs_5_.1), custom_call_target="tpu_custom_call" | custom-call | tf_op jit(solution)/shard_map/cut/pallas_call | solution.py:94
  2.6 2.7 %collective-permute-start.4 = (f32[2720,128]{1,0:T(8,128)}, f32[2720,128]{1,0:T(8,128)}, u32[]{:S(2)}, u32[]{:S(2)}) collective-permute-start(f32[2720,128]{1,0:T(8,128)} %get-tuple-element.42), channel_id=1, source_target_pairs={{0,2},{1,3},{2,0},{3,1},{4,6},{5,7},{6,4},{7,5},{8,10},{9,11},{10,... | collective-permute-start | bytes 4177928 | tf_op jit(solution)/shard_map/ppermute | solution.py:367
  5.2 1.0 slice.10
  6.3 2.4 %collective-permute-start.5 = (f32[864,128]{1,0:T(8,128)S(1)}, f32[864,128]{1,0:T(8,128)S(1)}, u32[]{:S(2)}, u32[]{:S(2)}) collective-permute-start(f32[864,128]{1,0:T(8,128)S(1)} %slice.10), channel_id=1, source_target_pairs={{1,2},{2,1},{5,6},{6,5},{9,10},{10,9},{13,14},{14,13},{17,18},{18,... | collective-permute-start | bytes 1327112 | tf_op jit(solution)/shard_map/ppermute | solution.py:369
  8.7 1.9 %collective-permute-start.7 = (f32[512,128]{1,0:T(8,128)S(1)}, f32[512,128]{1,0:T(8,128)S(1)}, u32[]{:S(2)}, u32[]{:S(2)}) collective-permute-start(f32[512,128]{1,0:T(8,128)S(1)} %get-tuple-element.51), channel_id=1, source_target_pairs={{4,6},{5,7},{6,4},{7,5},{8,10},{9,11},{10,8},{11,9},{12,14},{13,15... | collective-permute-start | bytes 786440 | tf_op jit(solution)/shard_map/ppermute | solution.py:340
  10.6 0.1 pad_add_fusion.refs_0_
  10.7 0.0 copy-done.2
  10.7 0.5 slice.11
  11.8 63.8 %conditional.1 = (f32[512,512]{1,0:T(8,128)}, f32[512,512]{1,0:T(8,128)}) conditional(s32[]{:T(128)} %bitcast.2, f32[4096,512]{1,0:T(8,128)} %refs_2_.1, (s32[2]{0:T(128)S(1)}, s32[512]{0:T(512)S(1)}, f32[4096,512]{1,0:T(8,128)}) %tuple.28), branch_computations={%region_0.0_spmd, %region_1.0_spmd} | conditional | flops 786432 | bytes 26214576 | solution.py:381
  11.9 6.8 %pick.1 = (f32[512,512]{1,0:T(8,128)S(1)}, f32[512,512]{1,0:T(8,128)S(1)}) custom-call(s32[2]{0:T(128)S(1)} %get-tuple-element.12.info, s32[512]{0:T(512)S(1)} %get-tuple-element.13.pivots, f32[4096,512]{1,0:T(8,128)} %get-tuple-element.14.slab), custom_call_target="tpu_custom_call" | custom-call | tf_op jit(solution)/shard_map/cond/branch_1_fun/pick/pallas_call | solution.py:156
  18.6 0.1 collective-permute-start
  18.7 2.6 %collective-permute-done = f32[512,512]{1,0:T(8,128)S(1)} collective-permute-done((f32[512,512]{1,0:T(8,128)S(1)}, f32[512,512]{1,0:T(8,128)S(1)}, u32[]{:S(2)}, u32[]{:S(2)}) %collective-permute-start) | collective-permute-done | bytes 1048608 | tf_op jit(solution)/shard_map/cond/branch_1_fun/ppermute | solution.py:336
  21.4 0.2 add.6
  21.6 0.6 collective-permute-start.1
  22.2 24.7 %collective-permute-done.1 = f32[512,512]{1,0:T(8,128)S(1)} collective-permute-done((f32[512,512]{1,0:T(8,128)S(1)}, f32[512,512]{1,0:T(8,128)S(1)}, u32[]{:S(2)}, u32[]{:S(2)}) %collective-permute-start.1) | collective-permute-done | bytes 1048608 | tf_op jit(solution)/shard_map/cond/branch_1_fun/ppermute | solution.py:336
  46.8 0.2 add.7
  47.0 0.6 collective-permute-start.2
  47.6 23.9 %collective-permute-done.2 = f32[512,512]{1,0:T(8,128)S(1)} collective-permute-done((f32[512,512]{1,0:T(8,128)S(1)}, f32[512,512]{1,0:T(8,128)S(1)}, u32[]{:S(2)}, u32[]{:S(2)}) %collective-permute-start.2) | collective-permute-done | bytes 1048608 | tf_op jit(solution)/shard_map/cond/branch_1_fun/ppermute | solution.py:336
  71.5 1.2 add.8
  72.7 0.0 collective-permute-start.3
  72.7 3.0 %collective-permute-done.3 = f32[512,512]{1,0:T(8,128)} collective-permute-done((f32[512,512]{1,0:T(8,128)}, f32[512,512]{1,0:T(8,128)}, u32[]{:S(2)}, u32[]{:S(2)}) %collective-permute-start.3) | collective-permute-done | bytes 1048608 | tf_op jit(solution)/shard_map/cond/branch_1_fun/ppermute | solution.py:336
  75.7 1.3 collective-permute-start.6
  77.0 0.0 collective-permute-done.5.refs_4_
  77.0 2.8 %collective-permute-done.4.refs_8_ = f32[2720,128]{1,0:T(8,128)} collective-permute-done((f32[2720,128]{1,0:T(8,128)}, f32[2720,128]{1,0:T(8,128)}, u32[]{:S(2)}, u32[]{:S(2)}) %collective-permute-start.4) | collective-permute-done | bytes 1392672 | tf_op jit(solution)/shard_map/ppermute | solution.py:367
  79.8 2.8 %collective-permute-start.9 = (f32[2720,128]{1,0:T(8,128)}, f32[2720,128]{1,0:T(8,128)S(1)}, u32[]{:S(2)}, u32[]{:S(2)}) collective-permute-start(f32[2720,128]{1,0:T(8,128)} %collective-permute-done.4.refs_8_), channel_id=1, source_target_pairs={{2,3},{1,0},{6,7},{5,4},{10,11},{9,8},{14,15},{13,12},{18,19},{17,... | collective-permute-start | bytes 4177928 | tf_op jit(solution)/shard_map/ppermute | solution.py:388
  82.6 0.0 copy-start.1
  82.7 1.2 copy-done.1
  83.9 3.3 %upper.1 = (f32[512,512]{1,0:T(8,128)S(1)}, bf16[1152,512]{1,0:T(8,128)(2,1)S(1)}, bf16[384,512]{1,0:T(8,128)(2,1)S(1)}, bf16[384,512]{1,0:T(8,128)(2,1)S(1)}) custom-call(s32[2]{0:T(128)S(1)} %pad_add_fusion.refs_0_, f32[512,512]{1,0:T(8,128)} %get-tuple-element.45.refs_1_.refs_3_, f32[512,512]{1,0:T(8,128)} %get-tuple-element.46.refs_2_.refs_4_, ...), custom_call_target="tpu_custom_call" | custom-call | tf_op jit(solution)/shard_map/upper/pallas_call | solution.py:202
  87.1 0.0 copy-start
  87.2 1.5 %load_pieces.1 = (f32[2656,128]{1,0:T(8,128)S(1)}, f32[576,128]{1,0:T(8,128)S(1)}) custom-call(f32[4096,128]{1,0:T(8,128)} %refs_5_.1), custom_call_target="tpu_custom_call" | custom-call | tf_op jit(solution)/shard_map/load_pieces/pallas_call | solution.py:59
  88.7 6.4 %collective-permute-done.7.refs_7_ = f32[512,128]{1,0:T(8,128)S(1)} collective-permute-done((f32[512,128]{1,0:T(8,128)S(1)}, f32[512,128]{1,0:T(8,128)S(1)}, u32[]{:S(2)}, u32[]{:S(2)}) %collective-permute-start.7) | collective-permute-done | bytes 262176 | tf_op jit(solution)/shard_map/ppermute | solution.py:340
  95.1 0.0 collective-permute-done.8.refs_6_
  95.1 2.3 %collective-permute-start.13 = (f32[2656,128]{1,0:T(8,128)S(1)}, f32[2656,128]{1,0:T(8,128)S(1)}, u32[]{:S(2)}, u32[]{:S(2)}) collective-permute-start(f32[2656,128]{1,0:T(8,128)S(1)} %get-tuple-element.66), channel_id=1, source_target_pairs={{1,2},{2,1},{5,6},{6,5},{9,10},{10,9},{13,14},{14,13},{17,18},{18,... | collective-permute-start | bytes 4079624 | tf_op jit(solution)/shard_map/ppermute | solution.py:391
  97.5 0.0 collective-permute-done.6.refs_3_
  97.5 0.1 pad_maximum_fusion
  97.5 2.8 %collective-permute-start.12 = (f32[1728,128]{1,0:T(8,128)S(1)}, f32[1728,128]{1,0:T(8,128)S(1)}, u32[]{:S(2)}, u32[]{:S(2)}) collective-permute-start(f32[1728,128]{1,0:T(8,128)S(1)} %pad_maximum_fusion), channel_id=1, source_target_pairs={{2,3},{1,0},{6,7},{5,4},{10,11},{9,8},{14,15},{13,12},{18,19},{17,... | collective-permute-start | bytes 2654216 | tf_op jit(solution)/shard_map/ppermute | solution.py:395
  100.3 3.5 %collective-permute-start.11 = (f32[576,128]{1,0:T(8,128)S(1)}, f32[576,128]{1,0:T(8,128)S(1)}, u32[]{:S(2)}, u32[]{:S(2)}) collective-permute-start(f32[576,128]{1,0:T(8,128)S(1)} %get-tuple-element.63), channel_id=1, source_target_pairs={{1,2},{2,1},{5,6},{6,5},{9,10},{10,9},{13,14},{14,13},{17,18},{18,... | collective-permute-start | bytes 884744 | tf_op jit(solution)/shard_map/ppermute | solution.py:392
  103.8 1.3 collective-permute-start.10
  105.1 0.0 copy-done
  105.1 14.9 %main_update.1.refs_0_ = f32[4096,512]{1,0:T(8,128)S(1)} custom-call(s32[2]{0:T(128)S(1)} %pad_add_fusion.refs_0_, s32[512]{0:T(512)S(1)} %copy-done.2, f32[4096,512]{1,0:T(8,128)} %refs_2_.1, f32[512,512]{1,0:T(8,128)} %get-tuple-element.45.refs_1_.refs_3_, f32[512,512]{1,0:T(8,128)} %get-tuple-element.46.refs_2_.refs_4_, f32[4096,128]{1,0:T(8,128)S(1)} %copy-done, ...), custom_call_target="tpu_custom_call" | custom-call | tf_op jit(solution)/shard_map/main_update/pallas_call | solution.py:281
  120.0 0.0 collective-permute-done.9.refs_2_
  120.1 9.7 %collective-permute-done.13.refs_3_ = f32[2656,128]{1,0:T(8,128)S(1)} collective-permute-done((f32[2656,128]{1,0:T(8,128)S(1)}, f32[2656,128]{1,0:T(8,128)S(1)}, u32[]{:S(2)}, u32[]{:S(2)}) %collective-permute-start.13) | collective-permute-done | bytes 1359904 | tf_op jit(solution)/shard_map/ppermute | solution.py:391
  129.7 2.7 %last_update.3.refs_6_ = f32[4096,512]{1,0:T(8,128)} custom-call(f32[4096,512]{1,0:T(8,128)S(1)} %main_update.1.refs_0_, bf16[384,512]{1,0:T(8,128)(2,1)S(1)} %get-tuple-element.62.refs_1_.refs_2_, f32[2720,128]{1,0:T(8,128)S(1)} %collective-permute-done.9.refs_2_, f32[2656,128]{1,0:T(8,128)S(1)} %collective-permute-done.13.refs_3_), custom_call_target="tpu_custom_call" | custom-call | tf_op jit(solution)/shard_map/last_update/pallas_call | solution.py:322
  132.4 2.5 %collective-permute-done.12.refs_5_ = f32[1728,128]{1,0:T(8,128)S(1)} collective-permute-done((f32[1728,128]{1,0:T(8,128)S(1)}, f32[1728,128]{1,0:T(8,128)S(1)}, u32[]{:S(2)}, u32[]{:S(2)}) %collective-permute-start.12) | collective-permute-done | bytes 884768 | tf_op jit(solution)/shard_map/ppermute | solution.py:395
  135.0 1.8 %last_update.4.refs_5_ = f32[4096,512]{1,0:T(8,128)} custom-call(f32[4096,512]{1,0:T(8,128)S(1)} %main_update.1.refs_0_, bf16[384,512]{1,0:T(8,128)(2,1)S(1)} %get-tuple-element.64.refs_1_, bf16[384,512]{1,0:T(8,128)(2,1)S(1)} %get-tuple-element.62.refs_1_.refs_2_, f32[864,128]{1,0:T(8,128)S(1)} %collective-permute-done.6.refs_3_, ...), custom_call_target="tpu_custom_call", output_to_operand_aliasing={{}: (6, {})} | custom-call | tf_op jit(solution)/shard_map/last_update/pallas_call | solution.py:322
  136.8 2.6 %collective-permute-done.10.refs_3_ = f32[512,128]{1,0:T(8,128)S(1)} collective-permute-done((f32[512,128]{1,0:T(8,128)S(1)}, f32[512,128]{1,0:T(8,128)S(1)}, u32[]{:S(2)}, u32[]{:S(2)}) %collective-permute-start.10) | collective-permute-done | bytes 262176 | tf_op jit(solution)/shard_map/ppermute | solution.py:340
  139.5 0.0 collective-permute-done.11.refs_4_
  139.5 1.3 last_update.5
Async XLA Ops:
  0.0 10.7 %copy-start.2 = (s32[512]{0:T(512)S(1)}, s32[512]{0:T(512)}, u32[]{:S(2)}) copy-start(s32[512]{0:T(512)} %refs_1_.1) | copy-start | bytes 6148
  0.0 95.1 %collective-permute-start.8 = (f32[4096,128]{1,0:T(8,128)}, f32[4096,128]{1,0:T(8,128)S(1)}, u32[]{:S(2)}, u32[]{:S(2)}) collective-permute-start(f32[4096,128]{1,0:T(8,128)} %refs_5_.1), channel_id=1, source_target_pairs={{0,1},{1,0},{2,3},{3,2},{4,5},{5,4},{6,7},{7,6},{8,9},{9,8},{10,11... | collective-permute-start | bytes 6291464 | tf_op jit(solution)/shard_map/ppermute | solution.py:365
  2.6 77.2 %collective-permute-start.4 = (f32[2720,128]{1,0:T(8,128)}, f32[2720,128]{1,0:T(8,128)}, u32[]{:S(2)}, u32[]{:S(2)}) collective-permute-start(f32[2720,128]{1,0:T(8,128)} %get-tuple-element.42), channel_id=1, source_target_pairs={{0,2},{1,3},{2,0},{3,1},{4,6},{5,7},{6,4},{7,5},{8,10},{9,11},{10,... | collective-permute-start | bytes 4177928 | tf_op jit(solution)/shard_map/ppermute | solution.py:367
  6.3 70.7 %collective-permute-start.5 = (f32[864,128]{1,0:T(8,128)S(1)}, f32[864,128]{1,0:T(8,128)S(1)}, u32[]{:S(2)}, u32[]{:S(2)}) collective-permute-start(f32[864,128]{1,0:T(8,128)S(1)} %slice.10), channel_id=1, source_target_pairs={{1,2},{2,1},{5,6},{6,5},{9,10},{10,9},{13,14},{14,13},{17,18},{18,... | collective-permute-start | bytes 1327112 | tf_op jit(solution)/shard_map/ppermute | solution.py:369
  8.7 86.4 %collective-permute-start.7 = (f32[512,128]{1,0:T(8,128)S(1)}, f32[512,128]{1,0:T(8,128)S(1)}, u32[]{:S(2)}, u32[]{:S(2)}) collective-permute-start(f32[512,128]{1,0:T(8,128)S(1)} %get-tuple-element.51), channel_id=1, source_target_pairs={{4,6},{5,7},{6,4},{7,5},{8,10},{9,11},{10,8},{11,9},{12,14},{13,15... | collective-permute-start | bytes 786440 | tf_op jit(solution)/shard_map/ppermute | solution.py:340
  18.6 2.7 %collective-permute-start = (f32[512,512]{1,0:T(8,128)S(1)}, f32[512,512]{1,0:T(8,128)S(1)}, u32[]{:S(2)}, u32[]{:S(2)}) collective-permute-start(f32[512,512]{1,0:T(8,128)S(1)} %get-tuple-element.16), channel_id=1, source_target_pairs={{0,4},{4,0},{8,12},{12,8},{16,20},{20,16},{24,28},{28,24},{1,5},{5... | collective-permute-start | bytes 3145736 | tf_op jit(solution)/shard_map/cond/branch_1_fun/ppermute | solution.py:336
  21.6 25.3 %collective-permute-start.1 = (f32[512,512]{1,0:T(8,128)S(1)}, f32[512,512]{1,0:T(8,128)S(1)}, u32[]{:S(2)}, u32[]{:S(2)}) collective-permute-start(f32[512,512]{1,0:T(8,128)S(1)} %add.6), channel_id=1, source_target_pairs={{0,8},{4,12},{8,0},{12,4},{16,24},{20,28},{24,16},{28,20},{1,9},{5... | collective-permute-start | bytes 3145736 | tf_op jit(solution)/shard_map/cond/branch_1_fun/ppermute | solution.py:336
  47.0 24.4 %collective-permute-start.2 = (f32[512,512]{1,0:T(8,128)S(1)}, f32[512,512]{1,0:T(8,128)S(1)}, u32[]{:S(2)}, u32[]{:S(2)}) collective-permute-start(f32[512,512]{1,0:T(8,128)S(1)} %add.7), channel_id=1, source_target_pairs={{0,16},{4,20},{8,24},{12,28},{16,0},{20,4},{24,8},{28,12},{1,17},{... | collective-permute-start | bytes 3145736 | tf_op jit(solution)/shard_map/cond/branch_1_fun/ppermute | solution.py:336
  72.7 3.0 %collective-permute-start.3 = (f32[512,512]{1,0:T(8,128)}, f32[512,512]{1,0:T(8,128)}, u32[]{:S(2)}, u32[]{:S(2)}) collective-permute-start(f32[512,512]{1,0:T(8,128)} %add.8), channel_id=1, source_target_pairs={{0,4},{4,0},{8,12},{12,8},{16,20},{20,16},{24,28},{28,24},{1,5},{5... | collective-permute-start | bytes 3145736 | tf_op jit(solution)/shard_map/cond/branch_1_fun/ppermute | solution.py:336
  75.7 21.8 %collective-permute-start.6 = (f32[864,128]{1,0:T(8,128)S(1)}, f32[864,128]{1,0:T(8,128)S(1)}, u32[]{:S(2)}, u32[]{:S(2)}) collective-permute-start(f32[864,128]{1,0:T(8,128)S(1)} %slice.10), channel_id=1, source_target_pairs={{0,2},{3,1},{4,6},{7,5},{8,10},{11,9},{12,14},{15,13},{16,18},{19,... | collective-permute-start | bytes 1327112 | tf_op jit(solution)/shard_map/ppermute | solution.py:383
  79.8 40.3 %collective-permute-start.9 = (f32[2720,128]{1,0:T(8,128)}, f32[2720,128]{1,0:T(8,128)S(1)}, u32[]{:S(2)}, u32[]{:S(2)}) collective-permute-start(f32[2720,128]{1,0:T(8,128)} %collective-permute-done.4.refs_8_), channel_id=1, source_target_pairs={{2,3},{1,0},{6,7},{5,4},{10,11},{9,8},{14,15},{13,12},{18,19},{17,... | collective-permute-start | bytes 4177928 | tf_op jit(solution)/shard_map/ppermute | solution.py:388
  82.6 1.2 copy-start.1
  87.1 18.0 %copy-start = (f32[4096,128]{1,0:T(8,128)S(1)}, f32[4096,128]{1,0:T(8,128)}, u32[]{:S(2)}) copy-start(f32[4096,128]{1,0:T(8,128)} %refs_5_.1) | copy-start | bytes 6291460
  95.1 34.7 %collective-permute-start.13 = (f32[2656,128]{1,0:T(8,128)S(1)}, f32[2656,128]{1,0:T(8,128)S(1)}, u32[]{:S(2)}, u32[]{:S(2)}) collective-permute-start(f32[2656,128]{1,0:T(8,128)S(1)} %get-tuple-element.66), channel_id=1, source_target_pairs={{1,2},{2,1},{5,6},{6,5},{9,10},{10,9},{13,14},{14,13},{17,18},{18,... | collective-permute-start | bytes 4079624 | tf_op jit(solution)/shard_map/ppermute | solution.py:391
  97.5 37.4 %collective-permute-start.12 = (f32[1728,128]{1,0:T(8,128)S(1)}, f32[1728,128]{1,0:T(8,128)S(1)}, u32[]{:S(2)}, u32[]{:S(2)}) collective-permute-start(f32[1728,128]{1,0:T(8,128)S(1)} %pad_maximum_fusion), channel_id=1, source_target_pairs={{2,3},{1,0},{6,7},{5,4},{10,11},{9,8},{14,15},{13,12},{18,19},{17,... | collective-permute-start | bytes 2654216 | tf_op jit(solution)/shard_map/ppermute | solution.py:395
  100.3 39.1 %collective-permute-start.11 = (f32[576,128]{1,0:T(8,128)S(1)}, f32[576,128]{1,0:T(8,128)S(1)}, u32[]{:S(2)}, u32[]{:S(2)}) collective-permute-start(f32[576,128]{1,0:T(8,128)S(1)} %get-tuple-element.63), channel_id=1, source_target_pairs={{1,2},{2,1},{5,6},{6,5},{9,10},{10,9},{13,14},{14,13},{17,18},{18,... | collective-permute-start | bytes 884744 | tf_op jit(solution)/shard_map/ppermute | solution.py:392
  103.8 35.6 %collective-permute-start.10 = (f32[512,128]{1,0:T(8,128)S(1)}, f32[512,128]{1,0:T(8,128)S(1)}, u32[]{:S(2)}, u32[]{:S(2)}) collective-permute-start(f32[512,128]{1,0:T(8,128)S(1)} %collective-permute-done.7.refs_7_), channel_id=1, source_target_pairs={{6,7},{5,4},{10,11},{9,8},{14,15},{13,12},{18,19},{17,16},{22,23},... | collective-permute-start | bytes 786440 | tf_op jit(solution)/shard_map/ppermute | solution.py:340

commit v16 on v15

--- a/solution.py
+++ b/solution.py
@@ -371,8 +371,12 @@
         def gather_rows(slab, pivots):
             send, keep = pick(info, pivots, slab, block)
             total = keep + exchange(send, 0, row_parts)
-            for bit in range(1, bits):
-                total = total + exchange(total, bit, row_parts)
+            halves = [total[: block // 2], total[block // 2 :]]
+            orders = [list(range(1, bits)), list(range(1, bits))[::-1]]
+            for step in range(bits - 1):
+                other = [exchange(half, order[step], row_parts) for half, order in zip(halves, orders)]
+                halves = [half + part for half, part in zip(halves, other)]
+            total = jnp.concatenate(halves, axis=0)
             return total, exchange(total, 0, row_parts)
 
         def no_rows(slab, pivots):
@@ -381,7 +385,7 @@
         total, other = lax.cond(pivots[0] >= 0, gather_rows, no_rows, slab, pivots)
         tail, total = lax.optimization_barrier((tail, total))
         far = lax.ppermute(tail, "pcol", FAR)
-        head, tail_mid, total = lax.optimization_barrier((across[0], tail_mid, total))
+        head, total = lax.optimization_barrier((across[0], total))
         upper, terms, across_terms, last_terms = make_upper(info, total, other, diag_inverse, width)
         later, upper = lax.optimization_barrier((panel, upper))
         head_mid, rest_mid = load_pieces(later, [(second_mid, first_mid), (0, second_mid)])

time: 143 us -> 140 us (0.979); the launches traced: 141 us -> 140 us
  waiting for transfers between devices: 78.3 us -> 75.9 us
    ppermute x4 -> x6, waiting for transfers between devices: 54.2 us -> 30.4 us  [exchange(): lax.ppermute(value, 'prow', [(i, i ^ 1 << bit) for i in range(count)])]
    ppermute x1, waiting for transfers between devices: 2.83 us -> 21.5 us  [shards(): lax.ppermute(pieces[0], 'pcol', ACROSS)]
    ppermute x1, waiting for transfers between devices: 0.01 us -> 9.42 us  [shards(): tail_mid = lax.ppermute(tail, 'pcol', MIDDLE)]
    ppermute x2, waiting for transfers between devices: 9.03 us -> 0.01 us  [on_rows(): lax.ppermute(value, ('prow', 'pcol'), [(4 * row + a, 4 * row + b) for row...]
    ppermute x1, waiting for transfers between devices: 0.01 us -> 3.81 us  [shards(): far = lax.ppermute(tail, 'pcol', FAR)]
    ppermute x1, waiting for transfers between devices: 2.53 us -> 0.01 us  [shards(): both = lax.ppermute(both, 'pcol', ENDS)]
    ppermute x1, starting transfers between devices: 2.36 us -> 4.61 us  [shards(): tail_mid = lax.ppermute(tail, 'pcol', MIDDLE)]
    ppermute x1, waiting for transfers between devices: 0.01 us -> 1.7 us  [shards(): rest_mid = lax.ppermute(rest_mid, 'pcol', MIDDLE)]
  transfers between devices with their start and end apart: 14 -> 16, of which waited for: 9 -> 11; matrix products, arithmetic and copies ran while one was open for 2% -> 3% of each run, Pallas kernels for 24% -> 24%
where the time goes in v16:
time: 140 us
  waiting for transfers between devices  75.9 us (54%)
  Pallas kernels  34.5 us (25%)
  starting transfers between devices  23.1 us (16%)
  local copies, waits for them, and re-layouts  3.62 us (3%)
  other arithmetic  1.8 us (1%)
    ppermute x6, waiting for transfers between devices, exchange(): lax.ppermute(value, 'prow', [(i, i ^ 1 << bit) for i in range(count)])  30.4 us
    ppermute x1, waiting for transfers between devices, shards(): lax.ppermute(pieces[0], 'pcol', ACROSS)  21.5 us
    pallas_call x1, Pallas kernels, main_update(): pl.pallas_call(lambda *refs: main_kernel(min(TILE, block), *refs), out_sh...  14.9 us
    ppermute x1, waiting for transfers between devices, shards(): tail_mid = lax.ppermute(tail, 'pcol', MIDDLE)  9.42 us
    ppermute x1, waiting for transfers between devices, shards(): head_mid = lax.ppermute(head_mid, 'pcol', MIDDLE)  9.09 us
    pallas_call x1, Pallas kernels, pick(): pl.pallas_call(pick_kernel, out_shape=(shape, shape), grid_spec=pltpu.Pre...  6.75 us
    pallas_call x3, Pallas kernels, last_update(): pl.pallas_call(lambda *refs: last_kernel(first_row, block, min(LAST_TILE,...  5.84 us
    ppermute x1, starting transfers between devices, shards(): tail_mid = lax.ppermute(tail, 'pcol', MIDDLE)  4.61 us
  transfers between devices with their start and end apart: 16, of which 11 were waited for; matrix products, arithmetic and copies ran while one was open for 3% of the time, Pallas kernels for 24%

profile of v16, /device:TPU:14, one launch (start us, length us, event | category | flops | bytes accessed | tf_op | source)
XLA Modules:
  0.0 139.8 jit_solution(13926495839615511334)
XLA Ops:
  0.0 0.0 copy-start.2
  0.0 0.4 collective-permute-start.9
  0.5 2.2 %cut.1 = (f32[2720,128]{1,0:T(8,128)}, f32[512,128]{1,0:T(8,128)}) custom-call(f32[4096,128]{1,0:T(8,128)} %refs_5_.1), custom_call_target="tpu_custom_call" | custom-call | tf_op jit(solution)/shard_map/cut/pallas_call | solution.py:94
  2.7 2.7 %collective-permute-start.6 = (f32[2720,128]{1,0:T(8,128)}, f32[2720,128]{1,0:T(8,128)S(1)}, u32[]{:S(2)}, u32[]{:S(2)}) collective-permute-start(f32[2720,128]{1,0:T(8,128)} %get-tuple-element.41), channel_id=1, source_target_pairs={{0,2},{1,3},{2,0},{3,1},{4,6},{5,7},{6,4},{7,5},{8,10},{9,11},{10,... | collective-permute-start | bytes 4177928 | tf_op jit(solution)/shard_map/ppermute | solution.py:367
  5.3 2.2 %collective-permute-start.8 = (f32[512,128]{1,0:T(8,128)}, f32[512,128]{1,0:T(8,128)}, u32[]{:S(2)}, u32[]{:S(2)}) collective-permute-start(f32[512,128]{1,0:T(8,128)} %get-tuple-element.50), channel_id=1, source_target_pairs={{4,6},{5,7},{6,4},{7,5},{8,10},{9,11},{10,8},{11,9},{12,14},{13,15... | collective-permute-start | bytes 786440 | tf_op jit(solution)/shard_map/ppermute | solution.py:340
  7.6 0.1 pad_add_fusion.refs_0_
  7.6 1.8 %slice.16 = f32[864,128]{1,0:T(8,128)} slice(f32[4096,128]{1,0:T(8,128)} %refs_5_.1), slice={[3232:4096], [0:128]} | slice | bytes 884736 | tf_op jit(solution)/shard_map/slice | solution.py:368
  9.5 0.0 copy-done.2
  9.5 0.5 slice.17
  10.5 41.7 %conditional.1 = (f32[512,512]{1,0:T(8,128)}, f32[512,512]{1,0:T(8,128)}) conditional(s32[]{:T(128)} %bitcast.2, f32[4096,512]{1,0:T(8,128)} %refs_2_.1, (s32[2]{0:T(128)S(1)}, s32[512]{0:T(512)S(1)}, f32[4096,512]{1,0:T(8,128)}) %tuple.30), branch_computations={%region_0.0_spmd, %region_1.0_spmd} | conditional | flops 1048576 | bytes 30408960 | solution.py:385
  10.6 6.8 %pick.1 = (f32[512,512]{1,0:T(8,128)S(1)}, f32[512,512]{1,0:T(8,128)S(1)}) custom-call(s32[2]{0:T(128)S(1)} %get-tuple-element.12.info, s32[512]{0:T(512)S(1)} %get-tuple-element.13.pivots, f32[4096,512]{1,0:T(8,128)} %get-tuple-element.14.slab), custom_call_target="tpu_custom_call" | custom-call | tf_op jit(solution)/shard_map/cond/branch_1_fun/pick/pallas_call | solution.py:156
  17.3 0.1 collective-permute-start
  17.4 2.6 %collective-permute-done = f32[512,512]{1,0:T(8,128)S(1)} collective-permute-done((f32[512,512]{1,0:T(8,128)S(1)}, f32[512,512]{1,0:T(8,128)S(1)}, u32[]{:S(2)}, u32[]{:S(2)}) %collective-permute-start) | collective-permute-done | bytes 1048608 | tf_op jit(solution)/shard_map/cond/branch_1_fun/ppermute | solution.py:336
  20.1 0.2 add.10
  20.3 0.1 fusion
  20.3 0.6 collective-permute-start.1
  20.9 0.1 collective-permute-start.3
  21.0 13.4 %collective-permute-done.1 = f32[256,512]{1,0:T(8,128)S(1)} collective-permute-done((f32[256,512]{1,0:T(8,128)S(1)}, f32[256,512]{1,0:T(8,128)S(1)}, u32[]{:S(2)}, u32[]{:S(2)}) %collective-permute-start.1) | collective-permute-done | bytes 524320 | tf_op jit(solution)/shard_map/cond/branch_1_fun/ppermute | solution.py:336
  34.4 0.3 collective-permute-done.3
  34.6 0.2 slice_add_fusion.1
  34.8 0.4 collective-permute-start.2
  35.2 1.7 %collective-permute-start.4 = (f32[256,512]{1,0:T(8,128)S(1)}, f32[256,512]{1,0:T(8,128)S(1)}, u32[]{:S(2)}, u32[]{:S(2)}) collective-permute-start(f32[256,512]{1,0:T(8,128)S(1)} %get-tuple-element.66), channel_id=1, source_target_pairs={{0,8},{4,12},{8,0},{12,4},{16,24},{20,28},{24,16},{28,20},{1,9},{5... | collective-permute-start | bytes 1572872 | tf_op jit(solution)/shard_map/cond/branch_1_fun/ppermute | solution.py:336
  36.9 10.9 %collective-permute-done.2 = f32[256,512]{1,0:T(8,128)S(1)} collective-permute-done((f32[256,512]{1,0:T(8,128)S(1)}, f32[256,512]{1,0:T(8,128)S(1)}, u32[]{:S(2)}, u32[]{:S(2)}) %collective-permute-start.2) | collective-permute-done | bytes 524320 | tf_op jit(solution)/shard_map/cond/branch_1_fun/ppermute | solution.py:336
  47.8 0.1 add.12
  47.9 0.2 collective-permute-done.4
  48.1 0.1 add.14
  48.2 1.1 pad_maximum_fusion
  49.3 0.0 collective-permute-start.5
  49.3 3.0 %collective-permute-done.5 = f32[512,512]{1,0:T(8,128)} collective-permute-done((f32[512,512]{1,0:T(8,128)}, f32[512,512]{1,0:T(8,128)}, u32[]{:S(2)}, u32[]{:S(2)}) %collective-permute-start.5) | collective-permute-done | bytes 1048608 | tf_op jit(solution)/shard_map/cond/branch_1_fun/ppermute | solution.py:336
  52.3 1.3 collective-permute-start.7
  53.6 4.6 %collective-permute-start.10 = (f32[864,128]{1,0:T(8,128)}, f32[864,128]{1,0:T(8,128)S(1)}, u32[]{:S(2)}, u32[]{:S(2)}) collective-permute-start(f32[864,128]{1,0:T(8,128)} %slice.16), channel_id=1, source_target_pairs={{1,2},{2,1},{5,6},{6,5},{9,10},{10,9},{13,14},{14,13},{17,18},{18,... | collective-permute-start | bytes 1327112 | tf_op jit(solution)/shard_map/ppermute | solution.py:369
  58.2 21.5 %collective-permute-done.6.refs_8_ = f32[2720,128]{1,0:T(8,128)S(1)} collective-permute-done((f32[2720,128]{1,0:T(8,128)}, f32[2720,128]{1,0:T(8,128)S(1)}, u32[]{:S(2)}, u32[]{:S(2)}) %collective-permute-start.6) | collective-permute-done | bytes 1392672 | tf_op jit(solution)/shard_map/ppermute | solution.py:367
  79.7 1.4 collective-permute-start.11
  81.1 0.0 copy-start.1
  81.1 1.2 copy-done.1
  82.3 3.3 %upper.1 = (f32[512,512]{1,0:T(8,128)S(1)}, bf16[1152,512]{1,0:T(8,128)(2,1)S(1)}, bf16[384,512]{1,0:T(8,128)(2,1)S(1)}, bf16[384,512]{1,0:T(8,128)(2,1)S(1)}) custom-call(s32[2]{0:T(128)S(1)} %pad_add_fusion.refs_0_, f32[512,512]{1,0:T(8,128)} %get-tuple-element.44.refs_1_.refs_3_, f32[512,512]{1,0:T(8,128)} %get-tuple-element.45.refs_2_.refs_4_, ...), custom_call_target="tpu_custom_call" | custom-call | tf_op jit(solution)/shard_map/upper/pallas_call | solution.py:202
  85.6 0.0 copy-start
  85.6 1.5 %load_pieces.1 = (f32[2656,128]{1,0:T(8,128)S(1)}, f32[576,128]{1,0:T(8,128)S(1)}) custom-call(f32[4096,128]{1,0:T(8,128)} %refs_5_.1), custom_call_target="tpu_custom_call" | custom-call | tf_op jit(solution)/shard_map/load_pieces/pallas_call | solution.py:59
  87.1 0.0 collective-permute-done.8.refs_7_
  87.1 0.0 collective-permute-done.9.refs_6_
  87.1 2.7 %collective-permute-start.15 = (f32[2656,128]{1,0:T(8,128)S(1)}, f32[2656,128]{1,0:T(8,128)S(1)}, u32[]{:S(2)}, u32[]{:S(2)}) collective-permute-start(f32[2656,128]{1,0:T(8,128)S(1)} %get-tuple-element.64), channel_id=1, source_target_pairs={{1,2},{2,1},{5,6},{6,5},{9,10},{10,9},{13,14},{14,13},{17,18},{18,... | collective-permute-start | bytes 4079624 | tf_op jit(solution)/shard_map/ppermute | solution.py:395
  89.8 3.8 %collective-permute-done.7.refs_3_ = f32[864,128]{1,0:T(8,128)S(1)} collective-permute-done((f32[864,128]{1,0:T(8,128)}, f32[864,128]{1,0:T(8,128)S(1)}, u32[]{:S(2)}, u32[]{:S(2)}) %collective-permute-start.7) | collective-permute-done | bytes 442400 | tf_op jit(solution)/shard_map/ppermute | solution.py:387
  93.6 9.4 %collective-permute-done.10.refs_4_ = f32[864,128]{1,0:T(8,128)S(1)} collective-permute-done((f32[864,128]{1,0:T(8,128)}, f32[864,128]{1,0:T(8,128)S(1)}, u32[]{:S(2)}, u32[]{:S(2)}) %collective-permute-start.10) | collective-permute-done | bytes 442400 | tf_op jit(solution)/shard_map/ppermute | solution.py:369
  103.1 0.1 pad_maximum_fusion.1
  103.1 1.3 collective-permute-start.14
  104.5 2.4 %collective-permute-start.13 = (f32[576,128]{1,0:T(8,128)S(1)}, f32[576,128]{1,0:T(8,128)S(1)}, u32[]{:S(2)}, u32[]{:S(2)}) collective-permute-start(f32[576,128]{1,0:T(8,128)S(1)} %get-tuple-element.61), channel_id=1, source_target_pairs={{1,2},{2,1},{5,6},{6,5},{9,10},{10,9},{13,14},{14,13},{17,18},{18,... | collective-permute-start | bytes 884744 | tf_op jit(solution)/shard_map/ppermute | solution.py:396
  106.9 1.3 collective-permute-start.12
  108.2 0.0 copy-done
  108.2 14.9 %main_update.1.refs_0_ = f32[4096,512]{1,0:T(8,128)S(1)} custom-call(s32[2]{0:T(128)S(1)} %pad_add_fusion.refs_0_, s32[512]{0:T(512)S(1)} %copy-done.2, f32[4096,512]{1,0:T(8,128)} %refs_2_.1, f32[512,512]{1,0:T(8,128)} %get-tuple-element.44.refs_1_.refs_3_, f32[512,512]{1,0:T(8,128)} %get-tuple-element.45.refs_2_.refs_4_, f32[4096,128]{1,0:T(8,128)S(1)} %copy-done, ...), custom_call_target="tpu_custom_call" | custom-call | tf_op jit(solution)/shard_map/main_update/pallas_call | solution.py:281
  123.1 0.0 collective-permute-done.11.refs_2_
  123.1 9.1 %collective-permute-done.15.refs_3_ = f32[2656,128]{1,0:T(8,128)S(1)} collective-permute-done((f32[2656,128]{1,0:T(8,128)S(1)}, f32[2656,128]{1,0:T(8,128)S(1)}, u32[]{:S(2)}, u32[]{:S(2)}) %collective-permute-start.15) | collective-permute-done | bytes 1359904 | tf_op jit(solution)/shard_map/ppermute | solution.py:395
  132.2 2.7 %last_update.3.refs_6_ = f32[4096,512]{1,0:T(8,128)} custom-call(f32[4096,512]{1,0:T(8,128)S(1)} %main_update.1.refs_0_, bf16[384,512]{1,0:T(8,128)(2,1)S(1)} %get-tuple-element.60.refs_1_.refs_2_, f32[2720,128]{1,0:T(8,128)S(1)} %collective-permute-done.11.refs_2_, f32[2656,128]{1,0:T(8,128)S(1)} %collective-permute-done.15.refs_3_), custom_call_target="tpu_custom_call" | custom-call | tf_op jit(solution)/shard_map/last_update/pallas_call | solution.py:322
  134.9 0.0 collective-permute-done.14.refs_5_
  134.9 1.9 %last_update.4.refs_5_ = f32[4096,512]{1,0:T(8,128)} custom-call(f32[4096,512]{1,0:T(8,128)S(1)} %main_update.1.refs_0_, bf16[384,512]{1,0:T(8,128)(2,1)S(1)} %get-tuple-element.62.refs_1_, bf16[384,512]{1,0:T(8,128)(2,1)S(1)} %get-tuple-element.60.refs_1_.refs_2_, f32[864,128]{1,0:T(8,128)S(1)} %collective-permute-done.7.refs_3_, ...), custom_call_target="tpu_custom_call", output_to_operand_aliasing={{}: (6, {})} | custom-call | tf_op jit(solution)/shard_map/last_update/pallas_call | solution.py:322
  136.8 0.0 collective-permute-done.12.refs_3_
  136.8 1.7 %collective-permute-done.13.refs_4_ = f32[576,128]{1,0:T(8,128)S(1)} collective-permute-done((f32[576,128]{1,0:T(8,128)S(1)}, f32[576,128]{1,0:T(8,128)S(1)}, u32[]{:S(2)}, u32[]{:S(2)}) %collective-permute-start.13) | collective-permute-done | bytes 294944 | tf_op jit(solution)/shard_map/ppermute | solution.py:396
  138.5 1.3 last_update.5
Async XLA Ops:
  0.0 9.5 %copy-start.2 = (s32[512]{0:T(512)S(1)}, s32[512]{0:T(512)}, u32[]{:S(2)}) copy-start(s32[512]{0:T(512)} %refs_1_.1) | copy-start | bytes 6148
  0.0 87.1 %collective-permute-start.9 = (f32[4096,128]{1,0:T(8,128)}, f32[4096,128]{1,0:T(8,128)S(1)}, u32[]{:S(2)}, u32[]{:S(2)}) collective-permute-start(f32[4096,128]{1,0:T(8,128)} %refs_5_.1), channel_id=1, source_target_pairs={{0,1},{1,0},{2,3},{3,2},{4,5},{5,4},{6,7},{7,6},{8,9},{9,8},{10,11... | collective-permute-start | bytes 6291464 | tf_op jit(solution)/shard_map/ppermute | solution.py:365
  2.7 77.0 %collective-permute-start.6 = (f32[2720,128]{1,0:T(8,128)}, f32[2720,128]{1,0:T(8,128)S(1)}, u32[]{:S(2)}, u32[]{:S(2)}) collective-permute-start(f32[2720,128]{1,0:T(8,128)} %get-tuple-element.41), channel_id=1, source_target_pairs={{0,2},{1,3},{2,0},{3,1},{4,6},{5,7},{6,4},{7,5},{8,10},{9,11},{10,... | collective-permute-start | bytes 4177928 | tf_op jit(solution)/shard_map/ppermute | solution.py:367
  5.3 81.8 %collective-permute-start.8 = (f32[512,128]{1,0:T(8,128)}, f32[512,128]{1,0:T(8,128)}, u32[]{:S(2)}, u32[]{:S(2)}) collective-permute-start(f32[512,128]{1,0:T(8,128)} %get-tuple-element.50), channel_id=1, source_target_pairs={{4,6},{5,7},{6,4},{7,5},{8,10},{9,11},{10,8},{11,9},{12,14},{13,15... | collective-permute-start | bytes 786440 | tf_op jit(solution)/shard_map/ppermute | solution.py:340
  17.3 2.7 %collective-permute-start = (f32[512,512]{1,0:T(8,128)S(1)}, f32[512,512]{1,0:T(8,128)S(1)}, u32[]{:S(2)}, u32[]{:S(2)}) collective-permute-start(f32[512,512]{1,0:T(8,128)S(1)} %get-tuple-element.16), channel_id=1, source_target_pairs={{0,4},{4,0},{8,12},{12,8},{16,20},{20,16},{24,28},{28,24},{1,5},{5... | collective-permute-start | bytes 3145736 | tf_op jit(solution)/shard_map/cond/branch_1_fun/ppermute | solution.py:336
  20.3 14.0 %collective-permute-start.1 = (f32[256,512]{1,0:T(8,128)S(1)}, f32[256,512]{1,0:T(8,128)S(1)}, u32[]{:S(2)}, u32[]{:S(2)}) collective-permute-start(f32[256,512]{1,0:T(8,128)S(1)} %get-tuple-element.67), channel_id=1, source_target_pairs={{0,8},{4,12},{8,0},{12,4},{16,24},{20,28},{24,16},{28,20},{1,9},{5... | collective-permute-start | bytes 1572872 | tf_op jit(solution)/shard_map/cond/branch_1_fun/ppermute | solution.py:336
  20.9 13.7 %collective-permute-start.3 = (f32[256,512]{1,0:T(8,128)S(1)}, f32[256,512]{1,0:T(8,128)S(1)}, u32[]{:S(2)}, u32[]{:S(2)}) collective-permute-start(f32[256,512]{1,0:T(8,128)S(1)} %get-tuple-element.68), channel_id=1, source_target_pairs={{0,16},{4,20},{8,24},{12,28},{16,0},{20,4},{24,8},{28,12},{1,17},{... | collective-permute-start | bytes 1572872 | tf_op jit(solution)/shard_map/cond/branch_1_fun/ppermute | solution.py:336
  34.8 13.0 %collective-permute-start.2 = (f32[256,512]{1,0:T(8,128)S(1)}, f32[256,512]{1,0:T(8,128)S(1)}, u32[]{:S(2)}, u32[]{:S(2)}) collective-permute-start(f32[256,512]{1,0:T(8,128)S(1)} %get-tuple-element.65), channel_id=1, source_target_pairs={{0,16},{4,20},{8,24},{12,28},{16,0},{20,4},{24,8},{28,12},{1,17},{... | collective-permute-start | bytes 1572872 | tf_op jit(solution)/shard_map/cond/branch_1_fun/ppermute | solution.py:336
  35.2 12.9 %collective-permute-start.4 = (f32[256,512]{1,0:T(8,128)S(1)}, f32[256,512]{1,0:T(8,128)S(1)}, u32[]{:S(2)}, u32[]{:S(2)}) collective-permute-start(f32[256,512]{1,0:T(8,128)S(1)} %get-tuple-element.66), channel_id=1, source_target_pairs={{0,8},{4,12},{8,0},{12,4},{16,24},{20,28},{24,16},{28,20},{1,9},{5... | collective-permute-start | bytes 1572872 | tf_op jit(solution)/shard_map/cond/branch_1_fun/ppermute | solution.py:336
  49.3 3.0 %collective-permute-start.5 = (f32[512,512]{1,0:T(8,128)}, f32[512,512]{1,0:T(8,128)}, u32[]{:S(2)}, u32[]{:S(2)}) collective-permute-start(f32[512,512]{1,0:T(8,128)} %pad_maximum_fusion), channel_id=1, source_target_pairs={{0,4},{4,0},{8,12},{12,8},{16,20},{20,16},{24,28},{28,24},{1,5},{5... | collective-permute-start | bytes 3145736 | tf_op jit(solution)/shard_map/cond/branch_1_fun/ppermute | solution.py:336
  52.3 41.4 %collective-permute-start.7 = (f32[864,128]{1,0:T(8,128)}, f32[864,128]{1,0:T(8,128)S(1)}, u32[]{:S(2)}, u32[]{:S(2)}) collective-permute-start(f32[864,128]{1,0:T(8,128)} %slice.16), channel_id=1, source_target_pairs={{0,2},{3,1},{4,6},{7,5},{8,10},{11,9},{12,14},{15,13},{16,18},{19,... | collective-permute-start | bytes 1327112 | tf_op jit(solution)/shard_map/ppermute | solution.py:387
  53.6 49.5 %collective-permute-start.10 = (f32[864,128]{1,0:T(8,128)}, f32[864,128]{1,0:T(8,128)S(1)}, u32[]{:S(2)}, u32[]{:S(2)}) collective-permute-start(f32[864,128]{1,0:T(8,128)} %slice.16), channel_id=1, source_target_pairs={{1,2},{2,1},{5,6},{6,5},{9,10},{10,9},{13,14},{14,13},{17,18},{18,... | collective-permute-start | bytes 1327112 | tf_op jit(solution)/shard_map/ppermute | solution.py:369
  79.7 43.4 %collective-permute-start.11 = (f32[2720,128]{1,0:T(8,128)S(1)}, f32[2720,128]{1,0:T(8,128)S(1)}, u32[]{:S(2)}, u32[]{:S(2)}) collective-permute-start(f32[2720,128]{1,0:T(8,128)S(1)} %collective-permute-done.6.refs_8_), channel_id=1, source_target_pairs={{2,3},{1,0},{6,7},{5,4},{10,11},{9,8},{14,15},{13,12},{18,19},{17,... | collective-permute-start | bytes 4177928 | tf_op jit(solution)/shard_map/ppermute | solution.py:392
  81.1 1.2 copy-start.1
  85.6 22.6 %copy-start = (f32[4096,128]{1,0:T(8,128)S(1)}, f32[4096,128]{1,0:T(8,128)}, u32[]{:S(2)}) copy-start(f32[4096,128]{1,0:T(8,128)} %refs_5_.1) | copy-start | bytes 6291460
  87.1 45.1 %collective-permute-start.15 = (f32[2656,128]{1,0:T(8,128)S(1)}, f32[2656,128]{1,0:T(8,128)S(1)}, u32[]{:S(2)}, u32[]{:S(2)}) collective-permute-start(f32[2656,128]{1,0:T(8,128)S(1)} %get-tuple-element.64), channel_id=1, source_target_pairs={{1,2},{2,1},{5,6},{6,5},{9,10},{10,9},{13,14},{14,13},{17,18},{18,... | collective-permute-start | bytes 4079624 | tf_op jit(solution)/shard_map/ppermute | solution.py:395
  103.1 31.8 %collective-permute-start.14 = (f32[1728,128]{1,0:T(8,128)S(1)}, f32[1728,128]{1,0:T(8,128)S(1)}, u32[]{:S(2)}, u32[]{:S(2)}) collective-permute-start(f32[1728,128]{1,0:T(8,128)S(1)} %pad_maximum_fusion.1), channel_id=1, source_target_pairs={{2,3},{1,0},{6,7},{5,4},{10,11},{9,8},{14,15},{13,12},{18,19},{17,... | collective-permute-start | bytes 2654216 | tf_op jit(solution)/shard_map/ppermute | solution.py:399
  104.5 34.0 %collective-permute-start.13 = (f32[576,128]{1,0:T(8,128)S(1)}, f32[576,128]{1,0:T(8,128)S(1)}, u32[]{:S(2)}, u32[]{:S(2)}) collective-permute-start(f32[576,128]{1,0:T(8,128)S(1)} %get-tuple-element.61), channel_id=1, source_target_pairs={{1,2},{2,1},{5,6},{6,5},{9,10},{10,9},{13,14},{14,13},{17,18},{18,... | collective-permute-start | bytes 884744 | tf_op jit(solution)/shard_map/ppermute | solution.py:396
  106.9 29.9 %collective-permute-start.12 = (f32[512,128]{1,0:T(8,128)}, f32[512,128]{1,0:T(8,128)S(1)}, u32[]{:S(2)}, u32[]{:S(2)}) collective-permute-start(f32[512,128]{1,0:T(8,128)} %collective-permute-done.8.refs_7_), channel_id=1, source_target_pairs={{6,7},{5,4},{10,11},{9,8},{14,15},{13,12},{18,19},{17,16},{22,23},... | collective-permute-start | bytes 786440 | tf_op jit(solution)/shard_map/ppermute | solution.py:340

commit v17 on v16

--- a/solution.py
+++ b/solution.py
@@ -10,8 +10,8 @@
 MIDDLE = [(1, 2), (2, 1)]
 ENDS = [(2, 3), (1, 0)]
 FAR = [(0, 2), (3, 1)]
-PIECES = (85, 16, 27)
-MIDDLE_PIECES = (83, 18, 27)
+PIECES = (169, 32, 55)
+MIDDLE_PIECES = (165, 36, 55)
 TILE = 512
 LAST_TILE = 256
 SMALL = pl.CostEstimate(flops=0, bytes_accessed=0, transcendentals=0)

time: 140 us -> 140 us (level)
  no operation moved by 1% of the time
where the time goes in v17:
time: 140 us
  waiting for transfers between devices  76 us (54%)
  Pallas kernels  34.5 us (25%)
  starting transfers between devices  23.1 us (16%)
  local copies, waits for them, and re-layouts  3.63 us (3%)
  other arithmetic  1.8 us (1%)
    ppermute x6, waiting for transfers between devices, exchange(): lax.ppermute(value, 'prow', [(i, i ^ 1 << bit) for i in range(count)])  30.4 us
    ppermute x1, waiting for transfers between devices, shards(): lax.ppermute(pieces[0], 'pcol', ACROSS)  21.3 us
    pallas_call x1, Pallas kernels, main_update(): pl.pallas_call(lambda *refs: main_kernel(min(TILE, block), *refs), out_sh...  14.9 us
    ppermute x1, waiting for transfers between devices, shards(): tail_mid = lax.ppermute(tail, 'pcol', MIDDLE)  9.6 us
    ppermute x1, waiting for transfers between devices, shards(): head_mid = lax.ppermute(head_mid, 'pcol', MIDDLE)  8.92 us
    pallas_call x1, Pallas kernels, pick(): pl.pallas_call(pick_kernel, out_shape=(shape, shape), grid_spec=pltpu.Pre...  6.75 us
    pallas_call x3, Pallas kernels, last_update(): pl.pallas_call(lambda *refs: last_kernel(first_row, block, min(LAST_TILE,...  5.82 us
    ppermute x1, starting transfers between devices, shards(): tail_mid = lax.ppermute(tail, 'pcol', MIDDLE)  4.61 us
  transfers between devices with their start and end apart: 16, of which 11 were waited for; matrix products, arithmetic and copies ran while one was open for 3% of the time, Pallas kernels for 24%

profile of v17, /device:TPU:14, one launch (start us, length us, event | category | flops | bytes accessed | tf_op | source)
XLA Modules:
  0.0 139.8 jit_solution(8068201530608377996)
XLA Ops:
  0.0 0.0 copy-start.2
  0.0 0.4 collective-permute-start.9
  0.5 2.2 %cut.1 = (f32[2704,128]{1,0:T(8,128)}, f32[512,128]{1,0:T(8,128)}) custom-call(f32[4096,128]{1,0:T(8,128)} %refs_5_.1), custom_call_target="tpu_custom_call" | custom-call | tf_op jit(solution)/shard_map/cut/pallas_call | solution.py:94
  2.7 2.7 %collective-permute-start.6 = (f32[2704,128]{1,0:T(8,128)}, f32[2704,128]{1,0:T(8,128)S(1)}, u32[]{:S(2)}, u32[]{:S(2)}) collective-permute-start(f32[2704,128]{1,0:T(8,128)} %get-tuple-element.41), channel_id=1, source_target_pairs={{0,2},{1,3},{2,0},{3,1},{4,6},{5,7},{6,4},{7,5},{8,10},{9,11},{10,... | collective-permute-start | bytes 4153352 | tf_op jit(solution)/shard_map/ppermute | solution.py:367
  5.3 2.2 %collective-permute-start.8 = (f32[512,128]{1,0:T(8,128)}, f32[512,128]{1,0:T(8,128)}, u32[]{:S(2)}, u32[]{:S(2)}) collective-permute-start(f32[512,128]{1,0:T(8,128)} %get-tuple-element.50), channel_id=1, source_target_pairs={{4,6},{5,7},{6,4},{7,5},{8,10},{9,11},{10,8},{11,9},{12,14},{13,15... | collective-permute-start | bytes 786440 | tf_op jit(solution)/shard_map/ppermute | solution.py:340
  7.6 0.1 pad_add_fusion.refs_0_
  7.7 1.8 %slice.16 = f32[880,128]{1,0:T(8,128)} slice(f32[4096,128]{1,0:T(8,128)} %refs_5_.1), slice={[3216:4096], [0:128]} | slice | bytes 901120 | tf_op jit(solution)/shard_map/slice | solution.py:368
  9.5 0.0 copy-done.2
  9.5 0.5 slice.17
  10.6 41.7 %conditional.1 = (f32[512,512]{1,0:T(8,128)}, f32[512,512]{1,0:T(8,128)}) conditional(s32[]{:T(128)} %bitcast.2, f32[4096,512]{1,0:T(8,128)} %refs_2_.1, (s32[2]{0:T(128)S(1)}, s32[512]{0:T(512)S(1)}, f32[4096,512]{1,0:T(8,128)}) %tuple.30), branch_computations={%region_0.0_spmd, %region_1.0_spmd} | conditional | flops 1048576 | bytes 30408960 | solution.py:385
  10.6 6.8 %pick.1 = (f32[512,512]{1,0:T(8,128)S(1)}, f32[512,512]{1,0:T(8,128)S(1)}) custom-call(s32[2]{0:T(128)S(1)} %get-tuple-element.12.info, s32[512]{0:T(512)S(1)} %get-tuple-element.13.pivots, f32[4096,512]{1,0:T(8,128)} %get-tuple-element.14.slab), custom_call_target="tpu_custom_call" | custom-call | tf_op jit(solution)/shard_map/cond/branch_1_fun/pick/pallas_call | solution.py:156
  17.3 0.1 collective-permute-start
  17.4 2.6 %collective-permute-done = f32[512,512]{1,0:T(8,128)S(1)} collective-permute-done((f32[512,512]{1,0:T(8,128)S(1)}, f32[512,512]{1,0:T(8,128)S(1)}, u32[]{:S(2)}, u32[]{:S(2)}) %collective-permute-start) | collective-permute-done | bytes 1048608 | tf_op jit(solution)/shard_map/cond/branch_1_fun/ppermute | solution.py:336
  20.1 0.2 add.10
  20.3 0.1 fusion
  20.4 0.6 collective-permute-start.1
  21.0 0.1 collective-permute-start.3
  21.0 13.4 %collective-permute-done.1 = f32[256,512]{1,0:T(8,128)S(1)} collective-permute-done((f32[256,512]{1,0:T(8,128)S(1)}, f32[256,512]{1,0:T(8,128)S(1)}, u32[]{:S(2)}, u32[]{:S(2)}) %collective-permute-start.1) | collective-permute-done | bytes 524320 | tf_op jit(solution)/shard_map/cond/branch_1_fun/ppermute | solution.py:336
  34.4 0.3 collective-permute-done.3
  34.6 0.2 slice_add_fusion.1
  34.8 0.4 collective-permute-start.2
  35.2 1.7 %collective-permute-start.4 = (f32[256,512]{1,0:T(8,128)S(1)}, f32[256,512]{1,0:T(8,128)S(1)}, u32[]{:S(2)}, u32[]{:S(2)}) collective-permute-start(f32[256,512]{1,0:T(8,128)S(1)} %get-tuple-element.66), channel_id=1, source_target_pairs={{0,8},{4,12},{8,0},{12,4},{16,24},{20,28},{24,16},{28,20},{1,9},{5... | collective-permute-start | bytes 1572872 | tf_op jit(solution)/shard_map/cond/branch_1_fun/ppermute | solution.py:336
  36.9 10.9 %collective-permute-done.2 = f32[256,512]{1,0:T(8,128)S(1)} collective-permute-done((f32[256,512]{1,0:T(8,128)S(1)}, f32[256,512]{1,0:T(8,128)S(1)}, u32[]{:S(2)}, u32[]{:S(2)}) %collective-permute-start.2) | collective-permute-done | bytes 524320 | tf_op jit(solution)/shard_map/cond/branch_1_fun/ppermute | solution.py:336
  47.8 0.1 add.12
  47.9 0.2 collective-permute-done.4
  48.1 0.1 add.14
  48.2 1.1 pad_maximum_fusion
  49.3 0.0 collective-permute-start.5
  49.3 3.0 %collective-permute-done.5 = f32[512,512]{1,0:T(8,128)} collective-permute-done((f32[512,512]{1,0:T(8,128)}, f32[512,512]{1,0:T(8,128)}, u32[]{:S(2)}, u32[]{:S(2)}) %collective-permute-start.5) | collective-permute-done | bytes 1048608 | tf_op jit(solution)/shard_map/cond/branch_1_fun/ppermute | solution.py:336
  52.3 1.3 collective-permute-start.7
  53.6 4.6 %collective-permute-start.10 = (f32[880,128]{1,0:T(8,128)}, f32[880,128]{1,0:T(8,128)S(1)}, u32[]{:S(2)}, u32[]{:S(2)}) collective-permute-start(f32[880,128]{1,0:T(8,128)} %slice.16), channel_id=1, source_target_pairs={{1,2},{2,1},{5,6},{6,5},{9,10},{10,9},{13,14},{14,13},{17,18},{18,... | collective-permute-start | bytes 1351688 | tf_op jit(solution)/shard_map/ppermute | solution.py:369
  58.2 21.3 %collective-permute-done.6.refs_8_ = f32[2704,128]{1,0:T(8,128)S(1)} collective-permute-done((f32[2704,128]{1,0:T(8,128)}, f32[2704,128]{1,0:T(8,128)S(1)}, u32[]{:S(2)}, u32[]{:S(2)}) %collective-permute-start.6) | collective-permute-done | bytes 1384480 | tf_op jit(solution)/shard_map/ppermute | solution.py:367
  79.5 1.4 collective-permute-start.11
  80.9 0.0 copy-start.1
  80.9 1.2 copy-done.1
  82.1 3.3 %upper.1 = (f32[512,512]{1,0:T(8,128)S(1)}, bf16[1152,512]{1,0:T(8,128)(2,1)S(1)}, bf16[384,512]{1,0:T(8,128)(2,1)S(1)}, bf16[384,512]{1,0:T(8,128)(2,1)S(1)}) custom-call(s32[2]{0:T(128)S(1)} %pad_add_fusion.refs_0_, f32[512,512]{1,0:T(8,128)} %get-tuple-element.44.refs_1_.refs_3_, f32[512,512]{1,0:T(8,128)} %get-tuple-element.45.refs_2_.refs_4_, ...), custom_call_target="tpu_custom_call" | custom-call | tf_op jit(solution)/shard_map/upper/pallas_call | solution.py:202
  85.4 0.0 copy-start
  85.4 1.5 %load_pieces.1 = (f32[2640,128]{1,0:T(8,128)S(1)}, f32[576,128]{1,0:T(8,128)S(1)}) custom-call(f32[4096,128]{1,0:T(8,128)} %refs_5_.1), custom_call_target="tpu_custom_call" | custom-call | tf_op jit(solution)/shard_map/load_pieces/pallas_call | solution.py:59
  86.9 0.0 collective-permute-done.8.refs_7_
  87.0 0.0 collective-permute-done.9.refs_6_
  87.0 2.7 %collective-permute-start.15 = (f32[2640,128]{1,0:T(8,128)S(1)}, f32[2640,128]{1,0:T(8,128)S(1)}, u32[]{:S(2)}, u32[]{:S(2)}) collective-permute-start(f32[2640,128]{1,0:T(8,128)S(1)} %get-tuple-element.64), channel_id=1, source_target_pairs={{1,2},{2,1},{5,6},{6,5},{9,10},{10,9},{13,14},{14,13},{17,18},{18,... | collective-permute-start | bytes 4055048 | tf_op jit(solution)/shard_map/ppermute | solution.py:395
  89.6 4.0 %collective-permute-done.7.refs_3_ = f32[880,128]{1,0:T(8,128)S(1)} collective-permute-done((f32[880,128]{1,0:T(8,128)}, f32[880,128]{1,0:T(8,128)S(1)}, u32[]{:S(2)}, u32[]{:S(2)}) %collective-permute-start.7) | collective-permute-done | bytes 450592 | tf_op jit(solution)/shard_map/ppermute | solution.py:387
  93.6 9.6 %collective-permute-done.10.refs_4_ = f32[880,128]{1,0:T(8,128)S(1)} collective-permute-done((f32[880,128]{1,0:T(8,128)}, f32[880,128]{1,0:T(8,128)S(1)}, u32[]{:S(2)}, u32[]{:S(2)}) %collective-permute-start.10) | collective-permute-done | bytes 450592 | tf_op jit(solution)/shard_map/ppermute | solution.py:369
  103.2 0.1 pad_maximum_fusion.1
  103.3 1.3 collective-permute-start.14
  104.7 2.4 %collective-permute-start.13 = (f32[576,128]{1,0:T(8,128)S(1)}, f32[576,128]{1,0:T(8,128)S(1)}, u32[]{:S(2)}, u32[]{:S(2)}) collective-permute-start(f32[576,128]{1,0:T(8,128)S(1)} %get-tuple-element.61), channel_id=1, source_target_pairs={{1,2},{2,1},{5,6},{6,5},{9,10},{10,9},{13,14},{14,13},{17,18},{18,... | collective-permute-start | bytes 884744 | tf_op jit(solution)/shard_map/ppermute | solution.py:396
  107.1 1.3 collective-permute-start.12
  108.4 0.0 copy-done
  108.4 14.9 %main_update.1.refs_0_ = f32[4096,512]{1,0:T(8,128)S(1)} custom-call(s32[2]{0:T(128)S(1)} %pad_add_fusion.refs_0_, s32[512]{0:T(512)S(1)} %copy-done.2, f32[4096,512]{1,0:T(8,128)} %refs_2_.1, f32[512,512]{1,0:T(8,128)} %get-tuple-element.44.refs_1_.refs_3_, f32[512,512]{1,0:T(8,128)} %get-tuple-element.45.refs_2_.refs_4_, f32[4096,128]{1,0:T(8,128)S(1)} %copy-done, ...), custom_call_target="tpu_custom_call" | custom-call | tf_op jit(solution)/shard_map/main_update/pallas_call | solution.py:281
  123.3 0.0 collective-permute-done.11.refs_2_
  123.3 8.9 %collective-permute-done.15.refs_3_ = f32[2640,128]{1,0:T(8,128)S(1)} collective-permute-done((f32[2640,128]{1,0:T(8,128)S(1)}, f32[2640,128]{1,0:T(8,128)S(1)}, u32[]{:S(2)}, u32[]{:S(2)}) %collective-permute-start.15) | collective-permute-done | bytes 1351712 | tf_op jit(solution)/shard_map/ppermute | solution.py:395
  132.2 2.7 %last_update.3.refs_6_ = f32[4096,512]{1,0:T(8,128)} custom-call(f32[4096,512]{1,0:T(8,128)S(1)} %main_update.1.refs_0_, bf16[384,512]{1,0:T(8,128)(2,1)S(1)} %get-tuple-element.60.refs_1_.refs_2_, f32[2704,128]{1,0:T(8,128)S(1)} %collective-permute-done.11.refs_2_, f32[2640,128]{1,0:T(8,128)S(1)} %collective-permute-done.15.refs_3_), custom_call_target="tpu_custom_call" | custom-call | tf_op jit(solution)/shard_map/last_update/pallas_call | solution.py:322
  134.9 0.0 collective-permute-done.14.refs_5_
  134.9 1.9 %last_update.4.refs_5_ = f32[4096,512]{1,0:T(8,128)} custom-call(f32[4096,512]{1,0:T(8,128)S(1)} %main_update.1.refs_0_, bf16[384,512]{1,0:T(8,128)(2,1)S(1)} %get-tuple-element.62.refs_1_, bf16[384,512]{1,0:T(8,128)(2,1)S(1)} %get-tuple-element.60.refs_1_.refs_2_, f32[880,128]{1,0:T(8,128)S(1)} %collective-permute-done.7.refs_3_, ...), custom_call_target="tpu_custom_call", output_to_operand_aliasing={{}: (6, {})} | custom-call | tf_op jit(solution)/shard_map/last_update/pallas_call | solution.py:322
  136.7 0.0 collective-permute-done.12.refs_3_
  136.8 1.7 %collective-permute-done.13.refs_4_ = f32[576,128]{1,0:T(8,128)S(1)} collective-permute-done((f32[576,128]{1,0:T(8,128)S(1)}, f32[576,128]{1,0:T(8,128)S(1)}, u32[]{:S(2)}, u32[]{:S(2)}) %collective-permute-start.13) | collective-permute-done | bytes 294944 | tf_op jit(solution)/shard_map/ppermute | solution.py:396
  138.5 1.3 last_update.5
Async XLA Ops:
  0.0 9.5 %copy-start.2 = (s32[512]{0:T(512)S(1)}, s32[512]{0:T(512)}, u32[]{:S(2)}) copy-start(s32[512]{0:T(512)} %refs_1_.1) | copy-start | bytes 6148
  0.0 87.0 %collective-permute-start.9 = (f32[4096,128]{1,0:T(8,128)}, f32[4096,128]{1,0:T(8,128)S(1)}, u32[]{:S(2)}, u32[]{:S(2)}) collective-permute-start(f32[4096,128]{1,0:T(8,128)} %refs_5_.1), channel_id=1, source_target_pairs={{0,1},{1,0},{2,3},{3,2},{4,5},{5,4},{6,7},{7,6},{8,9},{9,8},{10,11... | collective-permute-start | bytes 6291464 | tf_op jit(solution)/shard_map/ppermute | solution.py:365
  2.7 76.8 %collective-permute-start.6 = (f32[2704,128]{1,0:T(8,128)}, f32[2704,128]{1,0:T(8,128)S(1)}, u32[]{:S(2)}, u32[]{:S(2)}) collective-permute-start(f32[2704,128]{1,0:T(8,128)} %get-tuple-element.41), channel_id=1, source_target_pairs={{0,2},{1,3},{2,0},{3,1},{4,6},{5,7},{6,4},{7,5},{8,10},{9,11},{10,... | collective-permute-start | bytes 4153352 | tf_op jit(solution)/shard_map/ppermute | solution.py:367
  5.3 81.6 %collective-permute-start.8 = (f32[512,128]{1,0:T(8,128)}, f32[512,128]{1,0:T(8,128)}, u32[]{:S(2)}, u32[]{:S(2)}) collective-permute-start(f32[512,128]{1,0:T(8,128)} %get-tuple-element.50), channel_id=1, source_target_pairs={{4,6},{5,7},{6,4},{7,5},{8,10},{9,11},{10,8},{11,9},{12,14},{13,15... | collective-permute-start | bytes 786440 | tf_op jit(solution)/shard_map/ppermute | solution.py:340
  17.3 2.7 %collective-permute-start = (f32[512,512]{1,0:T(8,128)S(1)}, f32[512,512]{1,0:T(8,128)S(1)}, u32[]{:S(2)}, u32[]{:S(2)}) collective-permute-start(f32[512,512]{1,0:T(8,128)S(1)} %get-tuple-element.16), channel_id=1, source_target_pairs={{0,4},{4,0},{8,12},{12,8},{16,20},{20,16},{24,28},{28,24},{1,5},{5... | collective-permute-start | bytes 3145736 | tf_op jit(solution)/shard_map/cond/branch_1_fun/ppermute | solution.py:336
  20.4 14.0 %collective-permute-start.1 = (f32[256,512]{1,0:T(8,128)S(1)}, f32[256,512]{1,0:T(8,128)S(1)}, u32[]{:S(2)}, u32[]{:S(2)}) collective-permute-start(f32[256,512]{1,0:T(8,128)S(1)} %get-tuple-element.67), channel_id=1, source_target_pairs={{0,8},{4,12},{8,0},{12,4},{16,24},{20,28},{24,16},{28,20},{1,9},{5... | collective-permute-start | bytes 1572872 | tf_op jit(solution)/shard_map/cond/branch_1_fun/ppermute | solution.py:336
  21.0 13.7 %collective-permute-start.3 = (f32[256,512]{1,0:T(8,128)S(1)}, f32[256,512]{1,0:T(8,128)S(1)}, u32[]{:S(2)}, u32[]{:S(2)}) collective-permute-start(f32[256,512]{1,0:T(8,128)S(1)} %get-tuple-element.68), channel_id=1, source_target_pairs={{0,16},{4,20},{8,24},{12,28},{16,0},{20,4},{24,8},{28,12},{1,17},{... | collective-permute-start | bytes 1572872 | tf_op jit(solution)/shard_map/cond/branch_1_fun/ppermute | solution.py:336
  34.8 13.0 %collective-permute-start.2 = (f32[256,512]{1,0:T(8,128)S(1)}, f32[256,512]{1,0:T(8,128)S(1)}, u32[]{:S(2)}, u32[]{:S(2)}) collective-permute-start(f32[256,512]{1,0:T(8,128)S(1)} %get-tuple-element.65), channel_id=1, source_target_pairs={{0,16},{4,20},{8,24},{12,28},{16,0},{20,4},{24,8},{28,12},{1,17},{... | collective-permute-start | bytes 1572872 | tf_op jit(solution)/shard_map/cond/branch_1_fun/ppermute | solution.py:336
  35.2 12.9 %collective-permute-start.4 = (f32[256,512]{1,0:T(8,128)S(1)}, f32[256,512]{1,0:T(8,128)S(1)}, u32[]{:S(2)}, u32[]{:S(2)}) collective-permute-start(f32[256,512]{1,0:T(8,128)S(1)} %get-tuple-element.66), channel_id=1, source_target_pairs={{0,8},{4,12},{8,0},{12,4},{16,24},{20,28},{24,16},{28,20},{1,9},{5... | collective-permute-start | bytes 1572872 | tf_op jit(solution)/shard_map/cond/branch_1_fun/ppermute | solution.py:336
  49.3 3.0 %collective-permute-start.5 = (f32[512,512]{1,0:T(8,128)}, f32[512,512]{1,0:T(8,128)}, u32[]{:S(2)}, u32[]{:S(2)}) collective-permute-start(f32[512,512]{1,0:T(8,128)} %pad_maximum_fusion), channel_id=1, source_target_pairs={{0,4},{4,0},{8,12},{12,8},{16,20},{20,16},{24,28},{28,24},{1,5},{5... | collective-permute-start | bytes 3145736 | tf_op jit(solution)/shard_map/cond/branch_1_fun/ppermute | solution.py:336
  52.3 41.4 %collective-permute-start.7 = (f32[880,128]{1,0:T(8,128)}, f32[880,128]{1,0:T(8,128)S(1)}, u32[]{:S(2)}, u32[]{:S(2)}) collective-permute-start(f32[880,128]{1,0:T(8,128)} %slice.16), channel_id=1, source_target_pairs={{0,2},{3,1},{4,6},{7,5},{8,10},{11,9},{12,14},{15,13},{16,18},{19,... | collective-permute-start | bytes 1351688 | tf_op jit(solution)/shard_map/ppermute | solution.py:387
  53.6 49.7 %collective-permute-start.10 = (f32[880,128]{1,0:T(8,128)}, f32[880,128]{1,0:T(8,128)S(1)}, u32[]{:S(2)}, u32[]{:S(2)}) collective-permute-start(f32[880,128]{1,0:T(8,128)} %slice.16), channel_id=1, source_target_pairs={{1,2},{2,1},{5,6},{6,5},{9,10},{10,9},{13,14},{14,13},{17,18},{18,... | collective-permute-start | bytes 1351688 | tf_op jit(solution)/shard_map/ppermute | solution.py:369
  79.5 43.8 %collective-permute-start.11 = (f32[2704,128]{1,0:T(8,128)S(1)}, f32[2704,128]{1,0:T(8,128)S(1)}, u32[]{:S(2)}, u32[]{:S(2)}) collective-permute-start(f32[2704,128]{1,0:T(8,128)S(1)} %collective-permute-done.6.refs_8_), channel_id=1, source_target_pairs={{2,3},{1,0},{6,7},{5,4},{10,11},{9,8},{14,15},{13,12},{18,19},{17,... | collective-permute-start | bytes 4153352 | tf_op jit(solution)/shard_map/ppermute | solution.py:392
  80.9 1.2 copy-start.1
  85.4 23.0 %copy-start = (f32[4096,128]{1,0:T(8,128)S(1)}, f32[4096,128]{1,0:T(8,128)}, u32[]{:S(2)}) copy-start(f32[4096,128]{1,0:T(8,128)} %refs_5_.1) | copy-start | bytes 6291460
  87.0 45.2 %collective-permute-start.15 = (f32[2640,128]{1,0:T(8,128)S(1)}, f32[2640,128]{1,0:T(8,128)S(1)}, u32[]{:S(2)}, u32[]{:S(2)}) collective-permute-start(f32[2640,128]{1,0:T(8,128)S(1)} %get-tuple-element.64), channel_id=1, source_target_pairs={{1,2},{2,1},{5,6},{6,5},{9,10},{10,9},{13,14},{14,13},{17,18},{18,... | collective-permute-start | bytes 4055048 | tf_op jit(solution)/shard_map/ppermute | solution.py:395
  103.3 31.6 %collective-permute-start.14 = (f32[1760,128]{1,0:T(8,128)S(1)}, f32[1760,128]{1,0:T(8,128)S(1)}, u32[]{:S(2)}, u32[]{:S(2)}) collective-permute-start(f32[1760,128]{1,0:T(8,128)S(1)} %pad_maximum_fusion.1), channel_id=1, source_target_pairs={{2,3},{1,0},{6,7},{5,4},{10,11},{9,8},{14,15},{13,12},{18,19},{17,... | collective-permute-start | bytes 2703368 | tf_op jit(solution)/shard_map/ppermute | solution.py:399
  104.7 33.8 %collective-permute-start.13 = (f32[576,128]{1,0:T(8,128)S(1)}, f32[576,128]{1,0:T(8,128)S(1)}, u32[]{:S(2)}, u32[]{:S(2)}) collective-permute-start(f32[576,128]{1,0:T(8,128)S(1)} %get-tuple-element.61), channel_id=1, source_target_pairs={{1,2},{2,1},{5,6},{6,5},{9,10},{10,9},{13,14},{14,13},{17,18},{18,... | collective-permute-start | bytes 884744 | tf_op jit(solution)/shard_map/ppermute | solution.py:396
  107.1 29.7 %collective-permute-start.12 = (f32[512,128]{1,0:T(8,128)}, f32[512,128]{1,0:T(8,128)S(1)}, u32[]{:S(2)}, u32[]{:S(2)}) collective-permute-start(f32[512,128]{1,0:T(8,128)} %collective-permute-done.8.refs_7_), channel_id=1, source_target_pairs={{6,7},{5,4},{10,11},{9,8},{14,15},{13,12},{18,19},{17,16},{22,23},... | collective-permute-start | bytes 786440 | tf_op jit(solution)/shard_map/ppermute | solution.py:340
